TPU v7x, 256 devices: a whole 4x4x8 slice. The times are simulated.
256 devices in a mesh: req: 4 (over x_hi, core), tp: 64 (over z, x_lo, y).
Axes of the slice: x: 4 (x_hi: 2, x_lo: 2; x = x_hi * 2 + x_lo), y: 4, z: 8, core: 2. Of those that a mesh axis runs over, the one named last changes fastest.
Arguments:
- hidden: bfloat16 [4096, 8192], P('req', 'tp'), may hold values from -6 to 6
- query_weight: bfloat16 [8192, 8192], P(None, 'tp'), may hold values from -0.0625 to 0.0625
- key_value_weight: bfloat16 [8192, 2048], P(None, 'tp'), may hold values from -0.0625 to 0.0625
- adapter_down_maps: bfloat16 [64, 8192, 32], P('req', 'tp'), may hold values from -0.0625 to 0.0625
- adapter_up_maps: bfloat16 [64, 32, 8192], P('req', None, 'tp'), may hold values from -1 to 1
- token_request_start: int32 [4096], P('req'), may hold values from 0 to 31, as said below
- adapter_per_block: int32 [32], P('req'), may hold values from 0 to 63
Outputs:
- context: bfloat16 [4096, 8192], P('req', 'tp')
Inputs may be any that keep to these rules, and one draw needn't show every extreme that they name: `token_request_start`: each run of 1024 tokens along the req split holds whole requests; a request is a run of whole blocks of 128 tokens; the last block of each such run is a request of its own.
All inputs are finite; a program needn't handle non-finite values.
Results may differ from a plain program's by a relative error of at most 0.012.
Values may be sent and summed in bfloat16 or wider, within the bound.
No kernel may reach another device: no remote copies, remote signals or barrier semaphores. Data moves between devices by JAX's collectives and lax.ppermute only.
A program may use at most 64 MiB of HBM per device.

v0:
```python
import math

import jax
import jax.numpy as jnp
from jax import lax
from jax.sharding import PartitionSpec as P

HEAD_SIZE = 128
BLOCK = 128


ROPE_BASE = 500000.0
ADAPTER_SCALE = 2.0


def from_partner(block, axis, bit):
    count = lax.axis_size(axis)
    route = []
    for low in range(count):
        high = low | 1 << bit
        if high != low and high < count:
            route += [(low, high), (high, low)]
    return lax.ppermute(block, axis, route)


def rotate(vectors, positions):
    half_width = vectors.shape[-1] // 2
    steps_half = jnp.arange(half_width, dtype=jnp.float32)
    inverse = jnp.exp(-(2.0 * steps_half / vectors.shape[-1]) * math.log(ROPE_BASE))
    angles = positions.astype(jnp.float32)[:, None] * inverse[None, :]
    cosines = jnp.cos(angles)
    sines = jnp.sin(angles)
    front_half = vectors[:, :half_width]
    back_half = vectors[:, half_width:]
    return jnp.concatenate(
        [front_half * cosines - back_half * sines, back_half * cosines + front_half * sines], axis=1
    )


def attend(queries, key_rows, value_rows, request):
    group_rows = queries.shape[0]
    block_rows = min(512, group_rows)
    block_total = group_rows // block_rows
    places = jnp.arange(group_rows, dtype=jnp.int32)
    score_scale = 1.0 / math.sqrt(queries.shape[1])

    def one_block(block_index):
        begin_row = block_index * block_rows
        q_blk = lax.dynamic_slice_in_dim(queries, begin_row, block_rows, 0)
        r_blk = lax.dynamic_slice_in_dim(request, begin_row, block_rows, 0)
        p_blk = lax.dynamic_slice_in_dim(places, begin_row, block_rows, 0)
        scores = (
            lax.dot_general(
                q_blk, key_rows, (((1,), (1,)), ((), ())), preferred_element_type=jnp.float32
            )
            * score_scale
        )
        allowed = (r_blk[:, None] == request[None, :]) & (places[None, :] <= p_blk[:, None])
        scores = jnp.where(allowed, scores, jnp.float32(-1e30))
        row_max = jnp.max(scores, axis=1, keepdims=True)
        weights = jnp.exp(scores - row_max)
        probs = (weights / jnp.sum(weights, axis=1, keepdims=True)).astype(jnp.bfloat16)
        return jnp.dot(probs, value_rows, preferred_element_type=jnp.float32).astype(jnp.bfloat16)

    blocks = lax.map(one_block, jnp.arange(block_total, dtype=jnp.int32))
    return blocks.reshape(group_rows, value_rows.shape[1])


def body(
    hidden,
    query_weight,
    key_value_weight,
    adapter_down_maps,
    adapter_up_maps,
    token_request_start,
    adapter_per_block,
):
    group_rows = hidden.shape[0]
    local_width = hidden.shape[1]
    head_cols = query_weight.shape[1]
    kv_cols = key_value_weight.shape[1]
    device = lax.axis_index("tp")
    spread = 2 * HEAD_SIZE // kv_cols
    piece = lax.all_gather(hidden, "tp", axis=1, tiled=True)
    query_total = jnp.dot(piece, query_weight, preferred_element_type=jnp.float32)
    kv_sum = jnp.dot(piece, key_value_weight, preferred_element_type=jnp.float32)
    down_all, up_all = (
        lax.all_gather(adapter_down_maps, "req", axis=0, tiled=True),
        lax.all_gather(adapter_up_maps, "req", axis=0, tiled=True),
    )
    block_total = group_rows // BLOCK
    chosen_down = down_all[adapter_per_block]
    chosen_up = up_all[adapter_per_block]
    block_grouped = hidden.reshape(block_total, BLOCK, local_width)
    reduced_part = jnp.einsum(
        "uqo,uop->uqp", block_grouped, chosen_down, preferred_element_type=jnp.float32
    )
    reduced_rank = lax.psum(reduced_part, "tp").astype(jnp.bfloat16)
    adapter_term = jnp.einsum(
        "epl,elm->epm", reduced_rank, chosen_up, preferred_element_type=jnp.float32
    ).reshape(group_rows, head_cols)
    places = lax.axis_index("req") * group_rows + jnp.arange(group_rows, dtype=jnp.int32)
    positions = places - token_request_start * BLOCK
    complete_query = query_total + ADAPTER_SCALE * adapter_term
    kv_piece = kv_sum.astype(jnp.bfloat16)
    head_block = kv_piece
    for bit_number in range(spread.bit_length() - 1):
        partner = from_partner(head_block, "tp", bit_number)
        upper_side = device // 2**bit_number % 2
        head_block = jnp.where(
            upper_side == 1,
            jnp.concatenate([partner, head_block], axis=1),
            jnp.concatenate([head_block, partner], axis=1),
        )
    key_rows = rotate(head_block[:, :HEAD_SIZE].astype(jnp.float32), positions).astype(jnp.bfloat16)
    value_rows = head_block[:, HEAD_SIZE:]
    head_query = rotate(complete_query, positions).astype(jnp.bfloat16)
    outputs = attend(head_query, key_rows, value_rows, token_request_start)
    return outputs


def solution(mesh):
    in_specs = (
        P("req", "tp"),
        P(None, "tp"),
        P(None, "tp"),
        P("req", "tp", None),
        P("req", None, "tp"),
        P("req"),
        P("req"),
    )
    out_specs = P("req", "tp")
    return jax.shard_map(body, mesh=mesh, in_specs=in_specs, out_specs=out_specs, check_vma=False)
```

profile of v0, /device:TPU:2, one launch (start us, length us, event | category | flops | bytes accessed | tf_op | source)
XLA Modules:
  0.0 410.2 jit_solution(10693275927732517615)
XLA Ops:
  6.5 0.7 all-gather.2.cloned.1.call-update
  7.3 0.7 compare_select_fusion
  8.0 8.5 %all_gather.10 = bf16[64,128,32]{1,2,0:T(8,128)(2,1)S(1)} all-gather(bf16[16,128,32]{1,2,0:T(8,128)(2,1)} %param.12), channel_id=1, replica_groups=mesh['req'=4,'tp'=64] {'req'}, dimensions={0}, use_global_device_ids=true | all-gather | bytes 655360 | tf_op jit(solution)/shard_map/all_gather | solution.py:88
  17.0 1.2 convolution_bitcast_fusion
  18.2 10.1 %all_gather.11 = bf16[64,32,128]{2,1,0:T(8,128)(2,1)S(1)} all-gather(bf16[16,32,128]{2,1,0:T(8,128)(2,1)} %param.13), channel_id=1, replica_groups=mesh['req'=4,'tp'=64] {'req'}, dimensions={0}, use_global_device_ids=true | all-gather | bytes 655360 | tf_op jit(solution)/shard_map/all_gather | solution.py:89
  28.9 309.0 %all-reduce.1 = bf16[8,128,32]{1,2,0:T(8,128)(2,1)S(1)} all-reduce(f32[8,128,32]{1,2,0:T(8,128)S(1)} %convolution_bitcast_fusion), channel_id=1, replica_groups=mesh['req'=4,'tp'=64] {'tp'}, use_global_device_ids=true, to_apply=%region_0.0 | all-reduce | flops 32768 | bytes 196608 | tf_op jit(solution)/shard_map/psum | solution.py:98
  337.9 19.3 %all-gather.2.cloned.1.call-done = bf16[1024,8192]{1,0:T(8,128)(2,1)} async-done(((bf16[1024,128]{1,0:T(8,128)(2,1)}), bf16[1024,8192]{1,0:T(8,128)(2,1)}) %all-gather.2.cloned.1.call-update) | async-done | bytes 16777232 | tf_op jit(solution)/shard_map/all_gather | solution.py:84
  357.1 10.8 %convolution_convert_fusion.1 = bf16[1024,32]{0,1:T(8,128)(2,1)S(1)} fusion(bf16[1024,8192]{1,0:T(8,128)(2,1)} %all-gather.2.cloned.1.call-done, bf16[8192,32]{0,1:T(8,128)(2,1)S(1)} %copy-done.1), kind=kOutput, calls=%fused_computation.14 | convolution fusion | flops 536903680 | bytes 17367040 | tf_op jit(solution)/shard_map/dot_general | solution.py:86
  368.3 4.0 collective-permute-done
  372.3 2.1 collective-permute-start.1
  374.6 4.4 %collective-permute-done.1 = bf16[1024,64]{0,1:T(8,128)(2,1)} collective-permute-done((bf16[1024,64]{0,1:T(8,128)(2,1)S(1)}, bf16[1024,64]{0,1:T(8,128)(2,1)}, u32[]{:S(2)}, u32[]{:S(2)}) %collective-permute-start.1) | collective-permute-done | bytes 131104 | tf_op jit(solution)/shard_map/ppermute | solution.py:23
  378.9 1.0 maximum_select_fusion.1
  380.0 1.6 collective-permute-start.2
  381.6 11.4 %convolution_add_fusion = f32[1024,128]{0,1:T(8,128)S(1)} fusion(f32[1024,128]{0,1:T(8,128)S(1)} %copy.16, bf16[1024,8192]{1,0:T(8,128)(2,1)} %all-gather.2.cloned.1.call-done, bf16[8192,128]{1,0:T(8,128)(2,1)S(1)} %copy-done), kind=kOutput, calls=%fused_computation.12 | convolution fusion | flops 2147614720 | bytes 19922944 | tf_op jit(solution)/shard_map/dot_general | solution.py:85
  393.1 1.2 maximum_select_fusion
  394.4 1.2 fusion.18
  396.0 6.7 %while.11 = (s32[]{:T(128)}, bf16[2,512,128]{2,1,0:T(8,128)(2,1)S(1)}, s32[2]{0:T(128)S(1)}, s32[1024]{0:T(1024)S(1)}, s32[1024]{0:T(1024)S(1)}, /*index=5*/bf16...) while((s32[]{:T(128)}, ...), condition=%wide.region_4.5_spmd.clone, body=%wide.region_1.4_spmd.clone.sunk | while | flops 274267136 | bytes 7108799 | solution.py:65
  396.0 0.6 dynamic_slice.26
  397.4 0.8 fusion.41
  398.7 0.6 fusion.43
  399.4 0.6 dynamic_slice.26
  400.8 0.8 fusion.41
  402.1 0.6 fusion.43
  402.7 0.7 copy-done.4
  (33 shorter events, 3.5 us)
Async XLA Ops:
  6.5 375.1 %copy-start = (bf16[8192,128]{1,0:T(8,128)(2,1)S(1)}, bf16[8192,128]{1,0:T(8,128)(2,1)}, u32[]{:S(2)}) copy-start(bf16[8192,128]{1,0:T(8,128)(2,1)} %param.10) | copy-start | bytes 6291460
  6.5 350.6 %copy-start.1 = (bf16[8192,32]{0,1:T(8,128)(2,1)S(1)}, bf16[8192,32]{0,1:T(8,128)(2,1)}, u32[]{:S(2)}) copy-start(bf16[8192,32]{0,1:T(8,128)(2,1)} %param.11) | copy-start | bytes 1572868
  6.5 350.6 %all-gather.2.cloned.1.call-start = ((), (), s32[]{:S(2)}) async-start(), calls=%async_computation | async-start | bytes 17039360 | tf_op jit(solution)/shard_map/all_gather | solution.py:84
  337.9 36.5 %copy-start.2 = (s32[1024]{0:T(1024)S(1)}, s32[1024]{0:T(1024)}, u32[]{:S(2)}) copy-start(s32[1024]{0:T(1024)} %param.14) | copy-start | bytes 12292
  367.9 4.3 %collective-permute-start = (bf16[1024,32]{0,1:T(8,128)(2,1)S(1)}, bf16[1024,32]{0,1:T(8,128)(2,1)S(1)}, u32[]{:S(2)}, u32[]{:S(2)}) collective-permute-start(bf16[1024,32]{0,1:T(8,128)(2,1)S(1)} %convolution_convert_fusion.1), channel_id=1, source_target_pairs={{0,1},{1,0},{2,3},{3,2},{4,5},{5,4},{6,7},{7,6},{8,9},{9,8},{10,11... | collective-permute-start | bytes 196616 | tf_op jit(solution)/shard_map/ppermute | solution.py:23
  372.3 6.7 %collective-permute-start.1 = (bf16[1024,64]{0,1:T(8,128)(2,1)S(1)}, bf16[1024,64]{0,1:T(8,128)(2,1)}, u32[]{:S(2)}, u32[]{:S(2)}) collective-permute-start(bf16[1024,64]{0,1:T(8,128)(2,1)S(1)} %maximum_select_fusion.2), channel_id=1, source_target_pairs={{0,2},{2,0},{1,3},{3,1},{4,6},{6,4},{5,7},{7,5},{8,10},{10,8},{9,1... | collective-permute-start | bytes 393224 | tf_op jit(solution)/shard_map/ppermute | solution.py:23
  380.0 13.1 %collective-permute-start.2 = (bf16[1024,128]{0,1:T(8,128)(2,1)S(1)}, bf16[1024,128]{0,1:T(8,128)(2,1)}, u32[]{:S(2)}, u32[]{:S(2)}) collective-permute-start(bf16[1024,128]{0,1:T(8,128)(2,1)S(1)} %maximum_select_fusion.1), channel_id=1, source_target_pairs={{0,4},{4,0},{1,5},{5,1},{2,6},{6,2},{3,7},{7,3},{8,12},{12,8},{9,1... | collective-permute-start | bytes 786440 | tf_op jit(solution)/shard_map/ppermute | solution.py:23
  394.4 1.7 copy-start.3
  402.7 0.7 copy-start.4
Sparse Core Ops, SparseCore 0:
  9.1 347.9 all-gather.1
where the time goes:
time: 416 us; the launch traced here: 410 us
  blocking collectives  328 us (79%)
  waiting for transfers between devices  28.3 us (7%)
  matrix products  26.5 us (6%)
  between operations  13.6 us (3%)
  other arithmetic  5.36 us (1%)
    psum x1, blocking collectives, body(): reduced_rank = lax.psum(reduced_part, 'tp').astype(jnp.bfloat16)  309 us
    all_gather x1, waiting for transfers between devices, body(): piece = lax.all_gather(hidden, 'tp', axis=1, tiled=True)  19.3 us
    dot_general x1, matrix products, body(): jnp.dot(piece, query_weight, preferred_element_type=jnp.float32)  11.4 us
    dot_general x1, matrix products, body(): jnp.dot(piece, key_value_weight, preferred_element_type=jnp.float32)  10.8 us
    all_gather x1, blocking collectives, body(): lax.all_gather(adapter_up_maps, 'req', axis=0, tiled=True)  10.1 us
    all_gather x1, blocking collectives, body(): lax.all_gather(adapter_down_maps, 'req', axis=0, tiled=True)  8.48 us
  transfers between devices with their start and end apart: 4, of which 3 were waited for; matrix products, arithmetic and copies ran while one was open for 4% of the time, Pallas kernels for 0%

commit v1 on v0

v1 whole, which is shorter than its diff:
```python
import functools
import math

import jax
import jax.numpy as jnp
from jax import lax
from jax.experimental import pallas as pl
from jax.experimental.pallas import tpu as pltpu
from jax.sharding import Mesh, PartitionSpec as P

HEAD_SIZE = 128
BLOCK = 128
RANK = 32
ROPE_BASE = 500000.0
ADAPTER_SCALE = 2.0
NXH, NC, NZ, NX, NY = 2, 2, 8, 2, 4
REQ_AXES = ("xh", "c")
TP_AXES = ("z", "xl", "y")
NP = NX * NY
VMEM = pl.BlockSpec(memory_space=pltpu.VMEM)
SMEM = pl.BlockSpec(memory_space=pltpu.SMEM)


def z_shift(v, s):
    return lax.ppermute(v, "z", [(i, (i + s) % NZ) for i in range(NZ)])


def z_xor(v, s):
    return lax.ppermute(v, "z", [(i, i ^ s) for i in range(NZ)])


def y_xor(v, s):
    return lax.ppermute(v, "y", [(i, i ^ s) for i in range(NY)])


def x_swap(v):
    return lax.ppermute(v, "xl", [(0, 1), (1, 0)])


def core_swap(v):
    return lax.ppermute(v, "c", [(0, 1), (1, 0)])


def xh_swap(v):
    return lax.ppermute(v, "xh", [(0, 1), (1, 0)])


def plane_send(v, d):
    dx, dy = divmod(d, NY)
    route = [
        (a * NY + b, (a ^ dx) * NY + (b + dy) % NY) for a in range(NX) for b in range(NY)
    ]
    return lax.ppermute(v, ("xl", "y"), route)


def weight_send(v, d):
    dx, dy = divmod(d, NY)
    route = []
    for xh in range(NXH):
        for c in range(NC):
            for xl in range(NX):
                for y in range(NY):
                    at = xh * NX + xl
                    if dx:
                        to = at ^ 1 if c == 0 else (at + 1 if at % 2 else at - 1) % 4
                    else:
                        to = at
                    src = ((xh * NC + c) * NX + xl) * NY + y
                    dst = ((to // NX * NC + c) * NX + to % NX) * NY + (y + dy) % NY
                    route.append((src, dst))
    return lax.ppermute(v, ("xh", "c", "xl", "y"), route)


def pack_kernel(s_ref, wq_ref, kv_ref, *outs):
    z, xl, y, c = s_ref[0], s_ref[1], s_ref[2], s_ref[3]

    def fill(out, dx, dy, half):
        p = (xl ^ dx) * NY + ((y + dy) & (NY - 1))
        for j in range(NZ // 2):
            zz = (z + half * (NZ // 2) + j) & (NZ - 1)
            row = pl.multiple_of((zz * NP + p) * 128, 128)
            out[j * 128 : (j + 1) * 128, :] = wq_ref[pl.ds(row, 128), :]
            out[512 + j * 32 : 512 + (j + 1) * 32, :] = kv_ref[:, pl.ds(row, 128)]

    for d in range(NP):
        dx, dy = divmod(d, NY)
        fill(outs[d], dx, dy, c)
    fill(outs[NP], 0, 0, 1 - c)


def low_kernel(s_ref, ad_ref, h_ref, near_ref, far_ref, out_ref):
    c, xh = s_ref[3], s_ref[4]
    per = near_ref.shape[1]
    for b in range(h_ref.shape[0] // BLOCK):
        a = ad_ref[b]
        owner = a // per
        at = a - owner * per
        xr, cr = (owner // NC) ^ xh, (owner % NC) ^ c
        down = jnp.where(cr == 0, near_ref[xr, at, 0:RANK, :], far_ref[xr, at, 0:RANK, :])
        out_ref[:, b * BLOCK : (b + 1) * BLOCK] = lax.dot_general(
            down,
            h_ref[b * BLOCK : (b + 1) * BLOCK, :],
            (((1,), (1,)), ((), ())),
            preferred_element_type=jnp.float32,
        )


def matmul_kernel(s_ref, *refs):
    h_refs, wm = refs[0:8], refs[8:16]
    wo_own, wo_st = refs[16], refs[17]
    outs = refs[18:26]
    hbuf, wq_m, wq_o, kv_m, kv_o = refs[26:31]
    c = s_ref[3]
    for j in range(8):
        hbuf[:, j * 128 : (j + 1) * 128] = h_refs[j][...]
    for d in range(NP):
        own = wm[d]
        oth = wo_own if d == 0 else wo_st.at[d - 1]
        dx, dy = divmod(d, NY)
        wq_m[dy, :, dx * 128 : (dx + 1) * 128] = own[0:512, :]
        wq_o[dy, :, dx * 128 : (dx + 1) * 128] = oth[0:512, :]
        for j in range(4):
            kv_m[d * 32 : (d + 1) * 32, j * 128 : (j + 1) * 128] = own[512 + j * 32 : 544 + j * 32, :]
            kv_o[d * 32 : (d + 1) * 32, j * 128 : (j + 1) * 128] = oth[512 + j * 32 : 544 + j * 32, :]
    at_m = pl.multiple_of(c * 512, 512)
    at_o = pl.multiple_of((1 - c) * 512, 512)
    tile = 256
    nt = (((1,), (1,)), ((), ()))

    def step(i, carry):
        r = pl.multiple_of(i * tile, tile)
        hm = hbuf[pl.ds(r, tile), pl.ds(at_m, 512)]
        ho = hbuf[pl.ds(r, tile), pl.ds(at_o, 512)]
        kv = lax.dot_general(kv_m[...], hm, nt, preferred_element_type=jnp.float32)
        kv += lax.dot_general(kv_o[...], ho, nt, preferred_element_type=jnp.float32)
        kv = kv.astype(jnp.bfloat16)
        for d in range(NP):
            for t in range(tile // 128):
                at = pl.multiple_of(1024 + (i * (tile // 128) + t) * 32, 32)
                outs[d][pl.ds(at, 32), :] = kv[d * 32 : (d + 1) * 32, t * 128 : (t + 1) * 128]
        for dy in range(NY):
            q = jnp.dot(hm, wq_m[dy], preferred_element_type=jnp.float32)
            q += jnp.dot(ho, wq_o[dy], preferred_element_type=jnp.float32)
            q = q.astype(jnp.bfloat16)
            outs[dy][pl.ds(r, tile), :] = q[:, 0:128]
            outs[NY + dy][pl.ds(r, tile), :] = q[:, 128:256]
        return carry

    lax.fori_loop(0, 1024 // tile, step, 0)


def attention_kernel(s_ref, ad_ref, lo_ref, *refs):
    pieces = refs[0:8]
    kv_near, kv_far, low_ref, near_ref, far_ref, cos_ref, sin_ref = refs[8:15]
    out_ref = refs[15]
    kvt, k_buf, v_buf = refs[16:19]
    xl, y, c, xh = s_ref[1], s_ref[2], s_ref[3], s_ref[4]
    for half, ref in enumerate((kv_near, kv_far)):
        for i, m in enumerate((0, 2, 1, 3)):
            p = (xl ^ half) * NY + (y ^ m)
            at = pl.multiple_of(p * 32, 32)
            for t in range(8):
                kvt[pl.ds(at, 32), t * 128 : (t + 1) * 128] = ref[i * 256 + t * 32 : i * 256 + (t + 1) * 32, :]

    def rope(v, rows):
        return v * cos_ref[rows, :] + pltpu.roll(v, 64, 1) * sin_ref[rows, :]

    for t in range(8):
        rows = slice(t * 128, (t + 1) * 128)
        k = kvt[0:128, rows].astype(jnp.float32).T
        k_buf[rows, :] = rope(k, rows).astype(jnp.bfloat16)
        v_buf[rows, :] = kvt[128:256, rows].astype(jnp.float32).T.astype(jnp.bfloat16)
    per = near_ref.shape[1]
    factor = math.log2(math.e) / math.sqrt(HEAD_SIZE)
    for b in range(8):
        rows = slice(b * 128, (b + 1) * 128)
        a = ad_ref[b]
        owner = a // per
        at = a - owner * per
        xr, cr = (owner // NC) ^ xh, (owner % NC) ^ c
        up = jnp.where(cr == 0, near_ref[xr, at, RANK : 2 * RANK, :], far_ref[xr, at, RANK : 2 * RANK, :])
        low = low_ref[:, rows].T.astype(jnp.bfloat16)
        q = ADAPTER_SCALE * jnp.dot(low, up, preferred_element_type=jnp.float32)
        for piece in pieces:
            q += piece[rows, :].astype(jnp.float32)
        q = rope(q, rows).astype(jnp.bfloat16)
        n = (b + 1) * 128
        s = lax.dot_general(
            q, k_buf[0:n, :], (((1,), (1,)), ((), ())), preferred_element_type=jnp.float32
        )
        col = lax.broadcasted_iota(jnp.int32, (128, n), 1)
        row = lax.broadcasted_iota(jnp.int32, (128, n), 0) + b * 128
        allowed = (col >= lo_ref[b]) & (col <= row)
        s = jnp.where(allowed, s, -1e30)
        e = jnp.exp2((s - jnp.max(s, axis=1, keepdims=True)) * factor)
        probs = (e / jnp.sum(e, axis=1, keepdims=True)).astype(jnp.bfloat16)
        out_ref[rows, :] = jnp.dot(
            probs, v_buf[0:n, :], preferred_element_type=jnp.float32
        ).astype(jnp.bfloat16)


def rope_tables(positions):
    half = HEAD_SIZE // 2
    steps = jnp.arange(half, dtype=jnp.float32)
    inverse = jnp.exp(-(2.0 * steps / HEAD_SIZE) * math.log(ROPE_BASE))
    angles = positions.astype(jnp.float32)[:, None] * inverse[None, :]
    cosines, sines = jnp.cos(angles), jnp.sin(angles)
    return jnp.concatenate([cosines, cosines], 1), jnp.concatenate([-sines, sines], 1)


def after(value, *others):
    return lax.optimization_barrier((value, *others))[0]


def body(hidden, query_weight, key_value_weight, down_maps, up_maps, request_start, adapters):
    rows = hidden.shape[0]
    bf16, f32 = jnp.bfloat16, jnp.float32
    place = [lax.axis_index(a) for a in ("z", "xl", "y", "c", "xh")]
    scalars = jnp.stack(place).astype(jnp.int32)

    maps = jnp.concatenate([jnp.transpose(down_maps, (0, 2, 1)), up_maps], axis=1)
    near = jnp.stack([maps, xh_swap(maps)])
    far = core_swap(near)

    right, left = [hidden], [hidden]
    sends = pl.pallas_call(
        pack_kernel,
        out_shape=[jax.ShapeDtypeStruct((640, 128), bf16)] * (NP + 1),
        in_specs=[SMEM, VMEM, VMEM],
        out_specs=[VMEM] * (NP + 1),
        name="pack",
    )(scalars, query_weight, key_value_weight.T)
    got = {0: sends[0]}
    batches = ((6, 5), (7, 2), (1, 3), (4,))
    for step in range(4):
        right.append(z_shift(right[-1], 1))
        if step < 3:
            left.append(z_shift(left[-1], -1))
        for d in batches[step]:
            got[d] = weight_send(after(sends[d], right[step]) if step else sends[d], d)
    flip = [dx * NY + (-dy) % NY for dx in range(NX) for dy in range(NY)]
    mine = [got[flip[d]] for d in range(NP)]
    other = core_swap(jnp.stack(mine[1:]))

    low = pl.pallas_call(
        low_kernel,
        out_shape=jax.ShapeDtypeStruct((RANK, rows), f32),
        in_specs=[SMEM, SMEM, VMEM, VMEM, VMEM],
        out_specs=VMEM,
        name="low",
    )(scalars, adapters, hidden, near, far)
    low = low + x_swap(low)
    low = low + y_xor(low, 1)
    low = low + y_xor(low, 2)
    low = low + z_xor(low, 1)
    low = low + z_xor(low.astype(bf16), 2).astype(f32)
    low = low + z_xor(low.astype(bf16), 4).astype(f32)

    shards = [hidden, left[1], left[2], left[3], right[4], right[3], right[2], right[1]]
    parts = pl.pallas_call(
        matmul_kernel,
        out_shape=[jax.ShapeDtypeStruct((rows + 256, 128), bf16)] * NP,
        in_specs=[SMEM] + [VMEM] * 18,
        out_specs=[VMEM] * NP,
        scratch_shapes=[
            pltpu.VMEM((rows, 1024), bf16),
            pltpu.VMEM((NY, 512, 256), bf16),
            pltpu.VMEM((NY, 512, 256), bf16),
            pltpu.VMEM((256, 512), bf16),
            pltpu.VMEM((256, 512), bf16),
        ],
        name="product",
    )(scalars, *shards, *mine, sends[NP], other)
    pieces = [parts[0]] + [plane_send(parts[d], d) for d in (6, 5, 7, 2, 1, 3, 4)]
    kv = sum(p[rows:].astype(f32) for p in pieces).astype(bf16)
    kv = jnp.concatenate([kv, y_xor(kv, 2)])
    kv = jnp.concatenate([kv, y_xor(kv, 1)])
    kv_far = x_swap(kv)

    first = lax.axis_index("xh") * NC + lax.axis_index("c")
    places = first * rows + jnp.arange(rows, dtype=jnp.int32)
    cosines, sines = rope_tables(places - request_start * BLOCK)
    lowest = request_start[::BLOCK] * BLOCK - first * rows
    return pl.pallas_call(
        attention_kernel,
        out_shape=jax.ShapeDtypeStruct((rows, HEAD_SIZE), bf16),
        in_specs=[SMEM, SMEM, SMEM] + [VMEM] * 15,
        out_specs=VMEM,
        scratch_shapes=[
            pltpu.VMEM((256, rows), bf16),
            pltpu.VMEM((rows, HEAD_SIZE), bf16),
            pltpu.VMEM((rows, HEAD_SIZE), bf16),
        ],
        name="attention",
    )(scalars, adapters, lowest, *pieces, kv, kv_far, low, near, far, cosines, sines)


def solution(mesh):
    fine = Mesh(mesh.devices.reshape(NXH, NC, NZ, NX, NY), REQ_AXES + TP_AXES)
    in_specs = (
        P(REQ_AXES, TP_AXES),
        P(None, TP_AXES),
        P(None, TP_AXES),
        P(REQ_AXES, TP_AXES, None),
        P(REQ_AXES, None, TP_AXES),
        P(REQ_AXES),
        P(REQ_AXES),
    )
    return jax.shard_map(
        body, mesh=fine, in_specs=in_specs, out_specs=P(REQ_AXES, TP_AXES), check_vma=False
    )
```

time: 416 us -> 160 us (0.38); the launches traced: 410 us -> 160 us
  blocking collectives: 328 us -> 0 us
  starting transfers between devices: 3.78 us -> 55 us
  waiting for transfers between devices: 28.3 us -> 67.6 us
  matrix products: 26.5 us -> 0 us
  Pallas kernels: 0 us -> 21.7 us
  between operations: 13.6 us -> 0.35 us
  local copies, waits for them, and re-layouts: 3.86 us -> 8.39 us
    psum x1 -> x0, blocking collectives: 309 us -> none  [body(): reduced_rank = lax.psum(reduced_part, 'tp').astype(jnp.bfloat16)]
    ppermute x3 -> x33, waiting for transfers between devices: 8.3 us -> 67.6 us  [the longest x7 24 us: z_shift(): return lax.ppermute(v, 'z', [(i, (i + s) % NZ) for i in range(NZ)])]
    ppermute x3 -> x33, starting transfers between devices: 3.78 us -> 55 us  [the longest x7 16.8 us: plane_send(): return lax.ppermute(v, ('xl', 'y'), route)]
    dot_general x8 -> x0, matrix products: 26.5 us -> none  [the longest x1 11.4 us: body(): jnp.dot(piece, query_weight, preferred_element_type=jnp.float32)]
    pallas_call x0 -> x4, Pallas kernels: none -> 21.7 us  [the longest x1 8.47 us: body(): pl.pallas_call(attention_kernel, out_shape=jax.ShapeDtypeStruct((rows, HE...]
    all_gather x1 -> x0, waiting for transfers between devices: 19.3 us -> none  [body(): piece = lax.all_gather(hidden, 'tp', axis=1, tiled=True)]
    all_gather x2 -> x0, blocking collectives: 18.6 us -> none  [the longest x1 10.1 us: body(): lax.all_gather(adapter_up_maps, 'req', axis=0, tiled=True)]
    unnamed x12 -> x64, local copies, waits for them, and re-layouts: 1.06 us -> 6.96 us
  transfers between devices with their start and end apart: 4 -> 33, of which waited for: 3 -> 17; matrix products, arithmetic and copies ran while one was open for 4% -> 7% of each run, Pallas kernels for 0% -> 8%
where the time goes in v1:
time: 160 us
  waiting for transfers between devices  67.6 us (42%)
  starting transfers between devices  55 us (34%)
  Pallas kernels  21.7 us (14%)
  local copies, waits for them, and re-layouts  8.39 us (5%)
  other arithmetic  6.66 us (4%)
    ppermute x7, waiting for transfers between devices, z_shift(): return lax.ppermute(v, 'z', [(i, (i + s) % NZ) for i in range(NZ)])  24 us
    ppermute x7, starting transfers between devices, plane_send(): return lax.ppermute(v, ('xl', 'y'), route)  16.8 us
    ppermute x7, starting transfers between devices, weight_send(): return lax.ppermute(v, ('xh', 'c', 'xl', 'y'), route)  16.4 us
    ppermute x7, waiting for transfers between devices, weight_send(): return lax.ppermute(v, ('xh', 'c', 'xl', 'y'), route)  9.65 us
    ppermute x1, waiting for transfers between devices, xh_swap(): return lax.ppermute(v, 'xh', [(0, 1), (1, 0)])  9.22 us
    ppermute x4, waiting for transfers between devices, y_xor(): return lax.ppermute(v, 'y', [(i, i ^ s) for i in range(NY)])  8.48 us
    pallas_call x1, Pallas kernels, body(): pl.pallas_call(attention_kernel, out_shape=jax.ShapeDtypeStruct((rows, HE...  8.47 us
    pallas_call x1, Pallas kernels, body(): pl.pallas_call(matmul_kernel, out_shape=[jax.ShapeDtypeStruct((rows + 256...  8.1 us
  transfers between devices with their start and end apart: 33, of which 17 were waited for; matrix products, arithmetic and copies ran while one was open for 7% of the time, Pallas kernels for 8%

profile of v1, /device:TPU:2, one launch (start us, length us, event | category | flops | bytes accessed | tf_op | source)
XLA Modules:
  0.0 159.7 jit_solution(11895129537445002668)
XLA Ops:
  1.9 10.5 %collective-permute-done.3.refs_7_ = bf16[1024,128]{1,0:T(8,128)(2,1)S(1)} collective-permute-done((bf16[1024,128]{1,0:T(8,128)(2,1)}, bf16[1024,128]{1,0:T(8,128)(2,1)S(1)}, u32[]{:S(2)}, u32[]{:S(2)}) %collective-permute-start.3) | collective-permute-done | bytes 262176 | tf_op jit(solution)/shard_map/ppermute | solution.py:25
  13.0 2.9 %pack.1 = (bf16[640,128]{1,0:T(8,128)(2,1)}, bf16[640,128]{1,0:T(8,128)(2,1)}, bf16[640,128]{1,0:T(8,128)(2,1)}, bf16[640,128]{1,0:T(8,128)(2,1)}, bf16[640,128]...) custom-call(s32[5]{0:T(128)} %stack.56.s_ref, ...), custom_call_target="tpu_custom_call" | custom-call | tf_op jit(solution)/shard_map/pack/pallas_call | solution.py:226
  15.9 5.1 %collective-permute-done.4.refs_6_ = bf16[1024,128]{1,0:T(8,128)(2,1)S(1)} collective-permute-done((bf16[1024,128]{1,0:T(8,128)(2,1)S(1)}, bf16[1024,128]{1,0:T(8,128)(2,1)S(1)}, u32[]{:S(2)}, u32[]{:S(2)}) %collective-permute-start.4) | collective-permute-done | bytes 262176 | tf_op jit(solution)/shard_map/ppermute | solution.py:25
  21.1 3.0 %collective-permute-start.7 = (bf16[640,128]{1,0:T(8,128)(2,1)}, bf16[640,128]{1,0:T(8,128)(2,1)S(1)}, u32[]{:S(2)}, u32[]{:S(2)}) collective-permute-start(bf16[640,128]{1,0:T(8,128)(2,1)} %get-tuple-element.29), channel_id=1, source_target_pairs={{0,3},{1,0},{2,1},{3,2},{4,7},{5,4},{6,5},{7,6},{64,67},{65,64},{6... | collective-permute-start | bytes 491528 | tf_op jit(solution)/shard_map/ppermute | solution.py:71
  28.1 3.0 %collective-permute-start.11 = (bf16[640,128]{1,0:T(8,128)(2,1)}, bf16[640,128]{1,0:T(8,128)(2,1)S(1)}, u32[]{:S(2)}, u32[]{:S(2)}) collective-permute-start(bf16[640,128]{1,0:T(8,128)(2,1)} %get-tuple-element.37), channel_id=1, source_target_pairs={{0,7},{1,4},{2,5},{3,6},{4,3},{5,0},{6,1},{7,2},{64,199},{65,196},... | collective-permute-start | bytes 491528 | tf_op jit(solution)/shard_map/ppermute | solution.py:71
  33.7 5.0 %collective-permute-done.8.refs_10_ = bf16[640,128]{1,0:T(8,128)(2,1)S(1)} collective-permute-done((bf16[640,128]{1,0:T(8,128)(2,1)}, bf16[640,128]{1,0:T(8,128)(2,1)S(1)}, u32[]{:S(2)}, u32[]{:S(2)}) %collective-permute-start.8) | collective-permute-done | bytes 163872 | tf_op jit(solution)/shard_map/ppermute | solution.py:71
  40.5 5.4 %collective-permute-start.10 = (bf16[640,128]{1,0:T(8,128)(2,1)}, bf16[640,128]{1,0:T(8,128)(2,1)S(1)}, u32[]{:S(2)}, u32[]{:S(2)}) collective-permute-start(bf16[640,128]{1,0:T(8,128)(2,1)} %get-tuple-element.35), channel_id=1, source_target_pairs={{0,4},{1,5},{2,6},{3,7},{4,0},{5,1},{6,2},{7,3},{64,196},{65,197},... | collective-permute-start | bytes 491528 | tf_op jit(solution)/shard_map/ppermute | solution.py:71
  47.0 2.5 %collective-permute-done.10.refs_12_ = bf16[640,128]{1,0:T(8,128)(2,1)S(1)} collective-permute-done((bf16[640,128]{1,0:T(8,128)(2,1)}, bf16[640,128]{1,0:T(8,128)(2,1)S(1)}, u32[]{:S(2)}, u32[]{:S(2)}) %collective-permute-start.10) | collective-permute-done | bytes 163872 | tf_op jit(solution)/shard_map/ppermute | solution.py:71
  53.5 9.2 %collective-permute-done.25 = bf16[16,64,128]{2,1,0:T(8,128)(2,1)S(1)} collective-permute-done((bf16[16,64,128]{2,1,0:T(8,128)(2,1)S(1)}, bf16[16,64,128]{2,1,0:T(8,128)(2,1)S(1)}, u32[]{:S(2)}, u32[]{:S(2)}) %collective-permute-start.25) | collective-permute-done | bytes 262176 | tf_op jit(solution)/shard_map/ppermute | solution.py:45
  63.4 8.2 %collective-permute-done.1.refs_2_ = bf16[1024,128]{1,0:T(8,128)(2,1)S(1)} collective-permute-done((bf16[1024,128]{1,0:T(8,128)(2,1)S(1)}, bf16[1024,128]{1,0:T(8,128)(2,1)S(1)}, u32[]{:S(2)}, u32[]{:S(2)}) %collective-permute-start.1) | collective-permute-done | bytes 262176 | tf_op jit(solution)/shard_map/ppermute | solution.py:25
  74.5 2.2 %low.1 = f32[32,1024]{1,0:T(8,128)} custom-call(s32[5]{0:T(128)} %stack.56.s_ref, s32[8]{0:T(128)} %ad_ref.3, bf16[1024,128]{1,0:T(8,128)(2,1)} %h_ref.1, bf16[2,16,64,128]{3,2,1,0:T(8,128)(2,1)} %copy-done, bf16[2,16,64,128]{3,2,1,0:T(8,128)(2,1)} %copy-done.1), custom_call_target="tpu_custom_call" | custom-call | tf_op jit(solution)/shard_map/low/pallas_call | solution.py:245
  78.7 3.2 %collective-permute-done.27 = f32[32,1024]{1,0:T(8,128)S(1)} collective-permute-done((f32[32,1024]{1,0:T(8,128)}, f32[32,1024]{1,0:T(8,128)S(1)}, u32[]{:S(2)}, u32[]{:S(2)}) %collective-permute-start.27) | collective-permute-done | bytes 131104 | tf_op jit(solution)/shard_map/ppermute | solution.py:37
  84.1 8.1 %product.1 = (bf16[1280,128]{1,0:T(8,128)(2,1)}, bf16[1280,128]{1,0:T(8,128)(2,1)}, bf16[1280,128]{1,0:T(8,128)(2,1)}, bf16[1280,128]{1,0:T(8,128)(2,1)}, bf16[1...) custom-call(s32[5]{0:T(128)} %stack.56.s_ref, ...), custom_call_target="tpu_custom_call" | custom-call | tf_op jit(solution)/shard_map/product/pallas_call | solution.py:260
  92.2 6.5 %collective-permute-start.15 = (bf16[1280,128]{1,0:T(8,128)(2,1)}, bf16[1280,128]{1,0:T(8,128)(2,1)S(1)}, u32[]{:S(2)}, u32[]{:S(2)}) collective-permute-start(bf16[1280,128]{1,0:T(8,128)(2,1)} %get-tuple-element.42), channel_id=1, source_target_pairs={{0,6},{1,7},{2,4},{3,5},{4,2},{5,3},{6,0},{7,1},{8,14},{9,15},{10,... | collective-permute-start | bytes 983048 | tf_op jit(solution)/shard_map/ppermute | solution.py:53
  100.1 3.6 %collective-permute-start.17 = (bf16[1280,128]{1,0:T(8,128)(2,1)}, bf16[1280,128]{1,0:T(8,128)(2,1)S(1)}, u32[]{:S(2)}, u32[]{:S(2)}) collective-permute-start(bf16[1280,128]{1,0:T(8,128)(2,1)} %get-tuple-element.44), channel_id=1, source_target_pairs={{0,7},{1,4},{2,5},{3,6},{4,3},{5,0},{6,1},{7,2},{8,15},{9,12},{10,... | collective-permute-start | bytes 983048 | tf_op jit(solution)/shard_map/ppermute | solution.py:53
  103.6 2.9 %collective-permute-start.18 = (bf16[1280,128]{1,0:T(8,128)(2,1)}, bf16[1280,128]{1,0:T(8,128)(2,1)S(1)}, u32[]{:S(2)}, u32[]{:S(2)}) collective-permute-start(bf16[1280,128]{1,0:T(8,128)(2,1)} %get-tuple-element.45), channel_id=1, source_target_pairs={{0,2},{1,3},{2,0},{3,1},{4,6},{5,7},{6,4},{7,5},{8,10},{9,11},{10,... | collective-permute-start | bytes 983048 | tf_op jit(solution)/shard_map/ppermute | solution.py:53
  106.5 8.2 %collective-permute-done.29 = f32[32,1024]{1,0:T(8,128)S(1)} collective-permute-done((f32[32,1024]{1,0:T(8,128)S(1)}, f32[32,1024]{1,0:T(8,128)S(1)}, u32[]{:S(2)}, u32[]{:S(2)}) %collective-permute-start.29) | collective-permute-done | bytes 131104 | tf_op jit(solution)/shard_map/ppermute | solution.py:33
  114.7 3.2 %collective-permute-start.20 = (bf16[1280,128]{1,0:T(8,128)(2,1)}, bf16[1280,128]{1,0:T(8,128)(2,1)S(1)}, u32[]{:S(2)}, u32[]{:S(2)}) collective-permute-start(bf16[1280,128]{1,0:T(8,128)(2,1)} %get-tuple-element.47), channel_id=1, source_target_pairs={{0,3},{1,0},{2,1},{3,2},{4,7},{5,4},{6,5},{7,6},{8,11},{9,8},{10,9... | collective-permute-start | bytes 983048 | tf_op jit(solution)/shard_map/ppermute | solution.py:53
  121.8 6.9 %collective-permute-done.19.refs_5_ = bf16[1280,128]{1,0:T(8,128)(2,1)S(1)} collective-permute-done((bf16[1280,128]{1,0:T(8,128)(2,1)}, bf16[1280,128]{1,0:T(8,128)(2,1)S(1)}, u32[]{:S(2)}, u32[]{:S(2)}) %collective-permute-start.19) | collective-permute-done | bytes 327712 | tf_op jit(solution)/shard_map/ppermute | solution.py:53
  129.7 3.3 %collective-permute-start.22 = (bf16[256,128]{1,0:T(8,128)(2,1)S(1)}, bf16[256,128]{1,0:T(8,128)(2,1)S(1)}, u32[]{:S(2)}, u32[]{:S(2)}) collective-permute-start(bf16[256,128]{1,0:T(8,128)(2,1)S(1)} %add_convert_fusion), channel_id=1, source_target_pairs={{0,2},{1,3},{2,0},{3,1},{4,6},{5,7},{6,4},{7,5},{8,10},{9,11},{10,... | collective-permute-start | bytes 196616 | tf_op jit(solution)/shard_map/ppermute | solution.py:33
  133.1 2.2 %collective-permute-start.31 = (bf16[32,1024]{1,0:T(8,128)(2,1)S(1)}, bf16[32,1024]{1,0:T(8,128)(2,1)S(1)}, u32[]{:S(2)}, u32[]{:S(2)}) collective-permute-start(bf16[32,1024]{1,0:T(8,128)(2,1)S(1)} %get-tuple-element.49), channel_id=1, source_target_pairs={{0,16},{8,24},{16,0},{24,8},{32,48},{40,56},{48,32},{56,40},{1,17}... | collective-permute-start | bytes 196616 | tf_op jit(solution)/shard_map/ppermute | solution.py:29
  139.6 3.4 %collective-permute-start.32 = (bf16[32,1024]{1,0:T(8,128)(2,1)S(1)}, bf16[32,1024]{1,0:T(8,128)(2,1)S(1)}, u32[]{:S(2)}, u32[]{:S(2)}) collective-permute-start(bf16[32,1024]{1,0:T(8,128)(2,1)S(1)} %fusion.1), channel_id=1, source_target_pairs={{0,32},{8,40},{16,48},{24,56},{32,0},{40,8},{48,16},{56,24},{1,33}... | collective-permute-start | bytes 196616 | tf_op jit(solution)/shard_map/ppermute | solution.py:29
  146.3 2.3 %collective-permute-done.32 = bf16[32,1024]{1,0:T(8,128)(2,1)S(1)} collective-permute-done((bf16[32,1024]{1,0:T(8,128)(2,1)S(1)}, bf16[32,1024]{1,0:T(8,128)(2,1)S(1)}, u32[]{:S(2)}, u32[]{:S(2)}) %collective-permute-start.32) | collective-permute-done | bytes 65568 | tf_op jit(solution)/shard_map/ppermute | solution.py:29
  151.2 8.5 %attention.1 = bf16[1024,128]{1,0:T(8,128)(2,1)} custom-call(s32[5]{0:T(128)} %stack.56.s_ref, s32[8]{0:T(128)} %ad_ref.3, s32[8]{0:T(128)} %multiply_subtract_fusion.lo_ref, bf16[1280,128]{1,0:T(8,128)(2,1)} %get-tuple-element.41.refs_0_, bf16[1280,128]{1,0:T(8,128)(2,1)} %copy-done.12, bf16[1280,128]{1,0:T(8,128)(2,1)} %copy-done.13, ...), custom_call_target="tpu_custom_call" | custom-call | tf_op jit(solution)/shard_map/attention/pallas_call | solution.py:284
  (129 shorter events, 39.9 us)
Async XLA Ops:
  0.0 12.4 %collective-permute-start.3 = (bf16[1024,128]{1,0:T(8,128)(2,1)}, bf16[1024,128]{1,0:T(8,128)(2,1)S(1)}, u32[]{:S(2)}, u32[]{:S(2)}) collective-permute-start(bf16[1024,128]{1,0:T(8,128)(2,1)} %h_ref.1), channel_id=1, source_target_pairs={{0,8},{8,16},{16,24},{24,32},{32,40},{40,48},{48,56},{56,0},{1,9},... | collective-permute-start | bytes 786440 | tf_op jit(solution)/shard_map/ppermute | solution.py:25
  21.1 11.9 %collective-permute-start.7 = (bf16[640,128]{1,0:T(8,128)(2,1)}, bf16[640,128]{1,0:T(8,128)(2,1)S(1)}, u32[]{:S(2)}, u32[]{:S(2)}) collective-permute-start(bf16[640,128]{1,0:T(8,128)(2,1)} %get-tuple-element.29), channel_id=1, source_target_pairs={{0,3},{1,0},{2,1},{3,2},{4,7},{5,4},{6,5},{7,6},{64,67},{65,64},{6... | collective-permute-start | bytes 491528 | tf_op jit(solution)/shard_map/ppermute | solution.py:71
  24.1 26.8 %collective-permute-start.12 = (bf16[640,128]{1,0:T(8,128)(2,1)}, bf16[640,128]{1,0:T(8,128)(2,1)S(1)}, u32[]{:S(2)}, u32[]{:S(2)}) collective-permute-start(bf16[640,128]{1,0:T(8,128)(2,1)} %get-tuple-element.38), channel_id=1, source_target_pairs={{0,6},{1,7},{2,4},{3,5},{4,2},{5,3},{6,0},{7,1},{64,198},{65,199},... | collective-permute-start | bytes 491528 | tf_op jit(solution)/shard_map/ppermute | solution.py:71
  24.7 26.9 %collective-permute-start.13 = (bf16[640,128]{1,0:T(8,128)(2,1)}, bf16[640,128]{1,0:T(8,128)(2,1)S(1)}, u32[]{:S(2)}, u32[]{:S(2)}) collective-permute-start(bf16[640,128]{1,0:T(8,128)(2,1)} %get-tuple-element.39), channel_id=1, source_target_pairs={{0,5},{1,6},{2,7},{3,4},{4,1},{5,2},{6,3},{7,0},{64,197},{65,198},... | collective-permute-start | bytes 491528 | tf_op jit(solution)/shard_map/ppermute | solution.py:71
  26.6 12.1 %collective-permute-start.8 = (bf16[640,128]{1,0:T(8,128)(2,1)}, bf16[640,128]{1,0:T(8,128)(2,1)S(1)}, u32[]{:S(2)}, u32[]{:S(2)}) collective-permute-start(bf16[640,128]{1,0:T(8,128)(2,1)} %get-tuple-element.31), channel_id=1, source_target_pairs={{0,2},{1,3},{2,0},{3,1},{4,6},{5,7},{6,4},{7,5},{64,66},{65,67},{6... | collective-permute-start | bytes 491528 | tf_op jit(solution)/shard_map/ppermute | solution.py:71
  28.1 22.0 %collective-permute-start.11 = (bf16[640,128]{1,0:T(8,128)(2,1)}, bf16[640,128]{1,0:T(8,128)(2,1)S(1)}, u32[]{:S(2)}, u32[]{:S(2)}) collective-permute-start(bf16[640,128]{1,0:T(8,128)(2,1)} %get-tuple-element.37), channel_id=1, source_target_pairs={{0,7},{1,4},{2,5},{3,6},{4,3},{5,0},{6,1},{7,2},{64,199},{65,196},... | collective-permute-start | bytes 491528 | tf_op jit(solution)/shard_map/ppermute | solution.py:71
  40.5 8.9 %collective-permute-start.10 = (bf16[640,128]{1,0:T(8,128)(2,1)}, bf16[640,128]{1,0:T(8,128)(2,1)S(1)}, u32[]{:S(2)}, u32[]{:S(2)}) collective-permute-start(bf16[640,128]{1,0:T(8,128)(2,1)} %get-tuple-element.35), channel_id=1, source_target_pairs={{0,4},{1,5},{2,6},{3,7},{4,0},{5,1},{6,2},{7,3},{64,196},{65,197},... | collective-permute-start | bytes 491528 | tf_op jit(solution)/shard_map/ppermute | solution.py:71
  52.4 30.6 %collective-permute-start.14 = (bf16[7,640,128]{2,1,0:T(8,128)(2,1)}, bf16[7,640,128]{2,1,0:T(8,128)(2,1)S(1)}, u32[]{:S(2)}, u32[]{:S(2)}) collective-permute-start(bf16[7,640,128]{2,1,0:T(8,128)(2,1)} %bitcast_dynamic-update-slice_fusion), channel_id=1, source_target_pairs={{0,64},{64,0},{1,65},{65,1},{2,66},{66,2},{3,67},{67,3},{4,68},{68... | collective-permute-start | bytes 3440648 | tf_op jit(solution)/shard_map/ppermute | solution.py:41
  52.5 10.3 %collective-permute-start.25 = (bf16[16,64,128]{2,1,0:T(8,128)(2,1)S(1)}, bf16[16,64,128]{2,1,0:T(8,128)(2,1)S(1)}, u32[]{:S(2)}, u32[]{:S(2)}) collective-permute-start(bf16[16,64,128]{2,1,0:T(8,128)(2,1)S(1)} %get-tuple-element.52), channel_id=1, source_target_pairs={{0,128},{128,0},{1,129},{129,1},{2,130},{130,2},{3,131},{131,3},{4... | collective-permute-start | bytes 786440 | tf_op jit(solution)/shard_map/ppermute | solution.py:45
  53.5 9.4 %collective-permute-start = (bf16[1024,128]{1,0:T(8,128)(2,1)S(1)}, bf16[1024,128]{1,0:T(8,128)(2,1)S(1)}, u32[]{:S(2)}, u32[]{:S(2)}) collective-permute-start(bf16[1024,128]{1,0:T(8,128)(2,1)S(1)} %copy-done.3), channel_id=1, source_target_pairs={{0,56},{8,0},{16,8},{24,16},{32,24},{40,32},{48,40},{56,48},{1,57}... | collective-permute-start | bytes 786440 | tf_op jit(solution)/shard_map/ppermute | solution.py:25
  62.8 10.9 %collective-permute-start.26 = (bf16[2,16,64,128]{3,2,1,0:T(8,128)(2,1)S(1)}, bf16[2,16,64,128]{3,2,1,0:T(8,128)(2,1)S(1)}, u32[]{:S(2)}, u32[]{:S(2)}) collective-permute-start(bf16[2,16,64,128]{3,2,1,0:T(8,128)(2,1)S(1)} %pad_maximum_fusion.near_ref.refs_11_), channel_id=1, source_target_pairs={{0,64},{64,0},{1,65},{65,1},{2,66},{66,2},{3,67},{67,3},{4,68},{68... | collective-permute-start | bytes 1572872 | tf_op jit(solution)/shard_map/ppermute | solution.py:41
  71.7 11.2 %collective-permute-start.2 = (bf16[1024,128]{1,0:T(8,128)(2,1)S(1)}, bf16[1024,128]{1,0:T(8,128)(2,1)S(1)}, u32[]{:S(2)}, u32[]{:S(2)}) collective-permute-start(bf16[1024,128]{1,0:T(8,128)(2,1)S(1)} %collective-permute-done.1.refs_2_), channel_id=1, source_target_pairs={{0,56},{8,0},{16,8},{24,16},{32,24},{40,32},{48,40},{56,48},{1,57}... | collective-permute-start | bytes 786440 | tf_op jit(solution)/shard_map/ppermute | solution.py:25
  73.2 9.8 %collective-permute-start.6 = (bf16[1024,128]{1,0:T(8,128)(2,1)S(1)}, bf16[1024,128]{1,0:T(8,128)(2,1)}, u32[]{:S(2)}, u32[]{:S(2)}) collective-permute-start(bf16[1024,128]{1,0:T(8,128)(2,1)S(1)} %collective-permute-done.5.refs_5_), channel_id=1, source_target_pairs={{0,8},{8,16},{16,24},{24,32},{32,40},{40,48},{48,56},{56,0},{1,9},... | collective-permute-start | bytes 786440 | tf_op jit(solution)/shard_map/ppermute | solution.py:25
  82.8 16.0 %collective-permute-start.28 = (f32[32,1024]{1,0:T(8,128)S(1)}, f32[32,1024]{1,0:T(8,128)S(1)}, u32[]{:S(2)}, u32[]{:S(2)}) collective-permute-start(f32[32,1024]{1,0:T(8,128)S(1)} %add.56), channel_id=1, source_target_pairs={{0,1},{1,0},{2,3},{3,2},{4,5},{5,4},{6,7},{7,6},{8,9},{9,8},{10,11... | collective-permute-start | bytes 393224 | tf_op jit(solution)/shard_map/ppermute | solution.py:33
  92.2 22.6 %collective-permute-start.15 = (bf16[1280,128]{1,0:T(8,128)(2,1)}, bf16[1280,128]{1,0:T(8,128)(2,1)S(1)}, u32[]{:S(2)}, u32[]{:S(2)}) collective-permute-start(bf16[1280,128]{1,0:T(8,128)(2,1)} %get-tuple-element.42), channel_id=1, source_target_pairs={{0,6},{1,7},{2,4},{3,5},{4,2},{5,3},{6,0},{7,1},{8,14},{9,15},{10,... | collective-permute-start | bytes 983048 | tf_op jit(solution)/shard_map/ppermute | solution.py:53
  98.7 19.3 %collective-permute-start.16 = (bf16[1280,128]{1,0:T(8,128)(2,1)}, bf16[1280,128]{1,0:T(8,128)(2,1)S(1)}, u32[]{:S(2)}, u32[]{:S(2)}) collective-permute-start(bf16[1280,128]{1,0:T(8,128)(2,1)} %get-tuple-element.43), channel_id=1, source_target_pairs={{0,5},{1,6},{2,7},{3,4},{4,1},{5,2},{6,3},{7,0},{8,13},{9,14},{10,... | collective-permute-start | bytes 983048 | tf_op jit(solution)/shard_map/ppermute | solution.py:53
  98.8 15.9 %collective-permute-start.29 = (f32[32,1024]{1,0:T(8,128)S(1)}, f32[32,1024]{1,0:T(8,128)S(1)}, u32[]{:S(2)}, u32[]{:S(2)}) collective-permute-start(f32[32,1024]{1,0:T(8,128)S(1)} %add.57), channel_id=1, source_target_pairs={{0,2},{1,3},{2,0},{3,1},{4,6},{5,7},{6,4},{7,5},{8,10},{9,11},{10,... | collective-permute-start | bytes 393224 | tf_op jit(solution)/shard_map/ppermute | solution.py:33
  100.1 20.4 %collective-permute-start.17 = (bf16[1280,128]{1,0:T(8,128)(2,1)}, bf16[1280,128]{1,0:T(8,128)(2,1)S(1)}, u32[]{:S(2)}, u32[]{:S(2)}) collective-permute-start(bf16[1280,128]{1,0:T(8,128)(2,1)} %get-tuple-element.44), channel_id=1, source_target_pairs={{0,7},{1,4},{2,5},{3,6},{4,3},{5,0},{6,1},{7,2},{8,15},{9,12},{10,... | collective-permute-start | bytes 983048 | tf_op jit(solution)/shard_map/ppermute | solution.py:53
  103.6 18.2 %collective-permute-start.18 = (bf16[1280,128]{1,0:T(8,128)(2,1)}, bf16[1280,128]{1,0:T(8,128)(2,1)S(1)}, u32[]{:S(2)}, u32[]{:S(2)}) collective-permute-start(bf16[1280,128]{1,0:T(8,128)(2,1)} %get-tuple-element.45), channel_id=1, source_target_pairs={{0,2},{1,3},{2,0},{3,1},{4,6},{5,7},{6,4},{7,5},{8,10},{9,11},{10,... | collective-permute-start | bytes 983048 | tf_op jit(solution)/shard_map/ppermute | solution.py:53
  114.7 13.9 %collective-permute-start.19 = (bf16[1280,128]{1,0:T(8,128)(2,1)}, bf16[1280,128]{1,0:T(8,128)(2,1)S(1)}, u32[]{:S(2)}, u32[]{:S(2)}) collective-permute-start(bf16[1280,128]{1,0:T(8,128)(2,1)} %get-tuple-element.46), channel_id=1, source_target_pairs={{0,1},{1,2},{2,3},{3,0},{4,5},{5,6},{6,7},{7,4},{8,9},{9,10},{10,1... | collective-permute-start | bytes 983048 | tf_op jit(solution)/shard_map/ppermute | solution.py:53
  114.7 13.9 %collective-permute-start.20 = (bf16[1280,128]{1,0:T(8,128)(2,1)}, bf16[1280,128]{1,0:T(8,128)(2,1)S(1)}, u32[]{:S(2)}, u32[]{:S(2)}) collective-permute-start(bf16[1280,128]{1,0:T(8,128)(2,1)} %get-tuple-element.47), channel_id=1, source_target_pairs={{0,3},{1,0},{2,1},{3,2},{4,7},{5,4},{6,5},{7,6},{8,11},{9,8},{10,9... | collective-permute-start | bytes 983048 | tf_op jit(solution)/shard_map/ppermute | solution.py:53
  118.0 10.7 %collective-permute-start.21 = (bf16[1280,128]{1,0:T(8,128)(2,1)}, bf16[1280,128]{1,0:T(8,128)(2,1)S(1)}, u32[]{:S(2)}, u32[]{:S(2)}) collective-permute-start(bf16[1280,128]{1,0:T(8,128)(2,1)} %get-tuple-element.48), channel_id=1, source_target_pairs={{0,4},{1,5},{2,6},{3,7},{4,0},{5,1},{6,2},{7,3},{8,12},{9,13},{10,... | collective-permute-start | bytes 983048 | tf_op jit(solution)/shard_map/ppermute | solution.py:53
  120.5 12.5 %collective-permute-start.30 = (f32[32,1024]{1,0:T(8,128)S(1)}, f32[32,1024]{1,0:T(8,128)S(1)}, u32[]{:S(2)}, u32[]{:S(2)}) collective-permute-start(f32[32,1024]{1,0:T(8,128)S(1)} %add.58), channel_id=1, source_target_pairs={{0,8},{8,0},{16,24},{24,16},{32,40},{40,32},{48,56},{56,48},{1,9},... | collective-permute-start | bytes 393224 | tf_op jit(solution)/shard_map/ppermute | solution.py:29
  139.6 9.0 %collective-permute-start.32 = (bf16[32,1024]{1,0:T(8,128)(2,1)S(1)}, bf16[32,1024]{1,0:T(8,128)(2,1)S(1)}, u32[]{:S(2)}, u32[]{:S(2)}) collective-permute-start(bf16[32,1024]{1,0:T(8,128)(2,1)S(1)} %fusion.1), channel_id=1, source_target_pairs={{0,32},{8,40},{16,48},{24,56},{32,0},{40,8},{48,16},{56,24},{1,33}... | collective-permute-start | bytes 196616 | tf_op jit(solution)/shard_map/ppermute | solution.py:29
  (38 other events, 472.9 us)

commit v2 on v1

v2 whole, which is shorter than its diff:
```python
import functools
import math

import jax
import jax.numpy as jnp
from jax import lax
from jax.experimental import pallas as pl
from jax.experimental.pallas import tpu as pltpu
from jax.sharding import Mesh, PartitionSpec as P

HEAD_SIZE = 128
BLOCK = 128
RANK = 32
ROPE_BASE = 500000.0
ADAPTER_SCALE = 2.0
NXH, NC, NZ, NX, NY = 2, 2, 8, 2, 4
REQ_AXES = ("xh", "c")
TP_AXES = ("z", "xl", "y")
NP = NX * NY
VMEM = pl.BlockSpec(memory_space=pltpu.VMEM)
SMEM = pl.BlockSpec(memory_space=pltpu.SMEM)


def z_shift(v, s):
    return lax.ppermute(v, "z", [(i, (i + s) % NZ) for i in range(NZ)])


def z_xor(v, s):
    return lax.ppermute(v, "z", [(i, i ^ s) for i in range(NZ)])


def y_xor(v, s):
    return lax.ppermute(v, "y", [(i, i ^ s) for i in range(NY)])


def x_swap(v):
    return lax.ppermute(v, "xl", [(0, 1), (1, 0)])


def core_swap(v):
    return lax.ppermute(v, "c", [(0, 1), (1, 0)])


def xh_swap(v):
    return lax.ppermute(v, "xh", [(0, 1), (1, 0)])


def plane_send(v, d):
    dx, dy = divmod(d, NY)
    route = [
        (a * NY + b, (a ^ dx) * NY + (b + dy) % NY) for a in range(NX) for b in range(NY)
    ]
    return lax.ppermute(v, ("xl", "y"), route)


SERVED = ((4, 6, 1), (5, 7, 3, 2))
FLIP = [dx * NY + (-dy) % NY for dx in range(NX) for dy in range(NY)]


def weight_send(v, k):
    route = []
    for xh in range(NXH):
        for c in range(NC):
            if k >= len(SERVED[c]):
                continue
            dx, dy = divmod(SERVED[c][k], NY)
            for xl in range(NX):
                for y in range(NY):
                    at = xh * NX + xl
                    if dx:
                        to = at ^ 1 if c == 0 else (at + 1 if at % 2 else at - 1) % 4
                    else:
                        to = at
                    src = ((xh * NC + c) * NX + xl) * NY + y
                    dst = ((to // NX * NC + c) * NX + to % NX) * NY + (y + dy) % NY
                    route.append((src, dst))
    return lax.ppermute(v, ("xh", "c", "xl", "y"), route)


def weight_swap(v, k):
    return lax.ppermute(v, "c", [(c, 1 - c) for c in range(NC) if k < len(SERVED[c])])


def pack_kernel(s_ref, wq_ref, kv_ref, *outs):
    z, xl, y, c = s_ref[0], s_ref[1], s_ref[2], s_ref[3]
    for k in range(5):
        d = 0
        if k < 4:
            d = jnp.where(c == 0, (SERVED[0] + (0,))[k], SERVED[1][k])
        p = (xl ^ (d // NY)) * NY + ((y + d) & (NY - 1))
        for j in range(NZ):
            row = pl.multiple_of((((z + j) & (NZ - 1)) * NP + p) * 128, 128)
            outs[k][j * 128 : (j + 1) * 128, :] = wq_ref[pl.ds(row, 128), :]
            outs[k][1024 + j * 32 : 1024 + (j + 1) * 32, :] = kv_ref[:, pl.ds(row, 128)]


def low_kernel(s_ref, ad_ref, h_ref, near_ref, far_ref, out_ref):
    c, xh = s_ref[3], s_ref[4]
    per = near_ref.shape[1]
    for b in range(h_ref.shape[0] // BLOCK):
        a = ad_ref[b]
        owner = a // per
        at = a - owner * per
        xr, cr = (owner // NC) ^ xh, (owner % NC) ^ c
        down = jnp.where(cr == 0, near_ref[xr, at, 0:RANK, :], far_ref[xr, at, 0:RANK, :])
        out_ref[:, b * BLOCK : (b + 1) * BLOCK] = lax.dot_general(
            down,
            h_ref[b * BLOCK : (b + 1) * BLOCK, :],
            (((1,), (1,)), ((), ())),
            preferred_element_type=jnp.float32,
        )


def matmul_kernel(s_ref, *refs):
    h_refs, own, mine, other, low_ref = refs[0:8], refs[8], refs[9:13], refs[13:17], refs[17]
    outs = refs[18:26]
    hbuf, wq, kvw = refs[26:29]
    xl, y, c = s_ref[1], s_ref[2], s_ref[3]
    for j in range(8):
        hbuf[:, j * 128 : (j + 1) * 128] = h_refs[j][...]

    def place(ref, d):
        dx, dy = divmod(d, NY)
        wq[dy, :, dx * 128 : (dx + 1) * 128] = ref[0:1024, :]
        for j in range(NZ):
            kvw[d * 32 : (d + 1) * 32, j * 128 : (j + 1) * 128] = ref[1024 + j * 32 : 1056 + j * 32, :]

    place(own, 0)
    for core in range(NC):

        @pl.when(c == core)
        def _():
            for k, d in enumerate(SERVED[core]):
                place(mine[k], FLIP[d])
            for k, d in enumerate(SERVED[1 - core]):
                place(other[k], FLIP[d])

    for d in range(NP):
        dx, dy = divmod(d, NY)
        p = (xl ^ dx) * NY + ((y + dy) & (NY - 1))
        at = pl.multiple_of(p * 128, 128)
        outs[d][1280:1312, :] = low_ref[:, pl.ds(at, 128)].astype(jnp.bfloat16)
    tile = 512

    def step(i, carry):
        r = pl.multiple_of(i * tile, tile)
        h = hbuf[pl.ds(r, tile), :]
        kv = lax.dot_general(kvw[...], h, (((1,), (1,)), ((), ())), preferred_element_type=jnp.float32)
        kv = kv.astype(jnp.bfloat16)
        for d in range(NP):
            for t in range(tile // 128):
                at = pl.multiple_of(1024 + (i * (tile // 128) + t) * 32, 32)
                outs[d][pl.ds(at, 32), :] = kv[d * 32 : (d + 1) * 32, t * 128 : (t + 1) * 128]
        for dy in range(NY):
            q = jnp.dot(h, wq[dy], preferred_element_type=jnp.float32).astype(jnp.bfloat16)
            outs[dy][pl.ds(r, tile), :] = q[:, 0:128]
            outs[NY + dy][pl.ds(r, tile), :] = q[:, 128:256]
        return carry

    lax.fori_loop(0, 1024 // tile, step, 0)


def add_kernel(*refs):
    out_ref = refs[-1]

    def step(i, carry):
        rows = pl.ds(pl.multiple_of(i * 128, 128), 128)
        total = refs[0][rows, :].astype(jnp.float32)
        for piece in refs[1:-1]:
            total += piece[rows, :].astype(jnp.float32)
        out_ref[rows, :] = total
        return carry

    lax.fori_loop(0, out_ref.shape[0] // 128, step, 0)


def attention_kernel(s_ref, ad_ref, lo_ref, *refs):
    q_ref, kv_near, kv_far, near_ref, far_ref, cos_ref, sin_ref = refs[0:7]
    out_ref = refs[7]
    kvt, low_buf, k_buf, v_buf = refs[8:12]
    xl, y, c, xh = s_ref[1], s_ref[2], s_ref[3], s_ref[4]
    for half, ref in enumerate((kv_near, kv_far)):
        for i, m in enumerate((0, 2, 1, 3)):
            p = (xl ^ half) * NY + (y ^ m)
            at = pl.multiple_of(p * 32, 32)
            for t in range(8):
                kvt[pl.ds(at, 32), t * 128 : (t + 1) * 128] = ref[i * 288 + t * 32 : i * 288 + (t + 1) * 32, :]
            low_buf[p] = ref[i * 288 + 256 : (i + 1) * 288, :]

    def rope(v, rows):
        return v * cos_ref[rows, :] + pltpu.roll(v, 64, 1) * sin_ref[rows, :]

    for t in range(8):
        rows = slice(t * 128, (t + 1) * 128)
        k = kvt[0:128, rows].astype(jnp.float32).T
        k_buf[rows, :] = rope(k, rows).astype(jnp.bfloat16)
        v_buf[rows, :] = kvt[128:256, rows].T
    per = near_ref.shape[1]
    factor = math.log2(math.e) / math.sqrt(HEAD_SIZE)
    for b in range(8):
        rows = slice(b * 128, (b + 1) * 128)
        a = ad_ref[b]
        owner = a // per
        at = a - owner * per
        xr, cr = (owner // NC) ^ xh, (owner % NC) ^ c
        up = jnp.where(cr == 0, near_ref[xr, at, RANK : 2 * RANK, :], far_ref[xr, at, RANK : 2 * RANK, :])
        q = q_ref[rows, :] + ADAPTER_SCALE * lax.dot_general(
            low_buf[b], up, (((0,), (0,)), ((), ())), preferred_element_type=jnp.float32
        )
        q = rope(q, rows).astype(jnp.bfloat16)
        n = (b + 1) * 128
        s = lax.dot_general(
            q, k_buf[0:n, :], (((1,), (1,)), ((), ())), preferred_element_type=jnp.float32
        )
        col = lax.broadcasted_iota(jnp.int32, (128, n), 1)
        row = lax.broadcasted_iota(jnp.int32, (128, n), 0) + b * 128
        allowed = (col >= lo_ref[b]) & (col <= row)
        s = jnp.where(allowed, s, -1e30)
        e = jnp.exp2((s - jnp.max(s, axis=1, keepdims=True)) * factor)
        probs = (e * (1.0 / jnp.sum(e, axis=1, keepdims=True))).astype(jnp.bfloat16)
        out_ref[rows, :] = jnp.dot(
            probs, v_buf[0:n, :], preferred_element_type=jnp.float32
        ).astype(jnp.bfloat16)


def rope_tables(positions):
    half = HEAD_SIZE // 2
    steps = jnp.arange(half, dtype=jnp.float32)
    inverse = jnp.exp(-(2.0 * steps / HEAD_SIZE) * math.log(ROPE_BASE))
    angles = positions.astype(jnp.float32)[:, None] * inverse[None, :]
    cosines, sines = jnp.cos(angles), jnp.sin(angles)
    return jnp.concatenate([cosines, cosines], 1), jnp.concatenate([-sines, sines], 1)


def after(value, *others):
    return lax.optimization_barrier((value, *others))[0]


def body(hidden, query_weight, key_value_weight, down_maps, up_maps, request_start, adapters):
    rows = hidden.shape[0]
    bf16, f32 = jnp.bfloat16, jnp.float32
    place = [lax.axis_index(a) for a in ("z", "xl", "y", "c", "xh")]
    scalars = jnp.stack(place).astype(jnp.int32)

    maps = jnp.concatenate([jnp.transpose(down_maps, (0, 2, 1)), up_maps], axis=1)
    twin = xh_swap(maps)

    sends = pl.pallas_call(
        pack_kernel,
        out_shape=[jax.ShapeDtypeStruct((1280, 128), bf16)] * 5,
        in_specs=[SMEM, VMEM, VMEM],
        out_specs=[VMEM] * 5,
        name="pack",
    )(scalars, query_weight, key_value_weight.T)
    right, left = [hidden], [hidden]
    mine, other = [], []
    for step in range(4):
        gate = (right[-1], left[-1])
        right.append(z_shift(after(gate[0], gate[1]) if step else hidden, 1))
        if step < 3:
            left.append(z_shift(after(gate[1], gate[0]) if step else hidden, -1))
        if step < 2:
            for k in (2 * step, 2 * step + 1):
                mine.append(weight_send(after(sends[k], *gate) if step else sends[k], k))
    for k in range(4):
        other.append(weight_swap(mine[k], k))

    near = jnp.stack([maps, after(twin, right[1], left[1])])
    far = core_swap(near)
    low = pl.pallas_call(
        low_kernel,
        out_shape=jax.ShapeDtypeStruct((RANK, rows), f32),
        in_specs=[SMEM, SMEM, VMEM, VMEM, VMEM],
        out_specs=VMEM,
        name="low",
    )(scalars, adapters, hidden, near, far)
    low = low + z_xor(low, 1)
    low = low + z_xor(low, 2)
    low = low + z_xor(low.astype(bf16), 4).astype(f32)

    shards = [hidden, left[1], left[2], left[3], right[4], right[3], right[2], right[1]]
    parts = pl.pallas_call(
        matmul_kernel,
        out_shape=[jax.ShapeDtypeStruct((rows + 288, 128), bf16)] * NP,
        in_specs=[SMEM] + [VMEM] * 18,
        out_specs=[VMEM] * NP,
        scratch_shapes=[
            pltpu.VMEM((rows, 1024), bf16),
            pltpu.VMEM((NY, 1024, 256), bf16),
            pltpu.VMEM((256, 1024), bf16),
        ],
        name="product",
    )(scalars, *shards, sends[4], *mine, *other, low)
    pieces = [parts[0]] + [plane_send(parts[d], d) for d in (6, 5, 7, 2, 1, 3, 4)]
    kv = sum(p[rows:].astype(f32) for p in pieces).astype(bf16)
    kv = jnp.concatenate([kv, y_xor(kv, 2)])
    kv = jnp.concatenate([kv, y_xor(kv, 1)])
    kv_far = x_swap(kv)
    q = pl.pallas_call(
        add_kernel,
        out_shape=jax.ShapeDtypeStruct((rows, HEAD_SIZE), f32),
        in_specs=[VMEM] * NP,
        out_specs=VMEM,
        name="add",
    )(*pieces)

    first = lax.axis_index("xh") * NC + lax.axis_index("c")
    places = first * rows + jnp.arange(rows, dtype=jnp.int32)
    cosines, sines = rope_tables(places - request_start * BLOCK)
    lowest = request_start[::BLOCK] * BLOCK - first * rows
    return pl.pallas_call(
        attention_kernel,
        out_shape=jax.ShapeDtypeStruct((rows, HEAD_SIZE), bf16),
        in_specs=[SMEM, SMEM, SMEM] + [VMEM] * 7,
        out_specs=VMEM,
        scratch_shapes=[
            pltpu.VMEM((256, rows), bf16),
            pltpu.VMEM((NP, RANK, 128), bf16),
            pltpu.VMEM((rows, HEAD_SIZE), bf16),
            pltpu.VMEM((rows, HEAD_SIZE), bf16),
        ],
        name="attention",
    )(scalars, adapters, lowest, q, kv, kv_far, near, far, cosines, sines)


def solution(mesh):
    fine = Mesh(mesh.devices.reshape(NXH, NC, NZ, NX, NY), REQ_AXES + TP_AXES)
    in_specs = (
        P(REQ_AXES, TP_AXES),
        P(None, TP_AXES),
        P(None, TP_AXES),
        P(REQ_AXES, TP_AXES, None),
        P(REQ_AXES, None, TP_AXES),
        P(REQ_AXES),
        P(REQ_AXES),
    )
    return jax.shard_map(
        body, mesh=fine, in_specs=in_specs, out_specs=P(REQ_AXES, TP_AXES), check_vma=False
    )
```

time: 160 us -> 146 us (0.912)
  the two profiles are of different devices: /device:TPU:2 before, /device:TPU:6 now
where the time goes in v2:
time: 146 us; the launch traced here: 145 us
  waiting for transfers between devices  66.4 us (45%)
  starting transfers between devices  44.5 us (30%)
  Pallas kernels  23.4 us (16%)
  other arithmetic  7.57 us (5%)
  local copies, waits for them, and re-layouts  3.02 us (2%)
    ppermute x7, waiting for transfers between devices, plane_send(): return lax.ppermute(v, ('xl', 'y'), route)  24.7 us
    ppermute x7, starting transfers between devices, z_shift(): return lax.ppermute(v, 'z', [(i, (i + s) % NZ) for i in range(NZ)])  16.6 us
    ppermute x7, starting transfers between devices, plane_send(): return lax.ppermute(v, ('xl', 'y'), route)  13.9 us
    ppermute x3, waiting for transfers between devices, z_xor(): return lax.ppermute(v, 'z', [(i, i ^ s) for i in range(NZ)])  12.1 us
    ppermute x7, waiting for transfers between devices, z_shift(): return lax.ppermute(v, 'z', [(i, (i + s) % NZ) for i in range(NZ)])  11.6 us
    ppermute x2, waiting for transfers between devices, y_xor(): return lax.ppermute(v, 'y', [(i, i ^ s) for i in range(NY)])  9.05 us
    pallas_call x1, Pallas kernels, body(): pl.pallas_call(matmul_kernel, out_shape=[jax.ShapeDtypeStruct((rows + 288...  7.84 us
    pallas_call x1, Pallas kernels, body(): pl.pallas_call(attention_kernel, out_shape=jax.ShapeDtypeStruct((rows, HE...  7.55 us
  transfers between devices with their start and end apart: 30, of which 16 were waited for; matrix products, arithmetic and copies ran while one was open for 5% of the time, Pallas kernels for 6%

profile of v2, /device:TPU:6, one launch (start us, length us, event | category | flops | bytes accessed | tf_op | source)
XLA Modules:
  0.0 145.3 jit_solution(185980031709051983)
XLA Ops:
  0.0 5.9 %collective-permute-start = (bf16[1024,128]{1,0:T(8,128)(2,1)}, bf16[1024,128]{1,0:T(8,128)(2,1)S(1)}, u32[]{:S(2)}, u32[]{:S(2)}) collective-permute-start(bf16[1024,128]{1,0:T(8,128)(2,1)} %refs_0_.1), channel_id=1, source_target_pairs={{0,56},{8,0},{16,8},{24,16},{32,24},{40,32},{48,40},{56,48},{1,57}... | collective-permute-start | bytes 786440 | tf_op jit(solution)/shard_map/ppermute | solution.py:25
  8.4 3.3 %collective-permute-done.refs_1_ = bf16[1024,128]{1,0:T(8,128)(2,1)S(1)} collective-permute-done((bf16[1024,128]{1,0:T(8,128)(2,1)}, bf16[1024,128]{1,0:T(8,128)(2,1)S(1)}, u32[]{:S(2)}, u32[]{:S(2)}) %collective-permute-start) | collective-permute-done | bytes 262176 | tf_op jit(solution)/shard_map/ppermute | solution.py:25
  11.7 3.3 %collective-permute-done.1.refs_7_ = bf16[1024,128]{1,0:T(8,128)(2,1)S(1)} collective-permute-done((bf16[1024,128]{1,0:T(8,128)(2,1)}, bf16[1024,128]{1,0:T(8,128)(2,1)S(1)}, u32[]{:S(2)}, u32[]{:S(2)}) %collective-permute-start.1) | collective-permute-done | bytes 262176 | tf_op jit(solution)/shard_map/ppermute | solution.py:25
  17.1 3.1 %pack.1 = (bf16[1280,128]{1,0:T(8,128)(2,1)}, bf16[1280,128]{1,0:T(8,128)(2,1)}, bf16[1280,128]{1,0:T(8,128)(2,1)}, bf16[1280,128]{1,0:T(8,128)(2,1)}, bf16[1280,128]{1,0:T(8,128)(2,1)}) custom-call(s32[5]{0:T(128)} %stack.32.s_ref, bf16[8192,128]{1,0:T(8,128)(2,1)} %wq_ref.1, bf16[32,8192]{1,0:T(8,128)(2,1)} %bitcast.10), custom_call_target="tpu_custom_call" | custom-call | tf_op jit(solution)/shard_map/pack/pallas_call | solution.py:248
  20.1 3.0 %collective-permute-start.2 = (bf16[1024,128]{1,0:T(8,128)(2,1)S(1)}, bf16[1024,128]{1,0:T(8,128)(2,1)S(1)}, u32[]{:S(2)}, u32[]{:S(2)}) collective-permute-start(bf16[1024,128]{1,0:T(8,128)(2,1)S(1)} %collective-permute-done.refs_1_), channel_id=1, source_target_pairs={{0,56},{8,0},{16,8},{24,16},{32,24},{40,32},{48,40},{56,48},{1,57}... | collective-permute-start | bytes 786440 | tf_op jit(solution)/shard_map/ppermute | solution.py:25
  26.9 6.2 %collective-permute-done.17 = f32[32,1024]{1,0:T(8,128)S(1)} collective-permute-done((f32[32,1024]{1,0:T(8,128)}, f32[32,1024]{1,0:T(8,128)S(1)}, u32[]{:S(2)}, u32[]{:S(2)}) %collective-permute-start.17) | collective-permute-done | bytes 131104 | tf_op jit(solution)/shard_map/ppermute | solution.py:29
  34.9 3.2 %collective-permute-start.8 = (bf16[1280,128]{1,0:T(8,128)(2,1)}, bf16[1280,128]{1,0:T(8,128)(2,1)S(1)}, u32[]{:S(2)}, u32[]{:S(2)}) collective-permute-start(bf16[1280,128]{1,0:T(8,128)(2,1)} %get-tuple-element.33), channel_id=1, source_target_pairs={{0,6},{1,7},{2,4},{3,5},{4,2},{5,3},{6,0},{7,1},{64,199},{65,196},... | collective-permute-start | bytes 983048 | tf_op jit(solution)/shard_map/ppermute | solution.py:77
  43.1 2.7 %collective-permute-start.4 = (bf16[1024,128]{1,0:T(8,128)(2,1)S(1)}, bf16[1024,128]{1,0:T(8,128)(2,1)S(1)}, u32[]{:S(2)}, u32[]{:S(2)}) collective-permute-start(bf16[1024,128]{1,0:T(8,128)(2,1)S(1)} %collective-permute-done.2.refs_2_), channel_id=1, source_target_pairs={{0,56},{8,0},{16,8},{24,16},{32,24},{40,32},{48,40},{56,48},{1,57}... | collective-permute-start | bytes 786440 | tf_op jit(solution)/shard_map/ppermute | solution.py:25
  45.9 5.7 %collective-permute-done.9.refs_11_ = bf16[1280,128]{1,0:T(8,128)(2,1)S(1)} collective-permute-done((bf16[1280,128]{1,0:T(8,128)(2,1)}, bf16[1280,128]{1,0:T(8,128)(2,1)S(1)}, u32[]{:S(2)}, u32[]{:S(2)}) %collective-permute-start.9) | collective-permute-done | bytes 327712 | tf_op jit(solution)/shard_map/ppermute | solution.py:77
  52.1 4.3 %collective-permute-start.19 = (bf16[32,1024]{1,0:T(8,128)(2,1)S(1)}, bf16[32,1024]{1,0:T(8,128)(2,1)S(1)}, u32[]{:S(2)}, u32[]{:S(2)}) collective-permute-start(bf16[32,1024]{1,0:T(8,128)(2,1)S(1)} %get-tuple-element.47), channel_id=1, source_target_pairs={{0,32},{8,40},{16,48},{24,56},{32,0},{40,8},{48,16},{56,24},{1,33}... | collective-permute-start | bytes 196616 | tf_op jit(solution)/shard_map/ppermute | solution.py:29
  57.8 4.0 %collective-permute-done.19 = bf16[32,1024]{1,0:T(8,128)(2,1)S(1)} collective-permute-done((bf16[32,1024]{1,0:T(8,128)(2,1)S(1)}, bf16[32,1024]{1,0:T(8,128)(2,1)S(1)}, u32[]{:S(2)}, u32[]{:S(2)}) %collective-permute-start.19) | collective-permute-done | bytes 65568 | tf_op jit(solution)/shard_map/ppermute | solution.py:29
  61.7 3.0 %collective-permute-start.6 = (bf16[1024,128]{1,0:T(8,128)(2,1)S(1)}, bf16[1024,128]{1,0:T(8,128)(2,1)S(1)}, u32[]{:S(2)}, u32[]{:S(2)}) collective-permute-start(bf16[1024,128]{1,0:T(8,128)(2,1)S(1)} %collective-permute-done.5.refs_5_), channel_id=1, source_target_pairs={{0,8},{8,16},{16,24},{24,32},{32,40},{40,48},{48,56},{56,0},{1,9},... | collective-permute-start | bytes 786440 | tf_op jit(solution)/shard_map/ppermute | solution.py:25
  65.4 5.0 %collective-permute-done.6.refs_4_ = bf16[1024,128]{1,0:T(8,128)(2,1)S(1)} collective-permute-done((bf16[1024,128]{1,0:T(8,128)(2,1)S(1)}, bf16[1024,128]{1,0:T(8,128)(2,1)S(1)}, u32[]{:S(2)}, u32[]{:S(2)}) %collective-permute-start.6) | collective-permute-done | bytes 262176 | tf_op jit(solution)/shard_map/ppermute | solution.py:25
  71.2 7.8 %product.1 = (bf16[1312,128]{1,0:T(8,128)(2,1)}, bf16[1312,128]{1,0:T(8,128)(2,1)}, bf16[1312,128]{1,0:T(8,128)(2,1)}, bf16[1312,128]{1,0:T(8,128)(2,1)}, bf16[1...) custom-call(s32[5]{0:T(128)} %stack.32.s_ref, ...), custom_call_target="tpu_custom_call" | custom-call | tf_op jit(solution)/shard_map/product/pallas_call | solution.py:282
  79.9 4.6 %collective-permute-start.21 = (bf16[1312,128]{1,0:T(8,128)(2,1)}, bf16[1312,128]{1,0:T(8,128)(2,1)S(1)}, u32[]{:S(2)}, u32[]{:S(2)}) collective-permute-start(bf16[1312,128]{1,0:T(8,128)(2,1)} %get-tuple-element.41), channel_id=1, source_target_pairs={{0,5},{1,6},{2,7},{3,4},{4,1},{5,2},{6,3},{7,0},{8,13},{9,14},{10,... | collective-permute-start | bytes 1007624 | tf_op jit(solution)/shard_map/ppermute | solution.py:53
  86.6 6.1 %collective-permute-done.20.refs_1_ = bf16[1312,128]{1,0:T(8,128)(2,1)S(1)} collective-permute-done((bf16[1312,128]{1,0:T(8,128)(2,1)}, bf16[1312,128]{1,0:T(8,128)(2,1)S(1)}, u32[]{:S(2)}, u32[]{:S(2)}) %collective-permute-start.20) | collective-permute-done | bytes 335904 | tf_op jit(solution)/shard_map/ppermute | solution.py:53
  92.8 4.4 %collective-permute-start.25 = (bf16[1312,128]{1,0:T(8,128)(2,1)}, bf16[1312,128]{1,0:T(8,128)(2,1)S(1)}, u32[]{:S(2)}, u32[]{:S(2)}) collective-permute-start(bf16[1312,128]{1,0:T(8,128)(2,1)} %get-tuple-element.45), channel_id=1, source_target_pairs={{0,3},{1,0},{2,1},{3,2},{4,7},{5,4},{6,5},{7,6},{8,11},{9,8},{10,9... | collective-permute-start | bytes 1007624 | tf_op jit(solution)/shard_map/ppermute | solution.py:53
  97.2 3.8 %collective-permute-done.21.refs_2_ = bf16[1312,128]{1,0:T(8,128)(2,1)S(1)} collective-permute-done((bf16[1312,128]{1,0:T(8,128)(2,1)}, bf16[1312,128]{1,0:T(8,128)(2,1)S(1)}, u32[]{:S(2)}, u32[]{:S(2)}) %collective-permute-start.21) | collective-permute-done | bytes 335904 | tf_op jit(solution)/shard_map/ppermute | solution.py:53
  103.0 7.6 %collective-permute-done.22.refs_3_ = bf16[1312,128]{1,0:T(8,128)(2,1)S(1)} collective-permute-done((bf16[1312,128]{1,0:T(8,128)(2,1)}, bf16[1312,128]{1,0:T(8,128)(2,1)S(1)}, u32[]{:S(2)}, u32[]{:S(2)}) %collective-permute-start.22) | collective-permute-done | bytes 335904 | tf_op jit(solution)/shard_map/ppermute | solution.py:53
  112.3 5.4 %collective-permute-done.25.refs_6_ = bf16[1312,128]{1,0:T(8,128)(2,1)S(1)} collective-permute-done((bf16[1312,128]{1,0:T(8,128)(2,1)}, bf16[1312,128]{1,0:T(8,128)(2,1)S(1)}, u32[]{:S(2)}, u32[]{:S(2)}) %collective-permute-start.25) | collective-permute-done | bytes 335904 | tf_op jit(solution)/shard_map/ppermute | solution.py:53
  118.9 5.8 %collective-permute-done.27 = bf16[288,128]{1,0:T(8,128)(2,1)S(1)} collective-permute-done((bf16[288,128]{1,0:T(8,128)(2,1)S(1)}, bf16[288,128]{1,0:T(8,128)(2,1)S(1)}, u32[]{:S(2)}, u32[]{:S(2)}) %collective-permute-start.27) | collective-permute-done | bytes 73760 | tf_op jit(solution)/shard_map/ppermute | solution.py:33
  126.7 3.2 %collective-permute-done.28 = bf16[576,128]{1,0:T(8,128)(2,1)S(1)} collective-permute-done((bf16[576,128]{1,0:T(8,128)(2,1)S(1)}, bf16[576,128]{1,0:T(8,128)(2,1)S(1)}, u32[]{:S(2)}, u32[]{:S(2)}) %collective-permute-start.28) | collective-permute-done | bytes 147488 | tf_op jit(solution)/shard_map/ppermute | solution.py:33
  132.2 2.8 %add.64.refs_0_ = f32[1024,128]{1,0:T(8,128)} custom-call(bf16[1312,128]{1,0:T(8,128)(2,1)} %get-tuple-element.39.refs_0_, bf16[1312,128]{1,0:T(8,128)(2,1)} %copy-done.3, bf16[1312,128]{1,0:T(8,128)(2,1)} %copy-done.4, bf16[1312,128]{1,0:T(8,128)(2,1)} %copy-done.5, bf16[1312,128]{1,0:T(8,128)(2,1)} %copy-done.6, bf16[1312,128]{1,0:T(8,128)(2,1)} %copy-done.7, ...), custom_call_target="tpu_custom_call" | custom-call | tf_op jit(solution)/shard_map/add/pallas_call | solution.py:299
  137.7 7.5 %attention.1 = bf16[1024,128]{1,0:T(8,128)(2,1)} custom-call(s32[5]{0:T(128)} %stack.32.s_ref, s32[8]{0:T(128)} %ad_ref.3, s32[8]{0:T(128)} %multiply_subtract_fusion.lo_ref, f32[1024,128]{1,0:T(8,128)} %add.64.refs_0_, bf16[1152,128]{1,0:T(8,128)(2,1)} %copy-done.2, bf16[1152,128]{1,0:T(8,128)(2,1)} %copy-done.18, bf16[2,16,64,128]{3,2,1,0:T(8,128)(2,1)} %copy-done, ...), custom_call_target="tpu_custom_call" | custom-call | tf_op jit(solution)/shard_map/attention/pallas_call | solution.py:311
  (110 shorter events, 33.2 us)
Async XLA Ops:
  0.0 11.7 %collective-permute-start = (bf16[1024,128]{1,0:T(8,128)(2,1)}, bf16[1024,128]{1,0:T(8,128)(2,1)S(1)}, u32[]{:S(2)}, u32[]{:S(2)}) collective-permute-start(bf16[1024,128]{1,0:T(8,128)(2,1)} %refs_0_.1), channel_id=1, source_target_pairs={{0,56},{8,0},{16,8},{24,16},{32,24},{40,32},{48,40},{56,48},{1,57}... | collective-permute-start | bytes 786440 | tf_op jit(solution)/shard_map/ppermute | solution.py:25
  5.9 9.2 %collective-permute-start.1 = (bf16[1024,128]{1,0:T(8,128)(2,1)}, bf16[1024,128]{1,0:T(8,128)(2,1)S(1)}, u32[]{:S(2)}, u32[]{:S(2)}) collective-permute-start(bf16[1024,128]{1,0:T(8,128)(2,1)} %refs_0_.1), channel_id=1, source_target_pairs={{0,8},{8,16},{16,24},{24,32},{32,40},{40,48},{48,56},{56,0},{1,9},... | collective-permute-start | bytes 786440 | tf_op jit(solution)/shard_map/ppermute | solution.py:25
  6.9 9.4 %collective-permute-start.15 = (bf16[16,64,128]{2,1,0:T(8,128)(2,1)S(1)}, bf16[16,64,128]{2,1,0:T(8,128)(2,1)S(1)}, u32[]{:S(2)}, u32[]{:S(2)}) collective-permute-start(bf16[16,64,128]{2,1,0:T(8,128)(2,1)S(1)} %get-tuple-element.50), channel_id=1, source_target_pairs={{0,128},{128,0},{1,129},{129,1},{2,130},{130,2},{3,131},{131,3},{4... | collective-permute-start | bytes 786440 | tf_op jit(solution)/shard_map/ppermute | solution.py:45
  20.1 18.0 %collective-permute-start.2 = (bf16[1024,128]{1,0:T(8,128)(2,1)S(1)}, bf16[1024,128]{1,0:T(8,128)(2,1)S(1)}, u32[]{:S(2)}, u32[]{:S(2)}) collective-permute-start(bf16[1024,128]{1,0:T(8,128)(2,1)S(1)} %collective-permute-done.refs_1_), channel_id=1, source_target_pairs={{0,56},{8,0},{16,8},{24,16},{32,24},{40,32},{48,40},{56,48},{1,57}... | collective-permute-start | bytes 786440 | tf_op jit(solution)/shard_map/ppermute | solution.py:25
  23.1 15.3 %collective-permute-start.3 = (bf16[1024,128]{1,0:T(8,128)(2,1)S(1)}, bf16[1024,128]{1,0:T(8,128)(2,1)S(1)}, u32[]{:S(2)}, u32[]{:S(2)}) collective-permute-start(bf16[1024,128]{1,0:T(8,128)(2,1)S(1)} %collective-permute-done.1.refs_7_), channel_id=1, source_target_pairs={{0,8},{8,16},{16,24},{24,32},{32,40},{40,48},{48,56},{56,0},{1,9},... | collective-permute-start | bytes 786440 | tf_op jit(solution)/shard_map/ppermute | solution.py:25
  23.1 16.0 %collective-permute-start.7 = (bf16[1280,128]{1,0:T(8,128)(2,1)}, bf16[1280,128]{1,0:T(8,128)(2,1)S(1)}, u32[]{:S(2)}, u32[]{:S(2)}) collective-permute-start(bf16[1280,128]{1,0:T(8,128)(2,1)} %get-tuple-element.32), channel_id=1, source_target_pairs={{0,4},{1,5},{2,6},{3,7},{4,0},{5,1},{6,2},{7,3},{64,197},{65,198},... | collective-permute-start | bytes 983048 | tf_op jit(solution)/shard_map/ppermute | solution.py:77
  34.1 9.0 %collective-permute-start.18 = (f32[32,1024]{1,0:T(8,128)S(1)}, f32[32,1024]{1,0:T(8,128)S(1)}, u32[]{:S(2)}, u32[]{:S(2)}) collective-permute-start(f32[32,1024]{1,0:T(8,128)S(1)} %add.41), channel_id=1, source_target_pairs={{0,16},{8,24},{16,0},{24,8},{32,48},{40,56},{48,32},{56,40},{1,17}... | collective-permute-start | bytes 393224 | tf_op jit(solution)/shard_map/ppermute | solution.py:29
  34.9 10.9 %collective-permute-start.8 = (bf16[1280,128]{1,0:T(8,128)(2,1)}, bf16[1280,128]{1,0:T(8,128)(2,1)S(1)}, u32[]{:S(2)}, u32[]{:S(2)}) collective-permute-start(bf16[1280,128]{1,0:T(8,128)(2,1)} %get-tuple-element.33), channel_id=1, source_target_pairs={{0,6},{1,7},{2,4},{3,5},{4,2},{5,3},{6,0},{7,1},{64,199},{65,196},... | collective-permute-start | bytes 983048 | tf_op jit(solution)/shard_map/ppermute | solution.py:77
  38.1 13.5 %collective-permute-start.9 = (bf16[1280,128]{1,0:T(8,128)(2,1)}, bf16[1280,128]{1,0:T(8,128)(2,1)S(1)}, u32[]{:S(2)}, u32[]{:S(2)}) collective-permute-start(bf16[1280,128]{1,0:T(8,128)(2,1)} %get-tuple-element.35), channel_id=1, source_target_pairs={{0,1},{1,2},{2,3},{3,0},{4,5},{5,6},{6,7},{7,4},{64,67},{65,64},{6... | collective-permute-start | bytes 983048 | tf_op jit(solution)/shard_map/ppermute | solution.py:77
  38.4 13.3 %collective-permute-start.10 = (bf16[1280,128]{1,0:T(8,128)(2,1)}, bf16[1280,128]{1,0:T(8,128)(2,1)S(1)}, u32[]{:S(2)}, u32[]{:S(2)}) collective-permute-start(bf16[1280,128]{1,0:T(8,128)(2,1)} %get-tuple-element.37), channel_id=1, source_target_pairs={{64,66},{65,67},{66,64},{67,65},{68,70},{69,71},{70,68},{71,69},{1... | collective-permute-start | bytes 983048 | tf_op jit(solution)/shard_map/ppermute | solution.py:77
  39.1 13.1 %collective-permute-start.5 = (bf16[1024,128]{1,0:T(8,128)(2,1)S(1)}, bf16[1024,128]{1,0:T(8,128)(2,1)S(1)}, u32[]{:S(2)}, u32[]{:S(2)}) collective-permute-start(bf16[1024,128]{1,0:T(8,128)(2,1)S(1)} %collective-permute-done.3.refs_6_), channel_id=1, source_target_pairs={{0,8},{8,16},{16,24},{24,32},{32,40},{40,48},{48,56},{56,0},{1,9},... | collective-permute-start | bytes 786440 | tf_op jit(solution)/shard_map/ppermute | solution.py:25
  43.1 13.4 %collective-permute-start.4 = (bf16[1024,128]{1,0:T(8,128)(2,1)S(1)}, bf16[1024,128]{1,0:T(8,128)(2,1)S(1)}, u32[]{:S(2)}, u32[]{:S(2)}) collective-permute-start(bf16[1024,128]{1,0:T(8,128)(2,1)S(1)} %collective-permute-done.2.refs_2_), channel_id=1, source_target_pairs={{0,56},{8,0},{16,8},{24,16},{32,24},{40,32},{48,40},{56,48},{1,57}... | collective-permute-start | bytes 786440 | tf_op jit(solution)/shard_map/ppermute | solution.py:25
  45.8 19.6 %collective-permute-start.11 = (bf16[1280,128]{1,0:T(8,128)(2,1)S(1)}, bf16[1280,128]{1,0:T(8,128)(2,1)S(1)}, u32[]{:S(2)}, u32[]{:S(2)}) collective-permute-start(bf16[1280,128]{1,0:T(8,128)(2,1)S(1)} %collective-permute-done.7.refs_9_), channel_id=1, source_target_pairs={{0,64},{64,0},{1,65},{65,1},{2,66},{66,2},{3,67},{67,3},{4,68},{68... | collective-permute-start | bytes 983048 | tf_op jit(solution)/shard_map/ppermute | solution.py:81
  51.6 13.8 %collective-permute-start.12 = (bf16[1280,128]{1,0:T(8,128)(2,1)S(1)}, bf16[1280,128]{1,0:T(8,128)(2,1)S(1)}, u32[]{:S(2)}, u32[]{:S(2)}) collective-permute-start(bf16[1280,128]{1,0:T(8,128)(2,1)S(1)} %collective-permute-done.8.refs_10_), channel_id=1, source_target_pairs={{0,64},{64,0},{1,65},{65,1},{2,66},{66,2},{3,67},{67,3},{4,68},{68... | collective-permute-start | bytes 983048 | tf_op jit(solution)/shard_map/ppermute | solution.py:81
  51.6 13.7 %collective-permute-start.13 = (bf16[1280,128]{1,0:T(8,128)(2,1)S(1)}, bf16[1280,128]{1,0:T(8,128)(2,1)S(1)}, u32[]{:S(2)}, u32[]{:S(2)}) collective-permute-start(bf16[1280,128]{1,0:T(8,128)(2,1)S(1)} %collective-permute-done.9.refs_11_), channel_id=1, source_target_pairs={{0,64},{64,0},{1,65},{65,1},{2,66},{66,2},{3,67},{67,3},{4,68},{68... | collective-permute-start | bytes 983048 | tf_op jit(solution)/shard_map/ppermute | solution.py:81
  52.1 9.6 %collective-permute-start.19 = (bf16[32,1024]{1,0:T(8,128)(2,1)S(1)}, bf16[32,1024]{1,0:T(8,128)(2,1)S(1)}, u32[]{:S(2)}, u32[]{:S(2)}) collective-permute-start(bf16[32,1024]{1,0:T(8,128)(2,1)S(1)} %get-tuple-element.47), channel_id=1, source_target_pairs={{0,32},{8,40},{16,48},{24,56},{32,0},{40,8},{48,16},{56,24},{1,33}... | collective-permute-start | bytes 196616 | tf_op jit(solution)/shard_map/ppermute | solution.py:29
  56.5 8.9 %collective-permute-start.14 = (bf16[1280,128]{1,0:T(8,128)(2,1)S(1)}, bf16[1280,128]{1,0:T(8,128)(2,1)S(1)}, u32[]{:S(2)}, u32[]{:S(2)}) collective-permute-start(bf16[1280,128]{1,0:T(8,128)(2,1)S(1)} %collective-permute-done.10.refs_12_), channel_id=1, source_target_pairs={{64,0},{65,1},{66,2},{67,3},{68,4},{69,5},{70,6},{71,7},{72,8},{73... | collective-permute-start | bytes 983048 | tf_op jit(solution)/shard_map/ppermute | solution.py:81
  79.0 13.7 %collective-permute-start.20 = (bf16[1312,128]{1,0:T(8,128)(2,1)}, bf16[1312,128]{1,0:T(8,128)(2,1)S(1)}, u32[]{:S(2)}, u32[]{:S(2)}) collective-permute-start(bf16[1312,128]{1,0:T(8,128)(2,1)} %get-tuple-element.40), channel_id=1, source_target_pairs={{0,6},{1,7},{2,4},{3,5},{4,2},{5,3},{6,0},{7,1},{8,14},{9,15},{10,... | collective-permute-start | bytes 1007624 | tf_op jit(solution)/shard_map/ppermute | solution.py:53
  79.9 21.1 %collective-permute-start.21 = (bf16[1312,128]{1,0:T(8,128)(2,1)}, bf16[1312,128]{1,0:T(8,128)(2,1)S(1)}, u32[]{:S(2)}, u32[]{:S(2)}) collective-permute-start(bf16[1312,128]{1,0:T(8,128)(2,1)} %get-tuple-element.41), channel_id=1, source_target_pairs={{0,5},{1,6},{2,7},{3,4},{4,1},{5,2},{6,3},{7,0},{8,13},{9,14},{10,... | collective-permute-start | bytes 1007624 | tf_op jit(solution)/shard_map/ppermute | solution.py:53
  84.5 26.1 %collective-permute-start.22 = (bf16[1312,128]{1,0:T(8,128)(2,1)}, bf16[1312,128]{1,0:T(8,128)(2,1)S(1)}, u32[]{:S(2)}, u32[]{:S(2)}) collective-permute-start(bf16[1312,128]{1,0:T(8,128)(2,1)} %get-tuple-element.42), channel_id=1, source_target_pairs={{0,7},{1,4},{2,5},{3,6},{4,3},{5,0},{6,1},{7,2},{8,15},{9,12},{10,... | collective-permute-start | bytes 1007624 | tf_op jit(solution)/shard_map/ppermute | solution.py:53
  84.5 26.1 %collective-permute-start.23 = (bf16[1312,128]{1,0:T(8,128)(2,1)}, bf16[1312,128]{1,0:T(8,128)(2,1)S(1)}, u32[]{:S(2)}, u32[]{:S(2)}) collective-permute-start(bf16[1312,128]{1,0:T(8,128)(2,1)} %get-tuple-element.43), channel_id=1, source_target_pairs={{0,2},{1,3},{2,0},{3,1},{4,6},{5,7},{6,4},{7,5},{8,10},{9,11},{10,... | collective-permute-start | bytes 1007624 | tf_op jit(solution)/shard_map/ppermute | solution.py:53
  86.6 25.7 %collective-permute-start.24 = (bf16[1312,128]{1,0:T(8,128)(2,1)}, bf16[1312,128]{1,0:T(8,128)(2,1)S(1)}, u32[]{:S(2)}, u32[]{:S(2)}) collective-permute-start(bf16[1312,128]{1,0:T(8,128)(2,1)} %get-tuple-element.44), channel_id=1, source_target_pairs={{0,1},{1,2},{2,3},{3,0},{4,5},{5,6},{6,7},{7,4},{8,9},{9,10},{10,1... | collective-permute-start | bytes 1007624 | tf_op jit(solution)/shard_map/ppermute | solution.py:53
  92.8 24.9 %collective-permute-start.25 = (bf16[1312,128]{1,0:T(8,128)(2,1)}, bf16[1312,128]{1,0:T(8,128)(2,1)S(1)}, u32[]{:S(2)}, u32[]{:S(2)}) collective-permute-start(bf16[1312,128]{1,0:T(8,128)(2,1)} %get-tuple-element.45), channel_id=1, source_target_pairs={{0,3},{1,0},{2,1},{3,2},{4,7},{5,4},{6,5},{7,6},{8,11},{9,8},{10,9... | collective-permute-start | bytes 1007624 | tf_op jit(solution)/shard_map/ppermute | solution.py:53
  101.0 16.7 %collective-permute-start.26 = (bf16[1312,128]{1,0:T(8,128)(2,1)}, bf16[1312,128]{1,0:T(8,128)(2,1)S(1)}, u32[]{:S(2)}, u32[]{:S(2)}) collective-permute-start(bf16[1312,128]{1,0:T(8,128)(2,1)} %get-tuple-element.46), channel_id=1, source_target_pairs={{0,4},{1,5},{2,6},{3,7},{4,0},{5,1},{6,2},{7,3},{8,12},{9,13},{10,... | collective-permute-start | bytes 1007624 | tf_op jit(solution)/shard_map/ppermute | solution.py:53
  (33 other events, 477.5 us)

commit v3 on v2

v3 whole, which is shorter than its diff:
```python
import functools
import math

import jax
import jax.numpy as jnp
from jax import lax
from jax.experimental import pallas as pl
from jax.experimental.pallas import tpu as pltpu
from jax.sharding import Mesh, PartitionSpec as P

HEAD_SIZE = 128
BLOCK = 128
RANK = 32
ROPE_BASE = 500000.0
ADAPTER_SCALE = 2.0
NXH, NC, NZ, NX, NY = 2, 2, 8, 2, 4
REQ_AXES = ("xh", "c")
TP_AXES = ("z", "xl", "y")
NP = NX * NY
TA, TB = 384, 640
VMEM = pl.BlockSpec(memory_space=pltpu.VMEM)
SMEM = pl.BlockSpec(memory_space=pltpu.SMEM)


def z_shift(v, s):
    return lax.ppermute(v, "z", [(i, (i + s) % NZ) for i in range(NZ)])


def z_xor(v, s):
    return lax.ppermute(v, "z", [(i, i ^ s) for i in range(NZ)])


def y_xor(v, s):
    return lax.ppermute(v, "y", [(i, i ^ s) for i in range(NY)])


def x_swap(v):
    return lax.ppermute(v, "xl", [(0, 1), (1, 0)])


def core_swap(v):
    return lax.ppermute(v, "c", [(0, 1), (1, 0)])


def xh_swap(v):
    return lax.ppermute(v, "xh", [(0, 1), (1, 0)])


def y_shift(v, s):
    return lax.ppermute(v, "y", [(i, (i + s) % NY) for i in range(NY)])


SERVED = ((4, 6, 1), (5, 7, 3, 2))
FLIP = [dx * NY + (-dy) % NY for dx in range(NX) for dy in range(NY)]


def weight_send(v, k):
    route = []
    for xh in range(NXH):
        for c in range(NC):
            if k >= len(SERVED[c]):
                continue
            dx, dy = divmod(SERVED[c][k], NY)
            for xl in range(NX):
                for y in range(NY):
                    at = xh * NX + xl
                    if dx:
                        to = at ^ 1 if c == 0 else (at + 1 if at % 2 else at - 1) % 4
                    else:
                        to = at
                    src = ((xh * NC + c) * NX + xl) * NY + y
                    dst = ((to // NX * NC + c) * NX + to % NX) * NY + (y + dy) % NY
                    route.append((src, dst))
    return lax.ppermute(v, ("xh", "c", "xl", "y"), route)


def weight_swap(v, k):
    return lax.ppermute(v, "c", [(c, 1 - c) for c in range(NC) if k < len(SERVED[c])])


def pack_kernel(s_ref, wq_ref, kv_ref, *outs):
    z, xl, y, c = s_ref[0], s_ref[1], s_ref[2], s_ref[3]
    for k in range(5):
        d = 0
        if k < 4:
            d = jnp.where(c == 0, (SERVED[0] + (0,))[k], SERVED[1][k])
        p = (xl ^ (d // NY)) * NY + ((y + d) & (NY - 1))
        for j in range(NZ):
            row = pl.multiple_of((((z + j) & (NZ - 1)) * NP + p) * 128, 128)
            outs[k][j * 128 : (j + 1) * 128, :] = wq_ref[pl.ds(row, 128), :]
            outs[k][1024 + j * 32 : 1024 + (j + 1) * 32, :] = kv_ref[:, pl.ds(row, 128)]


def low_kernel(s_ref, ad_ref, h_ref, near_ref, far_ref, out_ref):
    c, xh = s_ref[3], s_ref[4]
    per = near_ref.shape[1]
    for b in range(h_ref.shape[0] // BLOCK):
        a = ad_ref[b]
        owner = a // per
        at = a - owner * per
        xr, cr = (owner // NC) ^ xh, (owner % NC) ^ c
        down = jnp.where(cr == 0, near_ref[xr, at, 0:RANK, :], far_ref[xr, at, 0:RANK, :])
        out_ref[:, b * BLOCK : (b + 1) * BLOCK] = lax.dot_general(
            down,
            h_ref[b * BLOCK : (b + 1) * BLOCK, :],
            (((1,), (1,)), ((), ())),
            preferred_element_type=jnp.float32,
        )


def for_each_piece(c, own, mine, other, place):
    place(own, 0)
    for core in range(NC):

        @pl.when(c == core)
        def _():
            for k, d in enumerate(SERVED[core]):
                place(mine[k], FLIP[d])
            for k, d in enumerate(SERVED[1 - core]):
                place(other[k], FLIP[d])


def kv_product_kernel(s_ref, *refs):
    h_refs, own, mine, other = refs[0:8], refs[8], refs[9:13], refs[13:17]
    outs, hbuf, kvw = refs[17:21], refs[21], refs[22]
    for j in range(8):
        hbuf[:, j * 128 : (j + 1) * 128] = h_refs[j][...]

    def place(ref, d):
        for j in range(NZ):
            kvw[d * 32 : (d + 1) * 32, j * 128 : (j + 1) * 128] = ref[1024 + j * 32 : 1056 + j * 32, :]

    for_each_piece(s_ref[3], own, mine, other, place)
    kv = lax.dot_general(
        kvw[...], hbuf[...], (((1,), (1,)), ((), ())), preferred_element_type=jnp.float32
    ).astype(jnp.bfloat16)
    for d in range(NP):
        dx, dy = divmod(d, NY)
        for t in range(8):
            at = t * 64 + dx * 32
            outs[dy][at : at + 32, :] = kv[d * 32 : (d + 1) * 32, t * 128 : (t + 1) * 128]


def q_product_kernel(s_ref, *refs):
    h_refs, own, mine, other = refs[0:8], refs[8], refs[9:13], refs[13:17]
    near_ref, far_ref, outs, hbuf, wq = refs[17], refs[18], refs[19:23], refs[23], refs[24]
    for j in range(8):
        hbuf[:, j * 128 : (j + 1) * 128] = h_refs[j][...]

    def place(ref, d):
        dx, dy = divmod(d, NY)
        wq[dy, :, dx * 128 : (dx + 1) * 128] = ref[0:1024, :]

    for_each_piece(s_ref[3], own, mine, other, place)
    for dy in range(NY):
        q = jnp.dot(hbuf[0:TA, :], wq[dy], preferred_element_type=jnp.float32).astype(jnp.bfloat16)
        near_ref[dy * TA : (dy + 1) * TA, :] = q[:, 0:128]
        far_ref[dy * TA : (dy + 1) * TA, :] = q[:, 128:256]
    for dy in range(NY):
        q = jnp.dot(hbuf[TA:1024, :], wq[dy], preferred_element_type=jnp.float32).astype(jnp.bfloat16)
        outs[dy][0:TB, :] = q[:, 0:128]
        outs[dy][TB : 2 * TB, :] = q[:, 128:256]


def wide(ref, rows):
    return ref[rows, :].astype(jnp.float32)


def kv_join_kernel(k0, k1, k2, k3, far_ref, sum_ref, send_ref):
    total = wide(k0, ...) + wide(k1, ...) + wide(k2, ...) + wide(k3, ...)
    sum_ref[...] = total
    send_ref[0 : NY * TA, :] = far_ref[...]
    send_ref[NY * TA : NY * TA + 512, :] = total.astype(jnp.bfloat16)


def stage_a_kernel(near_ref, got_ref, kv_ref, own_ref, kv_out, *sends):
    for t in range(8):
        for dx in range(NX):
            a, b = t * 64 + dx * 32, NY * TA + t * 64 + (1 - dx) * 32
            kv_out[a : a + 32, :] = (kv_ref[a : a + 32, :] + wide(got_ref, slice(b, b + 32))).astype(jnp.bfloat16)
    for dy in range(NY):
        rows = slice(dy * TA, (dy + 1) * TA)
        total = wide(near_ref, rows) + wide(got_ref, rows)
        if dy == 0:
            own_ref[...] = total
        else:
            sends[dy - 1][0:TA, :] = total.astype(jnp.bfloat16)
            sends[dy - 1][TA : TA + 512, :] = kv_out[...]


def stage_b_kernel(b0, b1, b2, b3, own_ref, send_ref):
    for dx, out in enumerate((own_ref, send_ref)):
        rows = slice(dx * TB, (dx + 1) * TB)
        out[...] = (wide(b0, rows) + wide(b1, rows) + wide(b2, rows) + wide(b3, rows)).astype(out.dtype)


def attention_kernel(s_ref, ad_ref, lo_ref, *refs):
    a_own, a_got, b_own, b_got, kv_own = refs[0], refs[1:4], refs[4], refs[5], refs[6]
    low_ref, near_ref, far_ref, cos_ref, sin_ref = refs[7:12]
    out_ref = refs[12]
    kvt, k_buf, v_buf = refs[13:16]
    xl, y, c, xh = s_ref[1], s_ref[2], s_ref[3], s_ref[4]
    for i in range(NY):
        ref, base = (kv_own, 0) if i == 0 else (a_got[i - 1], TA)
        for dx in range(NX):
            p = (xl ^ dx) * NY + ((y - i) & (NY - 1))
            at = pl.multiple_of(p * 32, 32)
            for t in range(8):
                kvt[pl.ds(at, 32), t * 128 : (t + 1) * 128] = ref[base + t * 64 + dx * 32 : base + t * 64 + dx * 32 + 32, :]

    def rope(v, rows):
        return v * cos_ref[rows, :] + pltpu.roll(v, 64, 1) * sin_ref[rows, :]

    for t in range(8):
        rows = slice(t * 128, (t + 1) * 128)
        k = kvt[0:128, rows].astype(jnp.float32).T
        k_buf[rows, :] = rope(k, rows).astype(jnp.bfloat16)
        v_buf[rows, :] = kvt[128:256, rows].T
    per = near_ref.shape[1]
    factor = math.log2(math.e) / math.sqrt(HEAD_SIZE)
    for b in range(8):
        rows = slice(b * 128, (b + 1) * 128)
        a = ad_ref[b]
        owner = a // per
        at = a - owner * per
        xr, cr = (owner // NC) ^ xh, (owner % NC) ^ c
        up = jnp.where(cr == 0, near_ref[xr, at, RANK : 2 * RANK, :], far_ref[xr, at, RANK : 2 * RANK, :])
        q = ADAPTER_SCALE * lax.dot_general(
            low_ref[:, rows].astype(jnp.bfloat16), up, (((0,), (0,)), ((), ())), preferred_element_type=jnp.float32
        )
        if b * 128 < TA:
            q += a_own[rows, :]
            for ref in a_got:
                q += wide(ref, rows)
        else:
            part = slice(b * 128 - TA, (b + 1) * 128 - TA)
            q += b_own[part, :] + wide(b_got, part)
        q = rope(q, rows).astype(jnp.bfloat16)
        n = (b + 1) * 128
        s = lax.dot_general(
            q, k_buf[0:n, :], (((1,), (1,)), ((), ())), preferred_element_type=jnp.float32
        )
        col = lax.broadcasted_iota(jnp.int32, (128, n), 1)
        row = lax.broadcasted_iota(jnp.int32, (128, n), 0) + b * 128
        allowed = (col >= lo_ref[b]) & (col <= row)
        s = jnp.where(allowed, s, -1e30)
        e = jnp.exp2((s - jnp.max(s, axis=1, keepdims=True)) * factor)
        probs = (e * (1.0 / jnp.sum(e, axis=1, keepdims=True))).astype(jnp.bfloat16)
        out_ref[rows, :] = jnp.dot(
            probs, v_buf[0:n, :], preferred_element_type=jnp.float32
        ).astype(jnp.bfloat16)


def call(kernel, name, outs, *args, scalars=0, scratch=()):
    single = isinstance(outs, jax.ShapeDtypeStruct)
    return pl.pallas_call(
        kernel,
        out_shape=outs,
        in_specs=[SMEM] * scalars + [VMEM] * (len(args) - scalars),
        out_specs=VMEM if single else [VMEM] * len(outs),
        scratch_shapes=scratch,
        name=name,
    )(*args)


def rope_tables(positions):
    half = HEAD_SIZE // 2
    steps = jnp.arange(half, dtype=jnp.float32)
    inverse = jnp.exp(-(2.0 * steps / HEAD_SIZE) * math.log(ROPE_BASE))
    angles = positions.astype(jnp.float32)[:, None] * inverse[None, :]
    cosines, sines = jnp.cos(angles), jnp.sin(angles)
    return jnp.concatenate([cosines, cosines], 1), jnp.concatenate([-sines, sines], 1)


def after(value, *others):
    return lax.optimization_barrier((value, *others))[0]


def body(hidden, query_weight, key_value_weight, down_maps, up_maps, request_start, adapters):
    rows = hidden.shape[0]
    bf16, f32 = jnp.bfloat16, jnp.float32
    of = jax.ShapeDtypeStruct
    place = [lax.axis_index(a) for a in ("z", "xl", "y", "c", "xh")]
    scalars = jnp.stack(place).astype(jnp.int32)

    maps = jnp.concatenate([jnp.transpose(down_maps, (0, 2, 1)), up_maps], axis=1)
    twin = xh_swap(maps)

    sends = call(
        pack_kernel, "pack", [of((1280, 128), bf16)] * 5, scalars, query_weight, key_value_weight.T, scalars=1
    )
    right, left = [hidden], [hidden]
    mine = [weight_send(sends[k], k) for k in range(2)]
    gates = ((), (0,), (1, 2), (3,))
    for step in range(4):
        r, l = right[-1], left[-1]
        if step:
            waits = [mine[k] for k in gates[step]]
            r, l = after(right[-1], left[-1], *waits), after(left[-1], right[-1], *waits)
        right.append(z_shift(r, 1))
        if step < 3:
            left.append(z_shift(l, -1))
        if step == 1:
            mine += [weight_send(after(sends[k], right[1], left[1]), k) for k in (2, 3)]
    other = [weight_swap(mine[k], k) for k in range(4)]

    near = jnp.stack([maps, after(twin, right[1], left[1])])
    far = core_swap(near)
    low = call(
        low_kernel, "low", of((RANK, rows), f32), scalars, adapters, hidden, near, after(far, right[2], left[2]), scalars=2
    )
    low = low + x_swap(low)
    low = low + y_xor(low, 1)
    low = low + y_xor(low, 2)

    shards = [hidden, left[1], left[2], left[3], right[4], right[3], right[2], right[1]]
    weights = (sends[4], *mine, *other)
    kv_parts = call(
        kv_product_kernel,
        "kv_product",
        [of((512, 128), bf16)] * NY,
        scalars,
        *shards,
        *weights,
        scalars=1,
        scratch=[pltpu.VMEM((rows, 1024), bf16), pltpu.VMEM((256, 1024), bf16)],
    )
    kv_got = [y_shift(kv_parts[dy], dy) for dy in (2, 1, 3)]
    near_a, far_a, *b_parts = call(
        q_product_kernel,
        "q_product",
        [of((NY * TA, 128), bf16)] * 2 + [of((2 * TB, 128), bf16)] * NY,
        after(scalars, kv_parts[0]),
        *shards,
        *weights,
        scalars=1,
        scratch=[pltpu.VMEM((rows, 1024), bf16), pltpu.VMEM((NY, 1024, 256), bf16)],
    )
    b_got = [y_shift(b_parts[dy], dy) for dy in (2, 1, 3)]
    kv_sum, x_send = call(
        kv_join_kernel,
        "kv_join",
        [of((512, 128), f32), of((NY * TA + 512, 128), bf16)],
        kv_parts[0],
        *kv_got,
        far_a,
    )
    x_got = x_swap(x_send)
    low = low + z_xor(low, 1)
    low = low + z_xor(low, 2)
    low = low + z_xor(low.astype(bf16), 4).astype(f32)
    a_own, kv_own, *a_sends = call(
        stage_a_kernel,
        "stage_a",
        [of((TA, 128), f32), of((512, 128), bf16)] + [of((TA + 512, 128), bf16)] * (NY - 1),
        near_a,
        x_got,
        kv_sum,
    )
    a_got = {dy: y_shift(a_sends[dy - 1], dy) for dy in (2, 1, 3)}
    b_own, b_send = call(
        stage_b_kernel, "stage_b", [of((TB, 128), f32), of((TB, 128), bf16)], b_parts[0], *b_got
    )
    b_last = x_swap(b_send)

    first = lax.axis_index("xh") * NC + lax.axis_index("c")
    places = first * rows + jnp.arange(rows, dtype=jnp.int32)
    cosines, sines = rope_tables(places - request_start * BLOCK)
    lowest = request_start[::BLOCK] * BLOCK - first * rows
    return call(
        attention_kernel,
        "attention",
        of((rows, HEAD_SIZE), bf16),
        scalars,
        adapters,
        lowest,
        a_own,
        *[a_got[dy] for dy in (1, 2, 3)],
        b_own,
        b_last,
        kv_own,
        low,
        near,
        far,
        cosines,
        sines,
        scalars=3,
        scratch=[pltpu.VMEM((256, rows), bf16)] + [pltpu.VMEM((rows, HEAD_SIZE), bf16)] * 2,
    )


def solution(mesh):
    fine = Mesh(mesh.devices.reshape(NXH, NC, NZ, NX, NY), REQ_AXES + TP_AXES)
    in_specs = (
        P(REQ_AXES, TP_AXES),
        P(None, TP_AXES),
        P(None, TP_AXES),
        P(REQ_AXES, TP_AXES, None),
        P(REQ_AXES, None, TP_AXES),
        P(REQ_AXES),
        P(REQ_AXES),
    )
    return jax.shard_map(
        body, mesh=fine, in_specs=in_specs, out_specs=P(REQ_AXES, TP_AXES), check_vma=False
    )
```

time: 146 us -> 131 us (0.90)
  the two profiles are of different devices: /device:TPU:6 before, /device:TPU:2 now
where the time goes in v3:
time: 131 us; the launch traced here: 130 us
  starting transfers between devices  47.4 us (36%)
  waiting for transfers between devices  37.4 us (29%)
  Pallas kernels  30.8 us (24%)
  other arithmetic  9.06 us (7%)
  local copies, waits for them, and re-layouts  5.26 us (4%)
    pallas_call x8, Pallas kernels, call(): pl.pallas_call(kernel, out_shape=outs, in_specs=[SMEM] * scalars + [VMEM]...  30.8 us
    ppermute x9, waiting for transfers between devices, y_shift(): return lax.ppermute(v, 'y', [(i, (i + s) % NY) for i in range(NY)])  16.4 us
    ppermute x9, starting transfers between devices, y_shift(): return lax.ppermute(v, 'y', [(i, (i + s) % NY) for i in range(NY)])  13.7 us
    ppermute x7, starting transfers between devices, z_shift(): return lax.ppermute(v, 'z', [(i, (i + s) % NZ) for i in range(NZ)])  11.2 us
    ppermute x7, waiting for transfers between devices, z_shift(): return lax.ppermute(v, 'z', [(i, (i + s) % NZ) for i in range(NZ)])  9.4 us
    ppermute x4, starting transfers between devices, weight_send(): return lax.ppermute(v, ('xh', 'c', 'xl', 'y'), route)  5.99 us
    unnamed x50, local copies, waits for them, and re-layouts  4.5 us
    ppermute x2, starting transfers between devices, y_xor(): return lax.ppermute(v, 'y', [(i, i ^ s) for i in range(NY)])  3.89 us
  transfers between devices with their start and end apart: 34, of which 13 were waited for; matrix products, arithmetic and copies ran while one was open for 8% of the time, Pallas kernels for 18%

profile of v3, /device:TPU:2, one launch (start us, length us, event | category | flops | bytes accessed | tf_op | source)
XLA Modules:
  0.0 130.3 jit_solution(3504596590924433399)
XLA Ops:
  0.0 5.9 %collective-permute-start = (bf16[1024,128]{1,0:T(8,128)(2,1)}, bf16[1024,128]{1,0:T(8,128)(2,1)S(1)}, u32[]{:S(2)}, u32[]{:S(2)}) collective-permute-start(bf16[1024,128]{1,0:T(8,128)(2,1)} %h_ref.1), channel_id=1, source_target_pairs={{0,56},{8,0},{16,8},{24,16},{32,24},{40,32},{48,40},{56,48},{1,57}... | collective-permute-start | bytes 786440 | tf_op jit(solution)/shard_map/ppermute | solution.py:26
  6.9 2.2 %collective-permute-start.26 = (bf16[16,64,128]{2,1,0:T(8,128)(2,1)S(1)}, bf16[16,64,128]{2,1,0:T(8,128)(2,1)S(1)}, u32[]{:S(2)}, u32[]{:S(2)}) collective-permute-start(bf16[16,64,128]{2,1,0:T(8,128)(2,1)S(1)} %get-tuple-element.76), channel_id=1, source_target_pairs={{0,128},{128,0},{1,129},{129,1},{2,130},{130,2},{3,131},{131,3},{4... | collective-permute-start | bytes 786440 | tf_op jit(solution)/shard_map/ppermute | solution.py:46
  9.8 3.1 %pack.1 = (bf16[1280,128]{1,0:T(8,128)(2,1)}, bf16[1280,128]{1,0:T(8,128)(2,1)}, bf16[1280,128]{1,0:T(8,128)(2,1)}, bf16[1280,128]{1,0:T(8,128)(2,1)}, bf16[1280,128]{1,0:T(8,128)(2,1)}) custom-call(s32[5]{0:T(128)} %stack.32.s_ref, bf16[8192,128]{1,0:T(8,128)(2,1)} %wq_ref.1, bf16[32,8192]{1,0:T(8,128)(2,1)} %bitcast.10), custom_call_target="tpu_custom_call" | custom-call | tf_op jit(solution)/shard_map/pack/pallas_call | solution.py:256
  16.5 3.2 %collective-permute-start.5 = (bf16[1280,128]{1,0:T(8,128)(2,1)}, bf16[1280,128]{1,0:T(8,128)(2,1)S(1)}, u32[]{:S(2)}, u32[]{:S(2)}) collective-permute-start(bf16[1280,128]{1,0:T(8,128)(2,1)} %get-tuple-element.42), channel_id=1, source_target_pairs={{0,6},{1,7},{2,4},{3,5},{4,2},{5,3},{6,0},{7,1},{64,199},{65,196},... | collective-permute-start | bytes 983048 | tf_op jit(solution)/shard_map/ppermute | solution.py:74
  20.4 3.0 %collective-permute-start.3 = (bf16[1024,128]{1,0:T(8,128)(2,1)S(1)}, bf16[1024,128]{1,0:T(8,128)(2,1)}, u32[]{:S(2)}, u32[]{:S(2)}) collective-permute-start(bf16[1024,128]{1,0:T(8,128)(2,1)S(1)} %collective-permute-done.refs_1_), channel_id=1, source_target_pairs={{0,56},{8,0},{16,8},{24,16},{32,24},{40,32},{48,40},{56,48},{1,57}... | collective-permute-start | bytes 786440 | tf_op jit(solution)/shard_map/ppermute | solution.py:26
  23.4 3.1 %collective-permute-done.5.refs_10_ = bf16[1280,128]{1,0:T(8,128)(2,1)S(1)} collective-permute-done((bf16[1280,128]{1,0:T(8,128)(2,1)}, bf16[1280,128]{1,0:T(8,128)(2,1)S(1)}, u32[]{:S(2)}, u32[]{:S(2)}) %collective-permute-start.5) | collective-permute-done | bytes 327712 | tf_op jit(solution)/shard_map/ppermute | solution.py:74
  27.2 2.3 %collective-permute-done.3.refs_2_ = bf16[1024,128]{1,0:T(8,128)(2,1)} collective-permute-done((bf16[1024,128]{1,0:T(8,128)(2,1)S(1)}, bf16[1024,128]{1,0:T(8,128)(2,1)}, u32[]{:S(2)}, u32[]{:S(2)}) %collective-permute-start.3) | collective-permute-done | bytes 262176 | tf_op jit(solution)/shard_map/ppermute | solution.py:26
  36.5 2.2 %low.1 = f32[32,1024]{1,0:T(8,128)} custom-call(s32[5]{0:T(128)} %stack.32.s_ref, s32[8]{0:T(128)} %ad_ref.3, bf16[1024,128]{1,0:T(8,128)(2,1)} %h_ref.1, bf16[2,16,64,128]{3,2,1,0:T(8,128)(2,1)} %copy-done, bf16[2,16,64,128]{3,2,1,0:T(8,128)(2,1)} %copy-done.1), custom_call_target="tpu_custom_call" | custom-call | tf_op jit(solution)/shard_map/low/pallas_call | solution.py:256
  40.3 3.6 %collective-permute-done.28 = f32[32,1024]{1,0:T(8,128)S(1)} collective-permute-done((f32[32,1024]{1,0:T(8,128)}, f32[32,1024]{1,0:T(8,128)S(1)}, u32[]{:S(2)}, u32[]{:S(2)}) %collective-permute-start.28) | collective-permute-done | bytes 131104 | tf_op jit(solution)/shard_map/ppermute | solution.py:38
  47.7 2.2 %collective-permute-done.29 = f32[32,1024]{1,0:T(8,128)} collective-permute-done((f32[32,1024]{1,0:T(8,128)S(1)}, f32[32,1024]{1,0:T(8,128)}, u32[]{:S(2)}, u32[]{:S(2)}) %collective-permute-start.29) | collective-permute-done | bytes 131104 | tf_op jit(solution)/shard_map/ppermute | solution.py:34
  51.8 2.7 %collective-permute-start.30 = (f32[32,1024]{1,0:T(8,128)}, f32[32,1024]{1,0:T(8,128)S(1)}, u32[]{:S(2)}, u32[]{:S(2)}) collective-permute-start(f32[32,1024]{1,0:T(8,128)} %add.29), channel_id=1, source_target_pairs={{0,2},{1,3},{2,0},{3,1},{4,6},{5,7},{6,4},{7,5},{8,10},{9,11},{10,... | collective-permute-start | bytes 393224 | tf_op jit(solution)/shard_map/ppermute | solution.py:34
  54.6 4.3 %collective-permute-done.10.refs_4_ = bf16[1024,128]{1,0:T(8,128)(2,1)S(1)} collective-permute-done((bf16[1024,128]{1,0:T(8,128)(2,1)}, bf16[1024,128]{1,0:T(8,128)(2,1)S(1)}, u32[]{:S(2)}, u32[]{:S(2)}) %collective-permute-start.10) | collective-permute-done | bytes 262176 | tf_op jit(solution)/shard_map/ppermute | solution.py:26
  59.6 4.6 %kv_product.1 = (bf16[512,128]{1,0:T(8,128)(2,1)}, bf16[512,128]{1,0:T(8,128)(2,1)}, bf16[512,128]{1,0:T(8,128)(2,1)}, bf16[512,128]{1,0:T(8,128)(2,1)}) custom-call(s32[5]{0:T(128)} %stack.32.s_ref, bf16[1024,128]{1,0:T(8,128)(2,1)} %h_ref.1, bf16[1024,128]{1,0:T(8,128)(2,1)} %copy-done.10, bf16[1024,128]{1,0:T(8,128)(2,1)} %collective-permute-done.3.refs_2_, ...), custom_call_target="tpu_custom_call" | custom-call | tf_op jit(solution)/shard_map/kv_product/pallas_call | solution.py:256
  64.2 3.3 %collective-permute-start.15 = (bf16[512,128]{1,0:T(8,128)(2,1)}, bf16[512,128]{1,0:T(8,128)(2,1)S(1)}, u32[]{:S(2)}, u32[]{:S(2)}) collective-permute-start(bf16[512,128]{1,0:T(8,128)(2,1)} %get-tuple-element.54), channel_id=1, source_target_pairs={{0,2},{1,3},{2,0},{3,1},{4,6},{5,7},{6,4},{7,5},{8,10},{9,11},{10,... | collective-permute-start | bytes 393224 | tf_op jit(solution)/shard_map/ppermute | solution.py:50
  68.3 2.4 %collective-permute-start.17 = (bf16[512,128]{1,0:T(8,128)(2,1)}, bf16[512,128]{1,0:T(8,128)(2,1)S(1)}, u32[]{:S(2)}, u32[]{:S(2)}) collective-permute-start(bf16[512,128]{1,0:T(8,128)(2,1)} %get-tuple-element.56), channel_id=1, source_target_pairs={{0,3},{1,0},{2,1},{3,2},{4,7},{5,4},{6,5},{7,6},{8,11},{9,8},{10,9... | collective-permute-start | bytes 393224 | tf_op jit(solution)/shard_map/ppermute | solution.py:50
  73.7 6.5 %q_product.1 = (bf16[1536,128]{1,0:T(8,128)(2,1)}, bf16[1536,128]{1,0:T(8,128)(2,1)}, bf16[1280,128]{1,0:T(8,128)(2,1)}, bf16[1280,128]{1,0:T(8,128)(2,1)}, bf16...) custom-call(s32[5]{0:T(128)} %stack.32.s_ref, bf16[1024,128]{1,0:T(8,128)(2,1)} %h_ref.1, bf16[1024,128]{1,0:T(8,128)(2,1)} %copy-done.10, ...), custom_call_target="tpu_custom_call" | custom-call | tf_op jit(solution)/shard_map/q_product/pallas_call | solution.py:256
  81.0 2.2 %kv_join.1 = (f32[512,128]{1,0:T(8,128)}, bf16[2048,128]{1,0:T(8,128)(2,1)}) custom-call(bf16[512,128]{1,0:T(8,128)(2,1)} %get-tuple-element.51.k0, bf16[512,128]{1,0:T(8,128)(2,1)} %copy-done.21, bf16[512,128]{1,0:T(8,128)(2,1)} %copy-done.22, bf16[512,128]{1,0:T(8,128)(2,1)} %copy-done.23, bf16[1536,128]{1,0:T(8,128)(2,1)} %get-tuple-element.57.far_ref), custom_call_target="tpu_custom_call" | custom-call | tf_op jit(solution)/shard_map/kv_join/pallas_call | solution.py:256
  86.1 2.9 %collective-permute-start.24 = (bf16[1280,128]{1,0:T(8,128)(2,1)}, bf16[1280,128]{1,0:T(8,128)(2,1)S(1)}, u32[]{:S(2)}, u32[]{:S(2)}) collective-permute-start(bf16[1280,128]{1,0:T(8,128)(2,1)} %get-tuple-element.67), channel_id=1, source_target_pairs={{0,3},{1,0},{2,1},{3,2},{4,7},{5,4},{6,5},{7,6},{8,11},{9,8},{10,9... | collective-permute-start | bytes 983048 | tf_op jit(solution)/shard_map/ppermute | solution.py:50
  90.5 2.9 %collective-permute-start.33 = (bf16[32,1024]{1,0:T(8,128)(2,1)S(1)}, bf16[32,1024]{1,0:T(8,128)(2,1)S(1)}, u32[]{:S(2)}, u32[]{:S(2)}) collective-permute-start(bf16[32,1024]{1,0:T(8,128)(2,1)S(1)} %get-tuple-element.73), channel_id=1, source_target_pairs={{0,32},{8,40},{16,48},{24,56},{32,0},{40,8},{48,16},{56,24},{1,33}... | collective-permute-start | bytes 196616 | tf_op jit(solution)/shard_map/ppermute | solution.py:30
  94.8 2.9 %collective-permute-done.22.b1 = bf16[1280,128]{1,0:T(8,128)(2,1)S(1)} collective-permute-done((bf16[1280,128]{1,0:T(8,128)(2,1)}, bf16[1280,128]{1,0:T(8,128)(2,1)S(1)}, u32[]{:S(2)}, u32[]{:S(2)}) %collective-permute-start.22) | collective-permute-done | bytes 327712 | tf_op jit(solution)/shard_map/ppermute | solution.py:50
  97.7 3.6 %collective-permute-done.23.b2 = bf16[1280,128]{1,0:T(8,128)(2,1)S(1)} collective-permute-done((bf16[1280,128]{1,0:T(8,128)(2,1)}, bf16[1280,128]{1,0:T(8,128)(2,1)S(1)}, u32[]{:S(2)}, u32[]{:S(2)}) %collective-permute-start.23) | collective-permute-done | bytes 327712 | tf_op jit(solution)/shard_map/ppermute | solution.py:50
  105.5 2.2 %stage_a.1 = (f32[384,128]{1,0:T(8,128)}, bf16[512,128]{1,0:T(8,128)(2,1)}, bf16[896,128]{1,0:T(8,128)(2,1)}, bf16[896,128]{1,0:T(8,128)(2,1)}, bf16[896,128]{1,0:T(8,128)(2,1)}) custom-call(bf16[1536,128]{1,0:T(8,128)(2,1)} %get-tuple-element.53.near_ref, bf16[2048,128]{1,0:T(8,128)(2,1)} %copy-done.13, f32[512,128]{1,0:T(8,128)} %get-tuple-element.59.kv_ref), custom_call_target="tpu_custom_call" | custom-call | tf_op jit(solution)/shard_map/stage_a/pallas_call | solution.py:256
  111.8 9.3 %collective-permute-done.19.refs_1_ = bf16[896,128]{1,0:T(8,128)(2,1)S(1)} collective-permute-done((bf16[896,128]{1,0:T(8,128)(2,1)}, bf16[896,128]{1,0:T(8,128)(2,1)S(1)}, u32[]{:S(2)}, u32[]{:S(2)}) %collective-permute-start.19) | collective-permute-done | bytes 229408 | tf_op jit(solution)/shard_map/ppermute | solution.py:50
  122.4 7.8 %attention.1 = bf16[1024,128]{1,0:T(8,128)(2,1)} custom-call(s32[5]{0:T(128)} %stack.32.s_ref, s32[8]{0:T(128)} %ad_ref.3, s32[8]{0:T(128)} %multiply_subtract_fusion.lo_ref, f32[384,128]{1,0:T(8,128)} %get-tuple-element.60.refs_0_, bf16[896,128]{1,0:T(8,128)(2,1)} %copy-done.17, bf16[896,128]{1,0:T(8,128)(2,1)} %copy-done.18, bf16[896,128]{1,0:T(8,128)(2,1)} %copy-done.19, ...), custom_call_target="tpu_custom_call" | custom-call | tf_op jit(solution)/shard_map/attention/pallas_call | solution.py:256
  (117 shorter events, 41.5 us)
Async XLA Ops:
  0.0 14.3 %collective-permute-start = (bf16[1024,128]{1,0:T(8,128)(2,1)}, bf16[1024,128]{1,0:T(8,128)(2,1)S(1)}, u32[]{:S(2)}, u32[]{:S(2)}) collective-permute-start(bf16[1024,128]{1,0:T(8,128)(2,1)} %h_ref.1), channel_id=1, source_target_pairs={{0,56},{8,0},{16,8},{24,16},{32,24},{40,32},{48,40},{56,48},{1,57}... | collective-permute-start | bytes 786440 | tf_op jit(solution)/shard_map/ppermute | solution.py:26
  5.9 9.2 %collective-permute-start.1 = (bf16[1024,128]{1,0:T(8,128)(2,1)}, bf16[1024,128]{1,0:T(8,128)(2,1)S(1)}, u32[]{:S(2)}, u32[]{:S(2)}) collective-permute-start(bf16[1024,128]{1,0:T(8,128)(2,1)} %h_ref.1), channel_id=1, source_target_pairs={{0,8},{8,16},{16,24},{24,32},{32,40},{40,48},{48,56},{56,0},{1,9},... | collective-permute-start | bytes 786440 | tf_op jit(solution)/shard_map/ppermute | solution.py:26
  6.9 9.4 %collective-permute-start.26 = (bf16[16,64,128]{2,1,0:T(8,128)(2,1)S(1)}, bf16[16,64,128]{2,1,0:T(8,128)(2,1)S(1)}, u32[]{:S(2)}, u32[]{:S(2)}) collective-permute-start(bf16[16,64,128]{2,1,0:T(8,128)(2,1)S(1)} %get-tuple-element.76), channel_id=1, source_target_pairs={{0,128},{128,0},{1,129},{129,1},{2,130},{130,2},{3,131},{131,3},{4... | collective-permute-start | bytes 786440 | tf_op jit(solution)/shard_map/ppermute | solution.py:46
  16.4 19.3 %collective-permute-start.27 = (bf16[2,16,64,128]{3,2,1,0:T(8,128)(2,1)S(1)}, bf16[2,16,64,128]{3,2,1,0:T(8,128)(2,1)S(1)}, u32[]{:S(2)}, u32[]{:S(2)}) collective-permute-start(bf16[2,16,64,128]{3,2,1,0:T(8,128)(2,1)S(1)} %pad_maximum_fusion.near_ref.refs_8_), channel_id=1, source_target_pairs={{0,64},{64,0},{1,65},{65,1},{2,66},{66,2},{3,67},{67,3},{4,68},{68... | collective-permute-start | bytes 1572872 | tf_op jit(solution)/shard_map/ppermute | solution.py:42
  16.5 10.0 %collective-permute-start.5 = (bf16[1280,128]{1,0:T(8,128)(2,1)}, bf16[1280,128]{1,0:T(8,128)(2,1)S(1)}, u32[]{:S(2)}, u32[]{:S(2)}) collective-permute-start(bf16[1280,128]{1,0:T(8,128)(2,1)} %get-tuple-element.42), channel_id=1, source_target_pairs={{0,6},{1,7},{2,4},{3,5},{4,2},{5,3},{6,0},{7,1},{64,199},{65,196},... | collective-permute-start | bytes 983048 | tf_op jit(solution)/shard_map/ppermute | solution.py:74
  19.7 13.9 %collective-permute-start.6 = (bf16[1280,128]{1,0:T(8,128)(2,1)}, bf16[1280,128]{1,0:T(8,128)(2,1)S(1)}, u32[]{:S(2)}, u32[]{:S(2)}) collective-permute-start(bf16[1280,128]{1,0:T(8,128)(2,1)} %get-tuple-element.44), channel_id=1, source_target_pairs={{0,1},{1,2},{2,3},{3,0},{4,5},{5,6},{6,7},{7,4},{64,67},{65,64},{6... | collective-permute-start | bytes 983048 | tf_op jit(solution)/shard_map/ppermute | solution.py:74
  23.4 10.2 %collective-permute-start.4 = (bf16[1024,128]{1,0:T(8,128)(2,1)S(1)}, bf16[1024,128]{1,0:T(8,128)(2,1)}, u32[]{:S(2)}, u32[]{:S(2)}) collective-permute-start(bf16[1024,128]{1,0:T(8,128)(2,1)S(1)} %collective-permute-done.1.refs_7_), channel_id=1, source_target_pairs={{0,8},{8,16},{16,24},{24,32},{32,40},{40,48},{48,56},{56,0},{1,9},... | collective-permute-start | bytes 786440 | tf_op jit(solution)/shard_map/ppermute | solution.py:26
  26.5 19.4 %collective-permute-start.9 = (bf16[1280,128]{1,0:T(8,128)(2,1)}, bf16[1280,128]{1,0:T(8,128)(2,1)S(1)}, u32[]{:S(2)}, u32[]{:S(2)}) collective-permute-start(bf16[1280,128]{1,0:T(8,128)(2,1)} %get-tuple-element.48), channel_id=1, source_target_pairs={{64,66},{65,67},{66,64},{67,65},{68,70},{69,71},{70,68},{71,69},{1... | collective-permute-start | bytes 983048 | tf_op jit(solution)/shard_map/ppermute | solution.py:74
  29.5 22.2 %collective-permute-start.11 = (bf16[1280,128]{1,0:T(8,128)(2,1)S(1)}, bf16[1280,128]{1,0:T(8,128)(2,1)S(1)}, u32[]{:S(2)}, u32[]{:S(2)}) collective-permute-start(bf16[1280,128]{1,0:T(8,128)(2,1)S(1)} %collective-permute-done.2.refs_9_), channel_id=1, source_target_pairs={{0,64},{64,0},{1,65},{65,1},{2,66},{66,2},{3,67},{67,3},{4,68},{68... | collective-permute-start | bytes 983048 | tf_op jit(solution)/shard_map/ppermute | solution.py:78
  33.7 12.3 %collective-permute-start.7 = (bf16[1024,128]{1,0:T(8,128)(2,1)}, bf16[1024,128]{1,0:T(8,128)(2,1)}, u32[]{:S(2)}, u32[]{:S(2)}) collective-permute-start(bf16[1024,128]{1,0:T(8,128)(2,1)} %collective-permute-done.3.refs_2_), channel_id=1, source_target_pairs={{0,56},{8,0},{16,8},{24,16},{32,24},{40,32},{48,40},{56,48},{1,57}... | collective-permute-start | bytes 786440 | tf_op jit(solution)/shard_map/ppermute | solution.py:26
  34.6 11.8 %collective-permute-start.8 = (bf16[1024,128]{1,0:T(8,128)(2,1)}, bf16[1024,128]{1,0:T(8,128)(2,1)}, u32[]{:S(2)}, u32[]{:S(2)}) collective-permute-start(bf16[1024,128]{1,0:T(8,128)(2,1)} %collective-permute-done.4.refs_6_), channel_id=1, source_target_pairs={{0,8},{8,16},{16,24},{24,32},{32,40},{40,48},{48,56},{56,0},{1,9},... | collective-permute-start | bytes 786440 | tf_op jit(solution)/shard_map/ppermute | solution.py:26
  51.8 18.9 %collective-permute-start.30 = (f32[32,1024]{1,0:T(8,128)}, f32[32,1024]{1,0:T(8,128)S(1)}, u32[]{:S(2)}, u32[]{:S(2)}) collective-permute-start(f32[32,1024]{1,0:T(8,128)} %add.29), channel_id=1, source_target_pairs={{0,2},{1,3},{2,0},{3,1},{4,6},{5,7},{6,4},{7,5},{8,10},{9,11},{10,... | collective-permute-start | bytes 393224 | tf_op jit(solution)/shard_map/ppermute | solution.py:34
  64.2 16.1 %collective-permute-start.15 = (bf16[512,128]{1,0:T(8,128)(2,1)}, bf16[512,128]{1,0:T(8,128)(2,1)S(1)}, u32[]{:S(2)}, u32[]{:S(2)}) collective-permute-start(bf16[512,128]{1,0:T(8,128)(2,1)} %get-tuple-element.54), channel_id=1, source_target_pairs={{0,2},{1,3},{2,0},{3,1},{4,6},{5,7},{6,4},{7,5},{8,10},{9,11},{10,... | collective-permute-start | bytes 393224 | tf_op jit(solution)/shard_map/ppermute | solution.py:50
  67.5 12.8 %collective-permute-start.16 = (bf16[512,128]{1,0:T(8,128)(2,1)}, bf16[512,128]{1,0:T(8,128)(2,1)S(1)}, u32[]{:S(2)}, u32[]{:S(2)}) collective-permute-start(bf16[512,128]{1,0:T(8,128)(2,1)} %get-tuple-element.55), channel_id=1, source_target_pairs={{0,1},{1,2},{2,3},{3,0},{4,5},{5,6},{6,7},{7,4},{8,9},{9,10},{10,1... | collective-permute-start | bytes 393224 | tf_op jit(solution)/shard_map/ppermute | solution.py:50
  68.3 12.0 %collective-permute-start.17 = (bf16[512,128]{1,0:T(8,128)(2,1)}, bf16[512,128]{1,0:T(8,128)(2,1)S(1)}, u32[]{:S(2)}, u32[]{:S(2)}) collective-permute-start(bf16[512,128]{1,0:T(8,128)(2,1)} %get-tuple-element.56), channel_id=1, source_target_pairs={{0,3},{1,0},{2,1},{3,2},{4,7},{5,4},{6,5},{7,6},{8,11},{9,8},{10,9... | collective-permute-start | bytes 393224 | tf_op jit(solution)/shard_map/ppermute | solution.py:50
  71.6 12.9 %collective-permute-start.31 = (f32[32,1024]{1,0:T(8,128)S(1)}, f32[32,1024]{1,0:T(8,128)S(1)}, u32[]{:S(2)}, u32[]{:S(2)}) collective-permute-start(f32[32,1024]{1,0:T(8,128)S(1)} %add.30), channel_id=1, source_target_pairs={{0,8},{8,0},{16,24},{24,16},{32,40},{40,32},{48,56},{56,48},{1,9},... | collective-permute-start | bytes 393224 | tf_op jit(solution)/shard_map/ppermute | solution.py:30
  83.2 21.4 %collective-permute-start.18 = (bf16[2048,128]{1,0:T(8,128)(2,1)}, bf16[2048,128]{1,0:T(8,128)(2,1)S(1)}, u32[]{:S(2)}, u32[]{:S(2)}) collective-permute-start(bf16[2048,128]{1,0:T(8,128)(2,1)} %get-tuple-element.58), channel_id=1, source_target_pairs={{0,4},{4,0},{1,5},{5,1},{2,6},{6,2},{3,7},{7,3},{8,12},{12,8},{9,1... | collective-permute-start | bytes 1572872 | tf_op jit(solution)/shard_map/ppermute | solution.py:38
  85.3 12.4 %collective-permute-start.22 = (bf16[1280,128]{1,0:T(8,128)(2,1)}, bf16[1280,128]{1,0:T(8,128)(2,1)S(1)}, u32[]{:S(2)}, u32[]{:S(2)}) collective-permute-start(bf16[1280,128]{1,0:T(8,128)(2,1)} %get-tuple-element.65), channel_id=1, source_target_pairs={{0,2},{1,3},{2,0},{3,1},{4,6},{5,7},{6,4},{7,5},{8,10},{9,11},{10,... | collective-permute-start | bytes 983048 | tf_op jit(solution)/shard_map/ppermute | solution.py:50
  85.8 15.4 %collective-permute-start.23 = (bf16[1280,128]{1,0:T(8,128)(2,1)}, bf16[1280,128]{1,0:T(8,128)(2,1)S(1)}, u32[]{:S(2)}, u32[]{:S(2)}) collective-permute-start(bf16[1280,128]{1,0:T(8,128)(2,1)} %get-tuple-element.66), channel_id=1, source_target_pairs={{0,1},{1,2},{2,3},{3,0},{4,5},{5,6},{6,7},{7,4},{8,9},{9,10},{10,1... | collective-permute-start | bytes 983048 | tf_op jit(solution)/shard_map/ppermute | solution.py:50
  86.1 15.1 %collective-permute-start.24 = (bf16[1280,128]{1,0:T(8,128)(2,1)}, bf16[1280,128]{1,0:T(8,128)(2,1)S(1)}, u32[]{:S(2)}, u32[]{:S(2)}) collective-permute-start(bf16[1280,128]{1,0:T(8,128)(2,1)} %get-tuple-element.67), channel_id=1, source_target_pairs={{0,3},{1,0},{2,1},{3,2},{4,7},{5,4},{6,5},{7,6},{8,11},{9,8},{10,9... | collective-permute-start | bytes 983048 | tf_op jit(solution)/shard_map/ppermute | solution.py:50
  90.5 20.6 %collective-permute-start.33 = (bf16[32,1024]{1,0:T(8,128)(2,1)S(1)}, bf16[32,1024]{1,0:T(8,128)(2,1)S(1)}, u32[]{:S(2)}, u32[]{:S(2)}) collective-permute-start(bf16[32,1024]{1,0:T(8,128)(2,1)S(1)} %get-tuple-element.73), channel_id=1, source_target_pairs={{0,32},{8,40},{16,48},{24,56},{32,0},{40,8},{48,16},{56,24},{1,33}... | collective-permute-start | bytes 196616 | tf_op jit(solution)/shard_map/ppermute | solution.py:30
  107.7 13.4 %collective-permute-start.19 = (bf16[896,128]{1,0:T(8,128)(2,1)}, bf16[896,128]{1,0:T(8,128)(2,1)S(1)}, u32[]{:S(2)}, u32[]{:S(2)}) collective-permute-start(bf16[896,128]{1,0:T(8,128)(2,1)} %get-tuple-element.61), channel_id=1, source_target_pairs={{0,1},{1,2},{2,3},{3,0},{4,5},{5,6},{6,7},{7,4},{8,9},{9,10},{10,1... | collective-permute-start | bytes 688136 | tf_op jit(solution)/shard_map/ppermute | solution.py:50
  107.8 13.3 %collective-permute-start.20 = (bf16[896,128]{1,0:T(8,128)(2,1)}, bf16[896,128]{1,0:T(8,128)(2,1)S(1)}, u32[]{:S(2)}, u32[]{:S(2)}) collective-permute-start(bf16[896,128]{1,0:T(8,128)(2,1)} %get-tuple-element.62), channel_id=1, source_target_pairs={{0,2},{1,3},{2,0},{3,1},{4,6},{5,7},{6,4},{7,5},{8,10},{9,11},{10,... | collective-permute-start | bytes 688136 | tf_op jit(solution)/shard_map/ppermute | solution.py:50
  110.0 11.8 %collective-permute-start.21 = (bf16[896,128]{1,0:T(8,128)(2,1)}, bf16[896,128]{1,0:T(8,128)(2,1)S(1)}, u32[]{:S(2)}, u32[]{:S(2)}) collective-permute-start(bf16[896,128]{1,0:T(8,128)(2,1)} %get-tuple-element.63), channel_id=1, source_target_pairs={{0,3},{1,0},{2,1},{3,2},{4,7},{5,4},{6,5},{7,6},{8,11},{9,8},{10,9... | collective-permute-start | bytes 688136 | tf_op jit(solution)/shard_map/ppermute | solution.py:50
  (35 other events, 375.1 us)

commit v4 on v3

--- a/solution.py
+++ b/solution.py
@@ -78,8 +78,10 @@
     return lax.ppermute(v, "c", [(c, 1 - c) for c in range(NC) if k < len(SERVED[c])])
 
 
-def pack_kernel(s_ref, wq_ref, kv_ref, *outs):
-    z, xl, y, c = s_ref[0], s_ref[1], s_ref[2], s_ref[3]
+def pack_kernel(wq_ref, kv_ref, *refs):
+    outs, sem = refs[:5], refs[5]
+    z, xl, y, c = (lax.axis_index(a) for a in ("z", "xl", "y", "c"))
+    copies = []
     for k in range(5):
         d = 0
         if k < 4:
@@ -87,12 +89,47 @@
         p = (xl ^ (d // NY)) * NY + ((y + d) & (NY - 1))
         for j in range(NZ):
             row = pl.multiple_of((((z + j) & (NZ - 1)) * NP + p) * 128, 128)
-            outs[k][j * 128 : (j + 1) * 128, :] = wq_ref[pl.ds(row, 128), :]
-            outs[k][1024 + j * 32 : 1024 + (j + 1) * 32, :] = kv_ref[:, pl.ds(row, 128)]
-
-
-def low_kernel(s_ref, ad_ref, h_ref, near_ref, far_ref, out_ref):
-    c, xh = s_ref[3], s_ref[4]
+            copies.append((wq_ref.at[pl.ds(row, 128), :], outs[k].at[j * 128 : (j + 1) * 128, :]))
+            copies.append((kv_ref.at[:, pl.ds(row, 128)], outs[k].at[1024 + j * 32 : 1056 + j * 32, :]))
+    copies = [pltpu.make_async_copy(src, dst, sem.at[i]) for i, (src, dst) in enumerate(copies)]
+    for copy in copies:
+        copy.start()
+    for copy in copies:
+        copy.wait()
+
+
+def add_kernel(a_ref, b_ref, *outs):
+    total = a_ref[...] + b_ref[...].astype(jnp.float32)
+    outs[0][...] = total
+    for out in outs[1:]:
+        out[...] = total.astype(out.dtype)
+
+
+def rope_kernel(start_ref, cos_ref, sin_ref):
+    half = HEAD_SIZE // 2
+    lane = lax.broadcasted_iota(jnp.int32, (BLOCK, HEAD_SIZE), 1)
+    row = lax.broadcasted_iota(jnp.int32, (BLOCK, HEAD_SIZE), 0)
+    steps = (lane & (half - 1)).astype(jnp.float32)
+    inverse = jnp.exp(-(2.0 * steps / HEAD_SIZE) * math.log(ROPE_BASE))
+    sign = jnp.where(lane < half, -1.0, 1.0).astype(jnp.float32)
+    place = row.astype(jnp.float32) * inverse
+    cos_in, sin_in = jnp.cos(place), jnp.sin(place)
+    blocks = cos_ref.shape[0] // BLOCK
+    ahead = lax.broadcasted_iota(jnp.int32, (8, HEAD_SIZE), 0).astype(jnp.float32) * BLOCK * inverse[0:8, :]
+    cos_out, sin_out = jnp.cos(ahead), jnp.sin(ahead)
+    first = (lax.axis_index("xh") * NC + lax.axis_index("c")) * blocks
+    which = lax.broadcasted_iota(jnp.int32, (8, HEAD_SIZE), 0)
+    for b in range(blocks):
+        chosen = which == first + b - start_ref[b * BLOCK]
+        co = jnp.sum(jnp.where(chosen, cos_out, 0.0), axis=0, keepdims=True)
+        so = jnp.sum(jnp.where(chosen, sin_out, 0.0), axis=0, keepdims=True)
+        rows = slice(b * BLOCK, (b + 1) * BLOCK)
+        cos_ref[rows, :] = cos_in * co - sin_in * so
+        sin_ref[rows, :] = (sin_in * co + cos_in * so) * sign
+
+
+def low_kernel(ad_ref, h_ref, near_ref, far_ref, out_ref):
+    c, xh = lax.axis_index("c"), lax.axis_index("xh")
     per = near_ref.shape[1]
     for b in range(h_ref.shape[0] // BLOCK):
         a = ad_ref[b]
@@ -108,8 +145,9 @@
         )
 
 
-def for_each_piece(c, own, mine, other, place):
+def for_each_piece(own, mine, other, place):
     place(own, 0)
+    c = lax.axis_index("c")
     for core in range(NC):
 
         @pl.when(c == core)
@@ -120,7 +158,7 @@
                 place(other[k], FLIP[d])
 
 
-def kv_product_kernel(s_ref, *refs):
+def kv_product_kernel(*refs):
     h_refs, own, mine, other = refs[0:8], refs[8], refs[9:13], refs[13:17]
     outs, hbuf, kvw = refs[17:21], refs[21], refs[22]
     for j in range(8):
@@ -130,7 +168,7 @@
         for j in range(NZ):
             kvw[d * 32 : (d + 1) * 32, j * 128 : (j + 1) * 128] = ref[1024 + j * 32 : 1056 + j * 32, :]
 
-    for_each_piece(s_ref[3], own, mine, other, place)
+    for_each_piece(own, mine, other, place)
     kv = lax.dot_general(
         kvw[...], hbuf[...], (((1,), (1,)), ((), ())), preferred_element_type=jnp.float32
     ).astype(jnp.bfloat16)
@@ -141,17 +179,15 @@
             outs[dy][at : at + 32, :] = kv[d * 32 : (d + 1) * 32, t * 128 : (t + 1) * 128]
 
 
-def q_product_kernel(s_ref, *refs):
-    h_refs, own, mine, other = refs[0:8], refs[8], refs[9:13], refs[13:17]
-    near_ref, far_ref, outs, hbuf, wq = refs[17], refs[18], refs[19:23], refs[23], refs[24]
-    for j in range(8):
-        hbuf[:, j * 128 : (j + 1) * 128] = h_refs[j][...]
+def q_product_kernel(hbuf, own, *refs):
+    mine, other = refs[0:4], refs[4:8]
+    near_ref, far_ref, outs, wq = refs[8], refs[9], refs[10:14], refs[14]
 
     def place(ref, d):
         dx, dy = divmod(d, NY)
         wq[dy, :, dx * 128 : (dx + 1) * 128] = ref[0:1024, :]
 
-    for_each_piece(s_ref[3], own, mine, other, place)
+    for_each_piece(own, mine, other, place)
     for dy in range(NY):
         q = jnp.dot(hbuf[0:TA, :], wq[dy], preferred_element_type=jnp.float32).astype(jnp.bfloat16)
         near_ref[dy * TA : (dy + 1) * TA, :] = q[:, 0:128]
@@ -194,12 +230,13 @@
         out[...] = (wide(b0, rows) + wide(b1, rows) + wide(b2, rows) + wide(b3, rows)).astype(out.dtype)
 
 
-def attention_kernel(s_ref, ad_ref, lo_ref, *refs):
+def attention_kernel(ad_ref, start_ref, *refs):
     a_own, a_got, b_own, b_got, kv_own = refs[0], refs[1:4], refs[4], refs[5], refs[6]
     low_ref, near_ref, far_ref, cos_ref, sin_ref = refs[7:12]
     out_ref = refs[12]
     kvt, k_buf, v_buf = refs[13:16]
-    xl, y, c, xh = s_ref[1], s_ref[2], s_ref[3], s_ref[4]
+    xl, y, c, xh = (lax.axis_index(a) for a in ("xl", "y", "c", "xh"))
+    first = (xh * NC + c) * 8
     for i in range(NY):
         ref, base = (kv_own, 0) if i == 0 else (a_got[i - 1], TA)
         for dx in range(NX):
@@ -226,7 +263,7 @@
         xr, cr = (owner // NC) ^ xh, (owner % NC) ^ c
         up = jnp.where(cr == 0, near_ref[xr, at, RANK : 2 * RANK, :], far_ref[xr, at, RANK : 2 * RANK, :])
         q = ADAPTER_SCALE * lax.dot_general(
-            low_ref[:, rows].astype(jnp.bfloat16), up, (((0,), (0,)), ((), ())), preferred_element_type=jnp.float32
+            low_ref[:, rows], up, (((0,), (0,)), ((), ())), preferred_element_type=jnp.float32
         )
         if b * 128 < TA:
             q += a_own[rows, :]
@@ -242,7 +279,7 @@
         )
         col = lax.broadcasted_iota(jnp.int32, (128, n), 1)
         row = lax.broadcasted_iota(jnp.int32, (128, n), 0) + b * 128
-        allowed = (col >= lo_ref[b]) & (col <= row)
+        allowed = (col >= (start_ref[b * BLOCK] - first) * BLOCK) & (col <= row)
         s = jnp.where(allowed, s, -1e30)
         e = jnp.exp2((s - jnp.max(s, axis=1, keepdims=True)) * factor)
         probs = (e * (1.0 / jnp.sum(e, axis=1, keepdims=True))).astype(jnp.bfloat16)
@@ -251,25 +288,17 @@
         ).astype(jnp.bfloat16)
 
 
-def call(kernel, name, outs, *args, scalars=0, scratch=()):
+def call(kernel, name, outs, *args, scalars=0, scratch=(), mib=4, space=pltpu.VMEM):
     single = isinstance(outs, jax.ShapeDtypeStruct)
     return pl.pallas_call(
         kernel,
         out_shape=outs,
-        in_specs=[SMEM] * scalars + [VMEM] * (len(args) - scalars),
+        in_specs=[SMEM] * scalars + [pl.BlockSpec(memory_space=space)] * (len(args) - scalars),
         out_specs=VMEM if single else [VMEM] * len(outs),
         scratch_shapes=scratch,
+        compiler_params=pltpu.CompilerParams(vmem_limit_bytes=mib << 20),
         name=name,
     )(*args)
-
-
-def rope_tables(positions):
-    half = HEAD_SIZE // 2
-    steps = jnp.arange(half, dtype=jnp.float32)
-    inverse = jnp.exp(-(2.0 * steps / HEAD_SIZE) * math.log(ROPE_BASE))
-    angles = positions.astype(jnp.float32)[:, None] * inverse[None, :]
-    cosines, sines = jnp.cos(angles), jnp.sin(angles)
-    return jnp.concatenate([cosines, cosines], 1), jnp.concatenate([-sines, sines], 1)
 
 
 def after(value, *others):
@@ -280,22 +309,26 @@
     rows = hidden.shape[0]
     bf16, f32 = jnp.bfloat16, jnp.float32
     of = jax.ShapeDtypeStruct
-    place = [lax.axis_index(a) for a in ("z", "xl", "y", "c", "xh")]
-    scalars = jnp.stack(place).astype(jnp.int32)
-
     maps = jnp.concatenate([jnp.transpose(down_maps, (0, 2, 1)), up_maps], axis=1)
     twin = xh_swap(maps)
 
     sends = call(
-        pack_kernel, "pack", [of((1280, 128), bf16)] * 5, scalars, query_weight, key_value_weight.T, scalars=1
-    )
+        pack_kernel,
+        "pack",
+        [of((1280, 128), bf16)] * 5,
+        query_weight,
+        key_value_weight.T,
+        scratch=[pltpu.SemaphoreType.DMA((10 * NZ,))],
+        space=pltpu.HBM,
+    )
+    cosines, sines = call(rope_kernel, "rope", [of((rows, HEAD_SIZE), f32)] * 2, request_start, scalars=1)
     right, left = [hidden], [hidden]
     mine = [weight_send(sends[k], k) for k in range(2)]
     gates = ((), (0,), (1, 2), (3,))
     for step in range(4):
         r, l = right[-1], left[-1]
         if step:
-            waits = [mine[k] for k in gates[step]]
+            waits = [mine[k] for k in gates[step]] + [cosines] * (step == 2)
             r, l = after(right[-1], left[-1], *waits), after(left[-1], right[-1], *waits)
         right.append(z_shift(r, 1))
         if step < 3:
@@ -307,34 +340,37 @@
     near = jnp.stack([maps, after(twin, right[1], left[1])])
     far = core_swap(near)
     low = call(
-        low_kernel, "low", of((RANK, rows), f32), scalars, adapters, hidden, near, after(far, right[2], left[2]), scalars=2
-    )
-    low = low + x_swap(low)
-    low = low + y_xor(low, 1)
-    low = low + y_xor(low, 2)
-
-    shards = [hidden, left[1], left[2], left[3], right[4], right[3], right[2], right[1]]
+        low_kernel, "low", of((RANK, rows), f32), adapters, hidden, near, far, scalars=1
+    )
+
+    def added(low, sent, also=()):
+        outs = [of((RANK, rows), f32)] + [of((RANK, rows), t) for t in also]
+        return call(add_kernel, "low_add", outs, low, sent)
+
+    (low,) = added(low, x_swap(low))
+    (low,) = added(low, y_xor(low, 1))
+    (low,) = added(low, y_xor(low, 2))
+
+    shards = [after(hidden, low), left[1], left[2], left[3], right[4], right[3], right[2], right[1]]
     weights = (sends[4], *mine, *other)
-    kv_parts = call(
+    *kv_parts, gathered = call(
         kv_product_kernel,
         "kv_product",
-        [of((512, 128), bf16)] * NY,
-        scalars,
+        [of((512, 128), bf16)] * NY + [of((rows, 1024), bf16)],
         *shards,
         *weights,
-        scalars=1,
-        scratch=[pltpu.VMEM((rows, 1024), bf16), pltpu.VMEM((256, 1024), bf16)],
+        scratch=[pltpu.VMEM((256, 1024), bf16)],
+        mib=8,
     )
     kv_got = [y_shift(kv_parts[dy], dy) for dy in (2, 1, 3)]
     near_a, far_a, *b_parts = call(
         q_product_kernel,
         "q_product",
         [of((NY * TA, 128), bf16)] * 2 + [of((2 * TB, 128), bf16)] * NY,
-        after(scalars, kv_parts[0]),
-        *shards,
+        gathered,
         *weights,
-        scalars=1,
-        scratch=[pltpu.VMEM((rows, 1024), bf16), pltpu.VMEM((NY, 1024, 256), bf16)],
+        scratch=[pltpu.VMEM((NY, 1024, 256), bf16)],
+        mib=10,
     )
     b_got = [y_shift(b_parts[dy], dy) for dy in (2, 1, 3)]
     kv_sum, x_send = call(
@@ -346,9 +382,11 @@
         far_a,
     )
     x_got = x_swap(x_send)
-    low = low + z_xor(low, 1)
-    low = low + z_xor(low, 2)
-    low = low + z_xor(low.astype(bf16), 4).astype(f32)
+    low = after(low, kv_sum)
+    (low,) = added(low, z_xor(low, 1))
+    low = after(low, x_got)
+    low, narrow = added(low, z_xor(low, 2), (bf16,))
+    _, low = added(low, z_xor(narrow, 4), (bf16,))
     a_own, kv_own, *a_sends = call(
         stage_a_kernel,
         "stage_a",
@@ -363,17 +401,12 @@
     )
     b_last = x_swap(b_send)
 
-    first = lax.axis_index("xh") * NC + lax.axis_index("c")
-    places = first * rows + jnp.arange(rows, dtype=jnp.int32)
-    cosines, sines = rope_tables(places - request_start * BLOCK)
-    lowest = request_start[::BLOCK] * BLOCK - first * rows
     return call(
         attention_kernel,
         "attention",
         of((rows, HEAD_SIZE), bf16),
-        scalars,
         adapters,
-        lowest,
+        request_start,
         a_own,
         *[a_got[dy] for dy in (1, 2, 3)],
         b_own,
@@ -384,8 +417,9 @@
         far,
         cosines,
         sines,
-        scalars=3,
+        scalars=2,
         scratch=[pltpu.VMEM((256, rows), bf16)] + [pltpu.VMEM((rows, HEAD_SIZE), bf16)] * 2,
+        mib=8,
     )
 
 

time: 131 us -> 112 us (0.85); the launches traced: 130 us -> 110 us
  Pallas kernels: 30.8 us -> 16.6 us
  other arithmetic: 9.06 us -> 1.19 us
  waiting for transfers between devices: 37.4 us -> 44.8 us
  starting transfers between devices: 47.4 us -> 44.3 us
  local copies, waits for them, and re-layouts: 5.26 us -> 2.64 us
    ppermute x9, waiting for transfers between devices: 16.4 us -> 1.93 us  [y_shift(): return lax.ppermute(v, 'y', [(i, (i + s) % NY) for i in range(NY)])]
    pallas_call x8 -> x15, Pallas kernels: 30.8 us -> 16.6 us  [call(): pl.pallas_call(kernel, out_shape=outs, in_specs=[SMEM] * scalars + [pl.Bl...]
    ppermute x3, waiting for transfers between devices: 1.47 us -> 10.4 us  [z_xor(): return lax.ppermute(v, 'z', [(i, i ^ s) for i in range(NZ)])]
    ppermute x2, waiting for transfers between devices: 2.19 us -> 8.28 us  [y_xor(): return lax.ppermute(v, 'y', [(i, i ^ s) for i in range(NY)])]
    ppermute x3, waiting for transfers between devices: 3.56 us -> 8.75 us  [x_swap(): return lax.ppermute(v, 'xl', [(0, 1), (1, 0)])]
    ppermute x4, waiting for transfers between devices: 3.1 us -> 7.35 us  [weight_send(): return lax.ppermute(v, ('xh', 'c', 'xl', 'y'), route)]
    add x5 -> x0, other arithmetic: 4.1 us -> none  [the longest x1 1.57 us: body(): low = low + y_xor(low, 1)]
    ppermute x2, starting transfers between devices: 3.89 us -> 0.19 us  [y_xor(): return lax.ppermute(v, 'y', [(i, i ^ s) for i in range(NY)])]
  transfers between devices with their start and end apart: 34 -> 34, of which waited for: 13 -> 12; matrix products, arithmetic and copies ran while one was open for 8% -> 1% of each run, Pallas kernels for 18% -> 8%
where the time goes in v4:
time: 112 us; the launch traced here: 110 us
  waiting for transfers between devices  44.8 us (40%)
  starting transfers between devices  44.3 us (40%)
  Pallas kernels  16.6 us (15%)
  local copies, waits for them, and re-layouts  2.64 us (2%)
  other arithmetic  1.19 us (1%)
    pallas_call x15, Pallas kernels, call(): pl.pallas_call(kernel, out_shape=outs, in_specs=[SMEM] * scalars + [pl.Bl...  16.6 us
    ppermute x9, starting transfers between devices, y_shift(): return lax.ppermute(v, 'y', [(i, (i + s) % NY) for i in range(NY)])  14 us
    ppermute x7, starting transfers between devices, z_shift(): return lax.ppermute(v, 'z', [(i, (i + s) % NZ) for i in range(NZ)])  12.2 us
    ppermute x3, waiting for transfers between devices, z_xor(): return lax.ppermute(v, 'z', [(i, i ^ s) for i in range(NZ)])  10.4 us
    ppermute x3, waiting for transfers between devices, x_swap(): return lax.ppermute(v, 'xl', [(0, 1), (1, 0)])  8.75 us
    ppermute x2, waiting for transfers between devices, y_xor(): return lax.ppermute(v, 'y', [(i, i ^ s) for i in range(NY)])  8.28 us
    ppermute x7, waiting for transfers between devices, z_shift(): return lax.ppermute(v, 'z', [(i, (i + s) % NZ) for i in range(NZ)])  8.02 us
    ppermute x4, waiting for transfers between devices, weight_send(): return lax.ppermute(v, ('xh', 'c', 'xl', 'y'), route)  7.35 us
  transfers between devices with their start and end apart: 34, of which 12 were waited for; matrix products, arithmetic and copies ran while one was open for 1% of the time, Pallas kernels for 8%

profile of v4, /device:TPU:2, one launch (start us, length us, event | category | flops | bytes accessed | tf_op | source)
XLA Modules:
  0.0 109.8 jit_solution(287878791187368691)
XLA Ops:
  0.0 5.9 %collective-permute-start.2 = (bf16[1024,128]{1,0:T(8,128)(2,1)}, bf16[1024,128]{1,0:T(8,128)(2,1)S(1)}, u32[]{:S(2)}, u32[]{:S(2)}) collective-permute-start(bf16[1024,128]{1,0:T(8,128)(2,1)} %refs_0_), channel_id=1, source_target_pairs={{0,56},{8,0},{16,8},{24,16},{32,24},{40,32},{48,40},{56,48},{1,57}... | collective-permute-start | bytes 786440 | tf_op jit(solution)/shard_map/ppermute | solution.py:26
  7.0 2.2 %collective-permute-start = (bf16[16,64,128]{2,1,0:T(8,128)(2,1)S(1)}, bf16[16,64,128]{2,1,0:T(8,128)(2,1)S(1)}, u32[]{:S(2)}, u32[]{:S(2)}) collective-permute-start(bf16[16,64,128]{2,1,0:T(8,128)(2,1)S(1)} %get-tuple-element.88), channel_id=1, source_target_pairs={{0,128},{128,0},{1,129},{129,1},{2,130},{130,2},{3,131},{131,3},{4... | collective-permute-start | bytes 786440 | tf_op jit(solution)/shard_map/ppermute | solution.py:46
  9.2 1.6 %copy-done = bf16[8192,128]{1,0:T(8,128)(2,1)S(1)} copy-done((bf16[8192,128]{1,0:T(8,128)(2,1)S(1)}, bf16[8192,128]{1,0:T(8,128)(2,1)}, u32[]{:S(2)}) %copy-start) | copy-done | bytes 2097176
  11.9 3.2 %pack.1 = (bf16[1280,128]{1,0:T(8,128)(2,1)S(1)}, bf16[1280,128]{1,0:T(8,128)(2,1)S(1)}, bf16[1280,128]{1,0:T(8,128)(2,1)S(1)}, bf16[1280,128]{1,0:T(8,128)(2,1)S(1)}, bf16[1280,128]{1,0:T(8,128)(2,1)S(1)}) custom-call(bf16[8192,128]{1,0:T(8,128)(2,1)S(1)} %copy-done, bf16[32,8192]{1,0:T(8,128)(2,1)S(1)} %bitcast.5), custom_call_target="tpu_custom_call" | custom-call | tf_op jit(solution)/shard_map/pack/pallas_call | solution.py:293
  16.8 3.5 %collective-permute-start.10 = (bf16[1280,128]{1,0:T(8,128)(2,1)S(1)}, bf16[1280,128]{1,0:T(8,128)(2,1)S(1)}, u32[]{:S(2)}, u32[]{:S(2)}) collective-permute-start(bf16[1280,128]{1,0:T(8,128)(2,1)S(1)} %get-tuple-element.51), channel_id=1, source_target_pairs={{0,6},{1,7},{2,4},{3,5},{4,2},{5,3},{6,0},{7,1},{64,199},{65,196},... | collective-permute-start | bytes 983048 | tf_op jit(solution)/shard_map/ppermute | solution.py:74
  22.2 3.2 %collective-permute-start.8 = (bf16[1024,128]{1,0:T(8,128)(2,1)S(1)}, bf16[1024,128]{1,0:T(8,128)(2,1)S(1)}, u32[]{:S(2)}, u32[]{:S(2)}) collective-permute-start(bf16[1024,128]{1,0:T(8,128)(2,1)S(1)} %collective-permute-done.2.refs_1_), channel_id=1, source_target_pairs={{0,56},{8,0},{16,8},{24,16},{32,24},{40,32},{48,40},{56,48},{1,57}... | collective-permute-start | bytes 786440 | tf_op jit(solution)/shard_map/ppermute | solution.py:26
  27.0 1.6 %collective-permute-done.10.refs_10_.refs_1_ = bf16[1280,128]{1,0:T(8,128)(2,1)S(1)} collective-permute-done((bf16[1280,128]{1,0:T(8,128)(2,1)S(1)}, bf16[1280,128]{1,0:T(8,128)(2,1)S(1)}, u32[]{:S(2)}, u32[]{:S(2)}) %collective-permute-start.10) | collective-permute-done | bytes 327712 | tf_op jit(solution)/shard_map/ppermute | solution.py:74
  28.6 1.7 %collective-permute-start.4 = (f32[32,1024]{1,0:T(8,128)S(1)}, f32[32,1024]{1,0:T(8,128)S(1)}, u32[]{:S(2)}, u32[]{:S(2)}) collective-permute-start(f32[32,1024]{1,0:T(8,128)S(1)} %low.1.a_ref), channel_id=1, source_target_pairs={{0,4},{4,0},{1,5},{5,1},{2,6},{6,2},{3,7},{7,3},{8,12},{12,8},{9,1... | collective-permute-start | bytes 393224 | tf_op jit(solution)/shard_map/ppermute | solution.py:38
  31.3 4.2 %collective-permute-done.11.refs_11_.refs_2_ = bf16[1280,128]{1,0:T(8,128)(2,1)S(1)} collective-permute-done((bf16[1280,128]{1,0:T(8,128)(2,1)S(1)}, bf16[1280,128]{1,0:T(8,128)(2,1)S(1)}, u32[]{:S(2)}, u32[]{:S(2)}) %collective-permute-start.11) | collective-permute-done | bytes 327712 | tf_op jit(solution)/shard_map/ppermute | solution.py:74
  35.5 3.1 %collective-permute-start.12 = (bf16[1024,128]{1,0:T(8,128)(2,1)S(1)}, bf16[1024,128]{1,0:T(8,128)(2,1)S(1)}, u32[]{:S(2)}, u32[]{:S(2)}) collective-permute-start(bf16[1024,128]{1,0:T(8,128)(2,1)S(1)} %collective-permute-done.8.refs_2_), channel_id=1, source_target_pairs={{0,56},{8,0},{16,8},{24,16},{32,24},{40,32},{48,40},{56,48},{1,57}... | collective-permute-start | bytes 786440 | tf_op jit(solution)/shard_map/ppermute | solution.py:26
  38.7 5.0 %collective-permute-done.5.b_ref = f32[32,1024]{1,0:T(8,128)S(1)} collective-permute-done((f32[32,1024]{1,0:T(8,128)S(1)}, f32[32,1024]{1,0:T(8,128)S(1)}, u32[]{:S(2)}, u32[]{:S(2)}) %collective-permute-start.5) | collective-permute-done | bytes 131104 | tf_op jit(solution)/shard_map/ppermute | solution.py:34
  46.9 3.3 %collective-permute-done.6.b_ref = f32[32,1024]{1,0:T(8,128)S(1)} collective-permute-done((f32[32,1024]{1,0:T(8,128)S(1)}, f32[32,1024]{1,0:T(8,128)S(1)}, u32[]{:S(2)}, u32[]{:S(2)}) %collective-permute-start.6) | collective-permute-done | bytes 131104 | tf_op jit(solution)/shard_map/ppermute | solution.py:34
  50.3 7.5 %collective-permute-done.15.refs_4_ = bf16[1024,128]{1,0:T(8,128)(2,1)S(1)} collective-permute-done((bf16[1024,128]{1,0:T(8,128)(2,1)S(1)}, bf16[1024,128]{1,0:T(8,128)(2,1)S(1)}, u32[]{:S(2)}, u32[]{:S(2)}) %collective-permute-start.15) | collective-permute-done | bytes 262176 | tf_op jit(solution)/shard_map/ppermute | solution.py:26
  59.3 2.4 %collective-permute-start.20 = (bf16[512,128]{1,0:T(8,128)(2,1)S(1)}, bf16[512,128]{1,0:T(8,128)(2,1)S(1)}, u32[]{:S(2)}, u32[]{:S(2)}) collective-permute-start(bf16[512,128]{1,0:T(8,128)(2,1)S(1)} %get-tuple-element.64), channel_id=1, source_target_pairs={{0,2},{1,3},{2,0},{3,1},{4,6},{5,7},{6,4},{7,5},{8,10},{9,11},{10,... | collective-permute-start | bytes 393224 | tf_op jit(solution)/shard_map/ppermute | solution.py:50
  61.7 3.2 %collective-permute-start.22 = (bf16[512,128]{1,0:T(8,128)(2,1)S(1)}, bf16[512,128]{1,0:T(8,128)(2,1)S(1)}, u32[]{:S(2)}, u32[]{:S(2)}) collective-permute-start(bf16[512,128]{1,0:T(8,128)(2,1)S(1)} %get-tuple-element.66), channel_id=1, source_target_pairs={{0,3},{1,0},{2,1},{3,2},{4,7},{5,4},{6,5},{7,6},{8,11},{9,8},{10,9... | collective-permute-start | bytes 393224 | tf_op jit(solution)/shard_map/ppermute | solution.py:50
  65.0 2.7 %q_product.1 = (bf16[1536,128]{1,0:T(8,128)(2,1)S(1)}, bf16[1536,128]{1,0:T(8,128)(2,1)S(1)}, bf16[1280,128]{1,0:T(8,128)(2,1)S(1)}, bf16[1280,128]{1,0:T(8,128)...) custom-call(bf16[1024,1024]{1,0:T(8,128)(2,1)S(1)} %get-tuple-element.61.hbuf, ...), custom_call_target="tpu_custom_call" | custom-call | tf_op jit(solution)/shard_map/q_product/pallas_call | solution.py:293
  70.5 2.2 %collective-permute-start.28 = (bf16[1280,128]{1,0:T(8,128)(2,1)S(1)}, bf16[1280,128]{1,0:T(8,128)(2,1)S(1)}, u32[]{:S(2)}, u32[]{:S(2)}) collective-permute-start(bf16[1280,128]{1,0:T(8,128)(2,1)S(1)} %get-tuple-element.76), channel_id=1, source_target_pairs={{0,1},{1,2},{2,3},{3,0},{4,5},{5,6},{6,7},{7,4},{8,9},{9,10},{10,1... | collective-permute-start | bytes 983048 | tf_op jit(solution)/shard_map/ppermute | solution.py:50
  73.8 8.7 %collective-permute-done.23.got_ref = bf16[2048,128]{1,0:T(8,128)(2,1)S(1)} collective-permute-done((bf16[2048,128]{1,0:T(8,128)(2,1)S(1)}, bf16[2048,128]{1,0:T(8,128)(2,1)S(1)}, u32[]{:S(2)}, u32[]{:S(2)}) %collective-permute-start.23) | collective-permute-done | bytes 524320 | tf_op jit(solution)/shard_map/ppermute | solution.py:38
  82.8 2.3 %collective-permute-start.25 = (bf16[896,128]{1,0:T(8,128)(2,1)S(1)}, bf16[896,128]{1,0:T(8,128)(2,1)S(1)}, u32[]{:S(2)}, u32[]{:S(2)}) collective-permute-start(bf16[896,128]{1,0:T(8,128)(2,1)S(1)} %get-tuple-element.72), channel_id=1, source_target_pairs={{0,2},{1,3},{2,0},{3,1},{4,6},{5,7},{6,4},{7,5},{8,10},{9,11},{10,... | collective-permute-start | bytes 688136 | tf_op jit(solution)/shard_map/ppermute | solution.py:50
  87.2 1.8 %collective-permute-start.30 = (bf16[640,128]{1,0:T(8,128)(2,1)S(1)}, bf16[640,128]{1,0:T(8,128)(2,1)S(1)}, u32[]{:S(2)}, u32[]{:S(2)}) collective-permute-start(bf16[640,128]{1,0:T(8,128)(2,1)S(1)} %get-tuple-element.79), channel_id=1, source_target_pairs={{0,4},{4,0},{1,5},{5,1},{2,6},{6,2},{3,7},{7,3},{8,12},{12,8},{9,1... | collective-permute-start | bytes 491528 | tf_op jit(solution)/shard_map/ppermute | solution.py:38
  89.0 4.9 %collective-permute-done.32.b_ref = f32[32,1024]{1,0:T(8,128)S(1)} collective-permute-done((f32[32,1024]{1,0:T(8,128)S(1)}, f32[32,1024]{1,0:T(8,128)S(1)}, u32[]{:S(2)}, u32[]{:S(2)}) %collective-permute-start.32) | collective-permute-done | bytes 131104 | tf_op jit(solution)/shard_map/ppermute | solution.py:30
  94.0 3.3 %collective-permute-start.33 = (bf16[32,1024]{1,0:T(8,128)(2,1)S(1)}, bf16[32,1024]{1,0:T(8,128)(2,1)S(1)}, u32[]{:S(2)}, u32[]{:S(2)}) collective-permute-start(bf16[32,1024]{1,0:T(8,128)(2,1)S(1)} %get-tuple-element.84), channel_id=1, source_target_pairs={{0,32},{8,40},{16,48},{24,56},{32,0},{40,8},{48,16},{56,24},{1,33}... | collective-permute-start | bytes 196616 | tf_op jit(solution)/shard_map/ppermute | solution.py:30
  97.3 5.5 %collective-permute-done.33.b_ref = bf16[32,1024]{1,0:T(8,128)(2,1)S(1)} collective-permute-done((bf16[32,1024]{1,0:T(8,128)(2,1)S(1)}, bf16[32,1024]{1,0:T(8,128)(2,1)S(1)}, u32[]{:S(2)}, u32[]{:S(2)}) %collective-permute-start.33) | collective-permute-done | bytes 65568 | tf_op jit(solution)/shard_map/ppermute | solution.py:30
  103.5 6.3 %attention.1 = bf16[1024,128]{1,0:T(8,128)(2,1)} custom-call(s32[8]{0:T(128)S(1)} %copy-done.4, s32[1024]{0:T(1024)S(1)} %copy-done.3, f32[384,128]{1,0:T(8,128)S(1)} %get-tuple-element.70.refs_0_, bf16[896,128]{1,0:T(8,128)(2,1)S(1)} %collective-permute-done.24.refs_1_, bf16[896,128]{1,0:T(8,128)(2,1)S(1)} %collective-permute-done.25.refs_2_, ...), custom_call_target="tpu_custom_call" | custom-call | tf_op jit(solution)/shard_map/attention/pallas_call | solution.py:293
  (71 shorter events, 20.1 us)
Async XLA Ops:
  0.0 16.6 %collective-permute-start.2 = (bf16[1024,128]{1,0:T(8,128)(2,1)}, bf16[1024,128]{1,0:T(8,128)(2,1)S(1)}, u32[]{:S(2)}, u32[]{:S(2)}) collective-permute-start(bf16[1024,128]{1,0:T(8,128)(2,1)} %refs_0_), channel_id=1, source_target_pairs={{0,56},{8,0},{16,8},{24,16},{32,24},{40,32},{48,40},{56,48},{1,57}... | collective-permute-start | bytes 786440 | tf_op jit(solution)/shard_map/ppermute | solution.py:26
  5.9 10.7 %collective-permute-start.1 = (bf16[1024,128]{1,0:T(8,128)(2,1)}, bf16[1024,128]{1,0:T(8,128)(2,1)S(1)}, u32[]{:S(2)}, u32[]{:S(2)}) collective-permute-start(bf16[1024,128]{1,0:T(8,128)(2,1)} %refs_0_), channel_id=1, source_target_pairs={{0,8},{8,16},{16,24},{24,32},{32,40},{40,48},{48,56},{56,0},{1,9},... | collective-permute-start | bytes 786440 | tf_op jit(solution)/shard_map/ppermute | solution.py:26
  7.0 9.6 %collective-permute-start = (bf16[16,64,128]{2,1,0:T(8,128)(2,1)S(1)}, bf16[16,64,128]{2,1,0:T(8,128)(2,1)S(1)}, u32[]{:S(2)}, u32[]{:S(2)}) collective-permute-start(bf16[16,64,128]{2,1,0:T(8,128)(2,1)S(1)} %get-tuple-element.88), channel_id=1, source_target_pairs={{0,128},{128,0},{1,129},{129,1},{2,130},{130,2},{3,131},{131,3},{4... | collective-permute-start | bytes 786440 | tf_op jit(solution)/shard_map/ppermute | solution.py:46
  16.7 8.8 %collective-permute-start.3 = (bf16[2,16,64,128]{3,2,1,0:T(8,128)(2,1)S(1)}, bf16[2,16,64,128]{3,2,1,0:T(8,128)(2,1)S(1)}, u32[]{:S(2)}, u32[]{:S(2)}) collective-permute-start(bf16[2,16,64,128]{3,2,1,0:T(8,128)(2,1)S(1)} %pad_maximum_fusion.near_ref.refs_8_), channel_id=1, source_target_pairs={{0,64},{64,0},{1,65},{65,1},{2,66},{66,2},{3,67},{67,3},{4,68},{68... | collective-permute-start | bytes 1572872 | tf_op jit(solution)/shard_map/ppermute | solution.py:42
  16.8 11.8 %collective-permute-start.10 = (bf16[1280,128]{1,0:T(8,128)(2,1)S(1)}, bf16[1280,128]{1,0:T(8,128)(2,1)S(1)}, u32[]{:S(2)}, u32[]{:S(2)}) collective-permute-start(bf16[1280,128]{1,0:T(8,128)(2,1)S(1)} %get-tuple-element.51), channel_id=1, source_target_pairs={{0,6},{1,7},{2,4},{3,5},{4,2},{5,3},{6,0},{7,1},{64,199},{65,196},... | collective-permute-start | bytes 983048 | tf_op jit(solution)/shard_map/ppermute | solution.py:74
  20.2 15.3 %collective-permute-start.11 = (bf16[1280,128]{1,0:T(8,128)(2,1)S(1)}, bf16[1280,128]{1,0:T(8,128)(2,1)S(1)}, u32[]{:S(2)}, u32[]{:S(2)}) collective-permute-start(bf16[1280,128]{1,0:T(8,128)(2,1)S(1)} %get-tuple-element.53), channel_id=1, source_target_pairs={{0,1},{1,2},{2,3},{3,0},{4,5},{5,6},{6,7},{7,4},{64,67},{65,64},{6... | collective-permute-start | bytes 983048 | tf_op jit(solution)/shard_map/ppermute | solution.py:74
  22.2 13.3 %collective-permute-start.8 = (bf16[1024,128]{1,0:T(8,128)(2,1)S(1)}, bf16[1024,128]{1,0:T(8,128)(2,1)S(1)}, u32[]{:S(2)}, u32[]{:S(2)}) collective-permute-start(bf16[1024,128]{1,0:T(8,128)(2,1)S(1)} %collective-permute-done.2.refs_1_), channel_id=1, source_target_pairs={{0,56},{8,0},{16,8},{24,16},{32,24},{40,32},{48,40},{56,48},{1,57}... | collective-permute-start | bytes 786440 | tf_op jit(solution)/shard_map/ppermute | solution.py:26
  25.5 10.0 %collective-permute-start.9 = (bf16[1024,128]{1,0:T(8,128)(2,1)S(1)}, bf16[1024,128]{1,0:T(8,128)(2,1)S(1)}, u32[]{:S(2)}, u32[]{:S(2)}) collective-permute-start(bf16[1024,128]{1,0:T(8,128)(2,1)S(1)} %collective-permute-done.1.refs_7_), channel_id=1, source_target_pairs={{0,8},{8,16},{16,24},{24,32},{32,40},{40,48},{48,56},{56,0},{1,9},... | collective-permute-start | bytes 786440 | tf_op jit(solution)/shard_map/ppermute | solution.py:26
  25.5 18.4 %collective-permute-start.14 = (bf16[1280,128]{1,0:T(8,128)(2,1)S(1)}, bf16[1280,128]{1,0:T(8,128)(2,1)S(1)}, u32[]{:S(2)}, u32[]{:S(2)}) collective-permute-start(bf16[1280,128]{1,0:T(8,128)(2,1)S(1)} %get-tuple-element.58), channel_id=1, source_target_pairs={{64,66},{65,67},{66,64},{67,65},{68,70},{69,71},{70,68},{71,69},{1... | collective-permute-start | bytes 983048 | tf_op jit(solution)/shard_map/ppermute | solution.py:74
  28.6 10.0 %collective-permute-start.4 = (f32[32,1024]{1,0:T(8,128)S(1)}, f32[32,1024]{1,0:T(8,128)S(1)}, u32[]{:S(2)}, u32[]{:S(2)}) collective-permute-start(f32[32,1024]{1,0:T(8,128)S(1)} %low.1.a_ref), channel_id=1, source_target_pairs={{0,4},{4,0},{1,5},{5,1},{2,6},{6,2},{3,7},{7,3},{8,12},{12,8},{9,1... | collective-permute-start | bytes 393224 | tf_op jit(solution)/shard_map/ppermute | solution.py:38
  35.5 8.9 %collective-permute-start.12 = (bf16[1024,128]{1,0:T(8,128)(2,1)S(1)}, bf16[1024,128]{1,0:T(8,128)(2,1)S(1)}, u32[]{:S(2)}, u32[]{:S(2)}) collective-permute-start(bf16[1024,128]{1,0:T(8,128)(2,1)S(1)} %collective-permute-done.8.refs_2_), channel_id=1, source_target_pairs={{0,56},{8,0},{16,8},{24,16},{32,24},{40,32},{48,40},{56,48},{1,57}... | collective-permute-start | bytes 786440 | tf_op jit(solution)/shard_map/ppermute | solution.py:26
  38.6 7.6 %collective-permute-start.13 = (bf16[1024,128]{1,0:T(8,128)(2,1)S(1)}, bf16[1024,128]{1,0:T(8,128)(2,1)S(1)}, u32[]{:S(2)}, u32[]{:S(2)}) collective-permute-start(bf16[1024,128]{1,0:T(8,128)(2,1)S(1)} %collective-permute-done.9.refs_6_), channel_id=1, source_target_pairs={{0,8},{8,16},{16,24},{24,32},{32,40},{40,48},{48,56},{56,0},{1,9},... | collective-permute-start | bytes 786440 | tf_op jit(solution)/shard_map/ppermute | solution.py:26
  50.3 7.6 %collective-permute-start.15 = (bf16[1024,128]{1,0:T(8,128)(2,1)S(1)}, bf16[1024,128]{1,0:T(8,128)(2,1)S(1)}, u32[]{:S(2)}, u32[]{:S(2)}) collective-permute-start(bf16[1024,128]{1,0:T(8,128)(2,1)S(1)} %collective-permute-done.13.refs_5_), channel_id=1, source_target_pairs={{0,8},{8,16},{16,24},{24,32},{32,40},{40,48},{48,56},{56,0},{1,9},... | collective-permute-start | bytes 786440 | tf_op jit(solution)/shard_map/ppermute | solution.py:26
  59.3 8.4 %collective-permute-start.20 = (bf16[512,128]{1,0:T(8,128)(2,1)S(1)}, bf16[512,128]{1,0:T(8,128)(2,1)S(1)}, u32[]{:S(2)}, u32[]{:S(2)}) collective-permute-start(bf16[512,128]{1,0:T(8,128)(2,1)S(1)} %get-tuple-element.64), channel_id=1, source_target_pairs={{0,2},{1,3},{2,0},{3,1},{4,6},{5,7},{6,4},{7,5},{8,10},{9,11},{10,... | collective-permute-start | bytes 393224 | tf_op jit(solution)/shard_map/ppermute | solution.py:50
  69.0 13.5 %collective-permute-start.23 = (bf16[2048,128]{1,0:T(8,128)(2,1)S(1)}, bf16[2048,128]{1,0:T(8,128)(2,1)S(1)}, u32[]{:S(2)}, u32[]{:S(2)}) collective-permute-start(bf16[2048,128]{1,0:T(8,128)(2,1)S(1)} %get-tuple-element.68), channel_id=1, source_target_pairs={{0,4},{4,0},{1,5},{5,1},{2,6},{6,2},{3,7},{7,3},{8,12},{12,8},{9,1... | collective-permute-start | bytes 1572872 | tf_op jit(solution)/shard_map/ppermute | solution.py:38
  69.1 16.0 %collective-permute-start.27 = (bf16[1280,128]{1,0:T(8,128)(2,1)S(1)}, bf16[1280,128]{1,0:T(8,128)(2,1)S(1)}, u32[]{:S(2)}, u32[]{:S(2)}) collective-permute-start(bf16[1280,128]{1,0:T(8,128)(2,1)S(1)} %get-tuple-element.75), channel_id=1, source_target_pairs={{0,2},{1,3},{2,0},{3,1},{4,6},{5,7},{6,4},{7,5},{8,10},{9,11},{10,... | collective-permute-start | bytes 983048 | tf_op jit(solution)/shard_map/ppermute | solution.py:50
  70.5 16.5 %collective-permute-start.28 = (bf16[1280,128]{1,0:T(8,128)(2,1)S(1)}, bf16[1280,128]{1,0:T(8,128)(2,1)S(1)}, u32[]{:S(2)}, u32[]{:S(2)}) collective-permute-start(bf16[1280,128]{1,0:T(8,128)(2,1)S(1)} %get-tuple-element.76), channel_id=1, source_target_pairs={{0,1},{1,2},{2,3},{3,0},{4,5},{5,6},{6,7},{7,4},{8,9},{9,10},{10,1... | collective-permute-start | bytes 983048 | tf_op jit(solution)/shard_map/ppermute | solution.py:50
  72.8 14.3 %collective-permute-start.29 = (bf16[1280,128]{1,0:T(8,128)(2,1)S(1)}, bf16[1280,128]{1,0:T(8,128)(2,1)S(1)}, u32[]{:S(2)}, u32[]{:S(2)}) collective-permute-start(bf16[1280,128]{1,0:T(8,128)(2,1)S(1)} %get-tuple-element.77), channel_id=1, source_target_pairs={{0,3},{1,0},{2,1},{3,2},{4,7},{5,4},{6,5},{7,6},{8,11},{9,8},{10,9... | collective-permute-start | bytes 983048 | tf_op jit(solution)/shard_map/ppermute | solution.py:50
  73.8 9.0 %collective-permute-start.31 = (f32[32,1024]{1,0:T(8,128)S(1)}, f32[32,1024]{1,0:T(8,128)S(1)}, u32[]{:S(2)}, u32[]{:S(2)}) collective-permute-start(f32[32,1024]{1,0:T(8,128)S(1)} %low_add.8.a_ref), channel_id=1, source_target_pairs={{0,8},{8,0},{16,24},{24,16},{32,40},{40,32},{48,56},{56,48},{1,9},... | collective-permute-start | bytes 393224 | tf_op jit(solution)/shard_map/ppermute | solution.py:30
  82.7 20.8 %collective-permute-start.24 = (bf16[896,128]{1,0:T(8,128)(2,1)S(1)}, bf16[896,128]{1,0:T(8,128)(2,1)S(1)}, u32[]{:S(2)}, u32[]{:S(2)}) collective-permute-start(bf16[896,128]{1,0:T(8,128)(2,1)S(1)} %get-tuple-element.71), channel_id=1, source_target_pairs={{0,1},{1,2},{2,3},{3,0},{4,5},{5,6},{6,7},{7,4},{8,9},{9,10},{10,1... | collective-permute-start | bytes 688136 | tf_op jit(solution)/shard_map/ppermute | solution.py:50
  82.8 20.7 %collective-permute-start.25 = (bf16[896,128]{1,0:T(8,128)(2,1)S(1)}, bf16[896,128]{1,0:T(8,128)(2,1)S(1)}, u32[]{:S(2)}, u32[]{:S(2)}) collective-permute-start(bf16[896,128]{1,0:T(8,128)(2,1)S(1)} %get-tuple-element.72), channel_id=1, source_target_pairs={{0,2},{1,3},{2,0},{3,1},{4,6},{5,7},{6,4},{7,5},{8,10},{9,11},{10,... | collective-permute-start | bytes 688136 | tf_op jit(solution)/shard_map/ppermute | solution.py:50
  85.1 18.4 %collective-permute-start.26 = (bf16[896,128]{1,0:T(8,128)(2,1)S(1)}, bf16[896,128]{1,0:T(8,128)(2,1)S(1)}, u32[]{:S(2)}, u32[]{:S(2)}) collective-permute-start(bf16[896,128]{1,0:T(8,128)(2,1)S(1)} %get-tuple-element.73), channel_id=1, source_target_pairs={{0,3},{1,0},{2,1},{3,2},{4,7},{5,4},{6,5},{7,6},{8,11},{9,8},{10,9... | collective-permute-start | bytes 688136 | tf_op jit(solution)/shard_map/ppermute | solution.py:50
  87.2 16.3 %collective-permute-start.30 = (bf16[640,128]{1,0:T(8,128)(2,1)S(1)}, bf16[640,128]{1,0:T(8,128)(2,1)S(1)}, u32[]{:S(2)}, u32[]{:S(2)}) collective-permute-start(bf16[640,128]{1,0:T(8,128)(2,1)S(1)} %get-tuple-element.79), channel_id=1, source_target_pairs={{0,4},{4,0},{1,5},{5,1},{2,6},{6,2},{3,7},{7,3},{8,12},{12,8},{9,1... | collective-permute-start | bytes 491528 | tf_op jit(solution)/shard_map/ppermute | solution.py:38
  94.0 8.8 %collective-permute-start.33 = (bf16[32,1024]{1,0:T(8,128)(2,1)S(1)}, bf16[32,1024]{1,0:T(8,128)(2,1)S(1)}, u32[]{:S(2)}, u32[]{:S(2)}) collective-permute-start(bf16[32,1024]{1,0:T(8,128)(2,1)S(1)} %get-tuple-element.84), channel_id=1, source_target_pairs={{0,32},{8,40},{16,48},{24,56},{32,0},{40,8},{48,16},{56,24},{1,33}... | collective-permute-start | bytes 196616 | tf_op jit(solution)/shard_map/ppermute | solution.py:30
  (15 other events, 124.5 us)

commit v5 on v4

--- a/solution.py
+++ b/solution.py
@@ -18,6 +18,7 @@
 TP_AXES = ("z", "xl", "y")
 NP = NX * NY
 TA, TB = 384, 640
+PACK_MIB = 4
 VMEM = pl.BlockSpec(memory_space=pltpu.VMEM)
 SMEM = pl.BlockSpec(memory_space=pltpu.SMEM)
 
@@ -74,14 +75,18 @@
     return lax.ppermute(v, ("xh", "c", "xl", "y"), route)
 
 
-def weight_swap(v, k):
-    return lax.ppermute(v, "c", [(c, 1 - c) for c in range(NC) if k < len(SERVED[c])])
-
-
-def pack_kernel(wq_ref, kv_ref, *refs):
-    outs, sem = refs[:5], refs[5]
+def run_copies(pairs, sem):
+    copies = [pltpu.make_async_copy(src, dst, sem.at[i]) for i, (src, dst) in enumerate(pairs)]
+    for copy in copies:
+        copy.start()
+    for copy in copies:
+        copy.wait()
+
+
+def pack_kernel(wq_ref, kv_ref, down_ref, up_ref, *refs):
+    outs, maps, sem = refs[:5], refs[5], refs[6]
     z, xl, y, c = (lax.axis_index(a) for a in ("z", "xl", "y", "c"))
-    copies = []
+    pairs = [(down_ref, maps.at[:, 0:RANK, :]), (up_ref, maps.at[:, RANK : 2 * RANK, :])]
     for k in range(5):
         d = 0
         if k < 4:
@@ -89,13 +94,14 @@
         p = (xl ^ (d // NY)) * NY + ((y + d) & (NY - 1))
         for j in range(NZ):
             row = pl.multiple_of((((z + j) & (NZ - 1)) * NP + p) * 128, 128)
-            copies.append((wq_ref.at[pl.ds(row, 128), :], outs[k].at[j * 128 : (j + 1) * 128, :]))
-            copies.append((kv_ref.at[:, pl.ds(row, 128)], outs[k].at[1024 + j * 32 : 1056 + j * 32, :]))
-    copies = [pltpu.make_async_copy(src, dst, sem.at[i]) for i, (src, dst) in enumerate(copies)]
-    for copy in copies:
-        copy.start()
-    for copy in copies:
-        copy.wait()
+            pairs.append((wq_ref.at[pl.ds(row, 128), :], outs[k].at[j * 128 : (j + 1) * 128, :]))
+            pairs.append((kv_ref.at[:, pl.ds(row, 128)], outs[k].at[1024 + j * 32 : 1056 + j * 32, :]))
+    run_copies(pairs, sem)
+
+
+def stack_kernel(*refs):
+    for i, ref in enumerate(refs[:-1]):
+        refs[-1][i] = ref[...]
 
 
 def add_kernel(a_ref, b_ref, *outs):
@@ -159,10 +165,16 @@
 
 
 def kv_product_kernel(*refs):
-    h_refs, own, mine, other = refs[0:8], refs[8], refs[9:13], refs[13:17]
-    outs, hbuf, kvw = refs[17:21], refs[21], refs[22]
+    h_refs, own, mine, other, low_ref = refs[0:8], refs[8], refs[9:13], refs[13], refs[14]
+    outs, hbuf, kvw = refs[15:19], refs[19], refs[20]
+    other = [other.at[k] for k in range(4)]
+    y = lax.axis_index("y")
     for j in range(8):
         hbuf[:, j * 128 : (j + 1) * 128] = h_refs[j][...]
+    for dy in range(NY):
+        for t in range(2):
+            at = pl.multiple_of((((y + dy) & (NY - 1)) * 2 + t) * 128, 128)
+            outs[dy][512 + t * 32 : 544 + t * 32, :] = low_ref[:, pl.ds(at, 128)].astype(jnp.bfloat16)
 
     def place(ref, d):
         for j in range(NZ):
@@ -180,8 +192,8 @@
 
 
 def q_product_kernel(hbuf, own, *refs):
-    mine, other = refs[0:4], refs[4:8]
-    near_ref, far_ref, outs, wq = refs[8], refs[9], refs[10:14], refs[14]
+    mine, other = refs[0:4], [refs[4].at[k] for k in range(4)]
+    near_ref, far_ref, outs, wq = refs[5], refs[6], refs[7:11], refs[11]
 
     def place(ref, d):
         dx, dy = divmod(d, NY)
@@ -206,7 +218,7 @@
     total = wide(k0, ...) + wide(k1, ...) + wide(k2, ...) + wide(k3, ...)
     sum_ref[...] = total
     send_ref[0 : NY * TA, :] = far_ref[...]
-    send_ref[NY * TA : NY * TA + 512, :] = total.astype(jnp.bfloat16)
+    send_ref[NY * TA :, :] = total.astype(jnp.bfloat16)
 
 
 def stage_a_kernel(near_ref, got_ref, kv_ref, own_ref, kv_out, *sends):
@@ -214,6 +226,7 @@
         for dx in range(NX):
             a, b = t * 64 + dx * 32, NY * TA + t * 64 + (1 - dx) * 32
             kv_out[a : a + 32, :] = (kv_ref[a : a + 32, :] + wide(got_ref, slice(b, b + 32))).astype(jnp.bfloat16)
+    kv_out[512:576, :] = (kv_ref[512:576, :] + wide(got_ref, slice(NY * TA + 512, NY * TA + 576))).astype(jnp.bfloat16)
     for dy in range(NY):
         rows = slice(dy * TA, (dy + 1) * TA)
         total = wide(near_ref, rows) + wide(got_ref, rows)
@@ -221,7 +234,7 @@
             own_ref[...] = total
         else:
             sends[dy - 1][0:TA, :] = total.astype(jnp.bfloat16)
-            sends[dy - 1][TA : TA + 512, :] = kv_out[...]
+            sends[dy - 1][TA:, :] = kv_out[...]
 
 
 def stage_b_kernel(b0, b1, b2, b3, own_ref, send_ref):
@@ -232,13 +245,15 @@
 
 def attention_kernel(ad_ref, start_ref, *refs):
     a_own, a_got, b_own, b_got, kv_own = refs[0], refs[1:4], refs[4], refs[5], refs[6]
-    low_ref, near_ref, far_ref, cos_ref, sin_ref = refs[7:12]
-    out_ref = refs[12]
-    kvt, k_buf, v_buf = refs[13:16]
+    near_ref, far_ref, cos_ref, sin_ref = refs[7:11]
+    out_ref = refs[11]
+    kvt, k_buf, v_buf, low_buf = refs[12:16]
     xl, y, c, xh = (lax.axis_index(a) for a in ("xl", "y", "c", "xh"))
     first = (xh * NC + c) * 8
     for i in range(NY):
         ref, base = (kv_own, 0) if i == 0 else (a_got[i - 1], TA)
+        for t in range(2):
+            low_buf[((y - i) & (NY - 1)) * 2 + t] = ref[base + 512 + t * 32 : base + 544 + t * 32, :]
         for dx in range(NX):
             p = (xl ^ dx) * NY + ((y - i) & (NY - 1))
             at = pl.multiple_of(p * 32, 32)
@@ -263,7 +278,7 @@
         xr, cr = (owner // NC) ^ xh, (owner % NC) ^ c
         up = jnp.where(cr == 0, near_ref[xr, at, RANK : 2 * RANK, :], far_ref[xr, at, RANK : 2 * RANK, :])
         q = ADAPTER_SCALE * lax.dot_general(
-            low_ref[:, rows], up, (((0,), (0,)), ((), ())), preferred_element_type=jnp.float32
+            low_buf[b], up, (((0,), (0,)), ((), ())), preferred_element_type=jnp.float32
         )
         if b * 128 < TA:
             q += a_own[rows, :]
@@ -282,10 +297,8 @@
         allowed = (col >= (start_ref[b * BLOCK] - first) * BLOCK) & (col <= row)
         s = jnp.where(allowed, s, -1e30)
         e = jnp.exp2((s - jnp.max(s, axis=1, keepdims=True)) * factor)
-        probs = (e * (1.0 / jnp.sum(e, axis=1, keepdims=True))).astype(jnp.bfloat16)
-        out_ref[rows, :] = jnp.dot(
-            probs, v_buf[0:n, :], preferred_element_type=jnp.float32
-        ).astype(jnp.bfloat16)
+        mixed = jnp.dot(e.astype(jnp.bfloat16), v_buf[0:n, :], preferred_element_type=jnp.float32)
+        out_ref[rows, :] = (mixed * (1.0 / jnp.sum(e, axis=1, keepdims=True))).astype(jnp.bfloat16)
 
 
 def call(kernel, name, outs, *args, scalars=0, scratch=(), mib=4, space=pltpu.VMEM):
@@ -309,56 +322,58 @@
     rows = hidden.shape[0]
     bf16, f32 = jnp.bfloat16, jnp.float32
     of = jax.ShapeDtypeStruct
-    maps = jnp.concatenate([jnp.transpose(down_maps, (0, 2, 1)), up_maps], axis=1)
-    twin = xh_swap(maps)
-
-    sends = call(
+    *sends, maps = call(
         pack_kernel,
         "pack",
-        [of((1280, 128), bf16)] * 5,
+        [of((1280, 128), bf16)] * 5 + [of((down_maps.shape[0], 2 * RANK, 128), bf16)],
         query_weight,
         key_value_weight.T,
-        scratch=[pltpu.SemaphoreType.DMA((10 * NZ,))],
+        jnp.transpose(down_maps, (0, 2, 1)),
+        up_maps,
+        scratch=[pltpu.SemaphoreType.DMA((10 * NZ + 2,))],
         space=pltpu.HBM,
-    )
+        mib=PACK_MIB,
+    )
+    twin = xh_swap(maps)
     cosines, sines = call(rope_kernel, "rope", [of((rows, HEAD_SIZE), f32)] * 2, request_start, scalars=1)
-    right, left = [hidden], [hidden]
-    mine = [weight_send(sends[k], k) for k in range(2)]
-    gates = ((), (0,), (1, 2), (3,))
-    for step in range(4):
-        r, l = right[-1], left[-1]
-        if step:
-            waits = [mine[k] for k in gates[step]] + [cosines] * (step == 2)
-            r, l = after(right[-1], left[-1], *waits), after(left[-1], right[-1], *waits)
-        right.append(z_shift(r, 1))
-        if step < 3:
-            left.append(z_shift(l, -1))
-        if step == 1:
-            mine += [weight_send(after(sends[k], right[1], left[1]), k) for k in (2, 3)]
-    other = [weight_swap(mine[k], k) for k in range(4)]
-
-    near = jnp.stack([maps, after(twin, right[1], left[1])])
-    far = core_swap(near)
-    low = call(
-        low_kernel, "low", of((RANK, rows), f32), adapters, hidden, near, far, scalars=1
-    )
+    ring = [(hidden, hidden)]
+
+    def ring_step(*others):
+        r, l = ring[-1]
+        if len(ring) > 1:
+            r, l = after(r, l, *others), after(l, r, *others)
+        ring.append((z_shift(r, 1), z_shift(l, -1) if len(ring) < 4 else None))
 
     def added(low, sent, also=()):
         outs = [of((RANK, rows), f32)] + [of((RANK, rows), t) for t in also]
         return call(add_kernel, "low_add", outs, low, sent)
 
-    (low,) = added(low, x_swap(low))
-    (low,) = added(low, y_xor(low, 1))
-    (low,) = added(low, y_xor(low, 2))
-
-    shards = [after(hidden, low), left[1], left[2], left[3], right[4], right[3], right[2], right[1]]
-    weights = (sends[4], *mine, *other)
+    ring_step()
+    mine = [weight_send(sends[0], 0), weight_send(after(sends[1], *ring[1]), 1)]
+    ring_step(mine[0], twin)
+    near = jnp.stack([maps, after(twin, *ring[1])])
+    far = core_swap(near)
+    mine += [weight_send(after(sends[k], *ring[2]), k) for k in (2, 3)]
+    low = call(low_kernel, "low", of((RANK, rows), f32), adapters, hidden, near, far, scalars=1)
+    ring_step(mine[1], low, cosines)
+    (low,) = added(low, z_xor(low, 1))
+    ring_step(mine[2], low)
+    mine[3] = after(mine[3], *ring[3])
+    other = core_swap(call(stack_kernel, "stack", of((4, 1280, 128), bf16), *mine))
+    low = after(low, *ring[3])
+    low, narrow = added(low, z_xor(low, 2), (bf16,))
+    (low,) = added(low, z_xor(narrow, 4))
+    right, left = zip(*ring)
+
+    shards = [hidden, left[1], left[2], left[3], right[4], right[3], right[2], right[1]]
+    weights = (sends[4], *mine, other)
     *kv_parts, gathered = call(
         kv_product_kernel,
         "kv_product",
-        [of((512, 128), bf16)] * NY + [of((rows, 1024), bf16)],
+        [of((576, 128), bf16)] * NY + [of((rows, 1024), bf16)],
         *shards,
         *weights,
+        low,
         scratch=[pltpu.VMEM((256, 1024), bf16)],
         mib=8,
     )
@@ -376,21 +391,16 @@
     kv_sum, x_send = call(
         kv_join_kernel,
         "kv_join",
-        [of((512, 128), f32), of((NY * TA + 512, 128), bf16)],
+        [of((576, 128), f32), of((NY * TA + 576, 128), bf16)],
         kv_parts[0],
         *kv_got,
         far_a,
     )
     x_got = x_swap(x_send)
-    low = after(low, kv_sum)
-    (low,) = added(low, z_xor(low, 1))
-    low = after(low, x_got)
-    low, narrow = added(low, z_xor(low, 2), (bf16,))
-    _, low = added(low, z_xor(narrow, 4), (bf16,))
     a_own, kv_own, *a_sends = call(
         stage_a_kernel,
         "stage_a",
-        [of((TA, 128), f32), of((512, 128), bf16)] + [of((TA + 512, 128), bf16)] * (NY - 1),
+        [of((TA, 128), f32), of((576, 128), bf16)] + [of((TA + 576, 128), bf16)] * (NY - 1),
         near_a,
         x_got,
         kv_sum,
@@ -412,13 +422,12 @@
         b_own,
         b_last,
         kv_own,
-        low,
         near,
         far,
         cosines,
         sines,
         scalars=2,
-        scratch=[pltpu.VMEM((256, rows), bf16)] + [pltpu.VMEM((rows, HEAD_SIZE), bf16)] * 2,
+        scratch=[pltpu.VMEM((256, rows), bf16)] + [pltpu.VMEM((rows, HEAD_SIZE), bf16)] * 2 + [pltpu.VMEM((8, RANK, 128), bf16)],
         mib=8,
     )
 

time: 112 us -> 122 us (1.089)
  waiting for transfers between devices: 44.8 us -> 59.8 us
  starting transfers between devices: 44.3 us -> 40.8 us
  local copies, waits for them, and re-layouts: 2.64 us -> 4.45 us
    ppermute x7, waiting for transfers between devices: 8.02 us -> 17 us  [z_shift(): return lax.ppermute(v, 'z', [(i, (i + s) % NZ) for i in range(NZ)])]
    ppermute x3, waiting for transfers between devices: 10.4 us -> 19.3 us  [z_xor(): return lax.ppermute(v, 'z', [(i, i ^ s) for i in range(NZ)])]
    ppermute x6 -> x0, waiting for transfers between devices: 8.29 us -> none  [the longest x2 8.28 us: y_xor(): return lax.ppermute(v, 'y', [(i, i ^ s) for i in range(NY)])]
    ppermute x4, waiting for transfers between devices: 7.35 us -> 0.1 us  [weight_send(): return lax.ppermute(v, ('xh', 'c', 'xl', 'y'), route)]
    ppermute x1, waiting for transfers between devices: 0.01 us -> 5.8 us  [xh_swap(): return lax.ppermute(v, 'xh', [(0, 1), (1, 0)])]
    ppermute x9, waiting for transfers between devices: 1.93 us -> 6.23 us  [y_shift(): return lax.ppermute(v, 'y', [(i, (i + s) % NY) for i in range(NY)])]
    ppermute x6 -> x0, starting transfers between devices: 2.8 us -> none  [the longest x4 2.61 us: weight_swap(): lax.ppermute(v, 'c', [(c, 1 - c) for c in range(NC) if k < len(SERVED[c])])]
    ppermute x3 -> x2, waiting for transfers between devices: 8.75 us -> 11.4 us  [x_swap(): return lax.ppermute(v, 'xl', [(0, 1), (1, 0)])]
  transfers between devices with their start and end apart: 34 -> 28, of which waited for: 12 -> 15; matrix products, arithmetic and copies ran while one was open for 1% -> 0% of each run, Pallas kernels for 8% -> 7%
where the time goes in v5:
time: 122 us; the launch traced here: 121 us
  waiting for transfers between devices  59.8 us (49%)
  starting transfers between devices  40.8 us (33%)
  Pallas kernels  15.4 us (13%)
  local copies, waits for them, and re-layouts  4.45 us (4%)
    ppermute x3, waiting for transfers between devices, z_xor(): return lax.ppermute(v, 'z', [(i, i ^ s) for i in range(NZ)])  19.3 us
    ppermute x7, waiting for transfers between devices, z_shift(): return lax.ppermute(v, 'z', [(i, (i + s) % NZ) for i in range(NZ)])  17 us
    pallas_call x13, Pallas kernels, call(): pl.pallas_call(kernel, out_shape=outs, in_specs=[SMEM] * scalars + [pl.Bl...  15.4 us
    ppermute x9, starting transfers between devices, y_shift(): return lax.ppermute(v, 'y', [(i, (i + s) % NY) for i in range(NY)])  14.2 us
    ppermute x2, waiting for transfers between devices, x_swap(): return lax.ppermute(v, 'xl', [(0, 1), (1, 0)])  11.4 us
    ppermute x7, starting transfers between devices, z_shift(): return lax.ppermute(v, 'z', [(i, (i + s) % NZ) for i in range(NZ)])  10.8 us
    ppermute x4, starting transfers between devices, weight_send(): return lax.ppermute(v, ('xh', 'c', 'xl', 'y'), route)  6.32 us
    ppermute x9, waiting for transfers between devices, y_shift(): return lax.ppermute(v, 'y', [(i, (i + s) % NY) for i in range(NY)])  6.23 us
  transfers between devices with their start and end apart: 28, of which 15 were waited for; matrix products, arithmetic and copies ran while one was open for 0% of the time, Pallas kernels for 7%

profile of v5, /device:TPU:2, one launch (start us, length us, event | category | flops | bytes accessed | tf_op | source)
XLA Modules:
  0.0 120.6 jit_solution(15474978506858407795)
XLA Ops:
  0.0 1.9 %collective-permute-start.1 = (bf16[1024,128]{1,0:T(8,128)(2,1)}, bf16[1024,128]{1,0:T(8,128)(2,1)S(1)}, u32[]{:S(2)}, u32[]{:S(2)}) collective-permute-start(bf16[1024,128]{1,0:T(8,128)(2,1)} %refs_0_.1), channel_id=1, source_target_pairs={{0,8},{8,16},{16,24},{24,32},{32,40},{40,48},{48,56},{56,0},{1,9},... | collective-permute-start | bytes 786440 | tf_op jit(solution)/shard_map/ppermute | solution.py:27
  1.9 4.0 %collective-permute-start = (bf16[1024,128]{1,0:T(8,128)(2,1)}, bf16[1024,128]{1,0:T(8,128)(2,1)S(1)}, u32[]{:S(2)}, u32[]{:S(2)}) collective-permute-start(bf16[1024,128]{1,0:T(8,128)(2,1)} %refs_0_.1), channel_id=1, source_target_pairs={{0,56},{8,0},{16,8},{24,16},{32,24},{40,32},{48,40},{56,48},{1,57}... | collective-permute-start | bytes 786440 | tf_op jit(solution)/shard_map/ppermute | solution.py:27
  10.4 3.3 %pack.1 = (bf16[1280,128]{1,0:T(8,128)(2,1)S(1)}, bf16[1280,128]{1,0:T(8,128)(2,1)S(1)}, bf16[1280,128]{1,0:T(8,128)(2,1)S(1)}, bf16[1280,128]{1,0:T(8,128)(2,1)...) custom-call(bf16[8192,128]{1,0:T(8,128)(2,1)S(1)} %copy-done, bf16[32,8192]{1,0:T(8,128)(2,1)S(1)} %bitcast.4, ...), custom_call_target="tpu_custom_call" | custom-call | tf_op jit(solution)/shard_map/pack/pallas_call | solution.py:306
  13.7 2.2 %collective-permute-start.3 = (bf16[16,64,128]{2,1,0:T(8,128)(2,1)S(1)}, bf16[16,64,128]{2,1,0:T(8,128)(2,1)S(1)}, u32[]{:S(2)}, u32[]{:S(2)}) collective-permute-start(bf16[16,64,128]{2,1,0:T(8,128)(2,1)S(1)} %get-tuple-element.47), channel_id=1, source_target_pairs={{0,128},{128,0},{1,129},{129,1},{2,130},{130,2},{3,131},{131,3},{4... | collective-permute-start | bytes 786440 | tf_op jit(solution)/shard_map/ppermute | solution.py:47
  17.4 5.8 %collective-permute-done.3 = bf16[16,64,128]{2,1,0:T(8,128)(2,1)S(1)} collective-permute-done((bf16[16,64,128]{2,1,0:T(8,128)(2,1)S(1)}, bf16[16,64,128]{2,1,0:T(8,128)(2,1)S(1)}, u32[]{:S(2)}, u32[]{:S(2)}) %collective-permute-start.3) | collective-permute-done | bytes 262176 | tf_op jit(solution)/shard_map/ppermute | solution.py:47
  23.3 3.2 %collective-permute-start.6 = (bf16[1280,128]{1,0:T(8,128)(2,1)S(1)}, bf16[1280,128]{1,0:T(8,128)(2,1)S(1)}, u32[]{:S(2)}, u32[]{:S(2)}) collective-permute-start(bf16[1280,128]{1,0:T(8,128)(2,1)S(1)} %get-tuple-element.51), channel_id=1, source_target_pairs={{0,6},{1,7},{2,4},{3,5},{4,2},{5,3},{6,0},{7,1},{64,199},{65,196},... | collective-permute-start | bytes 983048 | tf_op jit(solution)/shard_map/ppermute | solution.py:75
  28.7 5.9 %collective-permute-done.4.refs_2_ = bf16[1024,128]{1,0:T(8,128)(2,1)S(1)} collective-permute-done((bf16[1024,128]{1,0:T(8,128)(2,1)S(1)}, bf16[1024,128]{1,0:T(8,128)(2,1)S(1)}, u32[]{:S(2)}, u32[]{:S(2)}) %collective-permute-start.4) | collective-permute-done | bytes 262176 | tf_op jit(solution)/shard_map/ppermute | solution.py:27
  34.6 3.2 %collective-permute-done.5.refs_6_ = bf16[1024,128]{1,0:T(8,128)(2,1)S(1)} collective-permute-done((bf16[1024,128]{1,0:T(8,128)(2,1)S(1)}, bf16[1024,128]{1,0:T(8,128)(2,1)S(1)}, u32[]{:S(2)}, u32[]{:S(2)}) %collective-permute-start.5) | collective-permute-done | bytes 262176 | tf_op jit(solution)/shard_map/ppermute | solution.py:27
  43.4 6.4 %collective-permute-done.8.refs_3_ = bf16[1024,128]{1,0:T(8,128)(2,1)S(1)} collective-permute-done((bf16[1024,128]{1,0:T(8,128)(2,1)S(1)}, bf16[1024,128]{1,0:T(8,128)(2,1)S(1)}, u32[]{:S(2)}, u32[]{:S(2)}) %collective-permute-start.8) | collective-permute-done | bytes 262176 | tf_op jit(solution)/shard_map/ppermute | solution.py:27
  52.6 5.0 %collective-permute-done.11.b_ref = f32[32,1024]{1,0:T(8,128)S(1)} collective-permute-done((f32[32,1024]{1,0:T(8,128)S(1)}, f32[32,1024]{1,0:T(8,128)S(1)}, u32[]{:S(2)}, u32[]{:S(2)}) %collective-permute-start.11) | collective-permute-done | bytes 131104 | tf_op jit(solution)/shard_map/ppermute | solution.py:31
  58.3 8.2 %collective-permute-done.15.b_ref = f32[32,1024]{1,0:T(8,128)S(1)} collective-permute-done((f32[32,1024]{1,0:T(8,128)S(1)}, f32[32,1024]{1,0:T(8,128)S(1)}, u32[]{:S(2)}, u32[]{:S(2)}) %collective-permute-start.15) | collective-permute-done | bytes 131104 | tf_op jit(solution)/shard_map/ppermute | solution.py:31
  66.6 2.9 %collective-permute-start.16 = (bf16[32,1024]{1,0:T(8,128)(2,1)S(1)}, bf16[32,1024]{1,0:T(8,128)(2,1)S(1)}, u32[]{:S(2)}, u32[]{:S(2)}) collective-permute-start(bf16[32,1024]{1,0:T(8,128)(2,1)S(1)} %get-tuple-element.65), channel_id=1, source_target_pairs={{0,32},{8,40},{16,48},{24,56},{32,0},{40,8},{48,16},{56,24},{1,33}... | collective-permute-start | bytes 196616 | tf_op jit(solution)/shard_map/ppermute | solution.py:31
  69.5 6.1 %collective-permute-done.16.b_ref = bf16[32,1024]{1,0:T(8,128)(2,1)S(1)} collective-permute-done((bf16[32,1024]{1,0:T(8,128)(2,1)S(1)}, bf16[32,1024]{1,0:T(8,128)(2,1)S(1)}, u32[]{:S(2)}, u32[]{:S(2)}) %collective-permute-start.16) | collective-permute-done | bytes 65568 | tf_op jit(solution)/shard_map/ppermute | solution.py:31
  77.1 3.1 %collective-permute-start.17 = (bf16[576,128]{1,0:T(8,128)(2,1)S(1)}, bf16[576,128]{1,0:T(8,128)(2,1)S(1)}, u32[]{:S(2)}, u32[]{:S(2)}) collective-permute-start(bf16[576,128]{1,0:T(8,128)(2,1)S(1)} %get-tuple-element.69), channel_id=1, source_target_pairs={{0,2},{1,3},{2,0},{3,1},{4,6},{5,7},{6,4},{7,5},{8,10},{9,11},{10,... | collective-permute-start | bytes 442376 | tf_op jit(solution)/shard_map/ppermute | solution.py:51
  80.2 3.2 %collective-permute-start.19 = (bf16[576,128]{1,0:T(8,128)(2,1)S(1)}, bf16[576,128]{1,0:T(8,128)(2,1)S(1)}, u32[]{:S(2)}, u32[]{:S(2)}) collective-permute-start(bf16[576,128]{1,0:T(8,128)(2,1)S(1)} %get-tuple-element.71), channel_id=1, source_target_pairs={{0,3},{1,0},{2,1},{3,2},{4,7},{5,4},{6,5},{7,6},{8,11},{9,8},{10,9... | collective-permute-start | bytes 442376 | tf_op jit(solution)/shard_map/ppermute | solution.py:51
  83.5 2.7 %q_product.1 = (bf16[1536,128]{1,0:T(8,128)(2,1)S(1)}, bf16[1536,128]{1,0:T(8,128)(2,1)S(1)}, bf16[1280,128]{1,0:T(8,128)(2,1)S(1)}, bf16[1280,128]{1,0:T(8,128)...) custom-call(bf16[1024,1024]{1,0:T(8,128)(2,1)S(1)} %get-tuple-element.66.hbuf, ...), custom_call_target="tpu_custom_call" | custom-call | tf_op jit(solution)/shard_map/q_product/pallas_call | solution.py:306
  89.5 2.1 %collective-permute-start.25 = (bf16[1280,128]{1,0:T(8,128)(2,1)S(1)}, bf16[1280,128]{1,0:T(8,128)(2,1)S(1)}, u32[]{:S(2)}, u32[]{:S(2)}) collective-permute-start(bf16[1280,128]{1,0:T(8,128)(2,1)S(1)} %get-tuple-element.81), channel_id=1, source_target_pairs={{0,1},{1,2},{2,3},{3,0},{4,5},{5,6},{6,7},{7,4},{8,9},{9,10},{10,1... | collective-permute-start | bytes 983048 | tf_op jit(solution)/shard_map/ppermute | solution.py:51
  92.7 7.7 %collective-permute-done.20.got_ref = bf16[2112,128]{1,0:T(8,128)(2,1)S(1)} collective-permute-done((bf16[2112,128]{1,0:T(8,128)(2,1)S(1)}, bf16[2112,128]{1,0:T(8,128)(2,1)S(1)}, u32[]{:S(2)}, u32[]{:S(2)}) %collective-permute-start.20) | collective-permute-done | bytes 540704 | tf_op jit(solution)/shard_map/ppermute | solution.py:39
  100.7 3.3 %collective-permute-start.22 = (bf16[960,128]{1,0:T(8,128)(2,1)S(1)}, bf16[960,128]{1,0:T(8,128)(2,1)S(1)}, u32[]{:S(2)}, u32[]{:S(2)}) collective-permute-start(bf16[960,128]{1,0:T(8,128)(2,1)S(1)} %get-tuple-element.77), channel_id=1, source_target_pairs={{0,2},{1,3},{2,0},{3,1},{4,6},{5,7},{6,4},{7,5},{8,10},{9,11},{10,... | collective-permute-start | bytes 737288 | tf_op jit(solution)/shard_map/ppermute | solution.py:51
  104.6 1.8 %collective-permute-done.26.b3 = bf16[1280,128]{1,0:T(8,128)(2,1)S(1)} collective-permute-done((bf16[1280,128]{1,0:T(8,128)(2,1)S(1)}, bf16[1280,128]{1,0:T(8,128)(2,1)S(1)}, u32[]{:S(2)}, u32[]{:S(2)}) %collective-permute-start.26) | collective-permute-done | bytes 327712 | tf_op jit(solution)/shard_map/ppermute | solution.py:51
  106.5 1.9 %collective-permute-start.27 = (bf16[640,128]{1,0:T(8,128)(2,1)S(1)}, bf16[640,128]{1,0:T(8,128)(2,1)S(1)}, u32[]{:S(2)}, u32[]{:S(2)}) collective-permute-start(bf16[640,128]{1,0:T(8,128)(2,1)S(1)} %get-tuple-element.84), channel_id=1, source_target_pairs={{0,4},{4,0},{1,5},{5,1},{2,6},{6,2},{3,7},{7,3},{8,12},{12,8},{9,1... | collective-permute-start | bytes 491528 | tf_op jit(solution)/shard_map/ppermute | solution.py:39
  108.5 3.7 %collective-permute-done.27.refs_5_ = bf16[640,128]{1,0:T(8,128)(2,1)S(1)} collective-permute-done((bf16[640,128]{1,0:T(8,128)(2,1)S(1)}, bf16[640,128]{1,0:T(8,128)(2,1)S(1)}, u32[]{:S(2)}, u32[]{:S(2)}) %collective-permute-start.27) | collective-permute-done | bytes 163872 | tf_op jit(solution)/shard_map/ppermute | solution.py:39
  112.2 2.9 %collective-permute-done.22.refs_2_ = bf16[960,128]{1,0:T(8,128)(2,1)S(1)} collective-permute-done((bf16[960,128]{1,0:T(8,128)(2,1)S(1)}, bf16[960,128]{1,0:T(8,128)(2,1)S(1)}, u32[]{:S(2)}, u32[]{:S(2)}) %collective-permute-start.22) | collective-permute-done | bytes 245792 | tf_op jit(solution)/shard_map/ppermute | solution.py:51
  115.0 5.5 %attention.1 = bf16[1024,128]{1,0:T(8,128)(2,1)} custom-call(s32[8]{0:T(128)S(1)} %copy-done.6, s32[1024]{0:T(1024)S(1)} %copy-done.5, f32[384,128]{1,0:T(8,128)S(1)} %get-tuple-element.75.refs_0_, bf16[960,128]{1,0:T(8,128)(2,1)S(1)} %collective-permute-done.21.refs_1_, bf16[960,128]{1,0:T(8,128)(2,1)S(1)} %collective-permute-done.22.refs_2_, ...), custom_call_target="tpu_custom_call" | custom-call | tf_op jit(solution)/shard_map/attention/pallas_call | solution.py:306
  (60 shorter events, 24.2 us)
Async XLA Ops:
  0.0 17.4 %collective-permute-start.1 = (bf16[1024,128]{1,0:T(8,128)(2,1)}, bf16[1024,128]{1,0:T(8,128)(2,1)S(1)}, u32[]{:S(2)}, u32[]{:S(2)}) collective-permute-start(bf16[1024,128]{1,0:T(8,128)(2,1)} %refs_0_.1), channel_id=1, source_target_pairs={{0,8},{8,16},{16,24},{24,32},{32,40},{40,48},{48,56},{56,0},{1,9},... | collective-permute-start | bytes 786440 | tf_op jit(solution)/shard_map/ppermute | solution.py:27
  1.9 15.4 %collective-permute-start = (bf16[1024,128]{1,0:T(8,128)(2,1)}, bf16[1024,128]{1,0:T(8,128)(2,1)S(1)}, u32[]{:S(2)}, u32[]{:S(2)}) collective-permute-start(bf16[1024,128]{1,0:T(8,128)(2,1)} %refs_0_.1), channel_id=1, source_target_pairs={{0,56},{8,0},{16,8},{24,16},{32,24},{40,32},{48,40},{56,48},{1,57}... | collective-permute-start | bytes 786440 | tf_op jit(solution)/shard_map/ppermute | solution.py:27
  13.7 9.5 %collective-permute-start.3 = (bf16[16,64,128]{2,1,0:T(8,128)(2,1)S(1)}, bf16[16,64,128]{2,1,0:T(8,128)(2,1)S(1)}, u32[]{:S(2)}, u32[]{:S(2)}) collective-permute-start(bf16[16,64,128]{2,1,0:T(8,128)(2,1)S(1)} %get-tuple-element.47), channel_id=1, source_target_pairs={{0,128},{128,0},{1,129},{129,1},{2,130},{130,2},{3,131},{131,3},{4... | collective-permute-start | bytes 786440 | tf_op jit(solution)/shard_map/ppermute | solution.py:47
  15.9 10.7 %collective-permute-start.2 = (bf16[1280,128]{1,0:T(8,128)(2,1)S(1)}, bf16[1280,128]{1,0:T(8,128)(2,1)S(1)}, u32[]{:S(2)}, u32[]{:S(2)}) collective-permute-start(bf16[1280,128]{1,0:T(8,128)(2,1)S(1)} %get-tuple-element.46), channel_id=1, source_target_pairs={{0,4},{1,5},{2,6},{3,7},{4,0},{5,1},{6,2},{7,3},{64,197},{65,198},... | collective-permute-start | bytes 983048 | tf_op jit(solution)/shard_map/ppermute | solution.py:75
  23.2 17.2 %collective-permute-start.7 = (bf16[2,16,64,128]{3,2,1,0:T(8,128)(2,1)S(1)}, bf16[2,16,64,128]{3,2,1,0:T(8,128)(2,1)S(1)}, u32[]{:S(2)}, u32[]{:S(2)}) collective-permute-start(bf16[2,16,64,128]{3,2,1,0:T(8,128)(2,1)S(1)} %pad_maximum_fusion.near_ref.refs_7_), channel_id=1, source_target_pairs={{0,64},{64,0},{1,65},{65,1},{2,66},{66,2},{3,67},{67,3},{4,68},{68... | collective-permute-start | bytes 1572872 | tf_op jit(solution)/shard_map/ppermute | solution.py:43
  23.3 17.9 %collective-permute-start.6 = (bf16[1280,128]{1,0:T(8,128)(2,1)S(1)}, bf16[1280,128]{1,0:T(8,128)(2,1)S(1)}, u32[]{:S(2)}, u32[]{:S(2)}) collective-permute-start(bf16[1280,128]{1,0:T(8,128)(2,1)S(1)} %get-tuple-element.51), channel_id=1, source_target_pairs={{0,6},{1,7},{2,4},{3,5},{4,2},{5,3},{6,0},{7,1},{64,199},{65,196},... | collective-permute-start | bytes 983048 | tf_op jit(solution)/shard_map/ppermute | solution.py:75
  26.7 7.9 %collective-permute-start.4 = (bf16[1024,128]{1,0:T(8,128)(2,1)S(1)}, bf16[1024,128]{1,0:T(8,128)(2,1)S(1)}, u32[]{:S(2)}, u32[]{:S(2)}) collective-permute-start(bf16[1024,128]{1,0:T(8,128)(2,1)S(1)} %collective-permute-done.refs_1_), channel_id=1, source_target_pairs={{0,56},{8,0},{16,8},{24,16},{32,24},{40,32},{48,40},{56,48},{1,57}... | collective-permute-start | bytes 786440 | tf_op jit(solution)/shard_map/ppermute | solution.py:27
  28.3 9.5 %collective-permute-start.5 = (bf16[1024,128]{1,0:T(8,128)(2,1)S(1)}, bf16[1024,128]{1,0:T(8,128)(2,1)S(1)}, u32[]{:S(2)}, u32[]{:S(2)}) collective-permute-start(bf16[1024,128]{1,0:T(8,128)(2,1)S(1)} %collective-permute-done.1.refs_7_), channel_id=1, source_target_pairs={{0,8},{8,16},{16,24},{24,32},{32,40},{40,48},{48,56},{56,0},{1,9},... | collective-permute-start | bytes 786440 | tf_op jit(solution)/shard_map/ppermute | solution.py:27
  38.5 12.8 %collective-permute-start.10 = (bf16[1280,128]{1,0:T(8,128)(2,1)S(1)}, bf16[1280,128]{1,0:T(8,128)(2,1)S(1)}, u32[]{:S(2)}, u32[]{:S(2)}) collective-permute-start(bf16[1280,128]{1,0:T(8,128)(2,1)S(1)} %get-tuple-element.57), channel_id=1, source_target_pairs={{0,1},{1,2},{2,3},{3,0},{4,5},{5,6},{6,7},{7,4},{64,67},{65,64},{6... | collective-permute-start | bytes 983048 | tf_op jit(solution)/shard_map/ppermute | solution.py:75
  41.3 8.5 %collective-permute-start.8 = (bf16[1024,128]{1,0:T(8,128)(2,1)S(1)}, bf16[1024,128]{1,0:T(8,128)(2,1)S(1)}, u32[]{:S(2)}, u32[]{:S(2)}) collective-permute-start(bf16[1024,128]{1,0:T(8,128)(2,1)S(1)} %collective-permute-done.4.refs_2_), channel_id=1, source_target_pairs={{0,56},{8,0},{16,8},{24,16},{32,24},{40,32},{48,40},{56,48},{1,57}... | collective-permute-start | bytes 786440 | tf_op jit(solution)/shard_map/ppermute | solution.py:27
  41.6 9.6 %collective-permute-start.9 = (bf16[1024,128]{1,0:T(8,128)(2,1)S(1)}, bf16[1024,128]{1,0:T(8,128)(2,1)S(1)}, u32[]{:S(2)}, u32[]{:S(2)}) collective-permute-start(bf16[1024,128]{1,0:T(8,128)(2,1)S(1)} %collective-permute-done.5.refs_6_), channel_id=1, source_target_pairs={{0,8},{8,16},{16,24},{24,32},{32,40},{40,48},{48,56},{56,0},{1,9},... | collective-permute-start | bytes 786440 | tf_op jit(solution)/shard_map/ppermute | solution.py:27
  51.3 24.3 %collective-permute-start.14 = (bf16[4,1280,128]{2,1,0:T(8,128)(2,1)S(1)}, bf16[4,1280,128]{2,1,0:T(8,128)(2,1)S(1)}, u32[]{:S(2)}, u32[]{:S(2)}) collective-permute-start(bf16[4,1280,128]{2,1,0:T(8,128)(2,1)S(1)} %stack.13), channel_id=1, source_target_pairs={{0,64},{64,0},{1,65},{65,1},{2,66},{66,2},{3,67},{67,3},{4,68},{68... | collective-permute-start | bytes 3932168 | tf_op jit(solution)/shard_map/ppermute | solution.py:43
  57.5 18.1 %collective-permute-start.12 = (bf16[1024,128]{1,0:T(8,128)(2,1)S(1)}, bf16[1024,128]{1,0:T(8,128)(2,1)S(1)}, u32[]{:S(2)}, u32[]{:S(2)}) collective-permute-start(bf16[1024,128]{1,0:T(8,128)(2,1)S(1)} %collective-permute-done.9.refs_5_), channel_id=1, source_target_pairs={{0,8},{8,16},{16,24},{24,32},{32,40},{40,48},{48,56},{56,0},{1,9},... | collective-permute-start | bytes 786440 | tf_op jit(solution)/shard_map/ppermute | solution.py:27
  58.3 8.3 %collective-permute-start.15 = (f32[32,1024]{1,0:T(8,128)S(1)}, f32[32,1024]{1,0:T(8,128)S(1)}, u32[]{:S(2)}, u32[]{:S(2)}) collective-permute-start(f32[32,1024]{1,0:T(8,128)S(1)} %low_add.3.a_ref), channel_id=1, source_target_pairs={{0,16},{8,24},{16,0},{24,8},{32,48},{40,56},{48,32},{56,40},{1,17}... | collective-permute-start | bytes 393224 | tf_op jit(solution)/shard_map/ppermute | solution.py:31
  66.6 9.1 %collective-permute-start.16 = (bf16[32,1024]{1,0:T(8,128)(2,1)S(1)}, bf16[32,1024]{1,0:T(8,128)(2,1)S(1)}, u32[]{:S(2)}, u32[]{:S(2)}) collective-permute-start(bf16[32,1024]{1,0:T(8,128)(2,1)S(1)} %get-tuple-element.65), channel_id=1, source_target_pairs={{0,32},{8,40},{16,48},{24,56},{32,0},{40,8},{48,16},{56,24},{1,33}... | collective-permute-start | bytes 196616 | tf_op jit(solution)/shard_map/ppermute | solution.py:31
  77.1 9.0 %collective-permute-start.17 = (bf16[576,128]{1,0:T(8,128)(2,1)S(1)}, bf16[576,128]{1,0:T(8,128)(2,1)S(1)}, u32[]{:S(2)}, u32[]{:S(2)}) collective-permute-start(bf16[576,128]{1,0:T(8,128)(2,1)S(1)} %get-tuple-element.69), channel_id=1, source_target_pairs={{0,2},{1,3},{2,0},{3,1},{4,6},{5,7},{6,4},{7,5},{8,10},{9,11},{10,... | collective-permute-start | bytes 442376 | tf_op jit(solution)/shard_map/ppermute | solution.py:51
  80.2 6.9 %collective-permute-start.18 = (bf16[576,128]{1,0:T(8,128)(2,1)S(1)}, bf16[576,128]{1,0:T(8,128)(2,1)S(1)}, u32[]{:S(2)}, u32[]{:S(2)}) collective-permute-start(bf16[576,128]{1,0:T(8,128)(2,1)S(1)} %get-tuple-element.70), channel_id=1, source_target_pairs={{0,1},{1,2},{2,3},{3,0},{4,5},{5,6},{6,7},{7,4},{8,9},{9,10},{10,1... | collective-permute-start | bytes 442376 | tf_op jit(solution)/shard_map/ppermute | solution.py:51
  87.2 13.2 %collective-permute-start.20 = (bf16[2112,128]{1,0:T(8,128)(2,1)S(1)}, bf16[2112,128]{1,0:T(8,128)(2,1)S(1)}, u32[]{:S(2)}, u32[]{:S(2)}) collective-permute-start(bf16[2112,128]{1,0:T(8,128)(2,1)S(1)} %get-tuple-element.73), channel_id=1, source_target_pairs={{0,4},{4,0},{1,5},{5,1},{2,6},{6,2},{3,7},{7,3},{8,12},{12,8},{9,1... | collective-permute-start | bytes 1622024 | tf_op jit(solution)/shard_map/ppermute | solution.py:39
  88.3 15.7 %collective-permute-start.24 = (bf16[1280,128]{1,0:T(8,128)(2,1)S(1)}, bf16[1280,128]{1,0:T(8,128)(2,1)S(1)}, u32[]{:S(2)}, u32[]{:S(2)}) collective-permute-start(bf16[1280,128]{1,0:T(8,128)(2,1)S(1)} %get-tuple-element.80), channel_id=1, source_target_pairs={{0,2},{1,3},{2,0},{3,1},{4,6},{5,7},{6,4},{7,5},{8,10},{9,11},{10,... | collective-permute-start | bytes 983048 | tf_op jit(solution)/shard_map/ppermute | solution.py:51
  89.5 15.1 %collective-permute-start.25 = (bf16[1280,128]{1,0:T(8,128)(2,1)S(1)}, bf16[1280,128]{1,0:T(8,128)(2,1)S(1)}, u32[]{:S(2)}, u32[]{:S(2)}) collective-permute-start(bf16[1280,128]{1,0:T(8,128)(2,1)S(1)} %get-tuple-element.81), channel_id=1, source_target_pairs={{0,1},{1,2},{2,3},{3,0},{4,5},{5,6},{6,7},{7,4},{8,9},{9,10},{10,1... | collective-permute-start | bytes 983048 | tf_op jit(solution)/shard_map/ppermute | solution.py:51
  91.6 14.7 %collective-permute-start.26 = (bf16[1280,128]{1,0:T(8,128)(2,1)S(1)}, bf16[1280,128]{1,0:T(8,128)(2,1)S(1)}, u32[]{:S(2)}, u32[]{:S(2)}) collective-permute-start(bf16[1280,128]{1,0:T(8,128)(2,1)S(1)} %get-tuple-element.82), channel_id=1, source_target_pairs={{0,3},{1,0},{2,1},{3,2},{4,7},{5,4},{6,5},{7,6},{8,11},{9,8},{10,9... | collective-permute-start | bytes 983048 | tf_op jit(solution)/shard_map/ppermute | solution.py:51
  100.6 11.6 %collective-permute-start.21 = (bf16[960,128]{1,0:T(8,128)(2,1)S(1)}, bf16[960,128]{1,0:T(8,128)(2,1)S(1)}, u32[]{:S(2)}, u32[]{:S(2)}) collective-permute-start(bf16[960,128]{1,0:T(8,128)(2,1)S(1)} %get-tuple-element.76), channel_id=1, source_target_pairs={{0,1},{1,2},{2,3},{3,0},{4,5},{5,6},{6,7},{7,4},{8,9},{9,10},{10,1... | collective-permute-start | bytes 737288 | tf_op jit(solution)/shard_map/ppermute | solution.py:51
  100.7 14.4 %collective-permute-start.22 = (bf16[960,128]{1,0:T(8,128)(2,1)S(1)}, bf16[960,128]{1,0:T(8,128)(2,1)S(1)}, u32[]{:S(2)}, u32[]{:S(2)}) collective-permute-start(bf16[960,128]{1,0:T(8,128)(2,1)S(1)} %get-tuple-element.77), channel_id=1, source_target_pairs={{0,2},{1,3},{2,0},{3,1},{4,6},{5,7},{6,4},{7,5},{8,10},{9,11},{10,... | collective-permute-start | bytes 737288 | tf_op jit(solution)/shard_map/ppermute | solution.py:51
  104.0 11.1 %collective-permute-start.23 = (bf16[960,128]{1,0:T(8,128)(2,1)S(1)}, bf16[960,128]{1,0:T(8,128)(2,1)S(1)}, u32[]{:S(2)}, u32[]{:S(2)}) collective-permute-start(bf16[960,128]{1,0:T(8,128)(2,1)S(1)} %get-tuple-element.78), channel_id=1, source_target_pairs={{0,3},{1,0},{2,1},{3,2},{4,7},{5,4},{6,5},{7,6},{8,11},{9,8},{10,9... | collective-permute-start | bytes 737288 | tf_op jit(solution)/shard_map/ppermute | solution.py:51
  (11 other events, 127.7 us)

commit v6 on v5

--- a/solution.py
+++ b/solution.py
@@ -18,7 +18,7 @@
 TP_AXES = ("z", "xl", "y")
 NP = NX * NY
 TA, TB = 384, 640
-PACK_MIB = 4
+PACK_MIB = 56
 VMEM = pl.BlockSpec(memory_space=pltpu.VMEM)
 SMEM = pl.BlockSpec(memory_space=pltpu.SMEM)
 
@@ -165,16 +165,11 @@
 
 
 def kv_product_kernel(*refs):
-    h_refs, own, mine, other, low_ref = refs[0:8], refs[8], refs[9:13], refs[13], refs[14]
-    outs, hbuf, kvw = refs[15:19], refs[19], refs[20]
+    h_refs, own, mine, other = refs[0:8], refs[8], refs[9:13], refs[13]
+    outs, hbuf, kvw = refs[14:18], refs[18], refs[19]
     other = [other.at[k] for k in range(4)]
-    y = lax.axis_index("y")
     for j in range(8):
         hbuf[:, j * 128 : (j + 1) * 128] = h_refs[j][...]
-    for dy in range(NY):
-        for t in range(2):
-            at = pl.multiple_of((((y + dy) & (NY - 1)) * 2 + t) * 128, 128)
-            outs[dy][512 + t * 32 : 544 + t * 32, :] = low_ref[:, pl.ds(at, 128)].astype(jnp.bfloat16)
 
     def place(ref, d):
         for j in range(NZ):
@@ -226,7 +221,6 @@
         for dx in range(NX):
             a, b = t * 64 + dx * 32, NY * TA + t * 64 + (1 - dx) * 32
             kv_out[a : a + 32, :] = (kv_ref[a : a + 32, :] + wide(got_ref, slice(b, b + 32))).astype(jnp.bfloat16)
-    kv_out[512:576, :] = (kv_ref[512:576, :] + wide(got_ref, slice(NY * TA + 512, NY * TA + 576))).astype(jnp.bfloat16)
     for dy in range(NY):
         rows = slice(dy * TA, (dy + 1) * TA)
         total = wide(near_ref, rows) + wide(got_ref, rows)
@@ -245,15 +239,13 @@
 
 def attention_kernel(ad_ref, start_ref, *refs):
     a_own, a_got, b_own, b_got, kv_own = refs[0], refs[1:4], refs[4], refs[5], refs[6]
-    near_ref, far_ref, cos_ref, sin_ref = refs[7:11]
-    out_ref = refs[11]
-    kvt, k_buf, v_buf, low_buf = refs[12:16]
+    low_ref, near_ref, far_ref, cos_ref, sin_ref = refs[7:12]
+    out_ref = refs[12]
+    kvt, k_buf, v_buf = refs[13:16]
     xl, y, c, xh = (lax.axis_index(a) for a in ("xl", "y", "c", "xh"))
     first = (xh * NC + c) * 8
     for i in range(NY):
         ref, base = (kv_own, 0) if i == 0 else (a_got[i - 1], TA)
-        for t in range(2):
-            low_buf[((y - i) & (NY - 1)) * 2 + t] = ref[base + 512 + t * 32 : base + 544 + t * 32, :]
         for dx in range(NX):
             p = (xl ^ dx) * NY + ((y - i) & (NY - 1))
             at = pl.multiple_of(p * 32, 32)
@@ -278,7 +270,7 @@
         xr, cr = (owner // NC) ^ xh, (owner % NC) ^ c
         up = jnp.where(cr == 0, near_ref[xr, at, RANK : 2 * RANK, :], far_ref[xr, at, RANK : 2 * RANK, :])
         q = ADAPTER_SCALE * lax.dot_general(
-            low_buf[b], up, (((0,), (0,)), ((), ())), preferred_element_type=jnp.float32
+            low_ref[:, rows], up, (((0,), (0,)), ((), ())), preferred_element_type=jnp.float32
         )
         if b * 128 < TA:
             q += a_own[rows, :]
@@ -348,21 +340,24 @@
         outs = [of((RANK, rows), f32)] + [of((RANK, rows), t) for t in also]
         return call(add_kernel, "low_add", outs, low, sent)
 
+    def added(low, sent, *first, also=()):
+        outs = [of((RANK, rows), f32)] + [of((RANK, rows), t) for t in also]
+        return call(add_kernel, "low_add", outs, low, after(sent, *first))
+
     ring_step()
     mine = [weight_send(sends[0], 0), weight_send(after(sends[1], *ring[1]), 1)]
-    ring_step(mine[0], twin)
+    ring_step(sends[1])
     near = jnp.stack([maps, after(twin, *ring[1])])
     far = core_swap(near)
     mine += [weight_send(after(sends[k], *ring[2]), k) for k in (2, 3)]
     low = call(low_kernel, "low", of((RANK, rows), f32), adapters, hidden, near, far, scalars=1)
-    ring_step(mine[1], low, cosines)
-    (low,) = added(low, z_xor(low, 1))
-    ring_step(mine[2], low)
+    ring_step(mine[0], low, cosines)
+    (low,) = added(low, x_swap(low), *ring[3])
+    ring_step(mine[1])
     mine[3] = after(mine[3], *ring[3])
     other = core_swap(call(stack_kernel, "stack", of((4, 1280, 128), bf16), *mine))
-    low = after(low, *ring[3])
-    low, narrow = added(low, z_xor(low, 2), (bf16,))
-    (low,) = added(low, z_xor(narrow, 4))
+    hidden = after(hidden, low)
+    (low,) = added(low, y_xor(low, 1), ring[4][0])
     right, left = zip(*ring)
 
     shards = [hidden, left[1], left[2], left[3], right[4], right[3], right[2], right[1]]
@@ -370,10 +365,9 @@
     *kv_parts, gathered = call(
         kv_product_kernel,
         "kv_product",
-        [of((576, 128), bf16)] * NY + [of((rows, 1024), bf16)],
+        [of((512, 128), bf16)] * NY + [of((rows, 1024), bf16)],
         *shards,
         *weights,
-        low,
         scratch=[pltpu.VMEM((256, 1024), bf16)],
         mib=8,
     )
@@ -382,33 +376,41 @@
         q_product_kernel,
         "q_product",
         [of((NY * TA, 128), bf16)] * 2 + [of((2 * TB, 128), bf16)] * NY,
-        gathered,
+        after(gathered, low),
         *weights,
         scratch=[pltpu.VMEM((NY, 1024, 256), bf16)],
         mib=10,
     )
+    (low,) = added(low, y_xor(low, 2))
     b_got = [y_shift(b_parts[dy], dy) for dy in (2, 1, 3)]
     kv_sum, x_send = call(
         kv_join_kernel,
         "kv_join",
-        [of((576, 128), f32), of((NY * TA + 576, 128), bf16)],
+        [of((512, 128), f32), of((NY * TA + 512, 128), bf16)],
         kv_parts[0],
         *kv_got,
-        far_a,
+        after(far_a, low),
     )
     x_got = x_swap(x_send)
+    (low,) = added(low, z_xor(low, 1))
     a_own, kv_own, *a_sends = call(
         stage_a_kernel,
         "stage_a",
-        [of((TA, 128), f32), of((576, 128), bf16)] + [of((TA + 576, 128), bf16)] * (NY - 1),
-        near_a,
+        [of((TA, 128), f32), of((512, 128), bf16)] + [of((TA + 512, 128), bf16)] * (NY - 1),
+        after(near_a, low),
         x_got,
         kv_sum,
     )
     a_got = {dy: y_shift(a_sends[dy - 1], dy) for dy in (2, 1, 3)}
+    low, narrow = added(low, z_xor(low, 2), x_got, also=(bf16,))
     b_own, b_send = call(
-        stage_b_kernel, "stage_b", [of((TB, 128), f32), of((TB, 128), bf16)], b_parts[0], *b_got
-    )
+        stage_b_kernel,
+        "stage_b",
+        [of((TB, 128), f32), of((TB, 128), bf16)],
+        after(b_parts[0], narrow),
+        *b_got,
+    )
+    _, low = added(low, z_xor(narrow, 4), also=(bf16,))
     b_last = x_swap(b_send)
 
     return call(
@@ -422,12 +424,13 @@
         b_own,
         b_last,
         kv_own,
+        low,
         near,
         far,
         cosines,
         sines,
         scalars=2,
-        scratch=[pltpu.VMEM((256, rows), bf16)] + [pltpu.VMEM((rows, HEAD_SIZE), bf16)] * 2 + [pltpu.VMEM((8, RANK, 128), bf16)],
+        scratch=[pltpu.VMEM((256, rows), bf16)] + [pltpu.VMEM((rows, HEAD_SIZE), bf16)] * 2,
         mib=8,
     )
 

time: 122 us -> 112 us (0.918)
  the two profiles are of different devices: /device:TPU:2 before, /device:TPU:90 now
where the time goes in v6:
time: 112 us; the launch traced here: 111 us
  waiting for transfers between devices  48.3 us (43%)
  starting transfers between devices  45.8 us (41%)
  Pallas kernels  16.2 us (14%)
    pallas_call x16, Pallas kernels, call(): pl.pallas_call(kernel, out_shape=outs, in_specs=[SMEM] * scalars + [pl.Bl...  16.2 us
    ppermute x7, waiting for transfers between devices, z_shift(): return lax.ppermute(v, 'z', [(i, (i + s) % NZ) for i in range(NZ)])  15 us
    ppermute x9, starting transfers between devices, y_shift(): return lax.ppermute(v, 'y', [(i, (i + s) % NY) for i in range(NY)])  9.89 us
    ppermute x3, waiting for transfers between devices, z_xor(): return lax.ppermute(v, 'z', [(i, i ^ s) for i in range(NZ)])  9.42 us
    ppermute x7, starting transfers between devices, z_shift(): return lax.ppermute(v, 'z', [(i, (i + s) % NZ) for i in range(NZ)])  8.57 us
    ppermute x9, waiting for transfers between devices, y_shift(): return lax.ppermute(v, 'y', [(i, (i + s) % NY) for i in range(NY)])  8.08 us
    ppermute x4, starting transfers between devices, weight_send(): return lax.ppermute(v, ('xh', 'c', 'xl', 'y'), route)  7.79 us
    ppermute x3, waiting for transfers between devices, x_swap(): return lax.ppermute(v, 'xl', [(0, 1), (1, 0)])  6.48 us
  transfers between devices with their start and end apart: 31, of which 16 were waited for; matrix products, arithmetic and copies ran while one was open for 0% of the time, Pallas kernels for 6%

profile of v6, /device:TPU:90, one launch (start us, length us, event | category | flops | bytes accessed | tf_op | source)
XLA Modules:
  0.0 111.5 jit_solution(2723225123370407061)
XLA Ops:
  0.0 3.5 %pack.1 = (bf16[1280,128]{1,0:T(8,128)(2,1)}, bf16[1280,128]{1,0:T(8,128)(2,1)}, bf16[1280,128]{1,0:T(8,128)(2,1)}, bf16[1280,128]{1,0:T(8,128)(2,1)}, bf16[1280...) custom-call(bf16[8192,128]{1,0:T(8,128)(2,1)} %wq_ref.1, bf16[32,8192]{1,0:T(8,128)(2,1)} %bitcast.4, ...), custom_call_target="tpu_custom_call" | custom-call | tf_op jit(solution)/shard_map/pack/pallas_call | solution.py:298
  3.5 2.2 %collective-permute-start = (bf16[16,64,128]{2,1,0:T(8,128)(2,1)}, bf16[16,64,128]{2,1,0:T(8,128)(2,1)S(1)}, u32[]{:S(2)}, u32[]{:S(2)}) collective-permute-start(bf16[16,64,128]{2,1,0:T(8,128)(2,1)} %get-tuple-element.54), channel_id=1, source_target_pairs={{0,128},{128,0},{1,129},{129,1},{2,130},{130,2},{3,131},{131,3},{4... | collective-permute-start | bytes 786440 | tf_op jit(solution)/shard_map/ppermute | solution.py:47
  5.7 1.9 %collective-permute-start.1 = (bf16[1024,128]{1,0:T(8,128)(2,1)S(1)}, bf16[1024,128]{1,0:T(8,128)(2,1)S(1)}, u32[]{:S(2)}, u32[]{:S(2)}) collective-permute-start(bf16[1024,128]{1,0:T(8,128)(2,1)S(1)} %copy-done.1), channel_id=1, source_target_pairs={{0,8},{8,16},{16,24},{24,32},{32,40},{40,48},{48,56},{56,0},{1,9},... | collective-permute-start | bytes 786440 | tf_op jit(solution)/shard_map/ppermute | solution.py:27
  7.7 5.6 %collective-permute-done = bf16[16,64,128]{2,1,0:T(8,128)(2,1)S(1)} collective-permute-done((bf16[16,64,128]{2,1,0:T(8,128)(2,1)}, bf16[16,64,128]{2,1,0:T(8,128)(2,1)S(1)}, u32[]{:S(2)}, u32[]{:S(2)}) %collective-permute-start) | collective-permute-done | bytes 262176 | tf_op jit(solution)/shard_map/ppermute | solution.py:47
  13.5 3.0 %collective-permute-done.2.refs_1_ = bf16[1024,128]{1,0:T(8,128)(2,1)S(1)} collective-permute-done((bf16[1024,128]{1,0:T(8,128)(2,1)S(1)}, bf16[1024,128]{1,0:T(8,128)(2,1)S(1)}, u32[]{:S(2)}, u32[]{:S(2)}) %collective-permute-start.2) | collective-permute-done | bytes 262176 | tf_op jit(solution)/shard_map/ppermute | solution.py:27
  19.1 3.0 %collective-permute-start.5 = (bf16[1024,128]{1,0:T(8,128)(2,1)S(1)}, bf16[1024,128]{1,0:T(8,128)(2,1)S(1)}, u32[]{:S(2)}, u32[]{:S(2)}) collective-permute-start(bf16[1024,128]{1,0:T(8,128)(2,1)S(1)} %collective-permute-done.1.refs_7_), channel_id=1, source_target_pairs={{0,8},{8,16},{16,24},{24,32},{32,40},{40,48},{48,56},{56,0},{1,9},... | collective-permute-start | bytes 786440 | tf_op jit(solution)/shard_map/ppermute | solution.py:27
  22.1 4.7 %collective-permute-done.5.refs_6_ = bf16[1024,128]{1,0:T(8,128)(2,1)S(1)} collective-permute-done((bf16[1024,128]{1,0:T(8,128)(2,1)S(1)}, bf16[1024,128]{1,0:T(8,128)(2,1)S(1)}, u32[]{:S(2)}, u32[]{:S(2)}) %collective-permute-start.5) | collective-permute-done | bytes 262176 | tf_op jit(solution)/shard_map/ppermute | solution.py:27
  26.8 2.2 %collective-permute-done.6.refs_2_ = bf16[1024,128]{1,0:T(8,128)(2,1)S(1)} collective-permute-done((bf16[1024,128]{1,0:T(8,128)(2,1)S(1)}, bf16[1024,128]{1,0:T(8,128)(2,1)S(1)}, u32[]{:S(2)}, u32[]{:S(2)}) %collective-permute-start.6) | collective-permute-done | bytes 262176 | tf_op jit(solution)/shard_map/ppermute | solution.py:27
  29.7 3.2 %collective-permute-start.10 = (bf16[1280,128]{1,0:T(8,128)(2,1)}, bf16[1280,128]{1,0:T(8,128)(2,1)S(1)}, u32[]{:S(2)}, u32[]{:S(2)}) collective-permute-start(bf16[1280,128]{1,0:T(8,128)(2,1)} %get-tuple-element.65), channel_id=1, source_target_pairs={{0,6},{1,7},{2,4},{3,5},{4,2},{5,3},{6,0},{7,1},{64,199},{65,196},... | collective-permute-start | bytes 983048 | tf_op jit(solution)/shard_map/ppermute | solution.py:75
  32.9 2.4 %collective-permute-start.12 = (bf16[1280,128]{1,0:T(8,128)(2,1)}, bf16[1280,128]{1,0:T(8,128)(2,1)S(1)}, u32[]{:S(2)}, u32[]{:S(2)}) collective-permute-start(bf16[1280,128]{1,0:T(8,128)(2,1)} %get-tuple-element.69), channel_id=1, source_target_pairs={{0,1},{1,2},{2,3},{3,0},{4,5},{5,6},{6,7},{7,4},{64,67},{65,64},{6... | collective-permute-start | bytes 983048 | tf_op jit(solution)/shard_map/ppermute | solution.py:75
  37.2 2.0 %collective-permute-start.8 = (bf16[1024,128]{1,0:T(8,128)(2,1)S(1)}, bf16[1024,128]{1,0:T(8,128)(2,1)S(1)}, u32[]{:S(2)}, u32[]{:S(2)}) collective-permute-start(bf16[1024,128]{1,0:T(8,128)(2,1)S(1)} %collective-permute-done.5.refs_6_), channel_id=1, source_target_pairs={{0,8},{8,16},{16,24},{24,32},{32,40},{40,48},{48,56},{56,0},{1,9},... | collective-permute-start | bytes 786440 | tf_op jit(solution)/shard_map/ppermute | solution.py:27
  39.2 4.8 %collective-permute-done.9.refs_3_ = bf16[1024,128]{1,0:T(8,128)(2,1)S(1)} collective-permute-done((bf16[1024,128]{1,0:T(8,128)(2,1)S(1)}, bf16[1024,128]{1,0:T(8,128)(2,1)S(1)}, u32[]{:S(2)}, u32[]{:S(2)}) %collective-permute-start.9) | collective-permute-done | bytes 262176 | tf_op jit(solution)/shard_map/ppermute | solution.py:27
  44.2 3.5 %collective-permute-start.14 = (bf16[4,1280,128]{2,1,0:T(8,128)(2,1)S(1)}, bf16[4,1280,128]{2,1,0:T(8,128)(2,1)S(1)}, u32[]{:S(2)}, u32[]{:S(2)}) collective-permute-start(bf16[4,1280,128]{2,1,0:T(8,128)(2,1)S(1)} %stack.13), channel_id=1, source_target_pairs={{0,64},{64,0},{1,65},{65,1},{2,66},{66,2},{3,67},{67,3},{4,68},{68... | collective-permute-start | bytes 3932168 | tf_op jit(solution)/shard_map/ppermute | solution.py:43
  47.7 2.7 %collective-permute-start.4 = (f32[32,1024]{1,0:T(8,128)S(1)}, f32[32,1024]{1,0:T(8,128)S(1)}, u32[]{:S(2)}, u32[]{:S(2)}) collective-permute-start(f32[32,1024]{1,0:T(8,128)S(1)} %low.1.a_ref), channel_id=1, source_target_pairs={{0,4},{4,0},{1,5},{5,1},{2,6},{6,2},{3,7},{7,3},{8,12},{12,8},{9,1... | collective-permute-start | bytes 393224 | tf_op jit(solution)/shard_map/ppermute | solution.py:39
  51.9 2.3 %collective-permute-done.4.b_ref = f32[32,1024]{1,0:T(8,128)S(1)} collective-permute-done((f32[32,1024]{1,0:T(8,128)S(1)}, f32[32,1024]{1,0:T(8,128)S(1)}, u32[]{:S(2)}, u32[]{:S(2)}) %collective-permute-start.4) | collective-permute-done | bytes 131104 | tf_op jit(solution)/shard_map/ppermute | solution.py:39
  55.5 3.7 %collective-permute-done.15.b_ref = f32[32,1024]{1,0:T(8,128)S(1)} collective-permute-done((f32[32,1024]{1,0:T(8,128)S(1)}, f32[32,1024]{1,0:T(8,128)S(1)}, u32[]{:S(2)}, u32[]{:S(2)}) %collective-permute-start.15) | collective-permute-done | bytes 131104 | tf_op jit(solution)/shard_map/ppermute | solution.py:35
  59.3 3.0 %collective-permute-start.16 = (f32[32,1024]{1,0:T(8,128)S(1)}, f32[32,1024]{1,0:T(8,128)S(1)}, u32[]{:S(2)}, u32[]{:S(2)}) collective-permute-start(f32[32,1024]{1,0:T(8,128)S(1)} %low_add.7.a_ref), channel_id=1, source_target_pairs={{0,2},{1,3},{2,0},{3,1},{4,6},{5,7},{6,4},{7,5},{8,10},{9,11},{10,... | collective-permute-start | bytes 393224 | tf_op jit(solution)/shard_map/ppermute | solution.py:35
  66.7 2.7 %q_product.1 = (bf16[1536,128]{1,0:T(8,128)(2,1)S(1)}, bf16[1536,128]{1,0:T(8,128)(2,1)S(1)}, bf16[1280,128]{1,0:T(8,128)(2,1)S(1)}, bf16[1280,128]{1,0:T(8,128)...) custom-call(bf16[1024,1024]{1,0:T(8,128)(2,1)S(1)} %get-tuple-element.75.hbuf, ...), custom_call_target="tpu_custom_call" | custom-call | tf_op jit(solution)/shard_map/q_product/pallas_call | solution.py:298
  80.6 4.2 %collective-permute-done.21.got_ref = bf16[2048,128]{1,0:T(8,128)(2,1)S(1)} collective-permute-done((bf16[2048,128]{1,0:T(8,128)(2,1)S(1)}, bf16[2048,128]{1,0:T(8,128)(2,1)S(1)}, u32[]{:S(2)}, u32[]{:S(2)}) %collective-permute-start.21) | collective-permute-done | bytes 524320 | tf_op jit(solution)/shard_map/ppermute | solution.py:39
  86.5 3.4 %collective-permute-start.23 = (bf16[896,128]{1,0:T(8,128)(2,1)S(1)}, bf16[896,128]{1,0:T(8,128)(2,1)S(1)}, u32[]{:S(2)}, u32[]{:S(2)}) collective-permute-start(bf16[896,128]{1,0:T(8,128)(2,1)S(1)} %get-tuple-element.88), channel_id=1, source_target_pairs={{0,2},{1,3},{2,0},{3,1},{4,6},{5,7},{6,4},{7,5},{8,10},{9,11},{10,... | collective-permute-start | bytes 688136 | tf_op jit(solution)/shard_map/ppermute | solution.py:51
  89.9 5.1 %collective-permute-done.28.b3 = bf16[1280,128]{1,0:T(8,128)(2,1)S(1)} collective-permute-done((bf16[1280,128]{1,0:T(8,128)(2,1)S(1)}, bf16[1280,128]{1,0:T(8,128)(2,1)S(1)}, u32[]{:S(2)}, u32[]{:S(2)}) %collective-permute-start.28) | collective-permute-done | bytes 327712 | tf_op jit(solution)/shard_map/ppermute | solution.py:51
  95.2 1.9 %collective-permute-start.29 = (bf16[640,128]{1,0:T(8,128)(2,1)S(1)}, bf16[640,128]{1,0:T(8,128)(2,1)S(1)}, u32[]{:S(2)}, u32[]{:S(2)}) collective-permute-start(bf16[640,128]{1,0:T(8,128)(2,1)S(1)} %get-tuple-element.98), channel_id=1, source_target_pairs={{0,4},{4,0},{1,5},{5,1},{2,6},{6,2},{3,7},{7,3},{8,12},{12,8},{9,1... | collective-permute-start | bytes 491528 | tf_op jit(solution)/shard_map/ppermute | solution.py:39
  98.7 6.5 %collective-permute-done.30.b_ref = bf16[32,1024]{1,0:T(8,128)(2,1)S(1)} collective-permute-done((bf16[32,1024]{1,0:T(8,128)(2,1)S(1)}, bf16[32,1024]{1,0:T(8,128)(2,1)S(1)}, u32[]{:S(2)}, u32[]{:S(2)}) %collective-permute-start.30) | collective-permute-done | bytes 65568 | tf_op jit(solution)/shard_map/ppermute | solution.py:31
  105.9 5.6 %attention.1 = bf16[1024,128]{1,0:T(8,128)(2,1)} custom-call(s32[8]{0:T(128)S(1)} %copy-done.3, s32[1024]{0:T(1024)S(1)} %copy-done.2, f32[384,128]{1,0:T(8,128)S(1)} %get-tuple-element.86.refs_0_, bf16[896,128]{1,0:T(8,128)(2,1)S(1)} %collective-permute-done.22.refs_1_, bf16[896,128]{1,0:T(8,128)(2,1)S(1)} %collective-permute-done.23.refs_2_, ...), custom_call_target="tpu_custom_call" | custom-call | tf_op jit(solution)/shard_map/attention/pallas_call | solution.py:298
  (63 shorter events, 28.3 us)
Async XLA Ops:
  3.5 9.8 %collective-permute-start = (bf16[16,64,128]{2,1,0:T(8,128)(2,1)}, bf16[16,64,128]{2,1,0:T(8,128)(2,1)S(1)}, u32[]{:S(2)}, u32[]{:S(2)}) collective-permute-start(bf16[16,64,128]{2,1,0:T(8,128)(2,1)} %get-tuple-element.54), channel_id=1, source_target_pairs={{0,128},{128,0},{1,129},{129,1},{2,130},{130,2},{3,131},{131,3},{4... | collective-permute-start | bytes 786440 | tf_op jit(solution)/shard_map/ppermute | solution.py:47
  5.7 7.8 %collective-permute-start.1 = (bf16[1024,128]{1,0:T(8,128)(2,1)S(1)}, bf16[1024,128]{1,0:T(8,128)(2,1)S(1)}, u32[]{:S(2)}, u32[]{:S(2)}) collective-permute-start(bf16[1024,128]{1,0:T(8,128)(2,1)S(1)} %copy-done.1), channel_id=1, source_target_pairs={{0,8},{8,16},{16,24},{24,32},{32,40},{40,48},{48,56},{56,0},{1,9},... | collective-permute-start | bytes 786440 | tf_op jit(solution)/shard_map/ppermute | solution.py:27
  7.6 8.9 %collective-permute-start.2 = (bf16[1024,128]{1,0:T(8,128)(2,1)S(1)}, bf16[1024,128]{1,0:T(8,128)(2,1)S(1)}, u32[]{:S(2)}, u32[]{:S(2)}) collective-permute-start(bf16[1024,128]{1,0:T(8,128)(2,1)S(1)} %copy-done.1), channel_id=1, source_target_pairs={{0,56},{8,0},{16,8},{24,16},{32,24},{40,32},{48,40},{56,48},{1,57}... | collective-permute-start | bytes 786440 | tf_op jit(solution)/shard_map/ppermute | solution.py:27
  17.5 18.8 %collective-permute-start.3 = (bf16[2,16,64,128]{3,2,1,0:T(8,128)(2,1)S(1)}, bf16[2,16,64,128]{3,2,1,0:T(8,128)(2,1)S(1)}, u32[]{:S(2)}, u32[]{:S(2)}) collective-permute-start(bf16[2,16,64,128]{3,2,1,0:T(8,128)(2,1)S(1)} %pad_maximum_fusion.near_ref.refs_8_), channel_id=1, source_target_pairs={{0,64},{64,0},{1,65},{65,1},{2,66},{66,2},{3,67},{67,3},{4,68},{68... | collective-permute-start | bytes 1572872 | tf_op jit(solution)/shard_map/ppermute | solution.py:43
  17.6 19.5 %collective-permute-start.7 = (bf16[1280,128]{1,0:T(8,128)(2,1)}, bf16[1280,128]{1,0:T(8,128)(2,1)S(1)}, u32[]{:S(2)}, u32[]{:S(2)}) collective-permute-start(bf16[1280,128]{1,0:T(8,128)(2,1)} %get-tuple-element.59), channel_id=1, source_target_pairs={{0,4},{1,5},{2,6},{3,7},{4,0},{5,1},{6,2},{7,3},{64,197},{65,198},... | collective-permute-start | bytes 983048 | tf_op jit(solution)/shard_map/ppermute | solution.py:75
  19.1 7.7 %collective-permute-start.5 = (bf16[1024,128]{1,0:T(8,128)(2,1)S(1)}, bf16[1024,128]{1,0:T(8,128)(2,1)S(1)}, u32[]{:S(2)}, u32[]{:S(2)}) collective-permute-start(bf16[1024,128]{1,0:T(8,128)(2,1)S(1)} %collective-permute-done.1.refs_7_), channel_id=1, source_target_pairs={{0,8},{8,16},{16,24},{24,32},{32,40},{40,48},{48,56},{56,0},{1,9},... | collective-permute-start | bytes 786440 | tf_op jit(solution)/shard_map/ppermute | solution.py:27
  22.1 6.9 %collective-permute-start.6 = (bf16[1024,128]{1,0:T(8,128)(2,1)S(1)}, bf16[1024,128]{1,0:T(8,128)(2,1)S(1)}, u32[]{:S(2)}, u32[]{:S(2)}) collective-permute-start(bf16[1024,128]{1,0:T(8,128)(2,1)S(1)} %collective-permute-done.2.refs_1_), channel_id=1, source_target_pairs={{0,56},{8,0},{16,8},{24,16},{32,24},{40,32},{48,40},{56,48},{1,57}... | collective-permute-start | bytes 786440 | tf_op jit(solution)/shard_map/ppermute | solution.py:27
  29.0 10.2 %collective-permute-start.13 = (bf16[1280,128]{1,0:T(8,128)(2,1)}, bf16[1280,128]{1,0:T(8,128)(2,1)S(1)}, u32[]{:S(2)}, u32[]{:S(2)}) collective-permute-start(bf16[1280,128]{1,0:T(8,128)(2,1)} %get-tuple-element.71), channel_id=1, source_target_pairs={{64,66},{65,67},{66,64},{67,65},{68,70},{69,71},{70,68},{71,69},{1... | collective-permute-start | bytes 983048 | tf_op jit(solution)/shard_map/ppermute | solution.py:75
  29.7 14.4 %collective-permute-start.10 = (bf16[1280,128]{1,0:T(8,128)(2,1)}, bf16[1280,128]{1,0:T(8,128)(2,1)S(1)}, u32[]{:S(2)}, u32[]{:S(2)}) collective-permute-start(bf16[1280,128]{1,0:T(8,128)(2,1)} %get-tuple-element.65), channel_id=1, source_target_pairs={{0,6},{1,7},{2,4},{3,5},{4,2},{5,3},{6,0},{7,1},{64,199},{65,196},... | collective-permute-start | bytes 983048 | tf_op jit(solution)/shard_map/ppermute | solution.py:75
  32.9 11.2 %collective-permute-start.12 = (bf16[1280,128]{1,0:T(8,128)(2,1)}, bf16[1280,128]{1,0:T(8,128)(2,1)S(1)}, u32[]{:S(2)}, u32[]{:S(2)}) collective-permute-start(bf16[1280,128]{1,0:T(8,128)(2,1)} %get-tuple-element.69), channel_id=1, source_target_pairs={{0,1},{1,2},{2,3},{3,0},{4,5},{5,6},{6,7},{7,4},{64,67},{65,64},{6... | collective-permute-start | bytes 983048 | tf_op jit(solution)/shard_map/ppermute | solution.py:75
  37.2 6.9 %collective-permute-start.8 = (bf16[1024,128]{1,0:T(8,128)(2,1)S(1)}, bf16[1024,128]{1,0:T(8,128)(2,1)S(1)}, u32[]{:S(2)}, u32[]{:S(2)}) collective-permute-start(bf16[1024,128]{1,0:T(8,128)(2,1)S(1)} %collective-permute-done.5.refs_6_), channel_id=1, source_target_pairs={{0,8},{8,16},{16,24},{24,32},{32,40},{40,48},{48,56},{56,0},{1,9},... | collective-permute-start | bytes 786440 | tf_op jit(solution)/shard_map/ppermute | solution.py:27
  44.2 18.1 %collective-permute-start.14 = (bf16[4,1280,128]{2,1,0:T(8,128)(2,1)S(1)}, bf16[4,1280,128]{2,1,0:T(8,128)(2,1)S(1)}, u32[]{:S(2)}, u32[]{:S(2)}) collective-permute-start(bf16[4,1280,128]{2,1,0:T(8,128)(2,1)S(1)} %stack.13), channel_id=1, source_target_pairs={{0,64},{64,0},{1,65},{65,1},{2,66},{66,2},{3,67},{67,3},{4,68},{68... | collective-permute-start | bytes 3932168 | tf_op jit(solution)/shard_map/ppermute | solution.py:43
  50.4 8.9 %collective-permute-start.11 = (bf16[1024,128]{1,0:T(8,128)(2,1)S(1)}, bf16[1024,128]{1,0:T(8,128)(2,1)S(1)}, u32[]{:S(2)}, u32[]{:S(2)}) collective-permute-start(bf16[1024,128]{1,0:T(8,128)(2,1)S(1)} %collective-permute-done.8.refs_5_), channel_id=1, source_target_pairs={{0,8},{8,16},{16,24},{24,32},{32,40},{40,48},{48,56},{56,0},{1,9},... | collective-permute-start | bytes 786440 | tf_op jit(solution)/shard_map/ppermute | solution.py:27
  59.3 7.4 %collective-permute-start.16 = (f32[32,1024]{1,0:T(8,128)S(1)}, f32[32,1024]{1,0:T(8,128)S(1)}, u32[]{:S(2)}, u32[]{:S(2)}) collective-permute-start(f32[32,1024]{1,0:T(8,128)S(1)} %low_add.7.a_ref), channel_id=1, source_target_pairs={{0,2},{1,3},{2,0},{3,1},{4,6},{5,7},{6,4},{7,5},{8,10},{9,11},{10,... | collective-permute-start | bytes 393224 | tf_op jit(solution)/shard_map/ppermute | solution.py:35
  63.7 7.0 %collective-permute-start.18 = (bf16[512,128]{1,0:T(8,128)(2,1)S(1)}, bf16[512,128]{1,0:T(8,128)(2,1)S(1)}, u32[]{:S(2)}, u32[]{:S(2)}) collective-permute-start(bf16[512,128]{1,0:T(8,128)(2,1)S(1)} %get-tuple-element.79), channel_id=1, source_target_pairs={{0,2},{1,3},{2,0},{3,1},{4,6},{5,7},{6,4},{7,5},{8,10},{9,11},{10,... | collective-permute-start | bytes 393224 | tf_op jit(solution)/shard_map/ppermute | solution.py:51
  72.4 12.3 %collective-permute-start.21 = (bf16[2048,128]{1,0:T(8,128)(2,1)S(1)}, bf16[2048,128]{1,0:T(8,128)(2,1)S(1)}, u32[]{:S(2)}, u32[]{:S(2)}) collective-permute-start(bf16[2048,128]{1,0:T(8,128)(2,1)S(1)} %get-tuple-element.84), channel_id=1, source_target_pairs={{0,4},{4,0},{1,5},{5,1},{2,6},{6,2},{3,7},{7,3},{8,12},{12,8},{9,1... | collective-permute-start | bytes 1572872 | tf_op jit(solution)/shard_map/ppermute | solution.py:39
  74.0 15.9 %collective-permute-start.26 = (bf16[1280,128]{1,0:T(8,128)(2,1)S(1)}, bf16[1280,128]{1,0:T(8,128)(2,1)S(1)}, u32[]{:S(2)}, u32[]{:S(2)}) collective-permute-start(bf16[1280,128]{1,0:T(8,128)(2,1)S(1)} %get-tuple-element.94), channel_id=1, source_target_pairs={{0,2},{1,3},{2,0},{3,1},{4,6},{5,7},{6,4},{7,5},{8,10},{9,11},{10,... | collective-permute-start | bytes 983048 | tf_op jit(solution)/shard_map/ppermute | solution.py:51
  77.0 12.9 %collective-permute-start.27 = (bf16[1280,128]{1,0:T(8,128)(2,1)S(1)}, bf16[1280,128]{1,0:T(8,128)(2,1)S(1)}, u32[]{:S(2)}, u32[]{:S(2)}) collective-permute-start(bf16[1280,128]{1,0:T(8,128)(2,1)S(1)} %get-tuple-element.95), channel_id=1, source_target_pairs={{0,1},{1,2},{2,3},{3,0},{4,5},{5,6},{6,7},{7,4},{8,9},{9,10},{10,1... | collective-permute-start | bytes 983048 | tf_op jit(solution)/shard_map/ppermute | solution.py:51
  78.5 16.5 %collective-permute-start.28 = (bf16[1280,128]{1,0:T(8,128)(2,1)S(1)}, bf16[1280,128]{1,0:T(8,128)(2,1)S(1)}, u32[]{:S(2)}, u32[]{:S(2)}) collective-permute-start(bf16[1280,128]{1,0:T(8,128)(2,1)S(1)} %get-tuple-element.96), channel_id=1, source_target_pairs={{0,3},{1,0},{2,1},{3,2},{4,7},{5,4},{6,5},{7,6},{8,11},{9,8},{10,9... | collective-permute-start | bytes 983048 | tf_op jit(solution)/shard_map/ppermute | solution.py:51
  85.0 21.0 %collective-permute-start.22 = (bf16[896,128]{1,0:T(8,128)(2,1)S(1)}, bf16[896,128]{1,0:T(8,128)(2,1)S(1)}, u32[]{:S(2)}, u32[]{:S(2)}) collective-permute-start(bf16[896,128]{1,0:T(8,128)(2,1)S(1)} %get-tuple-element.87), channel_id=1, source_target_pairs={{0,1},{1,2},{2,3},{3,0},{4,5},{5,6},{6,7},{7,4},{8,9},{9,10},{10,1... | collective-permute-start | bytes 688136 | tf_op jit(solution)/shard_map/ppermute | solution.py:51
  86.5 19.4 %collective-permute-start.23 = (bf16[896,128]{1,0:T(8,128)(2,1)S(1)}, bf16[896,128]{1,0:T(8,128)(2,1)S(1)}, u32[]{:S(2)}, u32[]{:S(2)}) collective-permute-start(bf16[896,128]{1,0:T(8,128)(2,1)S(1)} %get-tuple-element.88), channel_id=1, source_target_pairs={{0,2},{1,3},{2,0},{3,1},{4,6},{5,7},{6,4},{7,5},{8,10},{9,11},{10,... | collective-permute-start | bytes 688136 | tf_op jit(solution)/shard_map/ppermute | solution.py:51
  89.9 16.1 %collective-permute-start.24 = (bf16[896,128]{1,0:T(8,128)(2,1)S(1)}, bf16[896,128]{1,0:T(8,128)(2,1)S(1)}, u32[]{:S(2)}, u32[]{:S(2)}) collective-permute-start(bf16[896,128]{1,0:T(8,128)(2,1)S(1)} %get-tuple-element.89), channel_id=1, source_target_pairs={{0,3},{1,0},{2,1},{3,2},{4,7},{5,4},{6,5},{7,6},{8,11},{9,8},{10,9... | collective-permute-start | bytes 688136 | tf_op jit(solution)/shard_map/ppermute | solution.py:51
  95.2 10.7 %collective-permute-start.29 = (bf16[640,128]{1,0:T(8,128)(2,1)S(1)}, bf16[640,128]{1,0:T(8,128)(2,1)S(1)}, u32[]{:S(2)}, u32[]{:S(2)}) collective-permute-start(bf16[640,128]{1,0:T(8,128)(2,1)S(1)} %get-tuple-element.98), channel_id=1, source_target_pairs={{0,4},{4,0},{1,5},{5,1},{2,6},{6,2},{3,7},{7,3},{8,12},{12,8},{9,1... | collective-permute-start | bytes 491528 | tf_op jit(solution)/shard_map/ppermute | solution.py:39
  97.1 8.2 %collective-permute-start.30 = (bf16[32,1024]{1,0:T(8,128)(2,1)S(1)}, bf16[32,1024]{1,0:T(8,128)(2,1)S(1)}, u32[]{:S(2)}, u32[]{:S(2)}) collective-permute-start(bf16[32,1024]{1,0:T(8,128)(2,1)S(1)} %get-tuple-element.92), channel_id=1, source_target_pairs={{0,32},{8,40},{16,48},{24,56},{32,0},{40,8},{48,16},{56,24},{1,33}... | collective-permute-start | bytes 196616 | tf_op jit(solution)/shard_map/ppermute | solution.py:31
  (11 other events, 145.0 us)

commit v7 on v6

--- a/solution.py
+++ b/solution.py
@@ -328,6 +328,7 @@
     )
     twin = xh_swap(maps)
     cosines, sines = call(rope_kernel, "rope", [of((rows, HEAD_SIZE), f32)] * 2, request_start, scalars=1)
+    hidden = after(hidden, sends[0])
     ring = [(hidden, hidden)]
 
     def ring_step(*others):
@@ -346,15 +347,15 @@
 
     ring_step()
     mine = [weight_send(sends[0], 0), weight_send(after(sends[1], *ring[1]), 1)]
-    ring_step(sends[1])
+    ring_step()
     near = jnp.stack([maps, after(twin, *ring[1])])
     far = core_swap(near)
-    mine += [weight_send(after(sends[k], *ring[2]), k) for k in (2, 3)]
-    low = call(low_kernel, "low", of((RANK, rows), f32), adapters, hidden, near, far, scalars=1)
-    ring_step(mine[0], low, cosines)
+    mine += [weight_send(after(sends[k], *ring[2], mine[k - 2]), k) for k in (2, 3)]
+    ring_step(near)
+    low = call(low_kernel, "low", of((RANK, rows), f32), adapters, hidden, near, after(far, *ring[2]), scalars=1)
+    ring_step(low)
     (low,) = added(low, x_swap(low), *ring[3])
-    ring_step(mine[1])
-    mine[3] = after(mine[3], *ring[3])
+    mine[3] = after(mine[3], *ring[3], cosines)
     other = core_swap(call(stack_kernel, "stack", of((4, 1280, 128), bf16), *mine))
     hidden = after(hidden, low)
     (low,) = added(low, y_xor(low, 1), ring[4][0])
@@ -403,14 +404,14 @@
     )
     a_got = {dy: y_shift(a_sends[dy - 1], dy) for dy in (2, 1, 3)}
     low, narrow = added(low, z_xor(low, 2), x_got, also=(bf16,))
+    _, low = added(low, z_xor(narrow, 4), also=(bf16,))
     b_own, b_send = call(
         stage_b_kernel,
         "stage_b",
         [of((TB, 128), f32), of((TB, 128), bf16)],
-        after(b_parts[0], narrow),
+        after(b_parts[0], low),
         *b_got,
     )
-    _, low = added(low, z_xor(narrow, 4), also=(bf16,))
     b_last = x_swap(b_send)
 
     return call(

time: 112 us -> 110 us (0.982)
  the two profiles are of different devices: /device:TPU:90 before, /device:TPU:2 now
where the time goes in v7:
time: 110 us
  starting transfers between devices  48.5 us (44%)
  waiting for transfers between devices  43.7 us (40%)
  Pallas kernels  16.2 us (15%)
    pallas_call x16, Pallas kernels, call(): pl.pallas_call(kernel, out_shape=outs, in_specs=[SMEM] * scalars + [pl.Bl...  16.2 us
    ppermute x9, starting transfers between devices, y_shift(): return lax.ppermute(v, 'y', [(i, (i + s) % NY) for i in range(NY)])  15.8 us
    ppermute x7, waiting for transfers between devices, z_shift(): return lax.ppermute(v, 'z', [(i, (i + s) % NZ) for i in range(NZ)])  12.6 us
    ppermute x7, starting transfers between devices, z_shift(): return lax.ppermute(v, 'z', [(i, (i + s) % NZ) for i in range(NZ)])  11.5 us
    ppermute x3, waiting for transfers between devices, x_swap(): return lax.ppermute(v, 'xl', [(0, 1), (1, 0)])  8.31 us
    ppermute x1, waiting for transfers between devices, xh_swap(): return lax.ppermute(v, 'xh', [(0, 1), (1, 0)])  7.76 us
    ppermute x3, starting transfers between devices, z_xor(): return lax.ppermute(v, 'z', [(i, i ^ s) for i in range(NZ)])  6.2 us
    ppermute x3, waiting for transfers between devices, z_xor(): return lax.ppermute(v, 'z', [(i, i ^ s) for i in range(NZ)])  5.7 us
  transfers between devices with their start and end apart: 31, of which 12 were waited for; matrix products, arithmetic and copies ran while one was open for 1% of the time, Pallas kernels for 6%

profile of v7, /device:TPU:2, one launch (start us, length us, event | category | flops | bytes accessed | tf_op | source)
XLA Modules:
  0.0 109.6 jit_solution(11834345343972706115)
XLA Ops:
  0.0 3.5 %pack.1 = (bf16[1280,128]{1,0:T(8,128)(2,1)}, bf16[1280,128]{1,0:T(8,128)(2,1)}, bf16[1280,128]{1,0:T(8,128)(2,1)}, bf16[1280,128]{1,0:T(8,128)(2,1)}, bf16[1280...) custom-call(bf16[8192,128]{1,0:T(8,128)(2,1)} %wq_ref.1, bf16[32,8192]{1,0:T(8,128)(2,1)} %bitcast.4, ...), custom_call_target="tpu_custom_call" | custom-call | tf_op jit(solution)/shard_map/pack/pallas_call | solution.py:298
  3.5 2.0 %collective-permute-start.1 = (bf16[1024,128]{1,0:T(8,128)(2,1)S(1)}, bf16[1024,128]{1,0:T(8,128)(2,1)S(1)}, u32[]{:S(2)}, u32[]{:S(2)}) collective-permute-start(bf16[1024,128]{1,0:T(8,128)(2,1)S(1)} %copy-done.1), channel_id=1, source_target_pairs={{0,8},{8,16},{16,24},{24,32},{32,40},{40,48},{48,56},{56,0},{1,9},... | collective-permute-start | bytes 786440 | tf_op jit(solution)/shard_map/ppermute | solution.py:27
  5.5 4.0 %collective-permute-start.2 = (bf16[1024,128]{1,0:T(8,128)(2,1)S(1)}, bf16[1024,128]{1,0:T(8,128)(2,1)S(1)}, u32[]{:S(2)}, u32[]{:S(2)}) collective-permute-start(bf16[1024,128]{1,0:T(8,128)(2,1)S(1)} %copy-done.1), channel_id=1, source_target_pairs={{0,56},{8,0},{16,8},{24,16},{32,24},{40,32},{48,40},{56,48},{1,57}... | collective-permute-start | bytes 786440 | tf_op jit(solution)/shard_map/ppermute | solution.py:27
  10.1 5.7 %collective-permute-done.1.refs_7_ = bf16[1024,128]{1,0:T(8,128)(2,1)S(1)} collective-permute-done((bf16[1024,128]{1,0:T(8,128)(2,1)S(1)}, bf16[1024,128]{1,0:T(8,128)(2,1)S(1)}, u32[]{:S(2)}, u32[]{:S(2)}) %collective-permute-start.1) | collective-permute-done | bytes 262176 | tf_op jit(solution)/shard_map/ppermute | solution.py:27
  15.8 3.2 %collective-permute-start.11 = (bf16[1280,128]{1,0:T(8,128)(2,1)}, bf16[1280,128]{1,0:T(8,128)(2,1)S(1)}, u32[]{:S(2)}, u32[]{:S(2)}) collective-permute-start(bf16[1280,128]{1,0:T(8,128)(2,1)} %get-tuple-element.70), channel_id=1, source_target_pairs={{0,6},{1,7},{2,4},{3,5},{4,2},{5,3},{6,0},{7,1},{64,199},{65,196},... | collective-permute-start | bytes 983048 | tf_op jit(solution)/shard_map/ppermute | solution.py:75
  18.9 2.4 %collective-permute-start = (bf16[16,64,128]{2,1,0:T(8,128)(2,1)}, bf16[16,64,128]{2,1,0:T(8,128)(2,1)S(1)}, u32[]{:S(2)}, u32[]{:S(2)}) collective-permute-start(bf16[16,64,128]{2,1,0:T(8,128)(2,1)} %get-tuple-element.58), channel_id=1, source_target_pairs={{0,128},{128,0},{1,129},{129,1},{2,130},{130,2},{3,131},{131,3},{4... | collective-permute-start | bytes 786440 | tf_op jit(solution)/shard_map/ppermute | solution.py:47
  21.4 3.0 %collective-permute-start.5 = (bf16[1024,128]{1,0:T(8,128)(2,1)S(1)}, bf16[1024,128]{1,0:T(8,128)(2,1)S(1)}, u32[]{:S(2)}, u32[]{:S(2)}) collective-permute-start(bf16[1024,128]{1,0:T(8,128)(2,1)S(1)} %collective-permute-done.2.refs_1_), channel_id=1, source_target_pairs={{0,56},{8,0},{16,8},{24,16},{32,24},{40,32},{48,40},{56,48},{1,57}... | collective-permute-start | bytes 786440 | tf_op jit(solution)/shard_map/ppermute | solution.py:27
  24.4 7.8 %collective-permute-done = bf16[16,64,128]{2,1,0:T(8,128)(2,1)S(1)} collective-permute-done((bf16[16,64,128]{2,1,0:T(8,128)(2,1)}, bf16[16,64,128]{2,1,0:T(8,128)(2,1)S(1)}, u32[]{:S(2)}, u32[]{:S(2)}) %collective-permute-start) | collective-permute-done | bytes 262176 | tf_op jit(solution)/shard_map/ppermute | solution.py:47
  34.3 2.4 %collective-permute-start.8 = (bf16[1024,128]{1,0:T(8,128)(2,1)S(1)}, bf16[1024,128]{1,0:T(8,128)(2,1)S(1)}, u32[]{:S(2)}, u32[]{:S(2)}) collective-permute-start(bf16[1024,128]{1,0:T(8,128)(2,1)S(1)} %collective-permute-done.5.refs_2_), channel_id=1, source_target_pairs={{0,56},{8,0},{16,8},{24,16},{32,24},{40,32},{48,40},{56,48},{1,57}... | collective-permute-start | bytes 786440 | tf_op jit(solution)/shard_map/ppermute | solution.py:27
  37.8 3.0 %collective-permute-done.8.refs_3_ = bf16[1024,128]{1,0:T(8,128)(2,1)S(1)} collective-permute-done((bf16[1024,128]{1,0:T(8,128)(2,1)S(1)}, bf16[1024,128]{1,0:T(8,128)(2,1)S(1)}, u32[]{:S(2)}, u32[]{:S(2)}) %collective-permute-start.8) | collective-permute-done | bytes 262176 | tf_op jit(solution)/shard_map/ppermute | solution.py:27
  40.8 3.5 %collective-permute-done.7.refs_5_ = bf16[1024,128]{1,0:T(8,128)(2,1)S(1)} collective-permute-done((bf16[1024,128]{1,0:T(8,128)(2,1)S(1)}, bf16[1024,128]{1,0:T(8,128)(2,1)S(1)}, u32[]{:S(2)}, u32[]{:S(2)}) %collective-permute-start.7) | collective-permute-done | bytes 262176 | tf_op jit(solution)/shard_map/ppermute | solution.py:27
  45.0 3.3 %collective-permute-done.3.far_ref.refs_9_ = bf16[2,16,64,128]{3,2,1,0:T(8,128)(2,1)S(1)} collective-permute-done((bf16[2,16,64,128]{3,2,1,0:T(8,128)(2,1)S(1)}, bf16[2,16,64,128]{3,2,1,0:T(8,128)(2,1)S(1)}, u32[]{:S(2)}, u32[]{:S(2)}) %collective-permute-start.3) | collective-permute-done | bytes 524320 | tf_op jit(solution)/shard_map/ppermute | solution.py:43
  49.1 3.1 %collective-permute-start.6 = (f32[32,1024]{1,0:T(8,128)S(1)}, f32[32,1024]{1,0:T(8,128)S(1)}, u32[]{:S(2)}, u32[]{:S(2)}) collective-permute-start(f32[32,1024]{1,0:T(8,128)S(1)} %low.1.a_ref), channel_id=1, source_target_pairs={{0,4},{4,0},{1,5},{5,1},{2,6},{6,2},{3,7},{7,3},{8,12},{12,8},{9,1... | collective-permute-start | bytes 393224 | tf_op jit(solution)/shard_map/ppermute | solution.py:39
  52.2 3.8 %collective-permute-done.6.b_ref = f32[32,1024]{1,0:T(8,128)S(1)} collective-permute-done((f32[32,1024]{1,0:T(8,128)S(1)}, f32[32,1024]{1,0:T(8,128)S(1)}, u32[]{:S(2)}, u32[]{:S(2)}) %collective-permute-start.6) | collective-permute-done | bytes 131104 | tf_op jit(solution)/shard_map/ppermute | solution.py:39
  56.1 5.0 %collective-permute-done.15.b_ref = f32[32,1024]{1,0:T(8,128)S(1)} collective-permute-done((f32[32,1024]{1,0:T(8,128)S(1)}, f32[32,1024]{1,0:T(8,128)S(1)}, u32[]{:S(2)}, u32[]{:S(2)}) %collective-permute-start.15) | collective-permute-done | bytes 131104 | tf_op jit(solution)/shard_map/ppermute | solution.py:35
  64.6 2.2 %collective-permute-start.18 = (bf16[512,128]{1,0:T(8,128)(2,1)S(1)}, bf16[512,128]{1,0:T(8,128)(2,1)S(1)}, u32[]{:S(2)}, u32[]{:S(2)}) collective-permute-start(bf16[512,128]{1,0:T(8,128)(2,1)S(1)} %get-tuple-element.83), channel_id=1, source_target_pairs={{0,2},{1,3},{2,0},{3,1},{4,6},{5,7},{6,4},{7,5},{8,10},{9,11},{10,... | collective-permute-start | bytes 393224 | tf_op jit(solution)/shard_map/ppermute | solution.py:51
  66.8 3.2 %collective-permute-start.20 = (bf16[512,128]{1,0:T(8,128)(2,1)S(1)}, bf16[512,128]{1,0:T(8,128)(2,1)S(1)}, u32[]{:S(2)}, u32[]{:S(2)}) collective-permute-start(bf16[512,128]{1,0:T(8,128)(2,1)S(1)} %get-tuple-element.85), channel_id=1, source_target_pairs={{0,3},{1,0},{2,1},{3,2},{4,7},{5,4},{6,5},{7,6},{8,11},{9,8},{10,9... | collective-permute-start | bytes 393224 | tf_op jit(solution)/shard_map/ppermute | solution.py:51
  70.0 2.7 %q_product.1 = (bf16[1536,128]{1,0:T(8,128)(2,1)S(1)}, bf16[1536,128]{1,0:T(8,128)(2,1)S(1)}, bf16[1280,128]{1,0:T(8,128)(2,1)S(1)}, bf16[1280,128]{1,0:T(8,128)...) custom-call(bf16[1024,1024]{1,0:T(8,128)(2,1)S(1)} %get-tuple-element.79.hbuf, ...), custom_call_target="tpu_custom_call" | custom-call | tf_op jit(solution)/shard_map/q_product/pallas_call | solution.py:298
  80.3 1.9 %collective-permute-start.25 = (f32[32,1024]{1,0:T(8,128)S(1)}, f32[32,1024]{1,0:T(8,128)S(1)}, u32[]{:S(2)}, u32[]{:S(2)}) collective-permute-start(f32[32,1024]{1,0:T(8,128)S(1)} %low_add.9.a_ref), channel_id=1, source_target_pairs={{0,16},{8,24},{16,0},{24,8},{32,48},{40,56},{48,32},{56,40},{1,17}... | collective-permute-start | bytes 393224 | tf_op jit(solution)/shard_map/ppermute | solution.py:31
  82.2 5.5 %collective-permute-done.25.b_ref = f32[32,1024]{1,0:T(8,128)S(1)} collective-permute-done((f32[32,1024]{1,0:T(8,128)S(1)}, f32[32,1024]{1,0:T(8,128)S(1)}, u32[]{:S(2)}, u32[]{:S(2)}) %collective-permute-start.25) | collective-permute-done | bytes 131104 | tf_op jit(solution)/shard_map/ppermute | solution.py:31
  87.7 4.3 %collective-permute-start.26 = (bf16[32,1024]{1,0:T(8,128)(2,1)S(1)}, bf16[32,1024]{1,0:T(8,128)(2,1)S(1)}, u32[]{:S(2)}, u32[]{:S(2)}) collective-permute-start(bf16[32,1024]{1,0:T(8,128)(2,1)S(1)} %get-tuple-element.97), channel_id=1, source_target_pairs={{0,32},{8,40},{16,48},{24,56},{32,0},{40,8},{48,16},{56,24},{1,33}... | collective-permute-start | bytes 196616 | tf_op jit(solution)/shard_map/ppermute | solution.py:31
  92.3 4.4 %collective-permute-start.23 = (bf16[896,128]{1,0:T(8,128)(2,1)S(1)}, bf16[896,128]{1,0:T(8,128)(2,1)S(1)}, u32[]{:S(2)}, u32[]{:S(2)}) collective-permute-start(bf16[896,128]{1,0:T(8,128)(2,1)S(1)} %get-tuple-element.92), channel_id=1, source_target_pairs={{0,2},{1,3},{2,0},{3,1},{4,6},{5,7},{6,4},{7,5},{8,10},{9,11},{10,... | collective-permute-start | bytes 688136 | tf_op jit(solution)/shard_map/ppermute | solution.py:51
  99.5 4.5 %collective-permute-done.30.refs_5_ = bf16[640,128]{1,0:T(8,128)(2,1)S(1)} collective-permute-done((bf16[640,128]{1,0:T(8,128)(2,1)S(1)}, bf16[640,128]{1,0:T(8,128)(2,1)S(1)}, u32[]{:S(2)}, u32[]{:S(2)}) %collective-permute-start.30) | collective-permute-done | bytes 163872 | tf_op jit(solution)/shard_map/ppermute | solution.py:39
  104.0 5.6 %attention.1 = bf16[1024,128]{1,0:T(8,128)(2,1)} custom-call(s32[8]{0:T(128)S(1)} %copy-done.3, s32[1024]{0:T(1024)S(1)} %copy-done.2, f32[384,128]{1,0:T(8,128)S(1)} %get-tuple-element.90.refs_0_, bf16[896,128]{1,0:T(8,128)(2,1)S(1)} %collective-permute-done.22.refs_1_, bf16[896,128]{1,0:T(8,128)(2,1)S(1)} %collective-permute-done.23.refs_2_, ...), custom_call_target="tpu_custom_call" | custom-call | tf_op jit(solution)/shard_map/attention/pallas_call | solution.py:298
  (63 shorter events, 19.5 us)
Async XLA Ops:
  3.5 12.2 %collective-permute-start.1 = (bf16[1024,128]{1,0:T(8,128)(2,1)S(1)}, bf16[1024,128]{1,0:T(8,128)(2,1)S(1)}, u32[]{:S(2)}, u32[]{:S(2)}) collective-permute-start(bf16[1024,128]{1,0:T(8,128)(2,1)S(1)} %copy-done.1), channel_id=1, source_target_pairs={{0,8},{8,16},{16,24},{24,32},{32,40},{40,48},{48,56},{56,0},{1,9},... | collective-permute-start | bytes 786440 | tf_op jit(solution)/shard_map/ppermute | solution.py:27
  5.5 10.2 %collective-permute-start.2 = (bf16[1024,128]{1,0:T(8,128)(2,1)S(1)}, bf16[1024,128]{1,0:T(8,128)(2,1)S(1)}, u32[]{:S(2)}, u32[]{:S(2)}) collective-permute-start(bf16[1024,128]{1,0:T(8,128)(2,1)S(1)} %copy-done.1), channel_id=1, source_target_pairs={{0,56},{8,0},{16,8},{24,16},{32,24},{40,32},{48,40},{56,48},{1,57}... | collective-permute-start | bytes 786440 | tf_op jit(solution)/shard_map/ppermute | solution.py:27
  9.5 22.6 %collective-permute-start.10 = (bf16[1280,128]{1,0:T(8,128)(2,1)}, bf16[1280,128]{1,0:T(8,128)(2,1)S(1)}, u32[]{:S(2)}, u32[]{:S(2)}) collective-permute-start(bf16[1280,128]{1,0:T(8,128)(2,1)} %get-tuple-element.56), channel_id=1, source_target_pairs={{0,4},{1,5},{2,6},{3,7},{4,0},{5,1},{6,2},{7,3},{64,197},{65,198},... | collective-permute-start | bytes 983048 | tf_op jit(solution)/shard_map/ppermute | solution.py:75
  15.8 16.9 %collective-permute-start.11 = (bf16[1280,128]{1,0:T(8,128)(2,1)}, bf16[1280,128]{1,0:T(8,128)(2,1)S(1)}, u32[]{:S(2)}, u32[]{:S(2)}) collective-permute-start(bf16[1280,128]{1,0:T(8,128)(2,1)} %get-tuple-element.70), channel_id=1, source_target_pairs={{0,6},{1,7},{2,4},{3,5},{4,2},{5,3},{6,0},{7,1},{64,199},{65,196},... | collective-permute-start | bytes 983048 | tf_op jit(solution)/shard_map/ppermute | solution.py:75
  18.9 13.2 %collective-permute-start = (bf16[16,64,128]{2,1,0:T(8,128)(2,1)}, bf16[16,64,128]{2,1,0:T(8,128)(2,1)S(1)}, u32[]{:S(2)}, u32[]{:S(2)}) collective-permute-start(bf16[16,64,128]{2,1,0:T(8,128)(2,1)} %get-tuple-element.58), channel_id=1, source_target_pairs={{0,128},{128,0},{1,129},{129,1},{2,130},{130,2},{3,131},{131,3},{4... | collective-permute-start | bytes 786440 | tf_op jit(solution)/shard_map/ppermute | solution.py:47
  21.4 10.8 %collective-permute-start.5 = (bf16[1024,128]{1,0:T(8,128)(2,1)S(1)}, bf16[1024,128]{1,0:T(8,128)(2,1)S(1)}, u32[]{:S(2)}, u32[]{:S(2)}) collective-permute-start(bf16[1024,128]{1,0:T(8,128)(2,1)S(1)} %collective-permute-done.2.refs_1_), channel_id=1, source_target_pairs={{0,56},{8,0},{16,8},{24,16},{32,24},{40,32},{48,40},{56,48},{1,57}... | collective-permute-start | bytes 786440 | tf_op jit(solution)/shard_map/ppermute | solution.py:27
  24.4 7.8 %collective-permute-start.4 = (bf16[1024,128]{1,0:T(8,128)(2,1)S(1)}, bf16[1024,128]{1,0:T(8,128)(2,1)S(1)}, u32[]{:S(2)}, u32[]{:S(2)}) collective-permute-start(bf16[1024,128]{1,0:T(8,128)(2,1)S(1)} %collective-permute-done.1.refs_7_), channel_id=1, source_target_pairs={{0,8},{8,16},{16,24},{24,32},{32,40},{40,48},{48,56},{56,0},{1,9},... | collective-permute-start | bytes 786440 | tf_op jit(solution)/shard_map/ppermute | solution.py:27
  32.2 12.2 %collective-permute-start.12 = (bf16[1280,128]{1,0:T(8,128)(2,1)}, bf16[1280,128]{1,0:T(8,128)(2,1)S(1)}, u32[]{:S(2)}, u32[]{:S(2)}) collective-permute-start(bf16[1280,128]{1,0:T(8,128)(2,1)} %get-tuple-element.72), channel_id=1, source_target_pairs={{0,1},{1,2},{2,3},{3,0},{4,5},{5,6},{6,7},{7,4},{64,67},{65,64},{6... | collective-permute-start | bytes 983048 | tf_op jit(solution)/shard_map/ppermute | solution.py:75
  32.7 11.7 %collective-permute-start.13 = (bf16[1280,128]{1,0:T(8,128)(2,1)}, bf16[1280,128]{1,0:T(8,128)(2,1)S(1)}, u32[]{:S(2)}, u32[]{:S(2)}) collective-permute-start(bf16[1280,128]{1,0:T(8,128)(2,1)} %get-tuple-element.74), channel_id=1, source_target_pairs={{64,66},{65,67},{66,64},{67,65},{68,70},{69,71},{70,68},{71,69},{1... | collective-permute-start | bytes 983048 | tf_op jit(solution)/shard_map/ppermute | solution.py:75
  36.7 7.6 %collective-permute-start.7 = (bf16[1024,128]{1,0:T(8,128)(2,1)S(1)}, bf16[1024,128]{1,0:T(8,128)(2,1)S(1)}, u32[]{:S(2)}, u32[]{:S(2)}) collective-permute-start(bf16[1024,128]{1,0:T(8,128)(2,1)S(1)} %collective-permute-done.4.refs_6_), channel_id=1, source_target_pairs={{0,8},{8,16},{16,24},{24,32},{32,40},{40,48},{48,56},{56,0},{1,9},... | collective-permute-start | bytes 786440 | tf_op jit(solution)/shard_map/ppermute | solution.py:27
  44.4 18.7 %collective-permute-start.14 = (bf16[4,1280,128]{2,1,0:T(8,128)(2,1)S(1)}, bf16[4,1280,128]{2,1,0:T(8,128)(2,1)S(1)}, u32[]{:S(2)}, u32[]{:S(2)}) collective-permute-start(bf16[4,1280,128]{2,1,0:T(8,128)(2,1)S(1)} %stack.13), channel_id=1, source_target_pairs={{0,64},{64,0},{1,65},{65,1},{2,66},{66,2},{3,67},{67,3},{4,68},{68... | collective-permute-start | bytes 3932168 | tf_op jit(solution)/shard_map/ppermute | solution.py:43
  52.2 9.3 %collective-permute-start.9 = (bf16[1024,128]{1,0:T(8,128)(2,1)S(1)}, bf16[1024,128]{1,0:T(8,128)(2,1)S(1)}, u32[]{:S(2)}, u32[]{:S(2)}) collective-permute-start(bf16[1024,128]{1,0:T(8,128)(2,1)S(1)} %collective-permute-done.7.refs_5_), channel_id=1, source_target_pairs={{0,8},{8,16},{16,24},{24,32},{32,40},{40,48},{48,56},{56,0},{1,9},... | collective-permute-start | bytes 786440 | tf_op jit(solution)/shard_map/ppermute | solution.py:27
  61.4 8.6 %collective-permute-start.16 = (f32[32,1024]{1,0:T(8,128)S(1)}, f32[32,1024]{1,0:T(8,128)S(1)}, u32[]{:S(2)}, u32[]{:S(2)}) collective-permute-start(f32[32,1024]{1,0:T(8,128)S(1)} %low_add.7.a_ref), channel_id=1, source_target_pairs={{0,2},{1,3},{2,0},{3,1},{4,6},{5,7},{6,4},{7,5},{8,10},{9,11},{10,... | collective-permute-start | bytes 393224 | tf_op jit(solution)/shard_map/ppermute | solution.py:35
  64.6 8.2 %collective-permute-start.18 = (bf16[512,128]{1,0:T(8,128)(2,1)S(1)}, bf16[512,128]{1,0:T(8,128)(2,1)S(1)}, u32[]{:S(2)}, u32[]{:S(2)}) collective-permute-start(bf16[512,128]{1,0:T(8,128)(2,1)S(1)} %get-tuple-element.83), channel_id=1, source_target_pairs={{0,2},{1,3},{2,0},{3,1},{4,6},{5,7},{6,4},{7,5},{8,10},{9,11},{10,... | collective-permute-start | bytes 393224 | tf_op jit(solution)/shard_map/ppermute | solution.py:51
  66.8 7.0 %collective-permute-start.19 = (bf16[512,128]{1,0:T(8,128)(2,1)S(1)}, bf16[512,128]{1,0:T(8,128)(2,1)S(1)}, u32[]{:S(2)}, u32[]{:S(2)}) collective-permute-start(bf16[512,128]{1,0:T(8,128)(2,1)S(1)} %get-tuple-element.84), channel_id=1, source_target_pairs={{0,1},{1,2},{2,3},{3,0},{4,5},{5,6},{6,7},{7,4},{8,9},{9,10},{10,1... | collective-permute-start | bytes 393224 | tf_op jit(solution)/shard_map/ppermute | solution.py:51
  73.9 13.8 %collective-permute-start.21 = (bf16[2048,128]{1,0:T(8,128)(2,1)S(1)}, bf16[2048,128]{1,0:T(8,128)(2,1)S(1)}, u32[]{:S(2)}, u32[]{:S(2)}) collective-permute-start(bf16[2048,128]{1,0:T(8,128)(2,1)S(1)} %get-tuple-element.88), channel_id=1, source_target_pairs={{0,4},{4,0},{1,5},{5,1},{2,6},{6,2},{3,7},{7,3},{8,12},{12,8},{9,1... | collective-permute-start | bytes 1572872 | tf_op jit(solution)/shard_map/ppermute | solution.py:39
  75.3 16.9 %collective-permute-start.27 = (bf16[1280,128]{1,0:T(8,128)(2,1)S(1)}, bf16[1280,128]{1,0:T(8,128)(2,1)S(1)}, u32[]{:S(2)}, u32[]{:S(2)}) collective-permute-start(bf16[1280,128]{1,0:T(8,128)(2,1)S(1)} %get-tuple-element.100), channel_id=1, source_target_pairs={{0,2},{1,3},{2,0},{3,1},{4,6},{5,7},{6,4},{7,5},{8,10},{9,11},{10,... | collective-permute-start | bytes 983048 | tf_op jit(solution)/shard_map/ppermute | solution.py:51
  76.8 21.6 %collective-permute-start.28 = (bf16[1280,128]{1,0:T(8,128)(2,1)S(1)}, bf16[1280,128]{1,0:T(8,128)(2,1)S(1)}, u32[]{:S(2)}, u32[]{:S(2)}) collective-permute-start(bf16[1280,128]{1,0:T(8,128)(2,1)S(1)} %get-tuple-element.101), channel_id=1, source_target_pairs={{0,1},{1,2},{2,3},{3,0},{4,5},{5,6},{6,7},{7,4},{8,9},{9,10},{10,1... | collective-permute-start | bytes 983048 | tf_op jit(solution)/shard_map/ppermute | solution.py:51
  78.6 19.9 %collective-permute-start.29 = (bf16[1280,128]{1,0:T(8,128)(2,1)S(1)}, bf16[1280,128]{1,0:T(8,128)(2,1)S(1)}, u32[]{:S(2)}, u32[]{:S(2)}) collective-permute-start(bf16[1280,128]{1,0:T(8,128)(2,1)S(1)} %get-tuple-element.102), channel_id=1, source_target_pairs={{0,3},{1,0},{2,1},{3,2},{4,7},{5,4},{6,5},{7,6},{8,11},{9,8},{10,9... | collective-permute-start | bytes 983048 | tf_op jit(solution)/shard_map/ppermute | solution.py:51
  80.3 7.4 %collective-permute-start.25 = (f32[32,1024]{1,0:T(8,128)S(1)}, f32[32,1024]{1,0:T(8,128)S(1)}, u32[]{:S(2)}, u32[]{:S(2)}) collective-permute-start(f32[32,1024]{1,0:T(8,128)S(1)} %low_add.9.a_ref), channel_id=1, source_target_pairs={{0,16},{8,24},{16,0},{24,8},{32,48},{40,56},{48,32},{56,40},{1,17}... | collective-permute-start | bytes 393224 | tf_op jit(solution)/shard_map/ppermute | solution.py:31
  87.7 9.0 %collective-permute-start.26 = (bf16[32,1024]{1,0:T(8,128)(2,1)S(1)}, bf16[32,1024]{1,0:T(8,128)(2,1)S(1)}, u32[]{:S(2)}, u32[]{:S(2)}) collective-permute-start(bf16[32,1024]{1,0:T(8,128)(2,1)S(1)} %get-tuple-element.97), channel_id=1, source_target_pairs={{0,32},{8,40},{16,48},{24,56},{32,0},{40,8},{48,16},{56,24},{1,33}... | collective-permute-start | bytes 196616 | tf_op jit(solution)/shard_map/ppermute | solution.py:31
  92.2 11.9 %collective-permute-start.22 = (bf16[896,128]{1,0:T(8,128)(2,1)S(1)}, bf16[896,128]{1,0:T(8,128)(2,1)S(1)}, u32[]{:S(2)}, u32[]{:S(2)}) collective-permute-start(bf16[896,128]{1,0:T(8,128)(2,1)S(1)} %get-tuple-element.91), channel_id=1, source_target_pairs={{0,1},{1,2},{2,3},{3,0},{4,5},{5,6},{6,7},{7,4},{8,9},{9,10},{10,1... | collective-permute-start | bytes 688136 | tf_op jit(solution)/shard_map/ppermute | solution.py:51
  92.3 11.8 %collective-permute-start.23 = (bf16[896,128]{1,0:T(8,128)(2,1)S(1)}, bf16[896,128]{1,0:T(8,128)(2,1)S(1)}, u32[]{:S(2)}, u32[]{:S(2)}) collective-permute-start(bf16[896,128]{1,0:T(8,128)(2,1)S(1)} %get-tuple-element.92), channel_id=1, source_target_pairs={{0,2},{1,3},{2,0},{3,1},{4,6},{5,7},{6,4},{7,5},{8,10},{9,11},{10,... | collective-permute-start | bytes 688136 | tf_op jit(solution)/shard_map/ppermute | solution.py:51
  96.7 7.4 %collective-permute-start.24 = (bf16[896,128]{1,0:T(8,128)(2,1)S(1)}, bf16[896,128]{1,0:T(8,128)(2,1)S(1)}, u32[]{:S(2)}, u32[]{:S(2)}) collective-permute-start(bf16[896,128]{1,0:T(8,128)(2,1)S(1)} %get-tuple-element.93), channel_id=1, source_target_pairs={{0,3},{1,0},{2,1},{3,2},{4,7},{5,4},{6,5},{7,6},{8,11},{9,8},{10,9... | collective-permute-start | bytes 688136 | tf_op jit(solution)/shard_map/ppermute | solution.py:51
  (11 other events, 143.4 us)

commit v8 on v5

--- a/solution.py
+++ b/solution.py
@@ -18,7 +18,7 @@
 TP_AXES = ("z", "xl", "y")
 NP = NX * NY
 TA, TB = 384, 640
-PACK_MIB = 4
+PACK_MIB = 56
 VMEM = pl.BlockSpec(memory_space=pltpu.VMEM)
 SMEM = pl.BlockSpec(memory_space=pltpu.SMEM)
 
@@ -83,19 +83,30 @@
         copy.wait()
 
 
-def pack_kernel(wq_ref, kv_ref, down_ref, up_ref, *refs):
-    outs, maps, sem = refs[:5], refs[5], refs[6]
-    z, xl, y, c = (lax.axis_index(a) for a in ("z", "xl", "y", "c"))
+def weight_pairs(wq_ref, kv_ref, out, d):
+    z, xl, y = (lax.axis_index(a) for a in ("z", "xl", "y"))
+    p = (xl ^ (d // NY)) * NY + ((y + d) & (NY - 1))
+    pairs = []
+    for j in range(NZ):
+        row = pl.multiple_of((((z + j) & (NZ - 1)) * NP + p) * 128, 128)
+        pairs.append((wq_ref.at[pl.ds(row, 128), :], out.at[j * 128 : (j + 1) * 128, :]))
+        pairs.append((kv_ref.at[:, pl.ds(row, 128)], out.at[1024 + j * 32 : 1056 + j * 32, :]))
+    return pairs
+
+
+def pack_first_kernel(wq_ref, kv_ref, down_ref, up_ref, out, maps, sem):
+    d = jnp.where(lax.axis_index("c") == 0, SERVED[0][0], SERVED[1][0])
     pairs = [(down_ref, maps.at[:, 0:RANK, :]), (up_ref, maps.at[:, RANK : 2 * RANK, :])]
-    for k in range(5):
-        d = 0
-        if k < 4:
-            d = jnp.where(c == 0, (SERVED[0] + (0,))[k], SERVED[1][k])
-        p = (xl ^ (d // NY)) * NY + ((y + d) & (NY - 1))
-        for j in range(NZ):
-            row = pl.multiple_of((((z + j) & (NZ - 1)) * NP + p) * 128, 128)
-            pairs.append((wq_ref.at[pl.ds(row, 128), :], outs[k].at[j * 128 : (j + 1) * 128, :]))
-            pairs.append((kv_ref.at[:, pl.ds(row, 128)], outs[k].at[1024 + j * 32 : 1056 + j * 32, :]))
+    run_copies(pairs + weight_pairs(wq_ref, kv_ref, out, d), sem)
+
+
+def pack_kernel(wq_ref, kv_ref, *refs):
+    outs, sem = refs[:4], refs[4]
+    c = lax.axis_index("c")
+    pairs = []
+    for k, out in enumerate(outs, 1):
+        d = jnp.where(c == 0, (SERVED[0] + (0,))[k], SERVED[1][k]) if k < 4 else 0
+        pairs += weight_pairs(wq_ref, kv_ref, out, d)
     run_copies(pairs, sem)
 
 
@@ -104,11 +115,8 @@
         refs[-1][i] = ref[...]
 
 
-def add_kernel(a_ref, b_ref, *outs):
-    total = a_ref[...] + b_ref[...].astype(jnp.float32)
-    outs[0][...] = total
-    for out in outs[1:]:
-        out[...] = total.astype(out.dtype)
+def add_kernel(a_ref, b_ref, out_ref):
+    out_ref[...] = a_ref[...] + b_ref[...]
 
 
 def rope_kernel(start_ref, cos_ref, sin_ref):
@@ -214,19 +222,20 @@
     return ref[rows, :].astype(jnp.float32)
 
 
-def kv_join_kernel(k0, k1, k2, k3, far_ref, sum_ref, send_ref):
+def kv_join_kernel(k0, k1, k2, k3, far_ref, sum_ref, low_ref, send_ref):
     total = wide(k0, ...) + wide(k1, ...) + wide(k2, ...) + wide(k3, ...)
-    sum_ref[...] = total
+    sum_ref[...] = total[0:512, :]
+    low_ref[...] = total[512:576, :]
     send_ref[0 : NY * TA, :] = far_ref[...]
-    send_ref[NY * TA :, :] = total.astype(jnp.bfloat16)
-
-
-def stage_a_kernel(near_ref, got_ref, kv_ref, own_ref, kv_out, *sends):
+    send_ref[NY * TA :, :] = total[0:512, :].astype(jnp.bfloat16)
+
+
+def stage_a_kernel(near_ref, got_ref, kv_ref, low_ref, own_ref, kv_out, *sends):
     for t in range(8):
         for dx in range(NX):
             a, b = t * 64 + dx * 32, NY * TA + t * 64 + (1 - dx) * 32
             kv_out[a : a + 32, :] = (kv_ref[a : a + 32, :] + wide(got_ref, slice(b, b + 32))).astype(jnp.bfloat16)
-    kv_out[512:576, :] = (kv_ref[512:576, :] + wide(got_ref, slice(NY * TA + 512, NY * TA + 576))).astype(jnp.bfloat16)
+    kv_out[512:576, :] = low_ref[...].astype(jnp.bfloat16)
     for dy in range(NY):
         rows = slice(dy * TA, (dy + 1) * TA)
         total = wide(near_ref, rows) + wide(got_ref, rows)
@@ -322,21 +331,33 @@
     rows = hidden.shape[0]
     bf16, f32 = jnp.bfloat16, jnp.float32
     of = jax.ShapeDtypeStruct
-    *sends, maps = call(
+    kv_rows = key_value_weight.T
+    first, maps = call(
+        pack_first_kernel,
+        "pack_first",
+        [of((1280, 128), bf16), of((down_maps.shape[0], 2 * RANK, 128), bf16)],
+        query_weight,
+        kv_rows,
+        jnp.transpose(down_maps, (0, 2, 1)),
+        up_maps,
+        scratch=[pltpu.SemaphoreType.DMA((2 * NZ + 2,))],
+        space=pltpu.HBM,
+        mib=PACK_MIB,
+    )
+    sends = call(
         pack_kernel,
         "pack",
-        [of((1280, 128), bf16)] * 5 + [of((down_maps.shape[0], 2 * RANK, 128), bf16)],
-        query_weight,
-        key_value_weight.T,
-        jnp.transpose(down_maps, (0, 2, 1)),
-        up_maps,
-        scratch=[pltpu.SemaphoreType.DMA((10 * NZ + 2,))],
+        [of((1280, 128), bf16)] * 4,
+        after(query_weight, first),
+        kv_rows,
+        scratch=[pltpu.SemaphoreType.DMA((8 * NZ,))],
         space=pltpu.HBM,
         mib=PACK_MIB,
     )
+    sends = [first, *sends]
     twin = xh_swap(maps)
     cosines, sines = call(rope_kernel, "rope", [of((rows, HEAD_SIZE), f32)] * 2, request_start, scalars=1)
-    ring = [(hidden, hidden)]
+    ring = [(after(hidden, first),) * 2]
 
     def ring_step(*others):
         r, l = ring[-1]
@@ -344,25 +365,21 @@
             r, l = after(r, l, *others), after(l, r, *others)
         ring.append((z_shift(r, 1), z_shift(l, -1) if len(ring) < 4 else None))
 
-    def added(low, sent, also=()):
-        outs = [of((RANK, rows), f32)] + [of((RANK, rows), t) for t in also]
-        return call(add_kernel, "low_add", outs, low, sent)
+    def added(low, sent):
+        return call(add_kernel, "low_add", of(low.shape, f32), low, sent)
 
     ring_step()
     mine = [weight_send(sends[0], 0), weight_send(after(sends[1], *ring[1]), 1)]
-    ring_step(mine[0], twin)
     near = jnp.stack([maps, after(twin, *ring[1])])
+    ring_step(mine[0], near, sends[1])
     far = core_swap(near)
     mine += [weight_send(after(sends[k], *ring[2]), k) for k in (2, 3)]
     low = call(low_kernel, "low", of((RANK, rows), f32), adapters, hidden, near, far, scalars=1)
-    ring_step(mine[1], low, cosines)
-    (low,) = added(low, z_xor(low, 1))
-    ring_step(mine[2], low)
+    low = added(low, z_xor(low, 1))
+    ring_step(mine[1], low)
+    ring_step(*mine[2:], cosines)
     mine[3] = after(mine[3], *ring[3])
     other = core_swap(call(stack_kernel, "stack", of((4, 1280, 128), bf16), *mine))
-    low = after(low, *ring[3])
-    low, narrow = added(low, z_xor(low, 2), (bf16,))
-    (low,) = added(low, z_xor(narrow, 4))
     right, left = zip(*ring)
 
     shards = [hidden, left[1], left[2], left[3], right[4], right[3], right[2], right[1]]
@@ -388,15 +405,18 @@
         mib=10,
     )
     b_got = [y_shift(b_parts[dy], dy) for dy in (2, 1, 3)]
-    kv_sum, x_send = call(
+    kv_sum, low, x_send = call(
         kv_join_kernel,
         "kv_join",
-        [of((576, 128), f32), of((NY * TA + 576, 128), bf16)],
+        [of((512, 128), f32), of((64, 128), f32), of((NY * TA + 512, 128), bf16)],
         kv_parts[0],
         *kv_got,
         far_a,
     )
     x_got = x_swap(x_send)
+    low = added(low, z_xor(low, 2))
+    low = added(low, z_xor(low, 4))
+    low = added(low, x_swap(low))
     a_own, kv_own, *a_sends = call(
         stage_a_kernel,
         "stage_a",
@@ -404,6 +424,7 @@
         near_a,
         x_got,
         kv_sum,
+        low,
     )
     a_got = {dy: y_shift(a_sends[dy - 1], dy) for dy in (2, 1, 3)}
     b_own, b_send = call(

time: 122 us -> 112 us (0.918)
  starting transfers between devices: 40.8 us -> 35.6 us
  local copies, waits for them, and re-layouts: 4.45 us -> 0.02 us
  waiting for transfers between devices: 59.8 us -> 57.6 us
  Pallas kernels: 15.4 us -> 17.2 us
    ppermute x7, waiting for transfers between devices: 17 us -> 30.6 us  [z_shift(): return lax.ppermute(v, 'z', [(i, (i + s) % NZ) for i in range(NZ)])]
    ppermute x3, waiting for transfers between devices: 19.3 us -> 10.1 us  [z_xor(): return lax.ppermute(v, 'z', [(i, i ^ s) for i in range(NZ)])]
    unnamed x14 -> x8, local copies, waits for them, and re-layouts: 4.45 us -> 0.02 us
    ppermute x2 -> x3, waiting for transfers between devices: 11.4 us -> 8.6 us  [x_swap(): return lax.ppermute(v, 'xl', [(0, 1), (1, 0)])]
    ppermute x1, waiting for transfers between devices: 5.8 us -> 3.36 us  [xh_swap(): return lax.ppermute(v, 'xh', [(0, 1), (1, 0)])]
    ppermute x9, starting transfers between devices: 14.2 us -> 12 us  [y_shift(): return lax.ppermute(v, 'y', [(i, (i + s) % NY) for i in range(NY)])]
    ppermute x9, waiting for transfers between devices: 6.23 us -> 4.27 us  [y_shift(): return lax.ppermute(v, 'y', [(i, (i + s) % NY) for i in range(NY)])]
    pallas_call x13 -> x15, Pallas kernels: 15.4 us -> 17.2 us  [call(): pl.pallas_call(kernel, out_shape=outs, in_specs=[SMEM] * scalars + [pl.Bl...]
  transfers between devices with their start and end apart: 28 -> 29, of which waited for: 15 -> 15; matrix products, arithmetic and copies ran while one was open for 0% -> 1% of each run, Pallas kernels for 7% -> 7%
where the time goes in v8:
time: 112 us
  waiting for transfers between devices  57.6 us (51%)
  starting transfers between devices  35.6 us (32%)
  Pallas kernels  17.2 us (15%)
    ppermute x7, waiting for transfers between devices, z_shift(): return lax.ppermute(v, 'z', [(i, (i + s) % NZ) for i in range(NZ)])  30.6 us
    pallas_call x15, Pallas kernels, call(): pl.pallas_call(kernel, out_shape=outs, in_specs=[SMEM] * scalars + [pl.Bl...  17.2 us
    ppermute x9, starting transfers between devices, y_shift(): return lax.ppermute(v, 'y', [(i, (i + s) % NY) for i in range(NY)])  12 us
    ppermute x7, starting transfers between devices, z_shift(): return lax.ppermute(v, 'z', [(i, (i + s) % NZ) for i in range(NZ)])  10.2 us
    ppermute x3, waiting for transfers between devices, z_xor(): return lax.ppermute(v, 'z', [(i, i ^ s) for i in range(NZ)])  10.1 us
    ppermute x3, waiting for transfers between devices, x_swap(): return lax.ppermute(v, 'xl', [(0, 1), (1, 0)])  8.6 us
    ppermute x4, starting transfers between devices, weight_send(): return lax.ppermute(v, ('xh', 'c', 'xl', 'y'), route)  5.43 us
    ppermute x9, waiting for transfers between devices, y_shift(): return lax.ppermute(v, 'y', [(i, (i + s) % NY) for i in range(NY)])  4.27 us
  transfers between devices with their start and end apart: 29, of which 15 were waited for; matrix products, arithmetic and copies ran while one was open for 1% of the time, Pallas kernels for 7%

profile of v8, /device:TPU:2, one launch (start us, length us, event | category | flops | bytes accessed | tf_op | source)
XLA Modules:
  0.0 111.6 jit_solution(6979257343755616998)
XLA Ops:
  0.0 2.1 %pack_first.1 = (bf16[1280,128]{1,0:T(8,128)(2,1)}, bf16[16,64,128]{2,1,0:T(8,128)(2,1)}) custom-call(bf16[8192,128]{1,0:T(8,128)(2,1)} %wq_ref.2, bf16[32,8192]{1,0:T(8,128)(2,1)} %bitcast.4, bf16[16,32,128]{2,1,0:T(8,128)(2,1)} %bitcast.8, bf16[16,32,128]{2,1,0:T(8,128)(2,1)} %up_ref.1), custom_call_target="tpu_custom_call" | custom-call | tf_op jit(solution)/shard_map/pack_first/pallas_call | solution.py:315
  2.1 2.0 %collective-permute-start.1 = (bf16[1024,128]{1,0:T(8,128)(2,1)S(1)}, bf16[1024,128]{1,0:T(8,128)(2,1)S(1)}, u32[]{:S(2)}, u32[]{:S(2)}) collective-permute-start(bf16[1024,128]{1,0:T(8,128)(2,1)S(1)} %copy-done.1), channel_id=1, source_target_pairs={{0,8},{8,16},{16,24},{24,32},{32,40},{40,48},{48,56},{56,0},{1,9},... | collective-permute-start | bytes 786440 | tf_op jit(solution)/shard_map/ppermute | solution.py:27
  4.1 4.0 %collective-permute-start = (bf16[1024,128]{1,0:T(8,128)(2,1)S(1)}, bf16[1024,128]{1,0:T(8,128)(2,1)S(1)}, u32[]{:S(2)}, u32[]{:S(2)}) collective-permute-start(bf16[1024,128]{1,0:T(8,128)(2,1)S(1)} %copy-done.1), channel_id=1, source_target_pairs={{0,56},{8,0},{16,8},{24,16},{32,24},{40,32},{48,40},{56,48},{1,57}... | collective-permute-start | bytes 786440 | tf_op jit(solution)/shard_map/ppermute | solution.py:27
  8.1 2.1 %collective-permute-start.3 = (bf16[16,64,128]{2,1,0:T(8,128)(2,1)}, bf16[16,64,128]{2,1,0:T(8,128)(2,1)S(1)}, u32[]{:S(2)}, u32[]{:S(2)}) collective-permute-start(bf16[16,64,128]{2,1,0:T(8,128)(2,1)} %get-tuple-element.48), channel_id=1, source_target_pairs={{0,128},{128,0},{1,129},{129,1},{2,130},{130,2},{3,131},{131,3},{4... | collective-permute-start | bytes 786440 | tf_op jit(solution)/shard_map/ppermute | solution.py:47
  11.7 2.7 %collective-permute-done.1.refs_7_ = bf16[1024,128]{1,0:T(8,128)(2,1)S(1)} collective-permute-done((bf16[1024,128]{1,0:T(8,128)(2,1)S(1)}, bf16[1024,128]{1,0:T(8,128)(2,1)S(1)}, u32[]{:S(2)}, u32[]{:S(2)}) %collective-permute-start.1) | collective-permute-done | bytes 262176 | tf_op jit(solution)/shard_map/ppermute | solution.py:27
  14.3 3.4 %collective-permute-done.3 = bf16[16,64,128]{2,1,0:T(8,128)(2,1)S(1)} collective-permute-done((bf16[16,64,128]{2,1,0:T(8,128)(2,1)}, bf16[16,64,128]{2,1,0:T(8,128)(2,1)S(1)}, u32[]{:S(2)}, u32[]{:S(2)}) %collective-permute-start.3) | collective-permute-done | bytes 262176 | tf_op jit(solution)/shard_map/ppermute | solution.py:47
  18.8 3.0 %pack.1 = (bf16[1280,128]{1,0:T(8,128)(2,1)}, bf16[1280,128]{1,0:T(8,128)(2,1)}, bf16[1280,128]{1,0:T(8,128)(2,1)}, bf16[1280,128]{1,0:T(8,128)(2,1)}) custom-call(bf16[8192,128]{1,0:T(8,128)(2,1)} %wq_ref.2, bf16[32,8192]{1,0:T(8,128)(2,1)} %bitcast.5), custom_call_target="tpu_custom_call" | custom-call | tf_op jit(solution)/shard_map/pack/pallas_call | solution.py:315
  21.8 3.2 %collective-permute-start.6 = (bf16[1280,128]{1,0:T(8,128)(2,1)}, bf16[1280,128]{1,0:T(8,128)(2,1)S(1)}, u32[]{:S(2)}, u32[]{:S(2)}) collective-permute-start(bf16[1280,128]{1,0:T(8,128)(2,1)} %get-tuple-element.54), channel_id=1, source_target_pairs={{0,6},{1,7},{2,4},{3,5},{4,2},{5,3},{6,0},{7,1},{64,199},{65,196},... | collective-permute-start | bytes 983048 | tf_op jit(solution)/shard_map/ppermute | solution.py:75
  28.0 6.3 %collective-permute-done.4.refs_2_ = bf16[1024,128]{1,0:T(8,128)(2,1)S(1)} collective-permute-done((bf16[1024,128]{1,0:T(8,128)(2,1)S(1)}, bf16[1024,128]{1,0:T(8,128)(2,1)S(1)}, u32[]{:S(2)}, u32[]{:S(2)}) %collective-permute-start.4) | collective-permute-done | bytes 262176 | tf_op jit(solution)/shard_map/ppermute | solution.py:27
  34.2 2.6 %collective-permute-done.5.refs_6_ = bf16[1024,128]{1,0:T(8,128)(2,1)S(1)} collective-permute-done((bf16[1024,128]{1,0:T(8,128)(2,1)S(1)}, bf16[1024,128]{1,0:T(8,128)(2,1)S(1)}, u32[]{:S(2)}, u32[]{:S(2)}) %collective-permute-start.5) | collective-permute-done | bytes 262176 | tf_op jit(solution)/shard_map/ppermute | solution.py:27
  37.6 1.9 %collective-permute-start.9 = (bf16[1024,128]{1,0:T(8,128)(2,1)S(1)}, bf16[1024,128]{1,0:T(8,128)(2,1)S(1)}, u32[]{:S(2)}, u32[]{:S(2)}) collective-permute-start(bf16[1024,128]{1,0:T(8,128)(2,1)S(1)} %collective-permute-done.4.refs_2_), channel_id=1, source_target_pairs={{0,56},{8,0},{16,8},{24,16},{32,24},{40,32},{48,40},{56,48},{1,57}... | collective-permute-start | bytes 786440 | tf_op jit(solution)/shard_map/ppermute | solution.py:27
  39.8 6.5 %collective-permute-done.9.refs_3_ = bf16[1024,128]{1,0:T(8,128)(2,1)S(1)} collective-permute-done((bf16[1024,128]{1,0:T(8,128)(2,1)S(1)}, bf16[1024,128]{1,0:T(8,128)(2,1)S(1)}, u32[]{:S(2)}, u32[]{:S(2)}) %collective-permute-start.9) | collective-permute-done | bytes 262176 | tf_op jit(solution)/shard_map/ppermute | solution.py:27
  46.3 2.6 %collective-permute-done.10.refs_5_ = bf16[1024,128]{1,0:T(8,128)(2,1)S(1)} collective-permute-done((bf16[1024,128]{1,0:T(8,128)(2,1)S(1)}, bf16[1024,128]{1,0:T(8,128)(2,1)S(1)}, u32[]{:S(2)}, u32[]{:S(2)}) %collective-permute-start.10) | collective-permute-done | bytes 262176 | tf_op jit(solution)/shard_map/ppermute | solution.py:27
  50.9 9.9 %collective-permute-done.13.refs_4_ = bf16[1024,128]{1,0:T(8,128)(2,1)S(1)} collective-permute-done((bf16[1024,128]{1,0:T(8,128)(2,1)S(1)}, bf16[1024,128]{1,0:T(8,128)(2,1)S(1)}, u32[]{:S(2)}, u32[]{:S(2)}) %collective-permute-start.13) | collective-permute-done | bytes 262176 | tf_op jit(solution)/shard_map/ppermute | solution.py:27
  62.9 2.2 %collective-permute-start.16 = (bf16[576,128]{1,0:T(8,128)(2,1)S(1)}, bf16[576,128]{1,0:T(8,128)(2,1)S(1)}, u32[]{:S(2)}, u32[]{:S(2)}) collective-permute-start(bf16[576,128]{1,0:T(8,128)(2,1)S(1)} %get-tuple-element.69), channel_id=1, source_target_pairs={{0,1},{1,2},{2,3},{3,0},{4,5},{5,6},{6,7},{7,4},{8,9},{9,10},{10,1... | collective-permute-start | bytes 442376 | tf_op jit(solution)/shard_map/ppermute | solution.py:51
  66.1 2.7 %q_product.1 = (bf16[1536,128]{1,0:T(8,128)(2,1)S(1)}, bf16[1536,128]{1,0:T(8,128)(2,1)S(1)}, bf16[1280,128]{1,0:T(8,128)(2,1)S(1)}, bf16[1280,128]{1,0:T(8,128)...) custom-call(bf16[1024,1024]{1,0:T(8,128)(2,1)S(1)} %get-tuple-element.65.hbuf, ...), custom_call_target="tpu_custom_call" | custom-call | tf_op jit(solution)/shard_map/q_product/pallas_call | solution.py:315
  68.8 1.9 %collective-permute-done.15.k1 = bf16[576,128]{1,0:T(8,128)(2,1)S(1)} collective-permute-done((bf16[576,128]{1,0:T(8,128)(2,1)S(1)}, bf16[576,128]{1,0:T(8,128)(2,1)S(1)}, u32[]{:S(2)}, u32[]{:S(2)}) %collective-permute-start.15) | collective-permute-done | bytes 147488 | tf_op jit(solution)/shard_map/ppermute | solution.py:51
  78.1 4.8 %collective-permute-done.19.b_ref = f32[64,128]{1,0:T(8,128)S(1)} collective-permute-done((f32[64,128]{1,0:T(8,128)S(1)}, f32[64,128]{1,0:T(8,128)S(1)}, u32[]{:S(2)}, u32[]{:S(2)}) %collective-permute-start.19) | collective-permute-done | bytes 32800 | tf_op jit(solution)/shard_map/ppermute | solution.py:31
  82.9 2.8 %collective-permute-start.20 = (f32[64,128]{1,0:T(8,128)S(1)}, f32[64,128]{1,0:T(8,128)S(1)}, u32[]{:S(2)}, u32[]{:S(2)}) collective-permute-start(f32[64,128]{1,0:T(8,128)S(1)} %low_add.5.a_ref), channel_id=1, source_target_pairs={{0,32},{8,40},{16,48},{24,56},{32,0},{40,8},{48,16},{56,24},{1,33}... | collective-permute-start | bytes 98312 | tf_op jit(solution)/shard_map/ppermute | solution.py:31
  85.7 5.3 %collective-permute-done.20.b_ref = f32[64,128]{1,0:T(8,128)S(1)} collective-permute-done((f32[64,128]{1,0:T(8,128)S(1)}, f32[64,128]{1,0:T(8,128)S(1)}, u32[]{:S(2)}, u32[]{:S(2)}) %collective-permute-start.20) | collective-permute-done | bytes 32800 | tf_op jit(solution)/shard_map/ppermute | solution.py:31
  91.3 3.6 %collective-permute-done.21.b_ref = f32[64,128]{1,0:T(8,128)S(1)} collective-permute-done((f32[64,128]{1,0:T(8,128)S(1)}, f32[64,128]{1,0:T(8,128)S(1)}, u32[]{:S(2)}, u32[]{:S(2)}) %collective-permute-start.21) | collective-permute-done | bytes 32800 | tf_op jit(solution)/shard_map/ppermute | solution.py:39
  97.1 2.5 %collective-permute-start.24 = (bf16[960,128]{1,0:T(8,128)(2,1)S(1)}, bf16[960,128]{1,0:T(8,128)(2,1)S(1)}, u32[]{:S(2)}, u32[]{:S(2)}) collective-permute-start(bf16[960,128]{1,0:T(8,128)(2,1)S(1)} %get-tuple-element.78), channel_id=1, source_target_pairs={{0,3},{1,0},{2,1},{3,2},{4,7},{5,4},{6,5},{7,6},{8,11},{9,8},{10,9... | collective-permute-start | bytes 737288 | tf_op jit(solution)/shard_map/ppermute | solution.py:51
  100.4 5.0 %collective-permute-done.28.refs_5_ = bf16[640,128]{1,0:T(8,128)(2,1)S(1)} collective-permute-done((bf16[640,128]{1,0:T(8,128)(2,1)S(1)}, bf16[640,128]{1,0:T(8,128)(2,1)S(1)}, u32[]{:S(2)}, u32[]{:S(2)}) %collective-permute-start.28) | collective-permute-done | bytes 163872 | tf_op jit(solution)/shard_map/ppermute | solution.py:39
  106.1 5.5 %attention.1 = bf16[1024,128]{1,0:T(8,128)(2,1)} custom-call(s32[8]{0:T(128)S(1)} %copy-done.3, s32[1024]{0:T(1024)S(1)} %copy-done.2, f32[384,128]{1,0:T(8,128)S(1)} %get-tuple-element.75.refs_0_, bf16[960,128]{1,0:T(8,128)(2,1)S(1)} %collective-permute-done.22.refs_1_, bf16[960,128]{1,0:T(8,128)(2,1)S(1)} %collective-permute-done.23.refs_2_, ...), custom_call_target="tpu_custom_call" | custom-call | tf_op jit(solution)/shard_map/attention/pallas_call | solution.py:315
  (58 shorter events, 22.8 us)
Async XLA Ops:
  2.1 12.2 %collective-permute-start.1 = (bf16[1024,128]{1,0:T(8,128)(2,1)S(1)}, bf16[1024,128]{1,0:T(8,128)(2,1)S(1)}, u32[]{:S(2)}, u32[]{:S(2)}) collective-permute-start(bf16[1024,128]{1,0:T(8,128)(2,1)S(1)} %copy-done.1), channel_id=1, source_target_pairs={{0,8},{8,16},{16,24},{24,32},{32,40},{40,48},{48,56},{56,0},{1,9},... | collective-permute-start | bytes 786440 | tf_op jit(solution)/shard_map/ppermute | solution.py:27
  4.1 10.2 %collective-permute-start = (bf16[1024,128]{1,0:T(8,128)(2,1)S(1)}, bf16[1024,128]{1,0:T(8,128)(2,1)S(1)}, u32[]{:S(2)}, u32[]{:S(2)}) collective-permute-start(bf16[1024,128]{1,0:T(8,128)(2,1)S(1)} %copy-done.1), channel_id=1, source_target_pairs={{0,56},{8,0},{16,8},{24,16},{32,24},{40,32},{48,40},{56,48},{1,57}... | collective-permute-start | bytes 786440 | tf_op jit(solution)/shard_map/ppermute | solution.py:27
  8.1 9.6 %collective-permute-start.3 = (bf16[16,64,128]{2,1,0:T(8,128)(2,1)}, bf16[16,64,128]{2,1,0:T(8,128)(2,1)S(1)}, u32[]{:S(2)}, u32[]{:S(2)}) collective-permute-start(bf16[16,64,128]{2,1,0:T(8,128)(2,1)} %get-tuple-element.48), channel_id=1, source_target_pairs={{0,128},{128,0},{1,129},{129,1},{2,130},{130,2},{3,131},{131,3},{4... | collective-permute-start | bytes 786440 | tf_op jit(solution)/shard_map/ppermute | solution.py:47
  10.2 14.8 %collective-permute-start.2 = (bf16[1280,128]{1,0:T(8,128)(2,1)}, bf16[1280,128]{1,0:T(8,128)(2,1)S(1)}, u32[]{:S(2)}, u32[]{:S(2)}) collective-permute-start(bf16[1280,128]{1,0:T(8,128)(2,1)} %get-tuple-element.46), channel_id=1, source_target_pairs={{0,4},{1,5},{2,6},{3,7},{4,0},{5,1},{6,2},{7,3},{64,197},{65,198},... | collective-permute-start | bytes 983048 | tf_op jit(solution)/shard_map/ppermute | solution.py:75
  18.7 8.4 %collective-permute-start.7 = (bf16[2,16,64,128]{3,2,1,0:T(8,128)(2,1)S(1)}, bf16[2,16,64,128]{3,2,1,0:T(8,128)(2,1)S(1)}, u32[]{:S(2)}, u32[]{:S(2)}) collective-permute-start(bf16[2,16,64,128]{3,2,1,0:T(8,128)(2,1)S(1)} %pad_maximum_fusion.near_ref.refs_7_), channel_id=1, source_target_pairs={{0,64},{64,0},{1,65},{65,1},{2,66},{66,2},{3,67},{67,3},{4,68},{68... | collective-permute-start | bytes 1572872 | tf_op jit(solution)/shard_map/ppermute | solution.py:43
  21.8 15.8 %collective-permute-start.6 = (bf16[1280,128]{1,0:T(8,128)(2,1)}, bf16[1280,128]{1,0:T(8,128)(2,1)S(1)}, u32[]{:S(2)}, u32[]{:S(2)}) collective-permute-start(bf16[1280,128]{1,0:T(8,128)(2,1)} %get-tuple-element.54), channel_id=1, source_target_pairs={{0,6},{1,7},{2,4},{3,5},{4,2},{5,3},{6,0},{7,1},{64,199},{65,196},... | collective-permute-start | bytes 983048 | tf_op jit(solution)/shard_map/ppermute | solution.py:75
  25.1 9.2 %collective-permute-start.4 = (bf16[1024,128]{1,0:T(8,128)(2,1)S(1)}, bf16[1024,128]{1,0:T(8,128)(2,1)S(1)}, u32[]{:S(2)}, u32[]{:S(2)}) collective-permute-start(bf16[1024,128]{1,0:T(8,128)(2,1)S(1)} %collective-permute-done.refs_1_), channel_id=1, source_target_pairs={{0,56},{8,0},{16,8},{24,16},{32,24},{40,32},{48,40},{56,48},{1,57}... | collective-permute-start | bytes 786440 | tf_op jit(solution)/shard_map/ppermute | solution.py:27
  26.7 10.1 %collective-permute-start.5 = (bf16[1024,128]{1,0:T(8,128)(2,1)S(1)}, bf16[1024,128]{1,0:T(8,128)(2,1)S(1)}, u32[]{:S(2)}, u32[]{:S(2)}) collective-permute-start(bf16[1024,128]{1,0:T(8,128)(2,1)S(1)} %collective-permute-done.1.refs_7_), channel_id=1, source_target_pairs={{0,8},{8,16},{16,24},{24,32},{32,40},{40,48},{48,56},{56,0},{1,9},... | collective-permute-start | bytes 786440 | tf_op jit(solution)/shard_map/ppermute | solution.py:27
  27.9 9.7 %collective-permute-start.8 = (f32[32,1024]{1,0:T(8,128)S(1)}, f32[32,1024]{1,0:T(8,128)S(1)}, u32[]{:S(2)}, u32[]{:S(2)}) collective-permute-start(f32[32,1024]{1,0:T(8,128)S(1)} %low.1.a_ref), channel_id=1, source_target_pairs={{0,8},{8,0},{16,24},{24,16},{32,40},{40,32},{48,56},{56,48},{1,9},... | collective-permute-start | bytes 393224 | tf_op jit(solution)/shard_map/ppermute | solution.py:31
  37.5 12.1 %collective-permute-start.11 = (bf16[1280,128]{1,0:T(8,128)(2,1)}, bf16[1280,128]{1,0:T(8,128)(2,1)S(1)}, u32[]{:S(2)}, u32[]{:S(2)}) collective-permute-start(bf16[1280,128]{1,0:T(8,128)(2,1)} %get-tuple-element.58), channel_id=1, source_target_pairs={{0,1},{1,2},{2,3},{3,0},{4,5},{5,6},{6,7},{7,4},{64,67},{65,64},{6... | collective-permute-start | bytes 983048 | tf_op jit(solution)/shard_map/ppermute | solution.py:75
  37.6 8.6 %collective-permute-start.9 = (bf16[1024,128]{1,0:T(8,128)(2,1)S(1)}, bf16[1024,128]{1,0:T(8,128)(2,1)S(1)}, u32[]{:S(2)}, u32[]{:S(2)}) collective-permute-start(bf16[1024,128]{1,0:T(8,128)(2,1)S(1)} %collective-permute-done.4.refs_2_), channel_id=1, source_target_pairs={{0,56},{8,0},{16,8},{24,16},{32,24},{40,32},{48,40},{56,48},{1,57}... | collective-permute-start | bytes 786440 | tf_op jit(solution)/shard_map/ppermute | solution.py:27
  39.5 9.3 %collective-permute-start.10 = (bf16[1024,128]{1,0:T(8,128)(2,1)S(1)}, bf16[1024,128]{1,0:T(8,128)(2,1)S(1)}, u32[]{:S(2)}, u32[]{:S(2)}) collective-permute-start(bf16[1024,128]{1,0:T(8,128)(2,1)S(1)} %collective-permute-done.5.refs_6_), channel_id=1, source_target_pairs={{0,8},{8,16},{16,24},{24,32},{32,40},{40,48},{48,56},{56,0},{1,9},... | collective-permute-start | bytes 786440 | tf_op jit(solution)/shard_map/ppermute | solution.py:27
  49.7 11.1 %collective-permute-start.14 = (bf16[4,1280,128]{2,1,0:T(8,128)(2,1)S(1)}, bf16[4,1280,128]{2,1,0:T(8,128)(2,1)S(1)}, u32[]{:S(2)}, u32[]{:S(2)}) collective-permute-start(bf16[4,1280,128]{2,1,0:T(8,128)(2,1)S(1)} %stack.13), channel_id=1, source_target_pairs={{0,64},{64,0},{1,65},{65,1},{2,66},{66,2},{3,67},{67,3},{4,68},{68... | collective-permute-start | bytes 3932168 | tf_op jit(solution)/shard_map/ppermute | solution.py:43
  50.8 10.0 %collective-permute-start.13 = (bf16[1024,128]{1,0:T(8,128)(2,1)S(1)}, bf16[1024,128]{1,0:T(8,128)(2,1)S(1)}, u32[]{:S(2)}, u32[]{:S(2)}) collective-permute-start(bf16[1024,128]{1,0:T(8,128)(2,1)S(1)} %collective-permute-done.10.refs_5_), channel_id=1, source_target_pairs={{0,8},{8,16},{16,24},{24,32},{32,40},{40,48},{48,56},{56,0},{1,9},... | collective-permute-start | bytes 786440 | tf_op jit(solution)/shard_map/ppermute | solution.py:27
  62.4 8.3 %collective-permute-start.15 = (bf16[576,128]{1,0:T(8,128)(2,1)S(1)}, bf16[576,128]{1,0:T(8,128)(2,1)S(1)}, u32[]{:S(2)}, u32[]{:S(2)}) collective-permute-start(bf16[576,128]{1,0:T(8,128)(2,1)S(1)} %get-tuple-element.68), channel_id=1, source_target_pairs={{0,2},{1,3},{2,0},{3,1},{4,6},{5,7},{6,4},{7,5},{8,10},{9,11},{10,... | collective-permute-start | bytes 442376 | tf_op jit(solution)/shard_map/ppermute | solution.py:51
  62.9 9.5 %collective-permute-start.16 = (bf16[576,128]{1,0:T(8,128)(2,1)S(1)}, bf16[576,128]{1,0:T(8,128)(2,1)S(1)}, u32[]{:S(2)}, u32[]{:S(2)}) collective-permute-start(bf16[576,128]{1,0:T(8,128)(2,1)S(1)} %get-tuple-element.69), channel_id=1, source_target_pairs={{0,1},{1,2},{2,3},{3,0},{4,5},{5,6},{6,7},{7,4},{8,9},{9,10},{10,1... | collective-permute-start | bytes 442376 | tf_op jit(solution)/shard_map/ppermute | solution.py:51
  72.5 22.4 %collective-permute-start.18 = (bf16[2048,128]{1,0:T(8,128)(2,1)S(1)}, bf16[2048,128]{1,0:T(8,128)(2,1)S(1)}, u32[]{:S(2)}, u32[]{:S(2)}) collective-permute-start(bf16[2048,128]{1,0:T(8,128)(2,1)S(1)} %get-tuple-element.72), channel_id=1, source_target_pairs={{0,4},{4,0},{1,5},{5,1},{2,6},{6,2},{3,7},{7,3},{8,12},{12,8},{9,1... | collective-permute-start | bytes 1572872 | tf_op jit(solution)/shard_map/ppermute | solution.py:39
  74.4 22.7 %collective-permute-start.25 = (bf16[1280,128]{1,0:T(8,128)(2,1)S(1)}, bf16[1280,128]{1,0:T(8,128)(2,1)S(1)}, u32[]{:S(2)}, u32[]{:S(2)}) collective-permute-start(bf16[1280,128]{1,0:T(8,128)(2,1)S(1)} %get-tuple-element.80), channel_id=1, source_target_pairs={{0,2},{1,3},{2,0},{3,1},{4,6},{5,7},{6,4},{7,5},{8,10},{9,11},{10,... | collective-permute-start | bytes 983048 | tf_op jit(solution)/shard_map/ppermute | solution.py:51
  74.8 24.8 %collective-permute-start.26 = (bf16[1280,128]{1,0:T(8,128)(2,1)S(1)}, bf16[1280,128]{1,0:T(8,128)(2,1)S(1)}, u32[]{:S(2)}, u32[]{:S(2)}) collective-permute-start(bf16[1280,128]{1,0:T(8,128)(2,1)S(1)} %get-tuple-element.81), channel_id=1, source_target_pairs={{0,1},{1,2},{2,3},{3,0},{4,5},{5,6},{6,7},{7,4},{8,9},{9,10},{10,1... | collective-permute-start | bytes 983048 | tf_op jit(solution)/shard_map/ppermute | solution.py:51
  76.4 23.2 %collective-permute-start.27 = (bf16[1280,128]{1,0:T(8,128)(2,1)S(1)}, bf16[1280,128]{1,0:T(8,128)(2,1)S(1)}, u32[]{:S(2)}, u32[]{:S(2)}) collective-permute-start(bf16[1280,128]{1,0:T(8,128)(2,1)S(1)} %get-tuple-element.82), channel_id=1, source_target_pairs={{0,3},{1,0},{2,1},{3,2},{4,7},{5,4},{6,5},{7,6},{8,11},{9,8},{10,9... | collective-permute-start | bytes 983048 | tf_op jit(solution)/shard_map/ppermute | solution.py:51
  82.9 8.1 %collective-permute-start.20 = (f32[64,128]{1,0:T(8,128)S(1)}, f32[64,128]{1,0:T(8,128)S(1)}, u32[]{:S(2)}, u32[]{:S(2)}) collective-permute-start(f32[64,128]{1,0:T(8,128)S(1)} %low_add.5.a_ref), channel_id=1, source_target_pairs={{0,32},{8,40},{16,48},{24,56},{32,0},{40,8},{48,16},{56,24},{1,33}... | collective-permute-start | bytes 98312 | tf_op jit(solution)/shard_map/ppermute | solution.py:31
  95.1 10.3 %collective-permute-start.22 = (bf16[960,128]{1,0:T(8,128)(2,1)S(1)}, bf16[960,128]{1,0:T(8,128)(2,1)S(1)}, u32[]{:S(2)}, u32[]{:S(2)}) collective-permute-start(bf16[960,128]{1,0:T(8,128)(2,1)S(1)} %get-tuple-element.76), channel_id=1, source_target_pairs={{0,1},{1,2},{2,3},{3,0},{4,5},{5,6},{6,7},{7,4},{8,9},{9,10},{10,1... | collective-permute-start | bytes 737288 | tf_op jit(solution)/shard_map/ppermute | solution.py:51
  95.6 9.9 %collective-permute-start.23 = (bf16[960,128]{1,0:T(8,128)(2,1)S(1)}, bf16[960,128]{1,0:T(8,128)(2,1)S(1)}, u32[]{:S(2)}, u32[]{:S(2)}) collective-permute-start(bf16[960,128]{1,0:T(8,128)(2,1)S(1)} %get-tuple-element.77), channel_id=1, source_target_pairs={{0,2},{1,3},{2,0},{3,1},{4,6},{5,7},{6,4},{7,5},{8,10},{9,11},{10,... | collective-permute-start | bytes 737288 | tf_op jit(solution)/shard_map/ppermute | solution.py:51
  97.1 9.0 %collective-permute-start.24 = (bf16[960,128]{1,0:T(8,128)(2,1)S(1)}, bf16[960,128]{1,0:T(8,128)(2,1)S(1)}, u32[]{:S(2)}, u32[]{:S(2)}) collective-permute-start(bf16[960,128]{1,0:T(8,128)(2,1)S(1)} %get-tuple-element.78), channel_id=1, source_target_pairs={{0,3},{1,0},{2,1},{3,2},{4,7},{5,4},{6,5},{7,6},{8,11},{9,8},{10,9... | collective-permute-start | bytes 737288 | tf_op jit(solution)/shard_map/ppermute | solution.py:51
  (9 other events, 118.8 us)

commit v9 on v8

--- a/solution.py
+++ b/solution.py
@@ -51,7 +51,7 @@
     return lax.ppermute(v, "y", [(i, (i + s) % NY) for i in range(NY)])
 
 
-SERVED = ((4, 6, 1), (5, 7, 3, 2))
+SERVED = ((1, 4, 6), (3, 5, 7, 2))
 FLIP = [dx * NY + (-dy) % NY for dx in range(NX) for dy in range(NY)]
 
 
@@ -116,7 +116,7 @@
 
 
 def add_kernel(a_ref, b_ref, out_ref):
-    out_ref[...] = a_ref[...] + b_ref[...]
+    out_ref[...] = a_ref[...] + b_ref[...].astype(jnp.float32)
 
 
 def rope_kernel(start_ref, cos_ref, sin_ref):
@@ -142,7 +142,7 @@
         sin_ref[rows, :] = (sin_in * co + cos_in * so) * sign
 
 
-def low_kernel(ad_ref, h_ref, near_ref, far_ref, out_ref):
+def low_kernel(ad_ref, h_ref, near_ref, far_ref, out_ref, narrow_ref):
     c, xh = lax.axis_index("c"), lax.axis_index("xh")
     per = near_ref.shape[1]
     for b in range(h_ref.shape[0] // BLOCK):
@@ -157,6 +157,7 @@
             (((1,), (1,)), ((), ())),
             preferred_element_type=jnp.float32,
         )
+    narrow_ref[...] = out_ref[...].astype(jnp.bfloat16)
 
 
 def for_each_piece(own, mine, other, place):
@@ -344,11 +345,12 @@
         space=pltpu.HBM,
         mib=PACK_MIB,
     )
+    cosines, sines = call(rope_kernel, "rope", [of((rows, HEAD_SIZE), f32)] * 2, request_start, scalars=1)
     sends = call(
         pack_kernel,
         "pack",
         [of((1280, 128), bf16)] * 4,
-        after(query_weight, first),
+        after(query_weight, first, cosines),
         kv_rows,
         scratch=[pltpu.SemaphoreType.DMA((8 * NZ,))],
         space=pltpu.HBM,
@@ -356,8 +358,7 @@
     )
     sends = [first, *sends]
     twin = xh_swap(maps)
-    cosines, sines = call(rope_kernel, "rope", [of((rows, HEAD_SIZE), f32)] * 2, request_start, scalars=1)
-    ring = [(after(hidden, first),) * 2]
+    ring = [(hidden, hidden)]
 
     def ring_step(*others):
         r, l = ring[-1]
@@ -369,15 +370,17 @@
         return call(add_kernel, "low_add", of(low.shape, f32), low, sent)
 
     ring_step()
-    mine = [weight_send(sends[0], 0), weight_send(after(sends[1], *ring[1]), 1)]
+    mine = [weight_send(sends[0], 0), weight_send(after(sends[1], *ring[1]), 1), None, weight_send(sends[3], 3)]
     near = jnp.stack([maps, after(twin, *ring[1])])
-    ring_step(mine[0], near, sends[1])
+    ring_step(mine[0], mine[3], near)
     far = core_swap(near)
-    mine += [weight_send(after(sends[k], *ring[2]), k) for k in (2, 3)]
-    low = call(low_kernel, "low", of((RANK, rows), f32), adapters, hidden, near, far, scalars=1)
-    low = added(low, z_xor(low, 1))
+    mine[2] = weight_send(after(sends[2], *ring[2]), 2)
+    low, narrow = call(
+        low_kernel, "low", [of((RANK, rows), f32), of((RANK, rows), bf16)], adapters, hidden, near, far, scalars=1
+    )
+    low = added(low, z_xor(narrow, 4))
     ring_step(mine[1], low)
-    ring_step(*mine[2:], cosines)
+    ring_step(mine[2])
     mine[3] = after(mine[3], *ring[3])
     other = core_swap(call(stack_kernel, "stack", of((4, 1280, 128), bf16), *mine))
     right, left = zip(*ring)
@@ -414,8 +417,8 @@
         far_a,
     )
     x_got = x_swap(x_send)
+    low = added(low, z_xor(low, 1))
     low = added(low, z_xor(low, 2))
-    low = added(low, z_xor(low, 4))
     low = added(low, x_swap(low))
     a_own, kv_own, *a_sends = call(
         stage_a_kernel,

time: 112 us -> 106 us (0.946)
  waiting for transfers between devices: 57.6 us -> 40.9 us
  starting transfers between devices: 35.6 us -> 47.2 us
    ppermute x7, waiting for transfers between devices: 30.6 us -> 19.5 us  [z_shift(): return lax.ppermute(v, 'z', [(i, (i + s) % NZ) for i in range(NZ)])]
    ppermute x2, starting transfers between devices: 0.19 us -> 8.04 us  [core_swap(): return lax.ppermute(v, 'c', [(0, 1), (1, 0)])]
    ppermute x1, waiting for transfers between devices: 3.36 us -> 0.89 us  [xh_swap(): return lax.ppermute(v, 'xh', [(0, 1), (1, 0)])]
    ppermute x3, waiting for transfers between devices: 8.6 us -> 7.17 us  [x_swap(): return lax.ppermute(v, 'xl', [(0, 1), (1, 0)])]
    ppermute x3, starting transfers between devices: 2.9 us -> 4.3 us  [z_xor(): return lax.ppermute(v, 'z', [(i, i ^ s) for i in range(NZ)])]
    ppermute x3, waiting for transfers between devices: 10.1 us -> 8.72 us  [z_xor(): return lax.ppermute(v, 'z', [(i, i ^ s) for i in range(NZ)])]
    ppermute x4, starting transfers between devices: 5.43 us -> 6.75 us  [weight_send(): return lax.ppermute(v, ('xh', 'c', 'xl', 'y'), route)]
  transfers between devices with their start and end apart: 29 -> 29, of which waited for: 15 -> 13; matrix products, arithmetic and copies ran while one was open for 1% -> 0% of each run, Pallas kernels for 7% -> 9%
where the time goes in v9:
time: 106 us
  starting transfers between devices  47.2 us (45%)
  waiting for transfers between devices  40.9 us (39%)
  Pallas kernels  17.2 us (16%)
    ppermute x7, waiting for transfers between devices, z_shift(): return lax.ppermute(v, 'z', [(i, (i + s) % NZ) for i in range(NZ)])  19.5 us
    pallas_call x15, Pallas kernels, call(): pl.pallas_call(kernel, out_shape=outs, in_specs=[SMEM] * scalars + [pl.Bl...  17.2 us
    ppermute x9, starting transfers between devices, y_shift(): return lax.ppermute(v, 'y', [(i, (i + s) % NY) for i in range(NY)])  12.7 us
    ppermute x7, starting transfers between devices, z_shift(): return lax.ppermute(v, 'z', [(i, (i + s) % NZ) for i in range(NZ)])  10.1 us
    ppermute x3, waiting for transfers between devices, z_xor(): return lax.ppermute(v, 'z', [(i, i ^ s) for i in range(NZ)])  8.72 us
    ppermute x2, starting transfers between devices, core_swap(): return lax.ppermute(v, 'c', [(0, 1), (1, 0)])  8.04 us
    ppermute x3, waiting for transfers between devices, x_swap(): return lax.ppermute(v, 'xl', [(0, 1), (1, 0)])  7.17 us
    ppermute x4, starting transfers between devices, weight_send(): return lax.ppermute(v, ('xh', 'c', 'xl', 'y'), route)  6.75 us
  transfers between devices with their start and end apart: 29, of which 13 were waited for; matrix products, arithmetic and copies ran while one was open for 0% of the time, Pallas kernels for 9%

profile of v9, /device:TPU:2, one launch (start us, length us, event | category | flops | bytes accessed | tf_op | source)
XLA Modules:
  0.0 105.6 jit_solution(15461918666778346283)
XLA Ops:
  0.0 1.9 %collective-permute-start.1 = (bf16[1024,128]{1,0:T(8,128)(2,1)}, bf16[1024,128]{1,0:T(8,128)(2,1)S(1)}, u32[]{:S(2)}, u32[]{:S(2)}) collective-permute-start(bf16[1024,128]{1,0:T(8,128)(2,1)} %refs_0_.1), channel_id=1, source_target_pairs={{0,8},{8,16},{16,24},{24,32},{32,40},{40,48},{48,56},{56,0},{1,9},... | collective-permute-start | bytes 786440 | tf_op jit(solution)/shard_map/ppermute | solution.py:27
  1.9 4.0 %collective-permute-start = (bf16[1024,128]{1,0:T(8,128)(2,1)}, bf16[1024,128]{1,0:T(8,128)(2,1)S(1)}, u32[]{:S(2)}, u32[]{:S(2)}) collective-permute-start(bf16[1024,128]{1,0:T(8,128)(2,1)} %refs_0_.1), channel_id=1, source_target_pairs={{0,56},{8,0},{16,8},{24,16},{32,24},{40,32},{48,40},{56,48},{1,57}... | collective-permute-start | bytes 786440 | tf_op jit(solution)/shard_map/ppermute | solution.py:27
  5.9 2.0 %pack_first.1 = (bf16[1280,128]{1,0:T(8,128)(2,1)}, bf16[16,64,128]{2,1,0:T(8,128)(2,1)}) custom-call(bf16[8192,128]{1,0:T(8,128)(2,1)} %wq_ref.2, bf16[32,8192]{1,0:T(8,128)(2,1)} %bitcast.4, bf16[16,32,128]{2,1,0:T(8,128)(2,1)} %bitcast.8, bf16[16,32,128]{2,1,0:T(8,128)(2,1)} %up_ref.1), custom_call_target="tpu_custom_call" | custom-call | tf_op jit(solution)/shard_map/pack_first/pallas_call | solution.py:316
  8.0 2.2 %collective-permute-start.4 = (bf16[16,64,128]{2,1,0:T(8,128)(2,1)}, bf16[16,64,128]{2,1,0:T(8,128)(2,1)S(1)}, u32[]{:S(2)}, u32[]{:S(2)}) collective-permute-start(bf16[16,64,128]{2,1,0:T(8,128)(2,1)} %get-tuple-element.50), channel_id=1, source_target_pairs={{0,128},{128,0},{1,129},{129,1},{2,130},{130,2},{3,131},{131,3},{4... | collective-permute-start | bytes 786440 | tf_op jit(solution)/shard_map/ppermute | solution.py:47
  12.8 3.0 %pack.1 = (bf16[1280,128]{1,0:T(8,128)(2,1)}, bf16[1280,128]{1,0:T(8,128)(2,1)}, bf16[1280,128]{1,0:T(8,128)(2,1)}, bf16[1280,128]{1,0:T(8,128)(2,1)}) custom-call(bf16[8192,128]{1,0:T(8,128)(2,1)} %wq_ref.2, bf16[32,8192]{1,0:T(8,128)(2,1)} %bitcast.5), custom_call_target="tpu_custom_call" | custom-call | tf_op jit(solution)/shard_map/pack/pallas_call | solution.py:316
  20.3 1.7 %collective-permute-start.5 = (bf16[1024,128]{1,0:T(8,128)(2,1)S(1)}, bf16[1024,128]{1,0:T(8,128)(2,1)S(1)}, u32[]{:S(2)}, u32[]{:S(2)}) collective-permute-start(bf16[1024,128]{1,0:T(8,128)(2,1)S(1)} %collective-permute-done.refs_1_), channel_id=1, source_target_pairs={{0,56},{8,0},{16,8},{24,16},{32,24},{40,32},{48,40},{56,48},{1,57}... | collective-permute-start | bytes 786440 | tf_op jit(solution)/shard_map/ppermute | solution.py:27
  23.1 4.3 %collective-permute-start.9 = (bf16[32,1024]{1,0:T(8,128)(2,1)S(1)}, bf16[32,1024]{1,0:T(8,128)(2,1)S(1)}, u32[]{:S(2)}, u32[]{:S(2)}) collective-permute-start(bf16[32,1024]{1,0:T(8,128)(2,1)S(1)} %get-tuple-element.57), channel_id=1, source_target_pairs={{0,32},{8,40},{16,48},{24,56},{32,0},{40,8},{48,16},{56,24},{1,33}... | collective-permute-start | bytes 196616 | tf_op jit(solution)/shard_map/ppermute | solution.py:31
  27.4 2.8 %collective-permute-done.6.refs_6_ = bf16[1024,128]{1,0:T(8,128)(2,1)S(1)} collective-permute-done((bf16[1024,128]{1,0:T(8,128)(2,1)S(1)}, bf16[1024,128]{1,0:T(8,128)(2,1)S(1)}, u32[]{:S(2)}, u32[]{:S(2)}) %collective-permute-start.6) | collective-permute-done | bytes 262176 | tf_op jit(solution)/shard_map/ppermute | solution.py:27
  30.3 2.9 %collective-permute-start.12 = (bf16[1280,128]{1,0:T(8,128)(2,1)S(1)}, bf16[1280,128]{1,0:T(8,128)(2,1)S(1)}, u32[]{:S(2)}, u32[]{:S(2)}) collective-permute-start(bf16[1280,128]{1,0:T(8,128)(2,1)S(1)} %copy-done.5), channel_id=1, source_target_pairs={{0,6},{1,7},{2,4},{3,5},{4,2},{5,3},{6,0},{7,1},{64,199},{65,196},... | collective-permute-start | bytes 983048 | tf_op jit(solution)/shard_map/ppermute | solution.py:75
  35.3 5.8 %collective-permute-done.10.refs_3_ = bf16[1024,128]{1,0:T(8,128)(2,1)S(1)} collective-permute-done((bf16[1024,128]{1,0:T(8,128)(2,1)S(1)}, bf16[1024,128]{1,0:T(8,128)(2,1)S(1)}, u32[]{:S(2)}, u32[]{:S(2)}) %collective-permute-start.10) | collective-permute-done | bytes 262176 | tf_op jit(solution)/shard_map/ppermute | solution.py:27
  42.5 6.8 %collective-permute-start.14 = (bf16[4,1280,128]{2,1,0:T(8,128)(2,1)S(1)}, bf16[4,1280,128]{2,1,0:T(8,128)(2,1)S(1)}, u32[]{:S(2)}, u32[]{:S(2)}) collective-permute-start(bf16[4,1280,128]{2,1,0:T(8,128)(2,1)S(1)} %stack.13), channel_id=1, source_target_pairs={{0,64},{64,0},{1,65},{65,1},{2,66},{66,2},{3,67},{67,3},{4,68},{68... | collective-permute-start | bytes 3932168 | tf_op jit(solution)/shard_map/ppermute | solution.py:43
  49.4 9.5 %collective-permute-done.13.refs_4_ = bf16[1024,128]{1,0:T(8,128)(2,1)S(1)} collective-permute-done((bf16[1024,128]{1,0:T(8,128)(2,1)S(1)}, bf16[1024,128]{1,0:T(8,128)(2,1)S(1)}, u32[]{:S(2)}, u32[]{:S(2)}) %collective-permute-start.13) | collective-permute-done | bytes 262176 | tf_op jit(solution)/shard_map/ppermute | solution.py:27
  58.9 1.6 %kv_product.1 = (bf16[576,128]{1,0:T(8,128)(2,1)S(1)}, bf16[576,128]{1,0:T(8,128)(2,1)S(1)}, bf16[576,128]{1,0:T(8,128)(2,1)S(1)}, bf16[576,128]{1,0:T(8,128)(2,1)S(1)}, bf16[1024,1024]{1,0:T(8,128)(2,1)S(1)}) custom-call(bf16[1024,128]{1,0:T(8,128)(2,1)S(1)} %copy-done.1, bf16[1024,128]{1,0:T(8,128)(2,1)S(1)} %collective-permute-done.refs_1_, ...), custom_call_target="tpu_custom_call" | custom-call | tf_op jit(solution)/shard_map/kv_product/pallas_call | solution.py:316
  61.7 3.2 %collective-permute-start.17 = (bf16[576,128]{1,0:T(8,128)(2,1)S(1)}, bf16[576,128]{1,0:T(8,128)(2,1)S(1)}, u32[]{:S(2)}, u32[]{:S(2)}) collective-permute-start(bf16[576,128]{1,0:T(8,128)(2,1)S(1)} %get-tuple-element.70), channel_id=1, source_target_pairs={{0,3},{1,0},{2,1},{3,2},{4,7},{5,4},{6,5},{7,6},{8,11},{9,8},{10,9... | collective-permute-start | bytes 442376 | tf_op jit(solution)/shard_map/ppermute | solution.py:51
  64.9 2.7 %q_product.1 = (bf16[1536,128]{1,0:T(8,128)(2,1)S(1)}, bf16[1536,128]{1,0:T(8,128)(2,1)S(1)}, bf16[1280,128]{1,0:T(8,128)(2,1)S(1)}, bf16[1280,128]{1,0:T(8,128)...) custom-call(bf16[1024,1024]{1,0:T(8,128)(2,1)S(1)} %get-tuple-element.65.hbuf, ...), custom_call_target="tpu_custom_call" | custom-call | tf_op jit(solution)/shard_map/q_product/pallas_call | solution.py:316
  71.1 1.7 %collective-permute-start.25 = (bf16[1280,128]{1,0:T(8,128)(2,1)S(1)}, bf16[1280,128]{1,0:T(8,128)(2,1)S(1)}, u32[]{:S(2)}, u32[]{:S(2)}) collective-permute-start(bf16[1280,128]{1,0:T(8,128)(2,1)S(1)} %get-tuple-element.80), channel_id=1, source_target_pairs={{0,2},{1,3},{2,0},{3,1},{4,6},{5,7},{6,4},{7,5},{8,10},{9,11},{10,... | collective-permute-start | bytes 983048 | tf_op jit(solution)/shard_map/ppermute | solution.py:51
  73.8 2.3 %collective-permute-start.27 = (bf16[1280,128]{1,0:T(8,128)(2,1)S(1)}, bf16[1280,128]{1,0:T(8,128)(2,1)S(1)}, u32[]{:S(2)}, u32[]{:S(2)}) collective-permute-start(bf16[1280,128]{1,0:T(8,128)(2,1)S(1)} %get-tuple-element.82), channel_id=1, source_target_pairs={{0,3},{1,0},{2,1},{3,2},{4,7},{5,4},{6,5},{7,6},{8,11},{9,8},{10,9... | collective-permute-start | bytes 983048 | tf_op jit(solution)/shard_map/ppermute | solution.py:51
  76.1 3.9 %collective-permute-done.19.b_ref = f32[64,128]{1,0:T(8,128)S(1)} collective-permute-done((f32[64,128]{1,0:T(8,128)S(1)}, f32[64,128]{1,0:T(8,128)S(1)}, u32[]{:S(2)}, u32[]{:S(2)}) %collective-permute-start.19) | collective-permute-done | bytes 32800 | tf_op jit(solution)/shard_map/ppermute | solution.py:31
  80.0 4.8 %collective-permute-done.20.b_ref = f32[64,128]{1,0:T(8,128)S(1)} collective-permute-done((f32[64,128]{1,0:T(8,128)S(1)}, f32[64,128]{1,0:T(8,128)S(1)}, u32[]{:S(2)}, u32[]{:S(2)}) %collective-permute-start.20) | collective-permute-done | bytes 32800 | tf_op jit(solution)/shard_map/ppermute | solution.py:31
  85.6 3.2 %collective-permute-done.21.b_ref = f32[64,128]{1,0:T(8,128)S(1)} collective-permute-done((f32[64,128]{1,0:T(8,128)S(1)}, f32[64,128]{1,0:T(8,128)S(1)}, u32[]{:S(2)}, u32[]{:S(2)}) %collective-permute-start.21) | collective-permute-done | bytes 32800 | tf_op jit(solution)/shard_map/ppermute | solution.py:39
  89.0 1.6 %collective-permute-start.23 = (bf16[960,128]{1,0:T(8,128)(2,1)S(1)}, bf16[960,128]{1,0:T(8,128)(2,1)S(1)}, u32[]{:S(2)}, u32[]{:S(2)}) collective-permute-start(bf16[960,128]{1,0:T(8,128)(2,1)S(1)} %get-tuple-element.77), channel_id=1, source_target_pairs={{0,2},{1,3},{2,0},{3,1},{4,6},{5,7},{6,4},{7,5},{8,10},{9,11},{10,... | collective-permute-start | bytes 737288 | tf_op jit(solution)/shard_map/ppermute | solution.py:51
  92.4 1.7 %collective-permute-start.28 = (bf16[640,128]{1,0:T(8,128)(2,1)S(1)}, bf16[640,128]{1,0:T(8,128)(2,1)S(1)}, u32[]{:S(2)}, u32[]{:S(2)}) collective-permute-start(bf16[640,128]{1,0:T(8,128)(2,1)S(1)} %get-tuple-element.84), channel_id=1, source_target_pairs={{0,4},{4,0},{1,5},{5,1},{2,6},{6,2},{3,7},{7,3},{8,12},{12,8},{9,1... | collective-permute-start | bytes 491528 | tf_op jit(solution)/shard_map/ppermute | solution.py:39
  94.1 4.0 %collective-permute-done.28.refs_5_ = bf16[640,128]{1,0:T(8,128)(2,1)S(1)} collective-permute-done((bf16[640,128]{1,0:T(8,128)(2,1)S(1)}, bf16[640,128]{1,0:T(8,128)(2,1)S(1)}, u32[]{:S(2)}, u32[]{:S(2)}) %collective-permute-start.28) | collective-permute-done | bytes 163872 | tf_op jit(solution)/shard_map/ppermute | solution.py:39
  100.1 5.5 %attention.1 = bf16[1024,128]{1,0:T(8,128)(2,1)} custom-call(s32[8]{0:T(128)S(1)} %copy-done.3, s32[1024]{0:T(1024)S(1)} %copy-done.2, f32[384,128]{1,0:T(8,128)S(1)} %get-tuple-element.75.refs_0_, bf16[960,128]{1,0:T(8,128)(2,1)S(1)} %collective-permute-done.22.refs_1_, bf16[960,128]{1,0:T(8,128)(2,1)S(1)} %collective-permute-done.23.refs_2_, ...), custom_call_target="tpu_custom_call" | custom-call | tf_op jit(solution)/shard_map/attention/pallas_call | solution.py:316
  (62 shorter events, 22.1 us)
Async XLA Ops:
  0.0 16.7 %collective-permute-start.1 = (bf16[1024,128]{1,0:T(8,128)(2,1)}, bf16[1024,128]{1,0:T(8,128)(2,1)S(1)}, u32[]{:S(2)}, u32[]{:S(2)}) collective-permute-start(bf16[1024,128]{1,0:T(8,128)(2,1)} %refs_0_.1), channel_id=1, source_target_pairs={{0,8},{8,16},{16,24},{24,32},{32,40},{40,48},{48,56},{56,0},{1,9},... | collective-permute-start | bytes 786440 | tf_op jit(solution)/shard_map/ppermute | solution.py:27
  1.9 14.7 %collective-permute-start = (bf16[1024,128]{1,0:T(8,128)(2,1)}, bf16[1024,128]{1,0:T(8,128)(2,1)S(1)}, u32[]{:S(2)}, u32[]{:S(2)}) collective-permute-start(bf16[1024,128]{1,0:T(8,128)(2,1)} %refs_0_.1), channel_id=1, source_target_pairs={{0,56},{8,0},{16,8},{24,16},{32,24},{40,32},{48,40},{56,48},{1,57}... | collective-permute-start | bytes 786440 | tf_op jit(solution)/shard_map/ppermute | solution.py:27
  8.0 9.6 %collective-permute-start.4 = (bf16[16,64,128]{2,1,0:T(8,128)(2,1)}, bf16[16,64,128]{2,1,0:T(8,128)(2,1)S(1)}, u32[]{:S(2)}, u32[]{:S(2)}) collective-permute-start(bf16[16,64,128]{2,1,0:T(8,128)(2,1)} %get-tuple-element.50), channel_id=1, source_target_pairs={{0,128},{128,0},{1,129},{129,1},{2,130},{130,2},{3,131},{131,3},{4... | collective-permute-start | bytes 786440 | tf_op jit(solution)/shard_map/ppermute | solution.py:47
  10.2 10.1 %collective-permute-start.2 = (bf16[1280,128]{1,0:T(8,128)(2,1)}, bf16[1280,128]{1,0:T(8,128)(2,1)S(1)}, u32[]{:S(2)}, u32[]{:S(2)}) collective-permute-start(bf16[1280,128]{1,0:T(8,128)(2,1)} %get-tuple-element.46), channel_id=1, source_target_pairs={{0,1},{1,2},{2,3},{3,0},{4,5},{5,6},{6,7},{7,4},{64,67},{65,64},{6... | collective-permute-start | bytes 983048 | tf_op jit(solution)/shard_map/ppermute | solution.py:75
  18.9 14.4 %collective-permute-start.7 = (bf16[1280,128]{1,0:T(8,128)(2,1)}, bf16[1280,128]{1,0:T(8,128)(2,1)S(1)}, u32[]{:S(2)}, u32[]{:S(2)}) collective-permute-start(bf16[1280,128]{1,0:T(8,128)(2,1)} %get-tuple-element.55), channel_id=1, source_target_pairs={{0,4},{1,5},{2,6},{3,7},{4,0},{5,1},{6,2},{7,3},{64,197},{65,198},... | collective-permute-start | bytes 983048 | tf_op jit(solution)/shard_map/ppermute | solution.py:75
  20.3 7.1 %collective-permute-start.5 = (bf16[1024,128]{1,0:T(8,128)(2,1)S(1)}, bf16[1024,128]{1,0:T(8,128)(2,1)S(1)}, u32[]{:S(2)}, u32[]{:S(2)}) collective-permute-start(bf16[1024,128]{1,0:T(8,128)(2,1)S(1)} %collective-permute-done.refs_1_), channel_id=1, source_target_pairs={{0,56},{8,0},{16,8},{24,16},{32,24},{40,32},{48,40},{56,48},{1,57}... | collective-permute-start | bytes 786440 | tf_op jit(solution)/shard_map/ppermute | solution.py:27
  22.0 8.3 %collective-permute-start.6 = (bf16[1024,128]{1,0:T(8,128)(2,1)S(1)}, bf16[1024,128]{1,0:T(8,128)(2,1)S(1)}, u32[]{:S(2)}, u32[]{:S(2)}) collective-permute-start(bf16[1024,128]{1,0:T(8,128)(2,1)S(1)} %collective-permute-done.1.refs_7_), channel_id=1, source_target_pairs={{0,8},{8,16},{16,24},{24,32},{32,40},{40,48},{48,56},{56,0},{1,9},... | collective-permute-start | bytes 786440 | tf_op jit(solution)/shard_map/ppermute | solution.py:27
  23.1 10.1 %collective-permute-start.9 = (bf16[32,1024]{1,0:T(8,128)(2,1)S(1)}, bf16[32,1024]{1,0:T(8,128)(2,1)S(1)}, u32[]{:S(2)}, u32[]{:S(2)}) collective-permute-start(bf16[32,1024]{1,0:T(8,128)(2,1)S(1)} %get-tuple-element.57), channel_id=1, source_target_pairs={{0,32},{8,40},{16,48},{24,56},{32,0},{40,8},{48,16},{56,24},{1,33}... | collective-permute-start | bytes 196616 | tf_op jit(solution)/shard_map/ppermute | solution.py:31
  30.3 12.2 %collective-permute-start.12 = (bf16[1280,128]{1,0:T(8,128)(2,1)S(1)}, bf16[1280,128]{1,0:T(8,128)(2,1)S(1)}, u32[]{:S(2)}, u32[]{:S(2)}) collective-permute-start(bf16[1280,128]{1,0:T(8,128)(2,1)S(1)} %copy-done.5), channel_id=1, source_target_pairs={{0,6},{1,7},{2,4},{3,5},{4,2},{5,3},{6,0},{7,1},{64,199},{65,196},... | collective-permute-start | bytes 983048 | tf_op jit(solution)/shard_map/ppermute | solution.py:75
  33.2 7.9 %collective-permute-start.10 = (bf16[1024,128]{1,0:T(8,128)(2,1)S(1)}, bf16[1024,128]{1,0:T(8,128)(2,1)S(1)}, u32[]{:S(2)}, u32[]{:S(2)}) collective-permute-start(bf16[1024,128]{1,0:T(8,128)(2,1)S(1)} %collective-permute-done.5.refs_2_), channel_id=1, source_target_pairs={{0,56},{8,0},{16,8},{24,16},{32,24},{40,32},{48,40},{56,48},{1,57}... | collective-permute-start | bytes 786440 | tf_op jit(solution)/shard_map/ppermute | solution.py:27
  34.6 7.8 %collective-permute-start.11 = (bf16[1024,128]{1,0:T(8,128)(2,1)S(1)}, bf16[1024,128]{1,0:T(8,128)(2,1)S(1)}, u32[]{:S(2)}, u32[]{:S(2)}) collective-permute-start(bf16[1024,128]{1,0:T(8,128)(2,1)S(1)} %collective-permute-done.6.refs_6_), channel_id=1, source_target_pairs={{0,8},{8,16},{16,24},{24,32},{32,40},{40,48},{48,56},{56,0},{1,9},... | collective-permute-start | bytes 786440 | tf_op jit(solution)/shard_map/ppermute | solution.py:27
  42.5 16.3 %collective-permute-start.14 = (bf16[4,1280,128]{2,1,0:T(8,128)(2,1)S(1)}, bf16[4,1280,128]{2,1,0:T(8,128)(2,1)S(1)}, u32[]{:S(2)}, u32[]{:S(2)}) collective-permute-start(bf16[4,1280,128]{2,1,0:T(8,128)(2,1)S(1)} %stack.13), channel_id=1, source_target_pairs={{0,64},{64,0},{1,65},{65,1},{2,66},{66,2},{3,67},{67,3},{4,68},{68... | collective-permute-start | bytes 3932168 | tf_op jit(solution)/shard_map/ppermute | solution.py:43
  49.4 9.5 %collective-permute-start.13 = (bf16[1024,128]{1,0:T(8,128)(2,1)S(1)}, bf16[1024,128]{1,0:T(8,128)(2,1)S(1)}, u32[]{:S(2)}, u32[]{:S(2)}) collective-permute-start(bf16[1024,128]{1,0:T(8,128)(2,1)S(1)} %collective-permute-done.11.refs_5_), channel_id=1, source_target_pairs={{0,8},{8,16},{16,24},{24,32},{32,40},{40,48},{48,56},{56,0},{1,9},... | collective-permute-start | bytes 786440 | tf_op jit(solution)/shard_map/ppermute | solution.py:27
  60.5 8.2 %collective-permute-start.15 = (bf16[576,128]{1,0:T(8,128)(2,1)S(1)}, bf16[576,128]{1,0:T(8,128)(2,1)S(1)}, u32[]{:S(2)}, u32[]{:S(2)}) collective-permute-start(bf16[576,128]{1,0:T(8,128)(2,1)S(1)} %get-tuple-element.68), channel_id=1, source_target_pairs={{0,2},{1,3},{2,0},{3,1},{4,6},{5,7},{6,4},{7,5},{8,10},{9,11},{10,... | collective-permute-start | bytes 442376 | tf_op jit(solution)/shard_map/ppermute | solution.py:51
  61.7 8.6 %collective-permute-start.16 = (bf16[576,128]{1,0:T(8,128)(2,1)S(1)}, bf16[576,128]{1,0:T(8,128)(2,1)S(1)}, u32[]{:S(2)}, u32[]{:S(2)}) collective-permute-start(bf16[576,128]{1,0:T(8,128)(2,1)S(1)} %get-tuple-element.69), channel_id=1, source_target_pairs={{0,1},{1,2},{2,3},{3,0},{4,5},{5,6},{6,7},{7,4},{8,9},{9,10},{10,1... | collective-permute-start | bytes 442376 | tf_op jit(solution)/shard_map/ppermute | solution.py:51
  61.7 8.6 %collective-permute-start.17 = (bf16[576,128]{1,0:T(8,128)(2,1)S(1)}, bf16[576,128]{1,0:T(8,128)(2,1)S(1)}, u32[]{:S(2)}, u32[]{:S(2)}) collective-permute-start(bf16[576,128]{1,0:T(8,128)(2,1)S(1)} %get-tuple-element.70), channel_id=1, source_target_pairs={{0,3},{1,0},{2,1},{3,2},{4,7},{5,4},{6,5},{7,6},{8,11},{9,8},{10,9... | collective-permute-start | bytes 442376 | tf_op jit(solution)/shard_map/ppermute | solution.py:51
  70.4 18.4 %collective-permute-start.18 = (bf16[2048,128]{1,0:T(8,128)(2,1)S(1)}, bf16[2048,128]{1,0:T(8,128)(2,1)S(1)}, u32[]{:S(2)}, u32[]{:S(2)}) collective-permute-start(bf16[2048,128]{1,0:T(8,128)(2,1)S(1)} %get-tuple-element.72), channel_id=1, source_target_pairs={{0,4},{4,0},{1,5},{5,1},{2,6},{6,2},{3,7},{7,3},{8,12},{12,8},{9,1... | collective-permute-start | bytes 1572872 | tf_op jit(solution)/shard_map/ppermute | solution.py:39
  71.1 19.6 %collective-permute-start.25 = (bf16[1280,128]{1,0:T(8,128)(2,1)S(1)}, bf16[1280,128]{1,0:T(8,128)(2,1)S(1)}, u32[]{:S(2)}, u32[]{:S(2)}) collective-permute-start(bf16[1280,128]{1,0:T(8,128)(2,1)S(1)} %get-tuple-element.80), channel_id=1, source_target_pairs={{0,2},{1,3},{2,0},{3,1},{4,6},{5,7},{6,4},{7,5},{8,10},{9,11},{10,... | collective-permute-start | bytes 983048 | tf_op jit(solution)/shard_map/ppermute | solution.py:51
  72.8 19.4 %collective-permute-start.26 = (bf16[1280,128]{1,0:T(8,128)(2,1)S(1)}, bf16[1280,128]{1,0:T(8,128)(2,1)S(1)}, u32[]{:S(2)}, u32[]{:S(2)}) collective-permute-start(bf16[1280,128]{1,0:T(8,128)(2,1)S(1)} %get-tuple-element.81), channel_id=1, source_target_pairs={{0,1},{1,2},{2,3},{3,0},{4,5},{5,6},{6,7},{7,4},{8,9},{9,10},{10,1... | collective-permute-start | bytes 983048 | tf_op jit(solution)/shard_map/ppermute | solution.py:51
  73.8 18.5 %collective-permute-start.27 = (bf16[1280,128]{1,0:T(8,128)(2,1)S(1)}, bf16[1280,128]{1,0:T(8,128)(2,1)S(1)}, u32[]{:S(2)}, u32[]{:S(2)}) collective-permute-start(bf16[1280,128]{1,0:T(8,128)(2,1)S(1)} %get-tuple-element.82), channel_id=1, source_target_pairs={{0,3},{1,0},{2,1},{3,2},{4,7},{5,4},{6,5},{7,6},{8,11},{9,8},{10,9... | collective-permute-start | bytes 983048 | tf_op jit(solution)/shard_map/ppermute | solution.py:51
  88.9 10.6 %collective-permute-start.22 = (bf16[960,128]{1,0:T(8,128)(2,1)S(1)}, bf16[960,128]{1,0:T(8,128)(2,1)S(1)}, u32[]{:S(2)}, u32[]{:S(2)}) collective-permute-start(bf16[960,128]{1,0:T(8,128)(2,1)S(1)} %get-tuple-element.76), channel_id=1, source_target_pairs={{0,1},{1,2},{2,3},{3,0},{4,5},{5,6},{6,7},{7,4},{8,9},{9,10},{10,1... | collective-permute-start | bytes 737288 | tf_op jit(solution)/shard_map/ppermute | solution.py:51
  89.0 10.5 %collective-permute-start.23 = (bf16[960,128]{1,0:T(8,128)(2,1)S(1)}, bf16[960,128]{1,0:T(8,128)(2,1)S(1)}, u32[]{:S(2)}, u32[]{:S(2)}) collective-permute-start(bf16[960,128]{1,0:T(8,128)(2,1)S(1)} %get-tuple-element.77), channel_id=1, source_target_pairs={{0,2},{1,3},{2,0},{3,1},{4,6},{5,7},{6,4},{7,5},{8,10},{9,11},{10,... | collective-permute-start | bytes 737288 | tf_op jit(solution)/shard_map/ppermute | solution.py:51
  90.7 9.4 %collective-permute-start.24 = (bf16[960,128]{1,0:T(8,128)(2,1)S(1)}, bf16[960,128]{1,0:T(8,128)(2,1)S(1)}, u32[]{:S(2)}, u32[]{:S(2)}) collective-permute-start(bf16[960,128]{1,0:T(8,128)(2,1)S(1)} %get-tuple-element.78), channel_id=1, source_target_pairs={{0,3},{1,0},{2,1},{3,2},{4,7},{5,4},{6,5},{7,6},{8,11},{9,8},{10,9... | collective-permute-start | bytes 737288 | tf_op jit(solution)/shard_map/ppermute | solution.py:51
  92.4 5.6 %collective-permute-start.28 = (bf16[640,128]{1,0:T(8,128)(2,1)S(1)}, bf16[640,128]{1,0:T(8,128)(2,1)S(1)}, u32[]{:S(2)}, u32[]{:S(2)}) collective-permute-start(bf16[640,128]{1,0:T(8,128)(2,1)S(1)} %get-tuple-element.84), channel_id=1, source_target_pairs={{0,4},{4,0},{1,5},{5,1},{2,6},{6,2},{3,7},{7,3},{8,12},{12,8},{9,1... | collective-permute-start | bytes 491528 | tf_op jit(solution)/shard_map/ppermute | solution.py:39
  (11 other events, 126.3 us)

commit v10 on v9

--- a/solution.py
+++ b/solution.py
@@ -113,6 +113,12 @@
 def stack_kernel(*refs):
     for i, ref in enumerate(refs[:-1]):
         refs[-1][i] = ref[...]
+
+
+def split_kernel(a_ref, b_ref, low_half, high_half):
+    half = low_half.shape[0]
+    low_half[...] = a_ref[0:half, :]
+    high_half[...] = b_ref[half:, :]
 
 
 def add_kernel(a_ref, b_ref, out_ref):
@@ -174,12 +180,16 @@
 
 
 def kv_product_kernel(*refs):
-    h_refs, own, mine, other, low_ref = refs[0:8], refs[8], refs[9:13], refs[13], refs[14]
-    outs, hbuf, kvw = refs[15:19], refs[19], refs[20]
+    h_refs, own, mine, other, low_ref = refs[0:9], refs[9], refs[10:14], refs[14], refs[15]
+    outs, hbuf, kvw = refs[16:20], refs[20], refs[21]
     other = [other.at[k] for k in range(4)]
     y = lax.axis_index("y")
-    for j in range(8):
+    for j in range(4):
         hbuf[:, j * 128 : (j + 1) * 128] = h_refs[j][...]
+        if j:
+            hbuf[:, (4 + j) * 128 : (5 + j) * 128] = h_refs[5 + j][...]
+    hbuf[0:512, 512:640] = h_refs[4][...]
+    hbuf[512:1024, 512:640] = h_refs[5][...]
     for dy in range(NY):
         for t in range(2):
             at = pl.multiple_of((((y + dy) & (NY - 1)) * 2 + t) * 128, 128)
@@ -364,28 +374,30 @@
         r, l = ring[-1]
         if len(ring) > 1:
             r, l = after(r, l, *others), after(l, r, *others)
-        ring.append((z_shift(r, 1), z_shift(l, -1) if len(ring) < 4 else None))
+        ring.append((z_shift(r, 1), z_shift(l, -1)))
 
     def added(low, sent):
         return call(add_kernel, "low_add", of(low.shape, f32), low, sent)
 
     ring_step()
-    mine = [weight_send(sends[0], 0), weight_send(after(sends[1], *ring[1]), 1), None, weight_send(sends[3], 3)]
+    mine = [weight_send(sends[0], 0)]
+    mine += [weight_send(after(sends[k], *ring[1]), k) for k in (1, 2)] + [weight_send(sends[3], 3)]
     near = jnp.stack([maps, after(twin, *ring[1])])
-    ring_step(mine[0], mine[3], near)
     far = core_swap(near)
-    mine[2] = weight_send(after(sends[2], *ring[2]), 2)
     low, narrow = call(
         low_kernel, "low", [of((RANK, rows), f32), of((RANK, rows), bf16)], adapters, hidden, near, far, scalars=1
     )
+    ring_step(sends[1], narrow)
     low = added(low, z_xor(narrow, 4))
-    ring_step(mine[1], low)
-    ring_step(mine[2])
-    mine[3] = after(mine[3], *ring[3])
-    other = core_swap(call(stack_kernel, "stack", of((4, 1280, 128), bf16), *mine))
+    mine[3] = after(mine[3], *ring[2])
+    stacked = call(stack_kernel, "stack", of((4, 1280, 128), bf16), *mine)
+    ring_step(stacked)
+    other = core_swap(stacked)
+    halves = call(split_kernel, "split", [of((rows // 2, 128), bf16)] * 2, after(ring[2][0], stacked), ring[2][1])
+    across = [z_shift(halves[0], 2), z_shift(halves[1], -2)]
     right, left = zip(*ring)
 
-    shards = [hidden, left[1], left[2], left[3], right[4], right[3], right[2], right[1]]
+    shards = [hidden, left[1], left[2], left[3], *across, right[3], right[2], right[1]]
     weights = (sends[4], *mine, other)
     *kv_parts, gathered = call(
         kv_product_kernel,

time: 106 us -> 122 us (1.15)
  waiting for transfers between devices: 40.9 us -> 51.4 us
  starting transfers between devices: 47.2 us -> 50.7 us
    ppermute x3, waiting for transfers between devices: 8.72 us -> 18.8 us  [z_xor(): return lax.ppermute(v, 'z', [(i, i ^ s) for i in range(NZ)])]
    ppermute x1, waiting for transfers between devices: 0.89 us -> 5.19 us  [xh_swap(): return lax.ppermute(v, 'xh', [(0, 1), (1, 0)])]
    ppermute x7 -> x8, waiting for transfers between devices: 19.5 us -> 15.8 us  [z_shift(): return lax.ppermute(v, 'z', [(i, (i + s) % NZ) for i in range(NZ)])]
    ppermute x2, starting transfers between devices: 8.04 us -> 10 us  [core_swap(): return lax.ppermute(v, 'c', [(0, 1), (1, 0)])]
    ppermute x3, waiting for transfers between devices: 7.17 us -> 5.38 us  [x_swap(): return lax.ppermute(v, 'xl', [(0, 1), (1, 0)])]
    ppermute x4, waiting for transfers between devices: 0.01 us -> 1.28 us  [weight_send(): return lax.ppermute(v, ('xh', 'c', 'xl', 'y'), route)]
    pallas_call x15 -> x16, Pallas kernels: 17.2 us -> 17.1 us  [call(): pl.pallas_call(kernel, out_shape=outs, in_specs=[SMEM] * scalars + [pl.Bl...]
    ppermute x7 -> x8, starting transfers between devices: 10.1 us -> 10.1 us  [z_shift(): return lax.ppermute(v, 'z', [(i, (i + s) % NZ) for i in range(NZ)])]
  transfers between devices with their start and end apart: 29 -> 30, of which waited for: 13 -> 16; matrix products, arithmetic and copies ran while one was open for 0% -> 0% of each run, Pallas kernels for 9% -> 8%
where the time goes in v10:
time: 122 us; the launch traced here: 120 us
  waiting for transfers between devices  51.4 us (42%)
  starting transfers between devices  50.7 us (42%)
  Pallas kernels  17.1 us (14%)
    ppermute x3, waiting for transfers between devices, z_xor(): return lax.ppermute(v, 'z', [(i, i ^ s) for i in range(NZ)])  18.8 us
    pallas_call x16, Pallas kernels, call(): pl.pallas_call(kernel, out_shape=outs, in_specs=[SMEM] * scalars + [pl.Bl...  17.1 us
    ppermute x8, waiting for transfers between devices, z_shift(): return lax.ppermute(v, 'z', [(i, (i + s) % NZ) for i in range(NZ)])  15.8 us
    ppermute x9, starting transfers between devices, y_shift(): return lax.ppermute(v, 'y', [(i, (i + s) % NY) for i in range(NY)])  13.3 us
    ppermute x8, starting transfers between devices, z_shift(): return lax.ppermute(v, 'z', [(i, (i + s) % NZ) for i in range(NZ)])  10.1 us
    ppermute x2, starting transfers between devices, core_swap(): return lax.ppermute(v, 'c', [(0, 1), (1, 0)])  10 us
    ppermute x4, starting transfers between devices, weight_send(): return lax.ppermute(v, ('xh', 'c', 'xl', 'y'), route)  6.7 us
    ppermute x3, waiting for transfers between devices, x_swap(): return lax.ppermute(v, 'xl', [(0, 1), (1, 0)])  5.38 us
  transfers between devices with their start and end apart: 30, of which 16 were waited for; matrix products, arithmetic and copies ran while one was open for 0% of the time, Pallas kernels for 8%

profile of v10, /device:TPU:2, one launch (start us, length us, event | category | flops | bytes accessed | tf_op | source)
XLA Modules:
  0.0 120.4 jit_solution(793365126330440371)
XLA Ops:
  1.9 4.0 %collective-permute-start = (bf16[1024,128]{1,0:T(8,128)(2,1)}, bf16[1024,128]{1,0:T(8,128)(2,1)S(1)}, u32[]{:S(2)}, u32[]{:S(2)}) collective-permute-start(bf16[1024,128]{1,0:T(8,128)(2,1)} %refs_0_.1), channel_id=1, source_target_pairs={{0,56},{8,0},{16,8},{24,16},{32,24},{40,32},{48,40},{56,48},{1,57}... | collective-permute-start | bytes 786440 | tf_op jit(solution)/shard_map/ppermute | solution.py:27
  5.9 2.0 %pack_first.1 = (bf16[1280,128]{1,0:T(8,128)(2,1)}, bf16[16,64,128]{2,1,0:T(8,128)(2,1)}) custom-call(bf16[8192,128]{1,0:T(8,128)(2,1)} %wq_ref.2, bf16[32,8192]{1,0:T(8,128)(2,1)} %bitcast.4, bf16[16,32,128]{2,1,0:T(8,128)(2,1)} %bitcast.8, bf16[16,32,128]{2,1,0:T(8,128)(2,1)} %up_ref.1), custom_call_target="tpu_custom_call" | custom-call | tf_op jit(solution)/shard_map/pack_first/pallas_call | solution.py:326
  8.0 2.2 %collective-permute-start.2 = (bf16[16,64,128]{2,1,0:T(8,128)(2,1)}, bf16[16,64,128]{2,1,0:T(8,128)(2,1)S(1)}, u32[]{:S(2)}, u32[]{:S(2)}) collective-permute-start(bf16[16,64,128]{2,1,0:T(8,128)(2,1)} %get-tuple-element.52), channel_id=1, source_target_pairs={{0,128},{128,0},{1,129},{129,1},{2,130},{130,2},{3,131},{131,3},{4... | collective-permute-start | bytes 786440 | tf_op jit(solution)/shard_map/ppermute | solution.py:47
  10.2 2.2 %collective-permute-done.1.refs_8_ = bf16[1024,128]{1,0:T(8,128)(2,1)S(1)} collective-permute-done((bf16[1024,128]{1,0:T(8,128)(2,1)}, bf16[1024,128]{1,0:T(8,128)(2,1)S(1)}, u32[]{:S(2)}, u32[]{:S(2)}) %collective-permute-start.1) | collective-permute-done | bytes 262176 | tf_op jit(solution)/shard_map/ppermute | solution.py:27
  12.4 5.2 %collective-permute-done.2 = bf16[16,64,128]{2,1,0:T(8,128)(2,1)S(1)} collective-permute-done((bf16[16,64,128]{2,1,0:T(8,128)(2,1)}, bf16[16,64,128]{2,1,0:T(8,128)(2,1)S(1)}, u32[]{:S(2)}, u32[]{:S(2)}) %collective-permute-start.2) | collective-permute-done | bytes 262176 | tf_op jit(solution)/shard_map/ppermute | solution.py:47
  19.7 3.0 %pack.1 = (bf16[1280,128]{1,0:T(8,128)(2,1)}, bf16[1280,128]{1,0:T(8,128)(2,1)}, bf16[1280,128]{1,0:T(8,128)(2,1)}, bf16[1280,128]{1,0:T(8,128)(2,1)}) custom-call(bf16[8192,128]{1,0:T(8,128)(2,1)} %wq_ref.2, bf16[32,8192]{1,0:T(8,128)(2,1)} %bitcast.5), custom_call_target="tpu_custom_call" | custom-call | tf_op jit(solution)/shard_map/pack/pallas_call | solution.py:326
  25.6 3.8 %collective-permute-start.8 = (bf16[1280,128]{1,0:T(8,128)(2,1)}, bf16[1280,128]{1,0:T(8,128)(2,1)S(1)}, u32[]{:S(2)}, u32[]{:S(2)}) collective-permute-start(bf16[1280,128]{1,0:T(8,128)(2,1)} %get-tuple-element.59), channel_id=1, source_target_pairs={{0,6},{1,7},{2,4},{3,5},{4,2},{5,3},{6,0},{7,1},{64,199},{65,196},... | collective-permute-start | bytes 983048 | tf_op jit(solution)/shard_map/ppermute | solution.py:75
  32.3 5.0 %collective-permute-done.4.b_ref.refs_2_ = bf16[1024,128]{1,0:T(8,128)(2,1)S(1)} collective-permute-done((bf16[1024,128]{1,0:T(8,128)(2,1)S(1)}, bf16[1024,128]{1,0:T(8,128)(2,1)S(1)}, u32[]{:S(2)}, u32[]{:S(2)}) %collective-permute-start.4) | collective-permute-done | bytes 262176 | tf_op jit(solution)/shard_map/ppermute | solution.py:27
  37.3 2.2 %collective-permute-done.5.a_ref.refs_7_ = bf16[1024,128]{1,0:T(8,128)(2,1)S(1)} collective-permute-done((bf16[1024,128]{1,0:T(8,128)(2,1)S(1)}, bf16[1024,128]{1,0:T(8,128)(2,1)S(1)}, u32[]{:S(2)}, u32[]{:S(2)}) %collective-permute-start.5) | collective-permute-done | bytes 262176 | tf_op jit(solution)/shard_map/ppermute | solution.py:27
  40.9 9.9 %collective-permute-start.14 = (bf16[4,1280,128]{2,1,0:T(8,128)(2,1)S(1)}, bf16[4,1280,128]{2,1,0:T(8,128)(2,1)S(1)}, u32[]{:S(2)}, u32[]{:S(2)}) collective-permute-start(bf16[4,1280,128]{2,1,0:T(8,128)(2,1)S(1)} %stack.13), channel_id=1, source_target_pairs={{0,64},{64,0},{1,65},{65,1},{2,66},{66,2},{3,67},{67,3},{4,68},{68... | collective-permute-start | bytes 3932168 | tf_op jit(solution)/shard_map/ppermute | solution.py:43
  52.9 4.2 %collective-permute-start.15 = (bf16[32,1024]{1,0:T(8,128)(2,1)S(1)}, bf16[32,1024]{1,0:T(8,128)(2,1)S(1)}, u32[]{:S(2)}, u32[]{:S(2)}) collective-permute-start(bf16[32,1024]{1,0:T(8,128)(2,1)S(1)} %get-tuple-element.54), channel_id=1, source_target_pairs={{0,32},{8,40},{16,48},{24,56},{32,0},{40,8},{48,16},{56,24},{1,33}... | collective-permute-start | bytes 196616 | tf_op jit(solution)/shard_map/ppermute | solution.py:31
  57.2 10.1 %collective-permute-done.15.b_ref = bf16[32,1024]{1,0:T(8,128)(2,1)S(1)} collective-permute-done((bf16[32,1024]{1,0:T(8,128)(2,1)S(1)}, bf16[32,1024]{1,0:T(8,128)(2,1)S(1)}, u32[]{:S(2)}, u32[]{:S(2)}) %collective-permute-start.15) | collective-permute-done | bytes 65568 | tf_op jit(solution)/shard_map/ppermute | solution.py:31
  67.3 6.4 %collective-permute-done.12.refs_5_ = bf16[512,128]{1,0:T(8,128)(2,1)S(1)} collective-permute-done((bf16[512,128]{1,0:T(8,128)(2,1)S(1)}, bf16[512,128]{1,0:T(8,128)(2,1)S(1)}, u32[]{:S(2)}, u32[]{:S(2)}) %collective-permute-start.12) | collective-permute-done | bytes 131104 | tf_op jit(solution)/shard_map/ppermute | solution.py:27
  75.4 3.2 %collective-permute-start.18 = (bf16[576,128]{1,0:T(8,128)(2,1)S(1)}, bf16[576,128]{1,0:T(8,128)(2,1)S(1)}, u32[]{:S(2)}, u32[]{:S(2)}) collective-permute-start(bf16[576,128]{1,0:T(8,128)(2,1)S(1)} %get-tuple-element.74), channel_id=1, source_target_pairs={{0,3},{1,0},{2,1},{3,2},{4,7},{5,4},{6,5},{7,6},{8,11},{9,8},{10,9... | collective-permute-start | bytes 442376 | tf_op jit(solution)/shard_map/ppermute | solution.py:51
  78.6 2.7 %q_product.1 = (bf16[1536,128]{1,0:T(8,128)(2,1)S(1)}, bf16[1536,128]{1,0:T(8,128)(2,1)S(1)}, bf16[1280,128]{1,0:T(8,128)(2,1)S(1)}, bf16[1280,128]{1,0:T(8,128)...) custom-call(bf16[1024,1024]{1,0:T(8,128)(2,1)S(1)} %get-tuple-element.69.hbuf, ...), custom_call_target="tpu_custom_call" | custom-call | tf_op jit(solution)/shard_map/q_product/pallas_call | solution.py:326
  85.0 2.7 %collective-permute-start.26 = (bf16[1280,128]{1,0:T(8,128)(2,1)S(1)}, bf16[1280,128]{1,0:T(8,128)(2,1)S(1)}, u32[]{:S(2)}, u32[]{:S(2)}) collective-permute-start(bf16[1280,128]{1,0:T(8,128)(2,1)S(1)} %get-tuple-element.84), channel_id=1, source_target_pairs={{0,2},{1,3},{2,0},{3,1},{4,6},{5,7},{6,4},{7,5},{8,10},{9,11},{10,... | collective-permute-start | bytes 983048 | tf_op jit(solution)/shard_map/ppermute | solution.py:51
  87.7 2.0 %collective-permute-start.27 = (bf16[1280,128]{1,0:T(8,128)(2,1)S(1)}, bf16[1280,128]{1,0:T(8,128)(2,1)S(1)}, u32[]{:S(2)}, u32[]{:S(2)}) collective-permute-start(bf16[1280,128]{1,0:T(8,128)(2,1)S(1)} %get-tuple-element.85), channel_id=1, source_target_pairs={{0,1},{1,2},{2,3},{3,0},{4,5},{5,6},{6,7},{7,4},{8,9},{9,10},{10,1... | collective-permute-start | bytes 983048 | tf_op jit(solution)/shard_map/ppermute | solution.py:51
  91.0 3.9 %collective-permute-done.20.b_ref = f32[64,128]{1,0:T(8,128)S(1)} collective-permute-done((f32[64,128]{1,0:T(8,128)S(1)}, f32[64,128]{1,0:T(8,128)S(1)}, u32[]{:S(2)}, u32[]{:S(2)}) %collective-permute-start.20) | collective-permute-done | bytes 32800 | tf_op jit(solution)/shard_map/ppermute | solution.py:31
  94.9 4.8 %collective-permute-done.21.b_ref = f32[64,128]{1,0:T(8,128)S(1)} collective-permute-done((f32[64,128]{1,0:T(8,128)S(1)}, f32[64,128]{1,0:T(8,128)S(1)}, u32[]{:S(2)}, u32[]{:S(2)}) %collective-permute-start.21) | collective-permute-done | bytes 32800 | tf_op jit(solution)/shard_map/ppermute | solution.py:31
  101.7 2.0 %collective-permute-done.22.b_ref = f32[64,128]{1,0:T(8,128)S(1)} collective-permute-done((f32[64,128]{1,0:T(8,128)S(1)}, f32[64,128]{1,0:T(8,128)S(1)}, u32[]{:S(2)}, u32[]{:S(2)}) %collective-permute-start.22) | collective-permute-done | bytes 32800 | tf_op jit(solution)/shard_map/ppermute | solution.py:39
  104.7 2.5 %collective-permute-start.24 = (bf16[960,128]{1,0:T(8,128)(2,1)S(1)}, bf16[960,128]{1,0:T(8,128)(2,1)S(1)}, u32[]{:S(2)}, u32[]{:S(2)}) collective-permute-start(bf16[960,128]{1,0:T(8,128)(2,1)S(1)} %get-tuple-element.81), channel_id=1, source_target_pairs={{0,2},{1,3},{2,0},{3,1},{4,6},{5,7},{6,4},{7,5},{8,10},{9,11},{10,... | collective-permute-start | bytes 737288 | tf_op jit(solution)/shard_map/ppermute | solution.py:51
  108.0 2.0 %collective-permute-start.29 = (bf16[640,128]{1,0:T(8,128)(2,1)S(1)}, bf16[640,128]{1,0:T(8,128)(2,1)S(1)}, u32[]{:S(2)}, u32[]{:S(2)}) collective-permute-start(bf16[640,128]{1,0:T(8,128)(2,1)S(1)} %get-tuple-element.88), channel_id=1, source_target_pairs={{0,4},{4,0},{1,5},{5,1},{2,6},{6,2},{3,7},{7,3},{8,12},{12,8},{9,1... | collective-permute-start | bytes 491528 | tf_op jit(solution)/shard_map/ppermute | solution.py:39
  110.0 3.4 %collective-permute-done.29.refs_5_ = bf16[640,128]{1,0:T(8,128)(2,1)S(1)} collective-permute-done((bf16[640,128]{1,0:T(8,128)(2,1)S(1)}, bf16[640,128]{1,0:T(8,128)(2,1)S(1)}, u32[]{:S(2)}, u32[]{:S(2)}) %collective-permute-start.29) | collective-permute-done | bytes 163872 | tf_op jit(solution)/shard_map/ppermute | solution.py:39
  114.8 5.5 %attention.1 = bf16[1024,128]{1,0:T(8,128)(2,1)} custom-call(s32[8]{0:T(128)S(1)} %copy-done.3, s32[1024]{0:T(1024)S(1)} %copy-done.2, f32[384,128]{1,0:T(8,128)S(1)} %get-tuple-element.79.refs_0_, bf16[960,128]{1,0:T(8,128)(2,1)S(1)} %collective-permute-done.23.refs_1_, bf16[960,128]{1,0:T(8,128)(2,1)S(1)} %collective-permute-done.24.refs_2_, ...), custom_call_target="tpu_custom_call" | custom-call | tf_op jit(solution)/shard_map/attention/pallas_call | solution.py:326
  (63 shorter events, 25.1 us)
Async XLA Ops:
  0.0 12.4 %collective-permute-start.1 = (bf16[1024,128]{1,0:T(8,128)(2,1)}, bf16[1024,128]{1,0:T(8,128)(2,1)S(1)}, u32[]{:S(2)}, u32[]{:S(2)}) collective-permute-start(bf16[1024,128]{1,0:T(8,128)(2,1)} %refs_0_.1), channel_id=1, source_target_pairs={{0,8},{8,16},{16,24},{24,32},{32,40},{40,48},{48,56},{56,0},{1,9},... | collective-permute-start | bytes 786440 | tf_op jit(solution)/shard_map/ppermute | solution.py:27
  1.9 10.5 %collective-permute-start = (bf16[1024,128]{1,0:T(8,128)(2,1)}, bf16[1024,128]{1,0:T(8,128)(2,1)S(1)}, u32[]{:S(2)}, u32[]{:S(2)}) collective-permute-start(bf16[1024,128]{1,0:T(8,128)(2,1)} %refs_0_.1), channel_id=1, source_target_pairs={{0,56},{8,0},{16,8},{24,16},{32,24},{40,32},{48,40},{56,48},{1,57}... | collective-permute-start | bytes 786440 | tf_op jit(solution)/shard_map/ppermute | solution.py:27
  8.0 9.6 %collective-permute-start.2 = (bf16[16,64,128]{2,1,0:T(8,128)(2,1)}, bf16[16,64,128]{2,1,0:T(8,128)(2,1)S(1)}, u32[]{:S(2)}, u32[]{:S(2)}) collective-permute-start(bf16[16,64,128]{2,1,0:T(8,128)(2,1)} %get-tuple-element.52), channel_id=1, source_target_pairs={{0,128},{128,0},{1,129},{129,1},{2,130},{130,2},{3,131},{131,3},{4... | collective-permute-start | bytes 786440 | tf_op jit(solution)/shard_map/ppermute | solution.py:47
  18.6 10.8 %collective-permute-start.3 = (bf16[2,16,64,128]{3,2,1,0:T(8,128)(2,1)S(1)}, bf16[2,16,64,128]{3,2,1,0:T(8,128)(2,1)S(1)}, u32[]{:S(2)}, u32[]{:S(2)}) collective-permute-start(bf16[2,16,64,128]{3,2,1,0:T(8,128)(2,1)S(1)} %pad_maximum_fusion.near_ref.refs_7_), channel_id=1, source_target_pairs={{0,64},{64,0},{1,65},{65,1},{2,66},{66,2},{3,67},{67,3},{4,68},{68... | collective-permute-start | bytes 1572872 | tf_op jit(solution)/shard_map/ppermute | solution.py:43
  22.7 9.3 %collective-permute-start.9 = (bf16[1280,128]{1,0:T(8,128)(2,1)}, bf16[1280,128]{1,0:T(8,128)(2,1)S(1)}, u32[]{:S(2)}, u32[]{:S(2)}) collective-permute-start(bf16[1280,128]{1,0:T(8,128)(2,1)} %get-tuple-element.60), channel_id=1, source_target_pairs={{64,66},{65,67},{66,64},{67,65},{68,70},{69,71},{70,68},{71,69},{1... | collective-permute-start | bytes 983048 | tf_op jit(solution)/shard_map/ppermute | solution.py:75
  23.4 16.1 %collective-permute-start.6 = (bf16[1280,128]{1,0:T(8,128)(2,1)S(1)}, bf16[1280,128]{1,0:T(8,128)(2,1)S(1)}, u32[]{:S(2)}, u32[]{:S(2)}) collective-permute-start(bf16[1280,128]{1,0:T(8,128)(2,1)S(1)} %copy-done.4), channel_id=1, source_target_pairs={{0,1},{1,2},{2,3},{3,0},{4,5},{5,6},{6,7},{7,4},{64,67},{65,64},{6... | collective-permute-start | bytes 983048 | tf_op jit(solution)/shard_map/ppermute | solution.py:75
  25.1 14.5 %collective-permute-start.7 = (bf16[1280,128]{1,0:T(8,128)(2,1)}, bf16[1280,128]{1,0:T(8,128)(2,1)S(1)}, u32[]{:S(2)}, u32[]{:S(2)}) collective-permute-start(bf16[1280,128]{1,0:T(8,128)(2,1)} %get-tuple-element.57), channel_id=1, source_target_pairs={{0,4},{1,5},{2,6},{3,7},{4,0},{5,1},{6,2},{7,3},{64,197},{65,198},... | collective-permute-start | bytes 983048 | tf_op jit(solution)/shard_map/ppermute | solution.py:75
  25.6 15.2 %collective-permute-start.8 = (bf16[1280,128]{1,0:T(8,128)(2,1)}, bf16[1280,128]{1,0:T(8,128)(2,1)S(1)}, u32[]{:S(2)}, u32[]{:S(2)}) collective-permute-start(bf16[1280,128]{1,0:T(8,128)(2,1)} %get-tuple-element.59), channel_id=1, source_target_pairs={{0,6},{1,7},{2,4},{3,5},{4,2},{5,3},{6,0},{7,1},{64,199},{65,196},... | collective-permute-start | bytes 983048 | tf_op jit(solution)/shard_map/ppermute | solution.py:75
  30.2 7.1 %collective-permute-start.4 = (bf16[1024,128]{1,0:T(8,128)(2,1)S(1)}, bf16[1024,128]{1,0:T(8,128)(2,1)S(1)}, u32[]{:S(2)}, u32[]{:S(2)}) collective-permute-start(bf16[1024,128]{1,0:T(8,128)(2,1)S(1)} %collective-permute-done.refs_1_), channel_id=1, source_target_pairs={{0,56},{8,0},{16,8},{24,16},{32,24},{40,32},{48,40},{56,48},{1,57}... | collective-permute-start | bytes 786440 | tf_op jit(solution)/shard_map/ppermute | solution.py:27
  32.0 7.6 %collective-permute-start.5 = (bf16[1024,128]{1,0:T(8,128)(2,1)S(1)}, bf16[1024,128]{1,0:T(8,128)(2,1)S(1)}, u32[]{:S(2)}, u32[]{:S(2)}) collective-permute-start(bf16[1024,128]{1,0:T(8,128)(2,1)S(1)} %collective-permute-done.1.refs_8_), channel_id=1, source_target_pairs={{0,8},{8,16},{16,24},{24,32},{32,40},{40,48},{48,56},{56,0},{1,9},... | collective-permute-start | bytes 786440 | tf_op jit(solution)/shard_map/ppermute | solution.py:27
  40.9 32.8 %collective-permute-start.14 = (bf16[4,1280,128]{2,1,0:T(8,128)(2,1)S(1)}, bf16[4,1280,128]{2,1,0:T(8,128)(2,1)S(1)}, u32[]{:S(2)}, u32[]{:S(2)}) collective-permute-start(bf16[4,1280,128]{2,1,0:T(8,128)(2,1)S(1)} %stack.13), channel_id=1, source_target_pairs={{0,64},{64,0},{1,65},{65,1},{2,66},{66,2},{3,67},{67,3},{4,68},{68... | collective-permute-start | bytes 3932168 | tf_op jit(solution)/shard_map/ppermute | solution.py:43
  50.8 22.9 %collective-permute-start.10 = (bf16[1024,128]{1,0:T(8,128)(2,1)S(1)}, bf16[1024,128]{1,0:T(8,128)(2,1)S(1)}, u32[]{:S(2)}, u32[]{:S(2)}) collective-permute-start(bf16[1024,128]{1,0:T(8,128)(2,1)S(1)} %collective-permute-done.4.b_ref.refs_2_), channel_id=1, source_target_pairs={{0,56},{8,0},{16,8},{24,16},{32,24},{40,32},{48,40},{56,48},{1,57}... | collective-permute-start | bytes 786440 | tf_op jit(solution)/shard_map/ppermute | solution.py:27
  51.3 22.4 %collective-permute-start.13 = (bf16[1024,128]{1,0:T(8,128)(2,1)S(1)}, bf16[1024,128]{1,0:T(8,128)(2,1)S(1)}, u32[]{:S(2)}, u32[]{:S(2)}) collective-permute-start(bf16[1024,128]{1,0:T(8,128)(2,1)S(1)} %collective-permute-done.5.a_ref.refs_7_), channel_id=1, source_target_pairs={{0,8},{8,16},{16,24},{24,32},{32,40},{40,48},{48,56},{56,0},{1,9},... | collective-permute-start | bytes 786440 | tf_op jit(solution)/shard_map/ppermute | solution.py:27
  52.9 14.4 %collective-permute-start.15 = (bf16[32,1024]{1,0:T(8,128)(2,1)S(1)}, bf16[32,1024]{1,0:T(8,128)(2,1)S(1)}, u32[]{:S(2)}, u32[]{:S(2)}) collective-permute-start(bf16[32,1024]{1,0:T(8,128)(2,1)S(1)} %get-tuple-element.54), channel_id=1, source_target_pairs={{0,32},{8,40},{16,48},{24,56},{32,0},{40,8},{48,16},{56,24},{1,33}... | collective-permute-start | bytes 196616 | tf_op jit(solution)/shard_map/ppermute | solution.py:31
  57.1 10.2 %collective-permute-start.11 = (bf16[512,128]{1,0:T(8,128)(2,1)S(1)}, bf16[512,128]{1,0:T(8,128)(2,1)S(1)}, u32[]{:S(2)}, u32[]{:S(2)}) collective-permute-start(bf16[512,128]{1,0:T(8,128)(2,1)S(1)} %get-tuple-element.64), channel_id=1, source_target_pairs={{0,16},{8,24},{16,32},{24,40},{32,48},{40,56},{48,0},{56,8},{1,17}... | collective-permute-start | bytes 393224 | tf_op jit(solution)/shard_map/ppermute | solution.py:27
  75.3 8.0 %collective-permute-start.17 = (bf16[576,128]{1,0:T(8,128)(2,1)S(1)}, bf16[576,128]{1,0:T(8,128)(2,1)S(1)}, u32[]{:S(2)}, u32[]{:S(2)}) collective-permute-start(bf16[576,128]{1,0:T(8,128)(2,1)S(1)} %get-tuple-element.73), channel_id=1, source_target_pairs={{0,1},{1,2},{2,3},{3,0},{4,5},{5,6},{6,7},{7,4},{8,9},{9,10},{10,1... | collective-permute-start | bytes 442376 | tf_op jit(solution)/shard_map/ppermute | solution.py:51
  75.4 9.4 %collective-permute-start.18 = (bf16[576,128]{1,0:T(8,128)(2,1)S(1)}, bf16[576,128]{1,0:T(8,128)(2,1)S(1)}, u32[]{:S(2)}, u32[]{:S(2)}) collective-permute-start(bf16[576,128]{1,0:T(8,128)(2,1)S(1)} %get-tuple-element.74), channel_id=1, source_target_pairs={{0,3},{1,0},{2,1},{3,2},{4,7},{5,4},{6,5},{7,6},{8,11},{9,8},{10,9... | collective-permute-start | bytes 442376 | tf_op jit(solution)/shard_map/ppermute | solution.py:51
  84.9 18.7 %collective-permute-start.19 = (bf16[2048,128]{1,0:T(8,128)(2,1)S(1)}, bf16[2048,128]{1,0:T(8,128)(2,1)S(1)}, u32[]{:S(2)}, u32[]{:S(2)}) collective-permute-start(bf16[2048,128]{1,0:T(8,128)(2,1)S(1)} %get-tuple-element.76), channel_id=1, source_target_pairs={{0,4},{4,0},{1,5},{5,1},{2,6},{6,2},{3,7},{7,3},{8,12},{12,8},{9,1... | collective-permute-start | bytes 1572872 | tf_op jit(solution)/shard_map/ppermute | solution.py:39
  85.0 22.2 %collective-permute-start.26 = (bf16[1280,128]{1,0:T(8,128)(2,1)S(1)}, bf16[1280,128]{1,0:T(8,128)(2,1)S(1)}, u32[]{:S(2)}, u32[]{:S(2)}) collective-permute-start(bf16[1280,128]{1,0:T(8,128)(2,1)S(1)} %get-tuple-element.84), channel_id=1, source_target_pairs={{0,2},{1,3},{2,0},{3,1},{4,6},{5,7},{6,4},{7,5},{8,10},{9,11},{10,... | collective-permute-start | bytes 983048 | tf_op jit(solution)/shard_map/ppermute | solution.py:51
  87.7 20.1 %collective-permute-start.27 = (bf16[1280,128]{1,0:T(8,128)(2,1)S(1)}, bf16[1280,128]{1,0:T(8,128)(2,1)S(1)}, u32[]{:S(2)}, u32[]{:S(2)}) collective-permute-start(bf16[1280,128]{1,0:T(8,128)(2,1)S(1)} %get-tuple-element.85), channel_id=1, source_target_pairs={{0,1},{1,2},{2,3},{3,0},{4,5},{5,6},{6,7},{7,4},{8,9},{9,10},{10,1... | collective-permute-start | bytes 983048 | tf_op jit(solution)/shard_map/ppermute | solution.py:51
  89.8 18.0 %collective-permute-start.28 = (bf16[1280,128]{1,0:T(8,128)(2,1)S(1)}, bf16[1280,128]{1,0:T(8,128)(2,1)S(1)}, u32[]{:S(2)}, u32[]{:S(2)}) collective-permute-start(bf16[1280,128]{1,0:T(8,128)(2,1)S(1)} %get-tuple-element.86), channel_id=1, source_target_pairs={{0,3},{1,0},{2,1},{3,2},{4,7},{5,4},{6,5},{7,6},{8,11},{9,8},{10,9... | collective-permute-start | bytes 983048 | tf_op jit(solution)/shard_map/ppermute | solution.py:51
  103.8 9.5 %collective-permute-start.23 = (bf16[960,128]{1,0:T(8,128)(2,1)S(1)}, bf16[960,128]{1,0:T(8,128)(2,1)S(1)}, u32[]{:S(2)}, u32[]{:S(2)}) collective-permute-start(bf16[960,128]{1,0:T(8,128)(2,1)S(1)} %get-tuple-element.80), channel_id=1, source_target_pairs={{0,1},{1,2},{2,3},{3,0},{4,5},{5,6},{6,7},{7,4},{8,9},{9,10},{10,1... | collective-permute-start | bytes 737288 | tf_op jit(solution)/shard_map/ppermute | solution.py:51
  104.7 9.3 %collective-permute-start.24 = (bf16[960,128]{1,0:T(8,128)(2,1)S(1)}, bf16[960,128]{1,0:T(8,128)(2,1)S(1)}, u32[]{:S(2)}, u32[]{:S(2)}) collective-permute-start(bf16[960,128]{1,0:T(8,128)(2,1)S(1)} %get-tuple-element.81), channel_id=1, source_target_pairs={{0,2},{1,3},{2,0},{3,1},{4,6},{5,7},{6,4},{7,5},{8,10},{9,11},{10,... | collective-permute-start | bytes 737288 | tf_op jit(solution)/shard_map/ppermute | solution.py:51
  107.2 7.7 %collective-permute-start.25 = (bf16[960,128]{1,0:T(8,128)(2,1)S(1)}, bf16[960,128]{1,0:T(8,128)(2,1)S(1)}, u32[]{:S(2)}, u32[]{:S(2)}) collective-permute-start(bf16[960,128]{1,0:T(8,128)(2,1)S(1)} %get-tuple-element.82), channel_id=1, source_target_pairs={{0,3},{1,0},{2,1},{3,2},{4,7},{5,4},{6,5},{7,6},{8,11},{9,8},{10,9... | collective-permute-start | bytes 737288 | tf_op jit(solution)/shard_map/ppermute | solution.py:51
  (11 other events, 156.9 us)

commit v11 on v9

--- a/solution.py
+++ b/solution.py
@@ -119,7 +119,7 @@
     out_ref[...] = a_ref[...] + b_ref[...].astype(jnp.float32)
 
 
-def rope_kernel(start_ref, cos_ref, sin_ref):
+def rope_kernel(start_ref, cos_ref, sin_ref, cos_t_ref, sin_t_ref):
     half = HEAD_SIZE // 2
     lane = lax.broadcasted_iota(jnp.int32, (BLOCK, HEAD_SIZE), 1)
     row = lax.broadcasted_iota(jnp.int32, (BLOCK, HEAD_SIZE), 0)
@@ -140,6 +140,8 @@
         rows = slice(b * BLOCK, (b + 1) * BLOCK)
         cos_ref[rows, :] = cos_in * co - sin_in * so
         sin_ref[rows, :] = (sin_in * co + cos_in * so) * sign
+        cos_t_ref[:, rows] = cos_ref[rows, :].T
+        sin_t_ref[:, rows] = sin_ref[rows, :].T
 
 
 def low_kernel(ad_ref, h_ref, near_ref, far_ref, out_ref, narrow_ref):
@@ -255,9 +257,9 @@
 
 def attention_kernel(ad_ref, start_ref, *refs):
     a_own, a_got, b_own, b_got, kv_own = refs[0], refs[1:4], refs[4], refs[5], refs[6]
-    near_ref, far_ref, cos_ref, sin_ref = refs[7:11]
-    out_ref = refs[11]
-    kvt, k_buf, v_buf, low_buf = refs[12:16]
+    near_ref, far_ref, cos_ref, sin_ref, cos_t_ref, sin_t_ref = refs[7:13]
+    out_ref = refs[13]
+    kvt, k_buf, v_buf, low_buf = refs[14:18]
     xl, y, c, xh = (lax.axis_index(a) for a in ("xl", "y", "c", "xh"))
     first = (xh * NC + c) * 8
     for i in range(NY):
@@ -275,8 +277,9 @@
 
     for t in range(8):
         rows = slice(t * 128, (t + 1) * 128)
-        k = kvt[0:128, rows].astype(jnp.float32).T
-        k_buf[rows, :] = rope(k, rows).astype(jnp.bfloat16)
+        k = kvt[0:128, rows].astype(jnp.float32)
+        turned = jnp.concatenate([k[64:128, :], k[0:64, :]], axis=0)
+        k_buf[:, rows] = (k * cos_t_ref[:, rows] + turned * sin_t_ref[:, rows]).astype(jnp.bfloat16)
         v_buf[rows, :] = kvt[128:256, rows].T
     per = near_ref.shape[1]
     factor = math.log2(math.e) / math.sqrt(HEAD_SIZE)
@@ -299,9 +302,7 @@
             q += b_own[part, :] + wide(b_got, part)
         q = rope(q, rows).astype(jnp.bfloat16)
         n = (b + 1) * 128
-        s = lax.dot_general(
-            q, k_buf[0:n, :], (((1,), (1,)), ((), ())), preferred_element_type=jnp.float32
-        )
+        s = jnp.dot(q, k_buf[:, 0:n], preferred_element_type=jnp.float32)
         col = lax.broadcasted_iota(jnp.int32, (128, n), 1)
         row = lax.broadcasted_iota(jnp.int32, (128, n), 0) + b * 128
         allowed = (col >= (start_ref[b * BLOCK] - first) * BLOCK) & (col <= row)
@@ -345,7 +346,13 @@
         space=pltpu.HBM,
         mib=PACK_MIB,
     )
-    cosines, sines = call(rope_kernel, "rope", [of((rows, HEAD_SIZE), f32)] * 2, request_start, scalars=1)
+    cosines, *turns = call(
+        rope_kernel,
+        "rope",
+        [of((rows, HEAD_SIZE), f32)] * 2 + [of((HEAD_SIZE, rows), f32)] * 2,
+        request_start,
+        scalars=1,
+    )
     sends = call(
         pack_kernel,
         "pack",
@@ -370,16 +377,16 @@
         return call(add_kernel, "low_add", of(low.shape, f32), low, sent)
 
     ring_step()
-    mine = [weight_send(sends[0], 0), weight_send(after(sends[1], *ring[1]), 1), None, weight_send(sends[3], 3)]
+    mine = [weight_send(after(sends[0], sends[1]), 0), weight_send(after(sends[1], *ring[1]), 1), None, weight_send(sends[3], 3)]
     near = jnp.stack([maps, after(twin, *ring[1])])
-    ring_step(mine[0], mine[3], near)
+    ring_step(mine[0], near)
     far = core_swap(near)
     mine[2] = weight_send(after(sends[2], *ring[2]), 2)
     low, narrow = call(
         low_kernel, "low", [of((RANK, rows), f32), of((RANK, rows), bf16)], adapters, hidden, near, far, scalars=1
     )
     low = added(low, z_xor(narrow, 4))
-    ring_step(mine[1], low)
+    ring_step(mine[1], mine[3], low)
     ring_step(mine[2])
     mine[3] = after(mine[3], *ring[3])
     other = core_swap(call(stack_kernel, "stack", of((4, 1280, 128), bf16), *mine))
@@ -449,9 +456,9 @@
         near,
         far,
         cosines,
-        sines,
+        *turns,
         scalars=2,
-        scratch=[pltpu.VMEM((256, rows), bf16)] + [pltpu.VMEM((rows, HEAD_SIZE), bf16)] * 2 + [pltpu.VMEM((8, RANK, 128), bf16)],
+        scratch=[pltpu.VMEM((256, rows), bf16)] + [pltpu.VMEM((HEAD_SIZE, rows), bf16), pltpu.VMEM((rows, HEAD_SIZE), bf16)] + [pltpu.VMEM((8, RANK, 128), bf16)],
         mib=8,
     )
 

time: 106 us -> 107 us (level)
  waiting for transfers between devices: 40.9 us -> 50 us
  starting transfers between devices: 47.2 us -> 39.7 us
    ppermute x2, starting transfers between devices: 8.04 us -> 0.19 us  [core_swap(): return lax.ppermute(v, 'c', [(0, 1), (1, 0)])]
    ppermute x7, waiting for transfers between devices: 19.5 us -> 23.1 us  [z_shift(): return lax.ppermute(v, 'z', [(i, (i + s) % NZ) for i in range(NZ)])]
    ppermute x4, waiting for transfers between devices: 0.01 us -> 3.66 us  [weight_send(): return lax.ppermute(v, ('xh', 'c', 'xl', 'y'), route)]
    ppermute x3, waiting for transfers between devices: 7.17 us -> 8.53 us  [x_swap(): return lax.ppermute(v, 'xl', [(0, 1), (1, 0)])]
  transfers between devices with their start and end apart: 29 -> 29, of which waited for: 13 -> 15; matrix products, arithmetic and copies ran while one was open for 0% -> 0% of each run, Pallas kernels for 9% -> 9%
where the time goes in v11:
time: 107 us
  waiting for transfers between devices  50 us (47%)
  starting transfers between devices  39.7 us (37%)
  Pallas kernels  17.1 us (16%)
    ppermute x7, waiting for transfers between devices, z_shift(): return lax.ppermute(v, 'z', [(i, (i + s) % NZ) for i in range(NZ)])  23.1 us
    pallas_call x15, Pallas kernels, call(): pl.pallas_call(kernel, out_shape=outs, in_specs=[SMEM] * scalars + [pl.Bl...  17.1 us
    ppermute x9, starting transfers between devices, y_shift(): return lax.ppermute(v, 'y', [(i, (i + s) % NY) for i in range(NY)])  13.7 us
    ppermute x7, starting transfers between devices, z_shift(): return lax.ppermute(v, 'z', [(i, (i + s) % NZ) for i in range(NZ)])  10.6 us
    ppermute x3, waiting for transfers between devices, z_xor(): return lax.ppermute(v, 'z', [(i, i ^ s) for i in range(NZ)])  8.74 us
    ppermute x3, waiting for transfers between devices, x_swap(): return lax.ppermute(v, 'xl', [(0, 1), (1, 0)])  8.53 us
    ppermute x4, starting transfers between devices, weight_send(): return lax.ppermute(v, ('xh', 'c', 'xl', 'y'), route)  5.81 us
    ppermute x3, starting transfers between devices, z_xor(): return lax.ppermute(v, 'z', [(i, i ^ s) for i in range(NZ)])  4.58 us
  transfers between devices with their start and end apart: 29, of which 15 were waited for; matrix products, arithmetic and copies ran while one was open for 0% of the time, Pallas kernels for 9%

profile of v11, /device:TPU:2, one launch (start us, length us, event | category | flops | bytes accessed | tf_op | source)
XLA Modules:
  0.0 107.0 jit_solution(1635208675602072155)
XLA Ops:
  0.0 1.9 %collective-permute-start.1 = (bf16[1024,128]{1,0:T(8,128)(2,1)}, bf16[1024,128]{1,0:T(8,128)(2,1)S(1)}, u32[]{:S(2)}, u32[]{:S(2)}) collective-permute-start(bf16[1024,128]{1,0:T(8,128)(2,1)} %refs_0_.1), channel_id=1, source_target_pairs={{0,8},{8,16},{16,24},{24,32},{32,40},{40,48},{48,56},{56,0},{1,9},... | collective-permute-start | bytes 786440 | tf_op jit(solution)/shard_map/ppermute | solution.py:27
  1.9 4.0 %collective-permute-start = (bf16[1024,128]{1,0:T(8,128)(2,1)}, bf16[1024,128]{1,0:T(8,128)(2,1)S(1)}, u32[]{:S(2)}, u32[]{:S(2)}) collective-permute-start(bf16[1024,128]{1,0:T(8,128)(2,1)} %refs_0_.1), channel_id=1, source_target_pairs={{0,56},{8,0},{16,8},{24,16},{32,24},{40,32},{48,40},{56,48},{1,57}... | collective-permute-start | bytes 786440 | tf_op jit(solution)/shard_map/ppermute | solution.py:27
  5.9 2.0 %pack_first.1 = (bf16[1280,128]{1,0:T(8,128)(2,1)}, bf16[16,64,128]{2,1,0:T(8,128)(2,1)}) custom-call(bf16[8192,128]{1,0:T(8,128)(2,1)} %wq_ref.2, bf16[32,8192]{1,0:T(8,128)(2,1)} %bitcast.4, bf16[16,32,128]{2,1,0:T(8,128)(2,1)} %bitcast.8, bf16[16,32,128]{2,1,0:T(8,128)(2,1)} %up_ref.1), custom_call_target="tpu_custom_call" | custom-call | tf_op jit(solution)/shard_map/pack_first/pallas_call | solution.py:317
  8.0 2.2 %collective-permute-start.3 = (bf16[16,64,128]{2,1,0:T(8,128)(2,1)}, bf16[16,64,128]{2,1,0:T(8,128)(2,1)S(1)}, u32[]{:S(2)}, u32[]{:S(2)}) collective-permute-start(bf16[16,64,128]{2,1,0:T(8,128)(2,1)} %get-tuple-element.54), channel_id=1, source_target_pairs={{0,128},{128,0},{1,129},{129,1},{2,130},{130,2},{3,131},{131,3},{4... | collective-permute-start | bytes 786440 | tf_op jit(solution)/shard_map/ppermute | solution.py:47
  11.5 3.0 %pack.1 = (bf16[1280,128]{1,0:T(8,128)(2,1)}, bf16[1280,128]{1,0:T(8,128)(2,1)}, bf16[1280,128]{1,0:T(8,128)(2,1)}, bf16[1280,128]{1,0:T(8,128)(2,1)}) custom-call(bf16[8192,128]{1,0:T(8,128)(2,1)} %wq_ref.2, bf16[32,8192]{1,0:T(8,128)(2,1)} %bitcast.5), custom_call_target="tpu_custom_call" | custom-call | tf_op jit(solution)/shard_map/pack/pallas_call | solution.py:317
  19.2 3.7 %collective-permute-done.2.refs_0_.refs_9_ = bf16[1280,128]{1,0:T(8,128)(2,1)S(1)} collective-permute-done((bf16[1280,128]{1,0:T(8,128)(2,1)S(1)}, bf16[1280,128]{1,0:T(8,128)(2,1)S(1)}, u32[]{:S(2)}, u32[]{:S(2)}) %collective-permute-start.2) | collective-permute-done | bytes 327712 | tf_op jit(solution)/shard_map/ppermute | solution.py:75
  22.8 2.0 %collective-permute-start.4 = (bf16[1024,128]{1,0:T(8,128)(2,1)S(1)}, bf16[1024,128]{1,0:T(8,128)(2,1)S(1)}, u32[]{:S(2)}, u32[]{:S(2)}) collective-permute-start(bf16[1024,128]{1,0:T(8,128)(2,1)S(1)} %collective-permute-done.refs_1_), channel_id=1, source_target_pairs={{0,56},{8,0},{16,8},{24,16},{32,24},{40,32},{48,40},{56,48},{1,57}... | collective-permute-start | bytes 786440 | tf_op jit(solution)/shard_map/ppermute | solution.py:27
  25.7 4.6 %collective-permute-start.9 = (bf16[32,1024]{1,0:T(8,128)(2,1)S(1)}, bf16[32,1024]{1,0:T(8,128)(2,1)S(1)}, u32[]{:S(2)}, u32[]{:S(2)}) collective-permute-start(bf16[32,1024]{1,0:T(8,128)(2,1)S(1)} %get-tuple-element.61), channel_id=1, source_target_pairs={{0,32},{8,40},{16,48},{24,56},{32,0},{40,8},{48,16},{56,24},{1,33}... | collective-permute-start | bytes 196616 | tf_op jit(solution)/shard_map/ppermute | solution.py:31
  31.3 5.1 %collective-permute-done.5.refs_6_ = bf16[1024,128]{1,0:T(8,128)(2,1)S(1)} collective-permute-done((bf16[1024,128]{1,0:T(8,128)(2,1)S(1)}, bf16[1024,128]{1,0:T(8,128)(2,1)S(1)}, u32[]{:S(2)}, u32[]{:S(2)}) %collective-permute-start.5) | collective-permute-done | bytes 262176 | tf_op jit(solution)/shard_map/ppermute | solution.py:27
  36.4 2.7 %collective-permute-start.12 = (bf16[1280,128]{1,0:T(8,128)(2,1)S(1)}, bf16[1280,128]{1,0:T(8,128)(2,1)S(1)}, u32[]{:S(2)}, u32[]{:S(2)}) collective-permute-start(bf16[1280,128]{1,0:T(8,128)(2,1)S(1)} %copy-done.5), channel_id=1, source_target_pairs={{0,6},{1,7},{2,4},{3,5},{4,2},{5,3},{6,0},{7,1},{64,199},{65,196},... | collective-permute-start | bytes 983048 | tf_op jit(solution)/shard_map/ppermute | solution.py:75
  39.2 2.0 %collective-permute-start.11 = (bf16[1024,128]{1,0:T(8,128)(2,1)S(1)}, bf16[1024,128]{1,0:T(8,128)(2,1)S(1)}, u32[]{:S(2)}, u32[]{:S(2)}) collective-permute-start(bf16[1024,128]{1,0:T(8,128)(2,1)S(1)} %collective-permute-done.5.refs_6_), channel_id=1, source_target_pairs={{0,8},{8,16},{16,24},{24,32},{32,40},{40,48},{48,56},{56,0},{1,9},... | collective-permute-start | bytes 786440 | tf_op jit(solution)/shard_map/ppermute | solution.py:27
  41.2 6.3 %collective-permute-done.10.refs_3_ = bf16[1024,128]{1,0:T(8,128)(2,1)S(1)} collective-permute-done((bf16[1024,128]{1,0:T(8,128)(2,1)S(1)}, bf16[1024,128]{1,0:T(8,128)(2,1)S(1)}, u32[]{:S(2)}, u32[]{:S(2)}) %collective-permute-start.10) | collective-permute-done | bytes 262176 | tf_op jit(solution)/shard_map/ppermute | solution.py:27
  49.6 9.4 %collective-permute-done.13.refs_4_ = bf16[1024,128]{1,0:T(8,128)(2,1)S(1)} collective-permute-done((bf16[1024,128]{1,0:T(8,128)(2,1)S(1)}, bf16[1024,128]{1,0:T(8,128)(2,1)S(1)}, u32[]{:S(2)}, u32[]{:S(2)}) %collective-permute-start.13) | collective-permute-done | bytes 262176 | tf_op jit(solution)/shard_map/ppermute | solution.py:27
  60.6 2.2 %collective-permute-start.15 = (bf16[576,128]{1,0:T(8,128)(2,1)S(1)}, bf16[576,128]{1,0:T(8,128)(2,1)S(1)}, u32[]{:S(2)}, u32[]{:S(2)}) collective-permute-start(bf16[576,128]{1,0:T(8,128)(2,1)S(1)} %get-tuple-element.72), channel_id=1, source_target_pairs={{0,2},{1,3},{2,0},{3,1},{4,6},{5,7},{6,4},{7,5},{8,10},{9,11},{10,... | collective-permute-start | bytes 442376 | tf_op jit(solution)/shard_map/ppermute | solution.py:51
  63.3 2.8 %collective-permute-start.17 = (bf16[576,128]{1,0:T(8,128)(2,1)S(1)}, bf16[576,128]{1,0:T(8,128)(2,1)S(1)}, u32[]{:S(2)}, u32[]{:S(2)}) collective-permute-start(bf16[576,128]{1,0:T(8,128)(2,1)S(1)} %get-tuple-element.74), channel_id=1, source_target_pairs={{0,3},{1,0},{2,1},{3,2},{4,7},{5,4},{6,5},{7,6},{8,11},{9,8},{10,9... | collective-permute-start | bytes 442376 | tf_op jit(solution)/shard_map/ppermute | solution.py:51
  66.1 2.7 %q_product.1 = (bf16[1536,128]{1,0:T(8,128)(2,1)S(1)}, bf16[1536,128]{1,0:T(8,128)(2,1)S(1)}, bf16[1280,128]{1,0:T(8,128)(2,1)S(1)}, bf16[1280,128]{1,0:T(8,128)...) custom-call(bf16[1024,1024]{1,0:T(8,128)(2,1)S(1)} %get-tuple-element.69.hbuf, ...), custom_call_target="tpu_custom_call" | custom-call | tf_op jit(solution)/shard_map/q_product/pallas_call | solution.py:317
  70.9 1.9 %collective-permute-start.18 = (bf16[2048,128]{1,0:T(8,128)(2,1)S(1)}, bf16[2048,128]{1,0:T(8,128)(2,1)S(1)}, u32[]{:S(2)}, u32[]{:S(2)}) collective-permute-start(bf16[2048,128]{1,0:T(8,128)(2,1)S(1)} %get-tuple-element.76), channel_id=1, source_target_pairs={{0,4},{4,0},{1,5},{5,1},{2,6},{6,2},{3,7},{7,3},{8,12},{12,8},{9,1... | collective-permute-start | bytes 1572872 | tf_op jit(solution)/shard_map/ppermute | solution.py:39
  75.7 1.9 %collective-permute-start.27 = (bf16[1280,128]{1,0:T(8,128)(2,1)S(1)}, bf16[1280,128]{1,0:T(8,128)(2,1)S(1)}, u32[]{:S(2)}, u32[]{:S(2)}) collective-permute-start(bf16[1280,128]{1,0:T(8,128)(2,1)S(1)} %get-tuple-element.86), channel_id=1, source_target_pairs={{0,3},{1,0},{2,1},{3,2},{4,7},{5,4},{6,5},{7,6},{8,11},{9,8},{10,9... | collective-permute-start | bytes 983048 | tf_op jit(solution)/shard_map/ppermute | solution.py:51
  77.5 3.9 %collective-permute-done.19.b_ref = f32[64,128]{1,0:T(8,128)S(1)} collective-permute-done((f32[64,128]{1,0:T(8,128)S(1)}, f32[64,128]{1,0:T(8,128)S(1)}, u32[]{:S(2)}, u32[]{:S(2)}) %collective-permute-start.19) | collective-permute-done | bytes 32800 | tf_op jit(solution)/shard_map/ppermute | solution.py:31
  81.5 4.8 %collective-permute-done.20.b_ref = f32[64,128]{1,0:T(8,128)S(1)} collective-permute-done((f32[64,128]{1,0:T(8,128)S(1)}, f32[64,128]{1,0:T(8,128)S(1)}, u32[]{:S(2)}, u32[]{:S(2)}) %collective-permute-start.20) | collective-permute-done | bytes 32800 | tf_op jit(solution)/shard_map/ppermute | solution.py:31
  86.7 3.5 %collective-permute-done.21.b_ref = f32[64,128]{1,0:T(8,128)S(1)} collective-permute-done((f32[64,128]{1,0:T(8,128)S(1)}, f32[64,128]{1,0:T(8,128)S(1)}, u32[]{:S(2)}, u32[]{:S(2)}) %collective-permute-start.21) | collective-permute-done | bytes 32800 | tf_op jit(solution)/shard_map/ppermute | solution.py:39
  94.4 5.0 %collective-permute-done.28.refs_5_ = bf16[640,128]{1,0:T(8,128)(2,1)S(1)} collective-permute-done((bf16[640,128]{1,0:T(8,128)(2,1)S(1)}, bf16[640,128]{1,0:T(8,128)(2,1)S(1)}, u32[]{:S(2)}, u32[]{:S(2)}) %collective-permute-start.28) | collective-permute-done | bytes 163872 | tf_op jit(solution)/shard_map/ppermute | solution.py:39
  99.4 2.1 %collective-permute-done.22.refs_1_ = bf16[960,128]{1,0:T(8,128)(2,1)S(1)} collective-permute-done((bf16[960,128]{1,0:T(8,128)(2,1)S(1)}, bf16[960,128]{1,0:T(8,128)(2,1)S(1)}, u32[]{:S(2)}, u32[]{:S(2)}) %collective-permute-start.22) | collective-permute-done | bytes 245792 | tf_op jit(solution)/shard_map/ppermute | solution.py:51
  101.9 5.2 %attention.1 = bf16[1024,128]{1,0:T(8,128)(2,1)} custom-call(s32[8]{0:T(128)S(1)} %copy-done.3, s32[1024]{0:T(1024)S(1)} %copy-done.2, f32[384,128]{1,0:T(8,128)S(1)} %get-tuple-element.79.refs_0_, bf16[960,128]{1,0:T(8,128)(2,1)S(1)} %collective-permute-done.22.refs_1_, bf16[960,128]{1,0:T(8,128)(2,1)S(1)} %collective-permute-done.23.refs_2_, ...), custom_call_target="tpu_custom_call" | custom-call | tf_op jit(solution)/shard_map/attention/pallas_call | solution.py:317
  (64 shorter events, 22.0 us)
Async XLA Ops:
  0.0 16.2 %collective-permute-start.1 = (bf16[1024,128]{1,0:T(8,128)(2,1)}, bf16[1024,128]{1,0:T(8,128)(2,1)S(1)}, u32[]{:S(2)}, u32[]{:S(2)}) collective-permute-start(bf16[1024,128]{1,0:T(8,128)(2,1)} %refs_0_.1), channel_id=1, source_target_pairs={{0,8},{8,16},{16,24},{24,32},{32,40},{40,48},{48,56},{56,0},{1,9},... | collective-permute-start | bytes 786440 | tf_op jit(solution)/shard_map/ppermute | solution.py:27
  1.9 14.2 %collective-permute-start = (bf16[1024,128]{1,0:T(8,128)(2,1)}, bf16[1024,128]{1,0:T(8,128)(2,1)S(1)}, u32[]{:S(2)}, u32[]{:S(2)}) collective-permute-start(bf16[1024,128]{1,0:T(8,128)(2,1)} %refs_0_.1), channel_id=1, source_target_pairs={{0,56},{8,0},{16,8},{24,16},{32,24},{40,32},{48,40},{56,48},{1,57}... | collective-permute-start | bytes 786440 | tf_op jit(solution)/shard_map/ppermute | solution.py:27
  8.0 9.6 %collective-permute-start.3 = (bf16[16,64,128]{2,1,0:T(8,128)(2,1)}, bf16[16,64,128]{2,1,0:T(8,128)(2,1)S(1)}, u32[]{:S(2)}, u32[]{:S(2)}) collective-permute-start(bf16[16,64,128]{2,1,0:T(8,128)(2,1)} %get-tuple-element.54), channel_id=1, source_target_pairs={{0,128},{128,0},{1,129},{129,1},{2,130},{130,2},{3,131},{131,3},{4... | collective-permute-start | bytes 786440 | tf_op jit(solution)/shard_map/ppermute | solution.py:47
  14.5 8.4 %collective-permute-start.2 = (bf16[1280,128]{1,0:T(8,128)(2,1)S(1)}, bf16[1280,128]{1,0:T(8,128)(2,1)S(1)}, u32[]{:S(2)}, u32[]{:S(2)}) collective-permute-start(bf16[1280,128]{1,0:T(8,128)(2,1)S(1)} %copy-done.6), channel_id=1, source_target_pairs={{0,1},{1,2},{2,3},{3,0},{4,5},{5,6},{6,7},{7,4},{64,67},{65,64},{6... | collective-permute-start | bytes 983048 | tf_op jit(solution)/shard_map/ppermute | solution.py:75
  17.7 21.4 %collective-permute-start.7 = (bf16[1280,128]{1,0:T(8,128)(2,1)}, bf16[1280,128]{1,0:T(8,128)(2,1)S(1)}, u32[]{:S(2)}, u32[]{:S(2)}) collective-permute-start(bf16[1280,128]{1,0:T(8,128)(2,1)} %get-tuple-element.59), channel_id=1, source_target_pairs={{64,66},{65,67},{66,64},{67,65},{68,70},{69,71},{70,68},{71,69},{1... | collective-permute-start | bytes 983048 | tf_op jit(solution)/shard_map/ppermute | solution.py:75
  18.6 20.6 %collective-permute-start.6 = (bf16[1280,128]{1,0:T(8,128)(2,1)}, bf16[1280,128]{1,0:T(8,128)(2,1)S(1)}, u32[]{:S(2)}, u32[]{:S(2)}) collective-permute-start(bf16[1280,128]{1,0:T(8,128)(2,1)} %get-tuple-element.58), channel_id=1, source_target_pairs={{0,4},{1,5},{2,6},{3,7},{4,0},{5,1},{6,2},{7,3},{64,197},{65,198},... | collective-permute-start | bytes 983048 | tf_op jit(solution)/shard_map/ppermute | solution.py:75
  22.8 8.4 %collective-permute-start.4 = (bf16[1024,128]{1,0:T(8,128)(2,1)S(1)}, bf16[1024,128]{1,0:T(8,128)(2,1)S(1)}, u32[]{:S(2)}, u32[]{:S(2)}) collective-permute-start(bf16[1024,128]{1,0:T(8,128)(2,1)S(1)} %collective-permute-done.refs_1_), channel_id=1, source_target_pairs={{0,56},{8,0},{16,8},{24,16},{32,24},{40,32},{48,40},{56,48},{1,57}... | collective-permute-start | bytes 786440 | tf_op jit(solution)/shard_map/ppermute | solution.py:27
  24.8 11.6 %collective-permute-start.5 = (bf16[1024,128]{1,0:T(8,128)(2,1)S(1)}, bf16[1024,128]{1,0:T(8,128)(2,1)S(1)}, u32[]{:S(2)}, u32[]{:S(2)}) collective-permute-start(bf16[1024,128]{1,0:T(8,128)(2,1)S(1)} %collective-permute-done.1.refs_7_), channel_id=1, source_target_pairs={{0,8},{8,16},{16,24},{24,32},{32,40},{40,48},{48,56},{56,0},{1,9},... | collective-permute-start | bytes 786440 | tf_op jit(solution)/shard_map/ppermute | solution.py:27
  25.7 13.4 %collective-permute-start.9 = (bf16[32,1024]{1,0:T(8,128)(2,1)S(1)}, bf16[32,1024]{1,0:T(8,128)(2,1)S(1)}, u32[]{:S(2)}, u32[]{:S(2)}) collective-permute-start(bf16[32,1024]{1,0:T(8,128)(2,1)S(1)} %get-tuple-element.61), channel_id=1, source_target_pairs={{0,32},{8,40},{16,48},{24,56},{32,0},{40,8},{48,16},{56,24},{1,33}... | collective-permute-start | bytes 196616 | tf_op jit(solution)/shard_map/ppermute | solution.py:31
  36.4 12.5 %collective-permute-start.12 = (bf16[1280,128]{1,0:T(8,128)(2,1)S(1)}, bf16[1280,128]{1,0:T(8,128)(2,1)S(1)}, u32[]{:S(2)}, u32[]{:S(2)}) collective-permute-start(bf16[1280,128]{1,0:T(8,128)(2,1)S(1)} %copy-done.5), channel_id=1, source_target_pairs={{0,6},{1,7},{2,4},{3,5},{4,2},{5,3},{6,0},{7,1},{64,199},{65,196},... | collective-permute-start | bytes 983048 | tf_op jit(solution)/shard_map/ppermute | solution.py:75
  39.1 8.4 %collective-permute-start.10 = (bf16[1024,128]{1,0:T(8,128)(2,1)S(1)}, bf16[1024,128]{1,0:T(8,128)(2,1)S(1)}, u32[]{:S(2)}, u32[]{:S(2)}) collective-permute-start(bf16[1024,128]{1,0:T(8,128)(2,1)S(1)} %collective-permute-done.4.refs_2_), channel_id=1, source_target_pairs={{0,56},{8,0},{16,8},{24,16},{32,24},{40,32},{48,40},{56,48},{1,57}... | collective-permute-start | bytes 786440 | tf_op jit(solution)/shard_map/ppermute | solution.py:27
  39.2 9.6 %collective-permute-start.11 = (bf16[1024,128]{1,0:T(8,128)(2,1)S(1)}, bf16[1024,128]{1,0:T(8,128)(2,1)S(1)}, u32[]{:S(2)}, u32[]{:S(2)}) collective-permute-start(bf16[1024,128]{1,0:T(8,128)(2,1)S(1)} %collective-permute-done.5.refs_6_), channel_id=1, source_target_pairs={{0,8},{8,16},{16,24},{24,32},{32,40},{40,48},{48,56},{56,0},{1,9},... | collective-permute-start | bytes 786440 | tf_op jit(solution)/shard_map/ppermute | solution.py:27
  48.9 10.0 %collective-permute-start.14 = (bf16[4,1280,128]{2,1,0:T(8,128)(2,1)S(1)}, bf16[4,1280,128]{2,1,0:T(8,128)(2,1)S(1)}, u32[]{:S(2)}, u32[]{:S(2)}) collective-permute-start(bf16[4,1280,128]{2,1,0:T(8,128)(2,1)S(1)} %stack.13), channel_id=1, source_target_pairs={{0,64},{64,0},{1,65},{65,1},{2,66},{66,2},{3,67},{67,3},{4,68},{68... | collective-permute-start | bytes 3932168 | tf_op jit(solution)/shard_map/ppermute | solution.py:43
  49.0 9.9 %collective-permute-start.13 = (bf16[1024,128]{1,0:T(8,128)(2,1)S(1)}, bf16[1024,128]{1,0:T(8,128)(2,1)S(1)}, u32[]{:S(2)}, u32[]{:S(2)}) collective-permute-start(bf16[1024,128]{1,0:T(8,128)(2,1)S(1)} %collective-permute-done.11.refs_5_), channel_id=1, source_target_pairs={{0,8},{8,16},{16,24},{24,32},{32,40},{40,48},{48,56},{56,0},{1,9},... | collective-permute-start | bytes 786440 | tf_op jit(solution)/shard_map/ppermute | solution.py:27
  60.6 8.4 %collective-permute-start.15 = (bf16[576,128]{1,0:T(8,128)(2,1)S(1)}, bf16[576,128]{1,0:T(8,128)(2,1)S(1)}, u32[]{:S(2)}, u32[]{:S(2)}) collective-permute-start(bf16[576,128]{1,0:T(8,128)(2,1)S(1)} %get-tuple-element.72), channel_id=1, source_target_pairs={{0,2},{1,3},{2,0},{3,1},{4,6},{5,7},{6,4},{7,5},{8,10},{9,11},{10,... | collective-permute-start | bytes 442376 | tf_op jit(solution)/shard_map/ppermute | solution.py:51
  62.8 7.9 %collective-permute-start.16 = (bf16[576,128]{1,0:T(8,128)(2,1)S(1)}, bf16[576,128]{1,0:T(8,128)(2,1)S(1)}, u32[]{:S(2)}, u32[]{:S(2)}) collective-permute-start(bf16[576,128]{1,0:T(8,128)(2,1)S(1)} %get-tuple-element.73), channel_id=1, source_target_pairs={{0,1},{1,2},{2,3},{3,0},{4,5},{5,6},{6,7},{7,4},{8,9},{9,10},{10,1... | collective-permute-start | bytes 442376 | tf_op jit(solution)/shard_map/ppermute | solution.py:51
  63.3 7.5 %collective-permute-start.17 = (bf16[576,128]{1,0:T(8,128)(2,1)S(1)}, bf16[576,128]{1,0:T(8,128)(2,1)S(1)}, u32[]{:S(2)}, u32[]{:S(2)}) collective-permute-start(bf16[576,128]{1,0:T(8,128)(2,1)S(1)} %get-tuple-element.74), channel_id=1, source_target_pairs={{0,3},{1,0},{2,1},{3,2},{4,7},{5,4},{6,5},{7,6},{8,11},{9,8},{10,9... | collective-permute-start | bytes 442376 | tf_op jit(solution)/shard_map/ppermute | solution.py:51
  70.9 19.3 %collective-permute-start.18 = (bf16[2048,128]{1,0:T(8,128)(2,1)S(1)}, bf16[2048,128]{1,0:T(8,128)(2,1)S(1)}, u32[]{:S(2)}, u32[]{:S(2)}) collective-permute-start(bf16[2048,128]{1,0:T(8,128)(2,1)S(1)} %get-tuple-element.76), channel_id=1, source_target_pairs={{0,4},{4,0},{1,5},{5,1},{2,6},{6,2},{3,7},{7,3},{8,12},{12,8},{9,1... | collective-permute-start | bytes 1572872 | tf_op jit(solution)/shard_map/ppermute | solution.py:39
  72.7 19.4 %collective-permute-start.25 = (bf16[1280,128]{1,0:T(8,128)(2,1)S(1)}, bf16[1280,128]{1,0:T(8,128)(2,1)S(1)}, u32[]{:S(2)}, u32[]{:S(2)}) collective-permute-start(bf16[1280,128]{1,0:T(8,128)(2,1)S(1)} %get-tuple-element.84), channel_id=1, source_target_pairs={{0,2},{1,3},{2,0},{3,1},{4,6},{5,7},{6,4},{7,5},{8,10},{9,11},{10,... | collective-permute-start | bytes 983048 | tf_op jit(solution)/shard_map/ppermute | solution.py:51
  74.3 19.5 %collective-permute-start.26 = (bf16[1280,128]{1,0:T(8,128)(2,1)S(1)}, bf16[1280,128]{1,0:T(8,128)(2,1)S(1)}, u32[]{:S(2)}, u32[]{:S(2)}) collective-permute-start(bf16[1280,128]{1,0:T(8,128)(2,1)S(1)} %get-tuple-element.85), channel_id=1, source_target_pairs={{0,1},{1,2},{2,3},{3,0},{4,5},{5,6},{6,7},{7,4},{8,9},{9,10},{10,1... | collective-permute-start | bytes 983048 | tf_op jit(solution)/shard_map/ppermute | solution.py:51
  75.7 18.2 %collective-permute-start.27 = (bf16[1280,128]{1,0:T(8,128)(2,1)S(1)}, bf16[1280,128]{1,0:T(8,128)(2,1)S(1)}, u32[]{:S(2)}, u32[]{:S(2)}) collective-permute-start(bf16[1280,128]{1,0:T(8,128)(2,1)S(1)} %get-tuple-element.86), channel_id=1, source_target_pairs={{0,3},{1,0},{2,1},{3,2},{4,7},{5,4},{6,5},{7,6},{8,11},{9,8},{10,9... | collective-permute-start | bytes 983048 | tf_op jit(solution)/shard_map/ppermute | solution.py:51
  90.4 11.2 %collective-permute-start.22 = (bf16[960,128]{1,0:T(8,128)(2,1)S(1)}, bf16[960,128]{1,0:T(8,128)(2,1)S(1)}, u32[]{:S(2)}, u32[]{:S(2)}) collective-permute-start(bf16[960,128]{1,0:T(8,128)(2,1)S(1)} %get-tuple-element.80), channel_id=1, source_target_pairs={{0,1},{1,2},{2,3},{3,0},{4,5},{5,6},{6,7},{7,4},{8,9},{9,10},{10,1... | collective-permute-start | bytes 737288 | tf_op jit(solution)/shard_map/ppermute | solution.py:51
  90.6 10.9 %collective-permute-start.23 = (bf16[960,128]{1,0:T(8,128)(2,1)S(1)}, bf16[960,128]{1,0:T(8,128)(2,1)S(1)}, u32[]{:S(2)}, u32[]{:S(2)}) collective-permute-start(bf16[960,128]{1,0:T(8,128)(2,1)S(1)} %get-tuple-element.81), channel_id=1, source_target_pairs={{0,2},{1,3},{2,0},{3,1},{4,6},{5,7},{6,4},{7,5},{8,10},{9,11},{10,... | collective-permute-start | bytes 737288 | tf_op jit(solution)/shard_map/ppermute | solution.py:51
  92.1 9.7 %collective-permute-start.24 = (bf16[960,128]{1,0:T(8,128)(2,1)S(1)}, bf16[960,128]{1,0:T(8,128)(2,1)S(1)}, u32[]{:S(2)}, u32[]{:S(2)}) collective-permute-start(bf16[960,128]{1,0:T(8,128)(2,1)S(1)} %get-tuple-element.82), channel_id=1, source_target_pairs={{0,3},{1,0},{2,1},{3,2},{4,7},{5,4},{6,5},{7,6},{8,11},{9,8},{10,9... | collective-permute-start | bytes 737288 | tf_op jit(solution)/shard_map/ppermute | solution.py:51
  (12 other events, 148.5 us)

commit v12 on v11

--- a/solution.py
+++ b/solution.py
@@ -94,17 +94,11 @@
     return pairs
 
 
-def pack_first_kernel(wq_ref, kv_ref, down_ref, up_ref, out, maps, sem):
-    d = jnp.where(lax.axis_index("c") == 0, SERVED[0][0], SERVED[1][0])
+def pack_kernel(wq_ref, kv_ref, down_ref, up_ref, *refs):
+    outs, maps, sem = refs[:5], refs[5], refs[6]
+    c = lax.axis_index("c")
     pairs = [(down_ref, maps.at[:, 0:RANK, :]), (up_ref, maps.at[:, RANK : 2 * RANK, :])]
-    run_copies(pairs + weight_pairs(wq_ref, kv_ref, out, d), sem)
-
-
-def pack_kernel(wq_ref, kv_ref, *refs):
-    outs, sem = refs[:4], refs[4]
-    c = lax.axis_index("c")
-    pairs = []
-    for k, out in enumerate(outs, 1):
+    for k, out in enumerate(outs):
         d = jnp.where(c == 0, (SERVED[0] + (0,))[k], SERVED[1][k]) if k < 4 else 0
         pairs += weight_pairs(wq_ref, kv_ref, out, d)
     run_copies(pairs, sem)
@@ -115,8 +109,10 @@
         refs[-1][i] = ref[...]
 
 
-def add_kernel(a_ref, b_ref, out_ref):
-    out_ref[...] = a_ref[...] + b_ref[...].astype(jnp.float32)
+def add_kernel(a_ref, b_ref, *outs):
+    total = a_ref[...] + b_ref[...].astype(jnp.float32)
+    for out in outs:
+        out[...] = total.astype(out.dtype)
 
 
 def rope_kernel(start_ref, cos_ref, sin_ref, cos_t_ref, sin_t_ref):
@@ -333,16 +329,15 @@
     rows = hidden.shape[0]
     bf16, f32 = jnp.bfloat16, jnp.float32
     of = jax.ShapeDtypeStruct
-    kv_rows = key_value_weight.T
-    first, maps = call(
-        pack_first_kernel,
-        "pack_first",
-        [of((1280, 128), bf16), of((down_maps.shape[0], 2 * RANK, 128), bf16)],
+    *sends, maps = call(
+        pack_kernel,
+        "pack",
+        [of((1280, 128), bf16)] * 5 + [of((down_maps.shape[0], 2 * RANK, 128), bf16)],
         query_weight,
-        kv_rows,
+        key_value_weight.T,
         jnp.transpose(down_maps, (0, 2, 1)),
         up_maps,
-        scratch=[pltpu.SemaphoreType.DMA((2 * NZ + 2,))],
+        scratch=[pltpu.SemaphoreType.DMA((10 * NZ + 2,))],
         space=pltpu.HBM,
         mib=PACK_MIB,
     )
@@ -353,17 +348,6 @@
         request_start,
         scalars=1,
     )
-    sends = call(
-        pack_kernel,
-        "pack",
-        [of((1280, 128), bf16)] * 4,
-        after(query_weight, first, cosines),
-        kv_rows,
-        scratch=[pltpu.SemaphoreType.DMA((8 * NZ,))],
-        space=pltpu.HBM,
-        mib=PACK_MIB,
-    )
-    sends = [first, *sends]
     twin = xh_swap(maps)
     ring = [(hidden, hidden)]
 
@@ -373,21 +357,24 @@
             r, l = after(r, l, *others), after(l, r, *others)
         ring.append((z_shift(r, 1), z_shift(l, -1) if len(ring) < 4 else None))
 
-    def added(low, sent):
-        return call(add_kernel, "low_add", of(low.shape, f32), low, sent)
+    def added(low, sent, narrow=False):
+        outs = [of(low.shape, f32)] + [of(low.shape, bf16)] * narrow
+        out = call(add_kernel, "low_add", outs, low, sent)
+        return out if narrow else out[0]
 
     ring_step()
-    mine = [weight_send(after(sends[0], sends[1]), 0), weight_send(after(sends[1], *ring[1]), 1), None, weight_send(sends[3], 3)]
+    mine = [weight_send(sends[0], 0), weight_send(after(sends[1], *ring[1]), 1), None, weight_send(sends[3], 3)]
     near = jnp.stack([maps, after(twin, *ring[1])])
-    ring_step(mine[0], near)
+    ring_step(mine[0], mine[3], near)
     far = core_swap(near)
     mine[2] = weight_send(after(sends[2], *ring[2]), 2)
     low, narrow = call(
         low_kernel, "low", [of((RANK, rows), f32), of((RANK, rows), bf16)], adapters, hidden, near, far, scalars=1
     )
-    low = added(low, z_xor(narrow, 4))
-    ring_step(mine[1], mine[3], low)
+    low, narrow = added(low, z_xor(narrow, 4), narrow=True)
+    ring_step(mine[1], low)
     ring_step(mine[2])
+    low = added(low, z_xor(after(narrow, *ring[3]), 1))
     mine[3] = after(mine[3], *ring[3])
     other = core_swap(call(stack_kernel, "stack", of((4, 1280, 128), bf16), *mine))
     right, left = zip(*ring)
@@ -424,7 +411,6 @@
         far_a,
     )
     x_got = x_swap(x_send)
-    low = added(low, z_xor(low, 1))
     low = added(low, z_xor(low, 2))
     low = added(low, x_swap(low))
     a_own, kv_own, *a_sends = call(

time: 107 us -> 105 us (0.981)
  waiting for transfers between devices: 50 us -> 44.7 us
  starting transfers between devices: 39.7 us -> 42.8 us
  Pallas kernels: 17.1 us -> 15.6 us
    ppermute x7, waiting for transfers between devices: 23.1 us -> 12.1 us  [z_shift(): return lax.ppermute(v, 'z', [(i, (i + s) % NZ) for i in range(NZ)])]
    ppermute x4, starting transfers between devices: 5.81 us -> 11.2 us  [weight_send(): return lax.ppermute(v, ('xh', 'c', 'xl', 'y'), route)]
    ppermute x3, waiting for transfers between devices: 8.74 us -> 12.9 us  [z_xor(): return lax.ppermute(v, 'z', [(i, i ^ s) for i in range(NZ)])]
    ppermute x1, waiting for transfers between devices: 1.42 us -> 5.08 us  [xh_swap(): return lax.ppermute(v, 'xh', [(0, 1), (1, 0)])]
    ppermute x4, waiting for transfers between devices: 3.66 us -> 0.01 us  [weight_send(): return lax.ppermute(v, ('xh', 'c', 'xl', 'y'), route)]
    ppermute x9, waiting for transfers between devices: 4.46 us -> 7.82 us  [y_shift(): return lax.ppermute(v, 'y', [(i, (i + s) % NY) for i in range(NY)])]
    ppermute x9, starting transfers between devices: 13.7 us -> 12 us  [y_shift(): return lax.ppermute(v, 'y', [(i, (i + s) % NY) for i in range(NY)])]
    ppermute x3, waiting for transfers between devices: 8.53 us -> 6.86 us  [x_swap(): return lax.ppermute(v, 'xl', [(0, 1), (1, 0)])]
  transfers between devices with their start and end apart: 29 -> 29, of which waited for: 15 -> 12; matrix products, arithmetic and copies ran while one was open for 0% -> 1% of each run, Pallas kernels for 9% -> 8%
where the time goes in v12:
time: 105 us; the launch traced here: 104 us
  waiting for transfers between devices  44.7 us (43%)
  starting transfers between devices  42.8 us (41%)
  Pallas kernels  15.6 us (15%)
    pallas_call x14, Pallas kernels, call(): pl.pallas_call(kernel, out_shape=outs, in_specs=[SMEM] * scalars + [pl.Bl...  15.6 us
    ppermute x3, waiting for transfers between devices, z_xor(): return lax.ppermute(v, 'z', [(i, i ^ s) for i in range(NZ)])  12.9 us
    ppermute x7, waiting for transfers between devices, z_shift(): return lax.ppermute(v, 'z', [(i, (i + s) % NZ) for i in range(NZ)])  12.1 us
    ppermute x9, starting transfers between devices, y_shift(): return lax.ppermute(v, 'y', [(i, (i + s) % NY) for i in range(NY)])  12 us
    ppermute x4, starting transfers between devices, weight_send(): return lax.ppermute(v, ('xh', 'c', 'xl', 'y'), route)  11.2 us
    ppermute x7, starting transfers between devices, z_shift(): return lax.ppermute(v, 'z', [(i, (i + s) % NZ) for i in range(NZ)])  10.2 us
    ppermute x9, waiting for transfers between devices, y_shift(): return lax.ppermute(v, 'y', [(i, (i + s) % NY) for i in range(NY)])  7.82 us
    ppermute x3, waiting for transfers between devices, x_swap(): return lax.ppermute(v, 'xl', [(0, 1), (1, 0)])  6.86 us
  transfers between devices with their start and end apart: 29, of which 12 were waited for; matrix products, arithmetic and copies ran while one was open for 1% of the time, Pallas kernels for 8%

profile of v12, /device:TPU:2, one launch (start us, length us, event | category | flops | bytes accessed | tf_op | source)
XLA Modules:
  0.0 104.3 jit_solution(14633041068811871615)
XLA Ops:
  0.0 1.9 %collective-permute-start.1 = (bf16[1024,128]{1,0:T(8,128)(2,1)}, bf16[1024,128]{1,0:T(8,128)(2,1)S(1)}, u32[]{:S(2)}, u32[]{:S(2)}) collective-permute-start(bf16[1024,128]{1,0:T(8,128)(2,1)} %refs_0_.1), channel_id=1, source_target_pairs={{0,8},{8,16},{16,24},{24,32},{32,40},{40,48},{48,56},{56,0},{1,9},... | collective-permute-start | bytes 786440 | tf_op jit(solution)/shard_map/ppermute | solution.py:27
  1.9 4.0 %collective-permute-start = (bf16[1024,128]{1,0:T(8,128)(2,1)}, bf16[1024,128]{1,0:T(8,128)(2,1)S(1)}, u32[]{:S(2)}, u32[]{:S(2)}) collective-permute-start(bf16[1024,128]{1,0:T(8,128)(2,1)} %refs_0_.1), channel_id=1, source_target_pairs={{0,56},{8,0},{16,8},{24,16},{32,24},{40,32},{48,40},{56,48},{1,57}... | collective-permute-start | bytes 786440 | tf_op jit(solution)/shard_map/ppermute | solution.py:27
  5.9 3.5 %pack.1 = (bf16[1280,128]{1,0:T(8,128)(2,1)}, bf16[1280,128]{1,0:T(8,128)(2,1)}, bf16[1280,128]{1,0:T(8,128)(2,1)}, bf16[1280,128]{1,0:T(8,128)(2,1)}, bf16[1280...) custom-call(bf16[8192,128]{1,0:T(8,128)(2,1)} %wq_ref.1, bf16[32,8192]{1,0:T(8,128)(2,1)} %bitcast.4, ...), custom_call_target="tpu_custom_call" | custom-call | tf_op jit(solution)/shard_map/pack/pallas_call | solution.py:313
  9.5 2.2 %collective-permute-start.4 = (bf16[16,64,128]{2,1,0:T(8,128)(2,1)}, bf16[16,64,128]{2,1,0:T(8,128)(2,1)S(1)}, u32[]{:S(2)}, u32[]{:S(2)}) collective-permute-start(bf16[16,64,128]{2,1,0:T(8,128)(2,1)} %get-tuple-element.52), channel_id=1, source_target_pairs={{0,128},{128,0},{1,129},{129,1},{2,130},{130,2},{3,131},{131,3},{4... | collective-permute-start | bytes 786440 | tf_op jit(solution)/shard_map/ppermute | solution.py:47
  13.9 5.1 %collective-permute-done.4 = bf16[16,64,128]{2,1,0:T(8,128)(2,1)S(1)} collective-permute-done((bf16[16,64,128]{2,1,0:T(8,128)(2,1)}, bf16[16,64,128]{2,1,0:T(8,128)(2,1)S(1)}, u32[]{:S(2)}, u32[]{:S(2)}) %collective-permute-start.4) | collective-permute-done | bytes 262176 | tf_op jit(solution)/shard_map/ppermute | solution.py:47
  20.8 1.9 %collective-permute-start.5 = (bf16[1024,128]{1,0:T(8,128)(2,1)S(1)}, bf16[1024,128]{1,0:T(8,128)(2,1)S(1)}, u32[]{:S(2)}, u32[]{:S(2)}) collective-permute-start(bf16[1024,128]{1,0:T(8,128)(2,1)S(1)} %collective-permute-done.refs_1_), channel_id=1, source_target_pairs={{0,56},{8,0},{16,8},{24,16},{32,24},{40,32},{48,40},{56,48},{1,57}... | collective-permute-start | bytes 786440 | tf_op jit(solution)/shard_map/ppermute | solution.py:27
  23.6 4.5 %collective-permute-start.9 = (bf16[32,1024]{1,0:T(8,128)(2,1)S(1)}, bf16[32,1024]{1,0:T(8,128)(2,1)S(1)}, u32[]{:S(2)}, u32[]{:S(2)}) collective-permute-start(bf16[32,1024]{1,0:T(8,128)(2,1)S(1)} %get-tuple-element.59), channel_id=1, source_target_pairs={{0,32},{8,40},{16,48},{24,56},{32,0},{40,8},{48,16},{56,24},{1,33}... | collective-permute-start | bytes 196616 | tf_op jit(solution)/shard_map/ppermute | solution.py:31
  28.1 3.2 %collective-permute-done.6.refs_6_ = bf16[1024,128]{1,0:T(8,128)(2,1)S(1)} collective-permute-done((bf16[1024,128]{1,0:T(8,128)(2,1)S(1)}, bf16[1024,128]{1,0:T(8,128)(2,1)S(1)}, u32[]{:S(2)}, u32[]{:S(2)}) %collective-permute-start.6) | collective-permute-done | bytes 262176 | tf_op jit(solution)/shard_map/ppermute | solution.py:27
  31.3 8.3 %collective-permute-start.12 = (bf16[1280,128]{1,0:T(8,128)(2,1)S(1)}, bf16[1280,128]{1,0:T(8,128)(2,1)S(1)}, u32[]{:S(2)}, u32[]{:S(2)}) collective-permute-start(bf16[1280,128]{1,0:T(8,128)(2,1)S(1)} %copy-done.4), channel_id=1, source_target_pairs={{0,6},{1,7},{2,4},{3,5},{4,2},{5,3},{6,0},{7,1},{64,199},{65,196},... | collective-permute-start | bytes 983048 | tf_op jit(solution)/shard_map/ppermute | solution.py:75
  41.7 4.3 %collective-permute-done.10.refs_3_ = bf16[1024,128]{1,0:T(8,128)(2,1)S(1)} collective-permute-done((bf16[1024,128]{1,0:T(8,128)(2,1)S(1)}, bf16[1024,128]{1,0:T(8,128)(2,1)S(1)}, u32[]{:S(2)}, u32[]{:S(2)}) %collective-permute-start.10) | collective-permute-done | bytes 262176 | tf_op jit(solution)/shard_map/ppermute | solution.py:27
  46.1 2.5 %collective-permute-done.11.refs_5_ = bf16[1024,128]{1,0:T(8,128)(2,1)S(1)} collective-permute-done((bf16[1024,128]{1,0:T(8,128)(2,1)S(1)}, bf16[1024,128]{1,0:T(8,128)(2,1)S(1)}, u32[]{:S(2)}, u32[]{:S(2)}) %collective-permute-start.11) | collective-permute-done | bytes 262176 | tf_op jit(solution)/shard_map/ppermute | solution.py:27
  49.0 7.7 %collective-permute-done.15.b_ref = bf16[32,1024]{1,0:T(8,128)(2,1)S(1)} collective-permute-done((bf16[32,1024]{1,0:T(8,128)(2,1)S(1)}, bf16[32,1024]{1,0:T(8,128)(2,1)S(1)}, u32[]{:S(2)}, u32[]{:S(2)}) %collective-permute-start.15) | collective-permute-done | bytes 65568 | tf_op jit(solution)/shard_map/ppermute | solution.py:31
  56.7 2.0 %collective-permute-done.13.refs_4_ = bf16[1024,128]{1,0:T(8,128)(2,1)S(1)} collective-permute-done((bf16[1024,128]{1,0:T(8,128)(2,1)S(1)}, bf16[1024,128]{1,0:T(8,128)(2,1)S(1)}, u32[]{:S(2)}, u32[]{:S(2)}) %collective-permute-start.13) | collective-permute-done | bytes 262176 | tf_op jit(solution)/shard_map/ppermute | solution.py:27
  61.9 1.9 %collective-permute-start.18 = (bf16[576,128]{1,0:T(8,128)(2,1)S(1)}, bf16[576,128]{1,0:T(8,128)(2,1)S(1)}, u32[]{:S(2)}, u32[]{:S(2)}) collective-permute-start(bf16[576,128]{1,0:T(8,128)(2,1)S(1)} %get-tuple-element.75), channel_id=1, source_target_pairs={{0,3},{1,0},{2,1},{3,2},{4,7},{5,4},{6,5},{7,6},{8,11},{9,8},{10,9... | collective-permute-start | bytes 442376 | tf_op jit(solution)/shard_map/ppermute | solution.py:51
  63.8 2.7 %q_product.1 = (bf16[1536,128]{1,0:T(8,128)(2,1)S(1)}, bf16[1536,128]{1,0:T(8,128)(2,1)S(1)}, bf16[1280,128]{1,0:T(8,128)(2,1)S(1)}, bf16[1280,128]{1,0:T(8,128)...) custom-call(bf16[1024,1024]{1,0:T(8,128)(2,1)S(1)} %get-tuple-element.70.hbuf, ...), custom_call_target="tpu_custom_call" | custom-call | tf_op jit(solution)/shard_map/q_product/pallas_call | solution.py:313
  66.5 2.2 %collective-permute-done.16.k1 = bf16[576,128]{1,0:T(8,128)(2,1)S(1)} collective-permute-done((bf16[576,128]{1,0:T(8,128)(2,1)S(1)}, bf16[576,128]{1,0:T(8,128)(2,1)S(1)}, u32[]{:S(2)}, u32[]{:S(2)}) %collective-permute-start.16) | collective-permute-done | bytes 147488 | tf_op jit(solution)/shard_map/ppermute | solution.py:51
  70.7 2.1 %collective-permute-start.25 = (bf16[1280,128]{1,0:T(8,128)(2,1)S(1)}, bf16[1280,128]{1,0:T(8,128)(2,1)S(1)}, u32[]{:S(2)}, u32[]{:S(2)}) collective-permute-start(bf16[1280,128]{1,0:T(8,128)(2,1)S(1)} %get-tuple-element.85), channel_id=1, source_target_pairs={{0,2},{1,3},{2,0},{3,1},{4,6},{5,7},{6,4},{7,5},{8,10},{9,11},{10,... | collective-permute-start | bytes 983048 | tf_op jit(solution)/shard_map/ppermute | solution.py:51
  74.4 1.7 %collective-permute-start.27 = (bf16[1280,128]{1,0:T(8,128)(2,1)S(1)}, bf16[1280,128]{1,0:T(8,128)(2,1)S(1)}, u32[]{:S(2)}, u32[]{:S(2)}) collective-permute-start(bf16[1280,128]{1,0:T(8,128)(2,1)S(1)} %get-tuple-element.87), channel_id=1, source_target_pairs={{0,3},{1,0},{2,1},{3,2},{4,7},{5,4},{6,5},{7,6},{8,11},{9,8},{10,9... | collective-permute-start | bytes 983048 | tf_op jit(solution)/shard_map/ppermute | solution.py:51
  76.1 5.2 %collective-permute-done.20.b_ref = f32[64,128]{1,0:T(8,128)S(1)} collective-permute-done((f32[64,128]{1,0:T(8,128)S(1)}, f32[64,128]{1,0:T(8,128)S(1)}, u32[]{:S(2)}, u32[]{:S(2)}) %collective-permute-start.20) | collective-permute-done | bytes 32800 | tf_op jit(solution)/shard_map/ppermute | solution.py:31
  81.4 3.7 %collective-permute-done.21.b_ref = f32[64,128]{1,0:T(8,128)S(1)} collective-permute-done((f32[64,128]{1,0:T(8,128)S(1)}, f32[64,128]{1,0:T(8,128)S(1)}, u32[]{:S(2)}, u32[]{:S(2)}) %collective-permute-start.21) | collective-permute-done | bytes 32800 | tf_op jit(solution)/shard_map/ppermute | solution.py:39
  88.8 2.0 %collective-permute-start.28 = (bf16[640,128]{1,0:T(8,128)(2,1)S(1)}, bf16[640,128]{1,0:T(8,128)(2,1)S(1)}, u32[]{:S(2)}, u32[]{:S(2)}) collective-permute-start(bf16[640,128]{1,0:T(8,128)(2,1)S(1)} %get-tuple-element.89), channel_id=1, source_target_pairs={{0,4},{4,0},{1,5},{5,1},{2,6},{6,2},{3,7},{7,3},{8,12},{12,8},{9,1... | collective-permute-start | bytes 491528 | tf_op jit(solution)/shard_map/ppermute | solution.py:39
  92.0 3.2 %collective-permute-done.28.refs_5_ = bf16[640,128]{1,0:T(8,128)(2,1)S(1)} collective-permute-done((bf16[640,128]{1,0:T(8,128)(2,1)S(1)}, bf16[640,128]{1,0:T(8,128)(2,1)S(1)}, u32[]{:S(2)}, u32[]{:S(2)}) %collective-permute-start.28) | collective-permute-done | bytes 163872 | tf_op jit(solution)/shard_map/ppermute | solution.py:39
  95.2 4.0 %collective-permute-done.23.refs_2_ = bf16[960,128]{1,0:T(8,128)(2,1)S(1)} collective-permute-done((bf16[960,128]{1,0:T(8,128)(2,1)S(1)}, bf16[960,128]{1,0:T(8,128)(2,1)S(1)}, u32[]{:S(2)}, u32[]{:S(2)}) %collective-permute-start.23) | collective-permute-done | bytes 245792 | tf_op jit(solution)/shard_map/ppermute | solution.py:51
  99.1 5.2 %attention.1 = bf16[1024,128]{1,0:T(8,128)(2,1)} custom-call(s32[8]{0:T(128)S(1)} %copy-done.3, s32[1024]{0:T(1024)S(1)} %copy-done.2, f32[384,128]{1,0:T(8,128)S(1)} %get-tuple-element.80.refs_0_, bf16[960,128]{1,0:T(8,128)(2,1)S(1)} %collective-permute-done.22.refs_1_, bf16[960,128]{1,0:T(8,128)(2,1)S(1)} %collective-permute-done.23.refs_2_, ...), custom_call_target="tpu_custom_call" | custom-call | tf_op jit(solution)/shard_map/attention/pallas_call | solution.py:313
  (59 shorter events, 19.2 us)
Async XLA Ops:
  0.0 13.9 %collective-permute-start.1 = (bf16[1024,128]{1,0:T(8,128)(2,1)}, bf16[1024,128]{1,0:T(8,128)(2,1)S(1)}, u32[]{:S(2)}, u32[]{:S(2)}) collective-permute-start(bf16[1024,128]{1,0:T(8,128)(2,1)} %refs_0_.1), channel_id=1, source_target_pairs={{0,8},{8,16},{16,24},{24,32},{32,40},{40,48},{48,56},{56,0},{1,9},... | collective-permute-start | bytes 786440 | tf_op jit(solution)/shard_map/ppermute | solution.py:27
  1.9 12.0 %collective-permute-start = (bf16[1024,128]{1,0:T(8,128)(2,1)}, bf16[1024,128]{1,0:T(8,128)(2,1)S(1)}, u32[]{:S(2)}, u32[]{:S(2)}) collective-permute-start(bf16[1024,128]{1,0:T(8,128)(2,1)} %refs_0_.1), channel_id=1, source_target_pairs={{0,56},{8,0},{16,8},{24,16},{32,24},{40,32},{48,40},{56,48},{1,57}... | collective-permute-start | bytes 786440 | tf_op jit(solution)/shard_map/ppermute | solution.py:27
  9.5 9.6 %collective-permute-start.4 = (bf16[16,64,128]{2,1,0:T(8,128)(2,1)}, bf16[16,64,128]{2,1,0:T(8,128)(2,1)S(1)}, u32[]{:S(2)}, u32[]{:S(2)}) collective-permute-start(bf16[16,64,128]{2,1,0:T(8,128)(2,1)} %get-tuple-element.52), channel_id=1, source_target_pairs={{0,128},{128,0},{1,129},{129,1},{2,130},{130,2},{3,131},{131,3},{4... | collective-permute-start | bytes 786440 | tf_op jit(solution)/shard_map/ppermute | solution.py:47
  11.7 9.1 %collective-permute-start.2 = (bf16[1280,128]{1,0:T(8,128)(2,1)}, bf16[1280,128]{1,0:T(8,128)(2,1)S(1)}, u32[]{:S(2)}, u32[]{:S(2)}) collective-permute-start(bf16[1280,128]{1,0:T(8,128)(2,1)} %get-tuple-element.50), channel_id=1, source_target_pairs={{0,1},{1,2},{2,3},{3,0},{4,5},{5,6},{6,7},{7,4},{64,67},{65,64},{6... | collective-permute-start | bytes 983048 | tf_op jit(solution)/shard_map/ppermute | solution.py:75
  13.2 7.5 %collective-permute-start.3 = (bf16[1280,128]{1,0:T(8,128)(2,1)}, bf16[1280,128]{1,0:T(8,128)(2,1)S(1)}, u32[]{:S(2)}, u32[]{:S(2)}) collective-permute-start(bf16[1280,128]{1,0:T(8,128)(2,1)} %get-tuple-element.51), channel_id=1, source_target_pairs={{64,66},{65,67},{66,64},{67,65},{68,70},{69,71},{70,68},{71,69},{1... | collective-permute-start | bytes 983048 | tf_op jit(solution)/shard_map/ppermute | solution.py:75
  20.1 19.5 %collective-permute-start.7 = (bf16[1280,128]{1,0:T(8,128)(2,1)}, bf16[1280,128]{1,0:T(8,128)(2,1)S(1)}, u32[]{:S(2)}, u32[]{:S(2)}) collective-permute-start(bf16[1280,128]{1,0:T(8,128)(2,1)} %get-tuple-element.57), channel_id=1, source_target_pairs={{0,4},{1,5},{2,6},{3,7},{4,0},{5,1},{6,2},{7,3},{64,197},{65,198},... | collective-permute-start | bytes 983048 | tf_op jit(solution)/shard_map/ppermute | solution.py:75
  20.8 7.3 %collective-permute-start.5 = (bf16[1024,128]{1,0:T(8,128)(2,1)S(1)}, bf16[1024,128]{1,0:T(8,128)(2,1)S(1)}, u32[]{:S(2)}, u32[]{:S(2)}) collective-permute-start(bf16[1024,128]{1,0:T(8,128)(2,1)S(1)} %collective-permute-done.refs_1_), channel_id=1, source_target_pairs={{0,56},{8,0},{16,8},{24,16},{32,24},{40,32},{48,40},{56,48},{1,57}... | collective-permute-start | bytes 786440 | tf_op jit(solution)/shard_map/ppermute | solution.py:27
  22.6 8.6 %collective-permute-start.6 = (bf16[1024,128]{1,0:T(8,128)(2,1)S(1)}, bf16[1024,128]{1,0:T(8,128)(2,1)S(1)}, u32[]{:S(2)}, u32[]{:S(2)}) collective-permute-start(bf16[1024,128]{1,0:T(8,128)(2,1)S(1)} %collective-permute-done.1.refs_7_), channel_id=1, source_target_pairs={{0,8},{8,16},{16,24},{24,32},{32,40},{40,48},{48,56},{56,0},{1,9},... | collective-permute-start | bytes 786440 | tf_op jit(solution)/shard_map/ppermute | solution.py:27
  23.6 16.0 %collective-permute-start.9 = (bf16[32,1024]{1,0:T(8,128)(2,1)S(1)}, bf16[32,1024]{1,0:T(8,128)(2,1)S(1)}, u32[]{:S(2)}, u32[]{:S(2)}) collective-permute-start(bf16[32,1024]{1,0:T(8,128)(2,1)S(1)} %get-tuple-element.59), channel_id=1, source_target_pairs={{0,32},{8,40},{16,48},{24,56},{32,0},{40,8},{48,16},{56,24},{1,33}... | collective-permute-start | bytes 196616 | tf_op jit(solution)/shard_map/ppermute | solution.py:31
  31.3 17.4 %collective-permute-start.12 = (bf16[1280,128]{1,0:T(8,128)(2,1)S(1)}, bf16[1280,128]{1,0:T(8,128)(2,1)S(1)}, u32[]{:S(2)}, u32[]{:S(2)}) collective-permute-start(bf16[1280,128]{1,0:T(8,128)(2,1)S(1)} %copy-done.4), channel_id=1, source_target_pairs={{0,6},{1,7},{2,4},{3,5},{4,2},{5,3},{6,0},{7,1},{64,199},{65,196},... | collective-permute-start | bytes 983048 | tf_op jit(solution)/shard_map/ppermute | solution.py:75
  41.0 7.6 %collective-permute-start.11 = (bf16[1024,128]{1,0:T(8,128)(2,1)S(1)}, bf16[1024,128]{1,0:T(8,128)(2,1)S(1)}, u32[]{:S(2)}, u32[]{:S(2)}) collective-permute-start(bf16[1024,128]{1,0:T(8,128)(2,1)S(1)} %collective-permute-done.6.refs_6_), channel_id=1, source_target_pairs={{0,8},{8,16},{16,24},{24,32},{32,40},{40,48},{48,56},{56,0},{1,9},... | collective-permute-start | bytes 786440 | tf_op jit(solution)/shard_map/ppermute | solution.py:27
  48.7 10.0 %collective-permute-start.14 = (bf16[4,1280,128]{2,1,0:T(8,128)(2,1)S(1)}, bf16[4,1280,128]{2,1,0:T(8,128)(2,1)S(1)}, u32[]{:S(2)}, u32[]{:S(2)}) collective-permute-start(bf16[4,1280,128]{2,1,0:T(8,128)(2,1)S(1)} %stack.13), channel_id=1, source_target_pairs={{0,64},{64,0},{1,65},{65,1},{2,66},{66,2},{3,67},{67,3},{4,68},{68... | collective-permute-start | bytes 3932168 | tf_op jit(solution)/shard_map/ppermute | solution.py:43
  48.8 9.9 %collective-permute-start.13 = (bf16[1024,128]{1,0:T(8,128)(2,1)S(1)}, bf16[1024,128]{1,0:T(8,128)(2,1)S(1)}, u32[]{:S(2)}, u32[]{:S(2)}) collective-permute-start(bf16[1024,128]{1,0:T(8,128)(2,1)S(1)} %collective-permute-done.11.refs_5_), channel_id=1, source_target_pairs={{0,8},{8,16},{16,24},{24,32},{32,40},{40,48},{48,56},{56,0},{1,9},... | collective-permute-start | bytes 786440 | tf_op jit(solution)/shard_map/ppermute | solution.py:27
  48.9 7.8 %collective-permute-start.15 = (bf16[32,1024]{1,0:T(8,128)(2,1)S(1)}, bf16[32,1024]{1,0:T(8,128)(2,1)S(1)}, u32[]{:S(2)}, u32[]{:S(2)}) collective-permute-start(bf16[32,1024]{1,0:T(8,128)(2,1)S(1)} %get-tuple-element.69), channel_id=1, source_target_pairs={{0,8},{8,0},{16,24},{24,16},{32,40},{40,32},{48,56},{56,48},{1,9},... | collective-permute-start | bytes 196616 | tf_op jit(solution)/shard_map/ppermute | solution.py:31
  60.4 8.4 %collective-permute-start.16 = (bf16[576,128]{1,0:T(8,128)(2,1)S(1)}, bf16[576,128]{1,0:T(8,128)(2,1)S(1)}, u32[]{:S(2)}, u32[]{:S(2)}) collective-permute-start(bf16[576,128]{1,0:T(8,128)(2,1)S(1)} %get-tuple-element.73), channel_id=1, source_target_pairs={{0,2},{1,3},{2,0},{3,1},{4,6},{5,7},{6,4},{7,5},{8,10},{9,11},{10,... | collective-permute-start | bytes 442376 | tf_op jit(solution)/shard_map/ppermute | solution.py:51
  60.5 9.8 %collective-permute-start.17 = (bf16[576,128]{1,0:T(8,128)(2,1)S(1)}, bf16[576,128]{1,0:T(8,128)(2,1)S(1)}, u32[]{:S(2)}, u32[]{:S(2)}) collective-permute-start(bf16[576,128]{1,0:T(8,128)(2,1)S(1)} %get-tuple-element.74), channel_id=1, source_target_pairs={{0,1},{1,2},{2,3},{3,0},{4,5},{5,6},{6,7},{7,4},{8,9},{9,10},{10,1... | collective-permute-start | bytes 442376 | tf_op jit(solution)/shard_map/ppermute | solution.py:51
  61.9 8.4 %collective-permute-start.18 = (bf16[576,128]{1,0:T(8,128)(2,1)S(1)}, bf16[576,128]{1,0:T(8,128)(2,1)S(1)}, u32[]{:S(2)}, u32[]{:S(2)}) collective-permute-start(bf16[576,128]{1,0:T(8,128)(2,1)S(1)} %get-tuple-element.75), channel_id=1, source_target_pairs={{0,3},{1,0},{2,1},{3,2},{4,7},{5,4},{6,5},{7,6},{8,11},{9,8},{10,9... | collective-permute-start | bytes 442376 | tf_op jit(solution)/shard_map/ppermute | solution.py:51
  70.4 14.7 %collective-permute-start.19 = (bf16[2048,128]{1,0:T(8,128)(2,1)S(1)}, bf16[2048,128]{1,0:T(8,128)(2,1)S(1)}, u32[]{:S(2)}, u32[]{:S(2)}) collective-permute-start(bf16[2048,128]{1,0:T(8,128)(2,1)S(1)} %get-tuple-element.77), channel_id=1, source_target_pairs={{0,4},{4,0},{1,5},{5,1},{2,6},{6,2},{3,7},{7,3},{8,12},{12,8},{9,1... | collective-permute-start | bytes 1572872 | tf_op jit(solution)/shard_map/ppermute | solution.py:39
  70.7 16.5 %collective-permute-start.25 = (bf16[1280,128]{1,0:T(8,128)(2,1)S(1)}, bf16[1280,128]{1,0:T(8,128)(2,1)S(1)}, u32[]{:S(2)}, u32[]{:S(2)}) collective-permute-start(bf16[1280,128]{1,0:T(8,128)(2,1)S(1)} %get-tuple-element.85), channel_id=1, source_target_pairs={{0,2},{1,3},{2,0},{3,1},{4,6},{5,7},{6,4},{7,5},{8,10},{9,11},{10,... | collective-permute-start | bytes 983048 | tf_op jit(solution)/shard_map/ppermute | solution.py:51
  72.8 15.8 %collective-permute-start.26 = (bf16[1280,128]{1,0:T(8,128)(2,1)S(1)}, bf16[1280,128]{1,0:T(8,128)(2,1)S(1)}, u32[]{:S(2)}, u32[]{:S(2)}) collective-permute-start(bf16[1280,128]{1,0:T(8,128)(2,1)S(1)} %get-tuple-element.86), channel_id=1, source_target_pairs={{0,1},{1,2},{2,3},{3,0},{4,5},{5,6},{6,7},{7,4},{8,9},{9,10},{10,1... | collective-permute-start | bytes 983048 | tf_op jit(solution)/shard_map/ppermute | solution.py:51
  74.4 14.3 %collective-permute-start.27 = (bf16[1280,128]{1,0:T(8,128)(2,1)S(1)}, bf16[1280,128]{1,0:T(8,128)(2,1)S(1)}, u32[]{:S(2)}, u32[]{:S(2)}) collective-permute-start(bf16[1280,128]{1,0:T(8,128)(2,1)S(1)} %get-tuple-element.87), channel_id=1, source_target_pairs={{0,3},{1,0},{2,1},{3,2},{4,7},{5,4},{6,5},{7,6},{8,11},{9,8},{10,9... | collective-permute-start | bytes 983048 | tf_op jit(solution)/shard_map/ppermute | solution.py:51
  85.3 9.8 %collective-permute-start.22 = (bf16[960,128]{1,0:T(8,128)(2,1)S(1)}, bf16[960,128]{1,0:T(8,128)(2,1)S(1)}, u32[]{:S(2)}, u32[]{:S(2)}) collective-permute-start(bf16[960,128]{1,0:T(8,128)(2,1)S(1)} %get-tuple-element.81), channel_id=1, source_target_pairs={{0,1},{1,2},{2,3},{3,0},{4,5},{5,6},{6,7},{7,4},{8,9},{9,10},{10,1... | collective-permute-start | bytes 737288 | tf_op jit(solution)/shard_map/ppermute | solution.py:51
  85.7 13.4 %collective-permute-start.23 = (bf16[960,128]{1,0:T(8,128)(2,1)S(1)}, bf16[960,128]{1,0:T(8,128)(2,1)S(1)}, u32[]{:S(2)}, u32[]{:S(2)}) collective-permute-start(bf16[960,128]{1,0:T(8,128)(2,1)S(1)} %get-tuple-element.82), channel_id=1, source_target_pairs={{0,2},{1,3},{2,0},{3,1},{4,6},{5,7},{6,4},{7,5},{8,10},{9,11},{10,... | collective-permute-start | bytes 737288 | tf_op jit(solution)/shard_map/ppermute | solution.py:51
  87.3 11.9 %collective-permute-start.24 = (bf16[960,128]{1,0:T(8,128)(2,1)S(1)}, bf16[960,128]{1,0:T(8,128)(2,1)S(1)}, u32[]{:S(2)}, u32[]{:S(2)}) collective-permute-start(bf16[960,128]{1,0:T(8,128)(2,1)S(1)} %get-tuple-element.83), channel_id=1, source_target_pairs={{0,3},{1,0},{2,1},{3,2},{4,7},{5,4},{6,5},{7,6},{8,11},{9,8},{10,9... | collective-permute-start | bytes 737288 | tf_op jit(solution)/shard_map/ppermute | solution.py:51
  (10 other events, 154.9 us)

commit v13 on v12

--- a/solution.py
+++ b/solution.py
@@ -94,10 +94,10 @@
     return pairs
 
 
-def pack_kernel(wq_ref, kv_ref, down_ref, up_ref, *refs):
-    outs, maps, sem = refs[:5], refs[5], refs[6]
+def pack_kernel(wq_ref, kv_ref, *refs):
+    outs, sem = refs[:5], refs[5]
     c = lax.axis_index("c")
-    pairs = [(down_ref, maps.at[:, 0:RANK, :]), (up_ref, maps.at[:, RANK : 2 * RANK, :])]
+    pairs = []
     for k, out in enumerate(outs):
         d = jnp.where(c == 0, (SERVED[0] + (0,))[k], SERVED[1][k]) if k < 4 else 0
         pairs += weight_pairs(wq_ref, kv_ref, out, d)
@@ -148,7 +148,7 @@
         owner = a // per
         at = a - owner * per
         xr, cr = (owner // NC) ^ xh, (owner % NC) ^ c
-        down = jnp.where(cr == 0, near_ref[xr, at, 0:RANK, :], far_ref[xr, at, 0:RANK, :])
+        down = jnp.where(cr == 0, near_ref[xr, at], far_ref[xr, at])
         out_ref[:, b * BLOCK : (b + 1) * BLOCK] = lax.dot_general(
             down,
             h_ref[b * BLOCK : (b + 1) * BLOCK, :],
@@ -285,7 +285,7 @@
         owner = a // per
         at = a - owner * per
         xr, cr = (owner // NC) ^ xh, (owner % NC) ^ c
-        up = jnp.where(cr == 0, near_ref[xr, at, RANK : 2 * RANK, :], far_ref[xr, at, RANK : 2 * RANK, :])
+        up = jnp.where(cr == 0, near_ref[xr, at], far_ref[xr, at])
         q = ADAPTER_SCALE * lax.dot_general(
             low_buf[b], up, (((0,), (0,)), ((), ())), preferred_element_type=jnp.float32
         )
@@ -329,15 +329,13 @@
     rows = hidden.shape[0]
     bf16, f32 = jnp.bfloat16, jnp.float32
     of = jax.ShapeDtypeStruct
-    *sends, maps = call(
+    sends = call(
         pack_kernel,
         "pack",
-        [of((1280, 128), bf16)] * 5 + [of((down_maps.shape[0], 2 * RANK, 128), bf16)],
+        [of((1280, 128), bf16)] * 5,
         query_weight,
         key_value_weight.T,
-        jnp.transpose(down_maps, (0, 2, 1)),
-        up_maps,
-        scratch=[pltpu.SemaphoreType.DMA((10 * NZ + 2,))],
+        scratch=[pltpu.SemaphoreType.DMA((10 * NZ,))],
         space=pltpu.HBM,
         mib=PACK_MIB,
     )
@@ -348,7 +346,9 @@
         request_start,
         scalars=1,
     )
-    twin = xh_swap(maps)
+    down_maps = jnp.transpose(down_maps, (0, 2, 1))
+    pair = of((2, *down_maps.shape), bf16)
+    twin = xh_swap(down_maps)
     ring = [(hidden, hidden)]
 
     def ring_step(*others):
@@ -364,7 +364,7 @@
 
     ring_step()
     mine = [weight_send(sends[0], 0), weight_send(after(sends[1], *ring[1]), 1), None, weight_send(sends[3], 3)]
-    near = jnp.stack([maps, after(twin, *ring[1])])
+    near = call(stack_kernel, "near", pair, down_maps, after(twin, *ring[1]))
     ring_step(mine[0], mine[3], near)
     far = core_swap(near)
     mine[2] = weight_send(after(sends[2], *ring[2]), 2)
@@ -377,9 +377,11 @@
     low = added(low, z_xor(after(narrow, *ring[3]), 1))
     mine[3] = after(mine[3], *ring[3])
     other = core_swap(call(stack_kernel, "stack", of((4, 1280, 128), bf16), *mine))
+    near = call(stack_kernel, "near", pair, up_maps, xh_swap(after(up_maps, *ring[3])))
+    far = core_swap(near)
     right, left = zip(*ring)
 
-    shards = [hidden, left[1], left[2], left[3], right[4], right[3], right[2], right[1]]
+    shards = [after(hidden, near), left[1], left[2], left[3], right[4], right[3], right[2], right[1]]
     weights = (sends[4], *mine, other)
     *kv_parts, gathered = call(
         kv_product_kernel,

time: 105 us -> 106 us (level)
  starting transfers between devices: 42.8 us -> 47.3 us
  waiting for transfers between devices: 44.7 us -> 43.1 us
    ppermute x4, starting transfers between devices: 11.2 us -> 6.28 us  [weight_send(): return lax.ppermute(v, ('xh', 'c', 'xl', 'y'), route)]
    ppermute x3, waiting for transfers between devices: 12.9 us -> 8.85 us  [z_xor(): return lax.ppermute(v, 'z', [(i, i ^ s) for i in range(NZ)])]
    ppermute x1 -> x2, starting transfers between devices: 2.21 us -> 5.27 us  [xh_swap(): return lax.ppermute(v, 'xh', [(0, 1), (1, 0)])]
    ppermute x9, starting transfers between devices: 12 us -> 14.9 us  [y_shift(): return lax.ppermute(v, 'y', [(i, (i + s) % NY) for i in range(NY)])]
    ppermute x7, waiting for transfers between devices: 12.1 us -> 13.8 us  [z_shift(): return lax.ppermute(v, 'z', [(i, (i + s) % NZ) for i in range(NZ)])]
    ppermute x7, starting transfers between devices: 10.2 us -> 11.3 us  [z_shift(): return lax.ppermute(v, 'z', [(i, (i + s) % NZ) for i in range(NZ)])]
    ppermute x2 -> x3, starting transfers between devices: 0.19 us -> 1.37 us  [core_swap(): return lax.ppermute(v, 'c', [(0, 1), (1, 0)])]
    ppermute x1 -> x2, waiting for transfers between devices: 5.08 us -> 4.39 us  [xh_swap(): return lax.ppermute(v, 'xh', [(0, 1), (1, 0)])]
  transfers between devices with their start and end apart: 29 -> 31, of which waited for: 12 -> 14; matrix products, arithmetic and copies ran while one was open for 1% -> 0% of each run, Pallas kernels for 8% -> 5%
where the time goes in v13:
time: 106 us
  starting transfers between devices  47.3 us (45%)
  waiting for transfers between devices  43.1 us (41%)
  Pallas kernels  15.3 us (14%)
    pallas_call x16, Pallas kernels, call(): pl.pallas_call(kernel, out_shape=outs, in_specs=[SMEM] * scalars + [pl.Bl...  15.3 us
    ppermute x9, starting transfers between devices, y_shift(): return lax.ppermute(v, 'y', [(i, (i + s) % NY) for i in range(NY)])  14.9 us
    ppermute x7, waiting for transfers between devices, z_shift(): return lax.ppermute(v, 'z', [(i, (i + s) % NZ) for i in range(NZ)])  13.8 us
    ppermute x7, starting transfers between devices, z_shift(): return lax.ppermute(v, 'z', [(i, (i + s) % NZ) for i in range(NZ)])  11.3 us
    ppermute x3, waiting for transfers between devices, z_xor(): return lax.ppermute(v, 'z', [(i, i ^ s) for i in range(NZ)])  8.85 us
    ppermute x9, waiting for transfers between devices, y_shift(): return lax.ppermute(v, 'y', [(i, (i + s) % NY) for i in range(NY)])  8.35 us
    ppermute x3, waiting for transfers between devices, x_swap(): return lax.ppermute(v, 'xl', [(0, 1), (1, 0)])  7.76 us
    ppermute x4, starting transfers between devices, weight_send(): return lax.ppermute(v, ('xh', 'c', 'xl', 'y'), route)  6.28 us
  transfers between devices with their start and end apart: 31, of which 14 were waited for; matrix products, arithmetic and copies ran while one was open for 0% of the time, Pallas kernels for 5%

profile of v13, /device:TPU:2, one launch (start us, length us, event | category | flops | bytes accessed | tf_op | source)
XLA Modules:
  0.0 106.0 jit_solution(3580747183330451855)
XLA Ops:
  0.0 3.4 %pack.1 = (bf16[1280,128]{1,0:T(8,128)(2,1)}, bf16[1280,128]{1,0:T(8,128)(2,1)}, bf16[1280,128]{1,0:T(8,128)(2,1)}, bf16[1280,128]{1,0:T(8,128)(2,1)}, bf16[1280,128]{1,0:T(8,128)(2,1)}) custom-call(bf16[8192,128]{1,0:T(8,128)(2,1)} %wq_ref.1, bf16[32,8192]{1,0:T(8,128)(2,1)} %bitcast.4), custom_call_target="tpu_custom_call" | custom-call | tf_op jit(solution)/shard_map/pack/pallas_call | solution.py:313
  5.7 2.0 %collective-permute-start = (bf16[1024,128]{1,0:T(8,128)(2,1)S(1)}, bf16[1024,128]{1,0:T(8,128)(2,1)S(1)}, u32[]{:S(2)}, u32[]{:S(2)}) collective-permute-start(bf16[1024,128]{1,0:T(8,128)(2,1)S(1)} %copy-done.1), channel_id=1, source_target_pairs={{0,8},{8,16},{16,24},{24,32},{32,40},{40,48},{48,56},{56,0},{1,9},... | collective-permute-start | bytes 786440 | tf_op jit(solution)/shard_map/ppermute | solution.py:27
  7.7 4.0 %collective-permute-start.1 = (bf16[1024,128]{1,0:T(8,128)(2,1)S(1)}, bf16[1024,128]{1,0:T(8,128)(2,1)S(1)}, u32[]{:S(2)}, u32[]{:S(2)}) collective-permute-start(bf16[1024,128]{1,0:T(8,128)(2,1)S(1)} %copy-done.1), channel_id=1, source_target_pairs={{0,56},{8,0},{16,8},{24,16},{32,24},{40,32},{48,40},{56,48},{1,57}... | collective-permute-start | bytes 786440 | tf_op jit(solution)/shard_map/ppermute | solution.py:27
  11.7 2.1 %collective-permute-start.4 = (bf16[16,32,128]{2,1,0:T(8,128)(2,1)S(1)}, bf16[16,32,128]{2,1,0:T(8,128)(2,1)S(1)}, u32[]{:S(2)}, u32[]{:S(2)}) collective-permute-start(bf16[16,32,128]{2,1,0:T(8,128)(2,1)S(1)} %bitcast.2), channel_id=1, source_target_pairs={{0,128},{128,0},{1,129},{129,1},{2,130},{130,2},{3,131},{131,3},{4... | collective-permute-start | bytes 393224 | tf_op jit(solution)/shard_map/ppermute | solution.py:47
  13.9 4.4 %collective-permute-done.4.refs_1_ = bf16[16,32,128]{2,1,0:T(8,128)(2,1)S(1)} collective-permute-done((bf16[16,32,128]{2,1,0:T(8,128)(2,1)S(1)}, bf16[16,32,128]{2,1,0:T(8,128)(2,1)S(1)}, u32[]{:S(2)}, u32[]{:S(2)}) %collective-permute-start.4) | collective-permute-done | bytes 131104 | tf_op jit(solution)/shard_map/ppermute | solution.py:47
  20.1 2.5 %collective-permute-start.6 = (bf16[1024,128]{1,0:T(8,128)(2,1)S(1)}, bf16[1024,128]{1,0:T(8,128)(2,1)S(1)}, u32[]{:S(2)}, u32[]{:S(2)}) collective-permute-start(bf16[1024,128]{1,0:T(8,128)(2,1)S(1)} %collective-permute-done.1.refs_1_), channel_id=1, source_target_pairs={{0,56},{8,0},{16,8},{24,16},{32,24},{40,32},{48,40},{56,48},{1,57}... | collective-permute-start | bytes 786440 | tf_op jit(solution)/shard_map/ppermute | solution.py:27
  23.4 4.6 %collective-permute-start.9 = (bf16[32,1024]{1,0:T(8,128)(2,1)S(1)}, bf16[32,1024]{1,0:T(8,128)(2,1)S(1)}, u32[]{:S(2)}, u32[]{:S(2)}) collective-permute-start(bf16[32,1024]{1,0:T(8,128)(2,1)S(1)} %get-tuple-element.59), channel_id=1, source_target_pairs={{0,32},{8,40},{16,48},{24,56},{32,0},{40,8},{48,16},{56,24},{1,33}... | collective-permute-start | bytes 196616 | tf_op jit(solution)/shard_map/ppermute | solution.py:31
  28.5 5.9 %collective-permute-done.5.refs_6_ = bf16[1024,128]{1,0:T(8,128)(2,1)S(1)} collective-permute-done((bf16[1024,128]{1,0:T(8,128)(2,1)S(1)}, bf16[1024,128]{1,0:T(8,128)(2,1)S(1)}, u32[]{:S(2)}, u32[]{:S(2)}) %collective-permute-start.5) | collective-permute-done | bytes 262176 | tf_op jit(solution)/shard_map/ppermute | solution.py:27
  34.4 3.4 %collective-permute-start.13 = (bf16[1280,128]{1,0:T(8,128)(2,1)}, bf16[1280,128]{1,0:T(8,128)(2,1)S(1)}, u32[]{:S(2)}, u32[]{:S(2)}) collective-permute-start(bf16[1280,128]{1,0:T(8,128)(2,1)} %get-tuple-element.66), channel_id=1, source_target_pairs={{0,6},{1,7},{2,4},{3,5},{4,2},{5,3},{6,0},{7,1},{64,199},{65,196},... | collective-permute-start | bytes 983048 | tf_op jit(solution)/shard_map/ppermute | solution.py:75
  40.0 4.3 %collective-permute-done.11.refs_3_ = bf16[1024,128]{1,0:T(8,128)(2,1)S(1)} collective-permute-done((bf16[1024,128]{1,0:T(8,128)(2,1)S(1)}, bf16[1024,128]{1,0:T(8,128)(2,1)S(1)}, u32[]{:S(2)}, u32[]{:S(2)}) %collective-permute-start.11) | collective-permute-done | bytes 262176 | tf_op jit(solution)/shard_map/ppermute | solution.py:27
  46.6 3.1 %collective-permute-start.12 = (bf16[16,32,128]{2,1,0:T(8,128)(2,1)S(1)}, bf16[16,32,128]{2,1,0:T(8,128)(2,1)S(1)}, u32[]{:S(2)}, u32[]{:S(2)}) collective-permute-start(bf16[16,32,128]{2,1,0:T(8,128)(2,1)S(1)} %copy-done.3), channel_id=1, source_target_pairs={{0,128},{128,0},{1,129},{129,1},{2,130},{130,2},{3,131},{131,3},{4... | collective-permute-start | bytes 393224 | tf_op jit(solution)/shard_map/ppermute | solution.py:47
  50.0 4.1 %collective-permute-done.16.b_ref = bf16[32,1024]{1,0:T(8,128)(2,1)S(1)} collective-permute-done((bf16[32,1024]{1,0:T(8,128)(2,1)S(1)}, bf16[32,1024]{1,0:T(8,128)(2,1)S(1)}, u32[]{:S(2)}, u32[]{:S(2)}) %collective-permute-start.16) | collective-permute-done | bytes 65568 | tf_op jit(solution)/shard_map/ppermute | solution.py:31
  57.3 1.9 %collective-permute-start.17 = (bf16[576,128]{1,0:T(8,128)(2,1)S(1)}, bf16[576,128]{1,0:T(8,128)(2,1)S(1)}, u32[]{:S(2)}, u32[]{:S(2)}) collective-permute-start(bf16[576,128]{1,0:T(8,128)(2,1)S(1)} %get-tuple-element.75), channel_id=1, source_target_pairs={{0,2},{1,3},{2,0},{3,1},{4,6},{5,7},{6,4},{7,5},{8,10},{9,11},{10,... | collective-permute-start | bytes 442376 | tf_op jit(solution)/shard_map/ppermute | solution.py:51
  59.2 2.1 %collective-permute-start.18 = (bf16[576,128]{1,0:T(8,128)(2,1)S(1)}, bf16[576,128]{1,0:T(8,128)(2,1)S(1)}, u32[]{:S(2)}, u32[]{:S(2)}) collective-permute-start(bf16[576,128]{1,0:T(8,128)(2,1)S(1)} %get-tuple-element.76), channel_id=1, source_target_pairs={{0,1},{1,2},{2,3},{3,0},{4,5},{5,6},{6,7},{7,4},{8,9},{9,10},{10,1... | collective-permute-start | bytes 442376 | tf_op jit(solution)/shard_map/ppermute | solution.py:51
  62.4 2.7 %q_product.1 = (bf16[1536,128]{1,0:T(8,128)(2,1)S(1)}, bf16[1536,128]{1,0:T(8,128)(2,1)S(1)}, bf16[1280,128]{1,0:T(8,128)(2,1)S(1)}, bf16[1280,128]{1,0:T(8,128)...) custom-call(bf16[1024,1024]{1,0:T(8,128)(2,1)S(1)} %get-tuple-element.72.hbuf, ...), custom_call_target="tpu_custom_call" | custom-call | tf_op jit(solution)/shard_map/q_product/pallas_call | solution.py:313
  65.2 2.3 %collective-permute-done.18.k2 = bf16[576,128]{1,0:T(8,128)(2,1)S(1)} collective-permute-done((bf16[576,128]{1,0:T(8,128)(2,1)S(1)}, bf16[576,128]{1,0:T(8,128)(2,1)S(1)}, u32[]{:S(2)}, u32[]{:S(2)}) %collective-permute-start.18) | collective-permute-done | bytes 147488 | tf_op jit(solution)/shard_map/ppermute | solution.py:51
  69.7 3.0 %collective-permute-start.26 = (bf16[1280,128]{1,0:T(8,128)(2,1)S(1)}, bf16[1280,128]{1,0:T(8,128)(2,1)S(1)}, u32[]{:S(2)}, u32[]{:S(2)}) collective-permute-start(bf16[1280,128]{1,0:T(8,128)(2,1)S(1)} %get-tuple-element.87), channel_id=1, source_target_pairs={{0,2},{1,3},{2,0},{3,1},{4,6},{5,7},{6,4},{7,5},{8,10},{9,11},{10,... | collective-permute-start | bytes 983048 | tf_op jit(solution)/shard_map/ppermute | solution.py:51
  73.3 2.7 %collective-permute-start.28 = (bf16[1280,128]{1,0:T(8,128)(2,1)S(1)}, bf16[1280,128]{1,0:T(8,128)(2,1)S(1)}, u32[]{:S(2)}, u32[]{:S(2)}) collective-permute-start(bf16[1280,128]{1,0:T(8,128)(2,1)S(1)} %get-tuple-element.89), channel_id=1, source_target_pairs={{0,3},{1,0},{2,1},{3,2},{4,7},{5,4},{6,5},{7,6},{8,11},{9,8},{10,9... | collective-permute-start | bytes 983048 | tf_op jit(solution)/shard_map/ppermute | solution.py:51
  76.4 4.7 %collective-permute-done.21.b_ref = f32[64,128]{1,0:T(8,128)S(1)} collective-permute-done((f32[64,128]{1,0:T(8,128)S(1)}, f32[64,128]{1,0:T(8,128)S(1)}, u32[]{:S(2)}, u32[]{:S(2)}) %collective-permute-start.21) | collective-permute-done | bytes 32800 | tf_op jit(solution)/shard_map/ppermute | solution.py:31
  81.2 3.8 %collective-permute-done.22.b_ref = f32[64,128]{1,0:T(8,128)S(1)} collective-permute-done((f32[64,128]{1,0:T(8,128)S(1)}, f32[64,128]{1,0:T(8,128)S(1)}, u32[]{:S(2)}, u32[]{:S(2)}) %collective-permute-start.22) | collective-permute-done | bytes 32800 | tf_op jit(solution)/shard_map/ppermute | solution.py:39
  85.4 2.3 %collective-permute-start.24 = (bf16[960,128]{1,0:T(8,128)(2,1)S(1)}, bf16[960,128]{1,0:T(8,128)(2,1)S(1)}, u32[]{:S(2)}, u32[]{:S(2)}) collective-permute-start(bf16[960,128]{1,0:T(8,128)(2,1)S(1)} %get-tuple-element.84), channel_id=1, source_target_pairs={{0,2},{1,3},{2,0},{3,1},{4,6},{5,7},{6,4},{7,5},{8,10},{9,11},{10,... | collective-permute-start | bytes 737288 | tf_op jit(solution)/shard_map/ppermute | solution.py:51
  91.2 3.9 %collective-permute-done.29.refs_5_ = bf16[640,128]{1,0:T(8,128)(2,1)S(1)} collective-permute-done((bf16[640,128]{1,0:T(8,128)(2,1)S(1)}, bf16[640,128]{1,0:T(8,128)(2,1)S(1)}, u32[]{:S(2)}, u32[]{:S(2)}) %collective-permute-start.29) | collective-permute-done | bytes 163872 | tf_op jit(solution)/shard_map/ppermute | solution.py:39
  95.2 5.0 %collective-permute-done.23.refs_1_ = bf16[960,128]{1,0:T(8,128)(2,1)S(1)} collective-permute-done((bf16[960,128]{1,0:T(8,128)(2,1)S(1)}, bf16[960,128]{1,0:T(8,128)(2,1)S(1)}, u32[]{:S(2)}, u32[]{:S(2)}) %collective-permute-start.23) | collective-permute-done | bytes 245792 | tf_op jit(solution)/shard_map/ppermute | solution.py:51
  100.8 5.2 %attention.1 = bf16[1024,128]{1,0:T(8,128)(2,1)} custom-call(s32[8]{0:T(128)S(1)} %copy-done.5, s32[1024]{0:T(1024)S(1)} %copy-done.4, f32[384,128]{1,0:T(8,128)S(1)} %get-tuple-element.82.refs_0_, bf16[960,128]{1,0:T(8,128)(2,1)S(1)} %collective-permute-done.23.refs_1_, bf16[960,128]{1,0:T(8,128)(2,1)S(1)} %collective-permute-done.24.refs_2_, ...), custom_call_target="tpu_custom_call" | custom-call | tf_op jit(solution)/shard_map/attention/pallas_call | solution.py:313
  (66 shorter events, 22.2 us)
Async XLA Ops:
  3.4 16.7 %collective-permute-start.2 = (bf16[1280,128]{1,0:T(8,128)(2,1)}, bf16[1280,128]{1,0:T(8,128)(2,1)S(1)}, u32[]{:S(2)}, u32[]{:S(2)}) collective-permute-start(bf16[1280,128]{1,0:T(8,128)(2,1)} %get-tuple-element.51), channel_id=1, source_target_pairs={{0,1},{1,2},{2,3},{3,0},{4,5},{5,6},{6,7},{7,4},{64,67},{65,64},{6... | collective-permute-start | bytes 983048 | tf_op jit(solution)/shard_map/ppermute | solution.py:75
  5.0 15.1 %collective-permute-start.3 = (bf16[1280,128]{1,0:T(8,128)(2,1)}, bf16[1280,128]{1,0:T(8,128)(2,1)S(1)}, u32[]{:S(2)}, u32[]{:S(2)}) collective-permute-start(bf16[1280,128]{1,0:T(8,128)(2,1)} %get-tuple-element.52), channel_id=1, source_target_pairs={{64,66},{65,67},{66,64},{67,65},{68,70},{69,71},{70,68},{71,69},{1... | collective-permute-start | bytes 983048 | tf_op jit(solution)/shard_map/ppermute | solution.py:75
  5.7 12.5 %collective-permute-start = (bf16[1024,128]{1,0:T(8,128)(2,1)S(1)}, bf16[1024,128]{1,0:T(8,128)(2,1)S(1)}, u32[]{:S(2)}, u32[]{:S(2)}) collective-permute-start(bf16[1024,128]{1,0:T(8,128)(2,1)S(1)} %copy-done.1), channel_id=1, source_target_pairs={{0,8},{8,16},{16,24},{24,32},{32,40},{40,48},{48,56},{56,0},{1,9},... | collective-permute-start | bytes 786440 | tf_op jit(solution)/shard_map/ppermute | solution.py:27
  7.7 10.5 %collective-permute-start.1 = (bf16[1024,128]{1,0:T(8,128)(2,1)S(1)}, bf16[1024,128]{1,0:T(8,128)(2,1)S(1)}, u32[]{:S(2)}, u32[]{:S(2)}) collective-permute-start(bf16[1024,128]{1,0:T(8,128)(2,1)S(1)} %copy-done.1), channel_id=1, source_target_pairs={{0,56},{8,0},{16,8},{24,16},{32,24},{40,32},{48,40},{56,48},{1,57}... | collective-permute-start | bytes 786440 | tf_op jit(solution)/shard_map/ppermute | solution.py:27
  11.7 6.5 %collective-permute-start.4 = (bf16[16,32,128]{2,1,0:T(8,128)(2,1)S(1)}, bf16[16,32,128]{2,1,0:T(8,128)(2,1)S(1)}, u32[]{:S(2)}, u32[]{:S(2)}) collective-permute-start(bf16[16,32,128]{2,1,0:T(8,128)(2,1)S(1)} %bitcast.2), channel_id=1, source_target_pairs={{0,128},{128,0},{1,129},{129,1},{2,130},{130,2},{3,131},{131,3},{4... | collective-permute-start | bytes 393224 | tf_op jit(solution)/shard_map/ppermute | solution.py:47
  19.6 18.3 %collective-permute-start.7 = (bf16[1280,128]{1,0:T(8,128)(2,1)}, bf16[1280,128]{1,0:T(8,128)(2,1)S(1)}, u32[]{:S(2)}, u32[]{:S(2)}) collective-permute-start(bf16[1280,128]{1,0:T(8,128)(2,1)} %get-tuple-element.57), channel_id=1, source_target_pairs={{0,4},{1,5},{2,6},{3,7},{4,0},{5,1},{6,2},{7,3},{64,197},{65,198},... | collective-permute-start | bytes 983048 | tf_op jit(solution)/shard_map/ppermute | solution.py:75
  20.1 8.4 %collective-permute-start.6 = (bf16[1024,128]{1,0:T(8,128)(2,1)S(1)}, bf16[1024,128]{1,0:T(8,128)(2,1)S(1)}, u32[]{:S(2)}, u32[]{:S(2)}) collective-permute-start(bf16[1024,128]{1,0:T(8,128)(2,1)S(1)} %collective-permute-done.1.refs_1_), channel_id=1, source_target_pairs={{0,56},{8,0},{16,8},{24,16},{32,24},{40,32},{48,40},{56,48},{1,57}... | collective-permute-start | bytes 786440 | tf_op jit(solution)/shard_map/ppermute | solution.py:27
  22.6 11.8 %collective-permute-start.5 = (bf16[1024,128]{1,0:T(8,128)(2,1)S(1)}, bf16[1024,128]{1,0:T(8,128)(2,1)S(1)}, u32[]{:S(2)}, u32[]{:S(2)}) collective-permute-start(bf16[1024,128]{1,0:T(8,128)(2,1)S(1)} %collective-permute-done.refs_7_), channel_id=1, source_target_pairs={{0,8},{8,16},{16,24},{24,32},{32,40},{40,48},{48,56},{56,0},{1,9},... | collective-permute-start | bytes 786440 | tf_op jit(solution)/shard_map/ppermute | solution.py:27
  23.4 14.4 %collective-permute-start.9 = (bf16[32,1024]{1,0:T(8,128)(2,1)S(1)}, bf16[32,1024]{1,0:T(8,128)(2,1)S(1)}, u32[]{:S(2)}, u32[]{:S(2)}) collective-permute-start(bf16[32,1024]{1,0:T(8,128)(2,1)S(1)} %get-tuple-element.59), channel_id=1, source_target_pairs={{0,32},{8,40},{16,48},{24,56},{32,0},{40,8},{48,16},{56,24},{1,33}... | collective-permute-start | bytes 196616 | tf_op jit(solution)/shard_map/ppermute | solution.py:31
  34.4 11.3 %collective-permute-start.13 = (bf16[1280,128]{1,0:T(8,128)(2,1)}, bf16[1280,128]{1,0:T(8,128)(2,1)S(1)}, u32[]{:S(2)}, u32[]{:S(2)}) collective-permute-start(bf16[1280,128]{1,0:T(8,128)(2,1)} %get-tuple-element.66), channel_id=1, source_target_pairs={{0,6},{1,7},{2,4},{3,5},{4,2},{5,3},{6,0},{7,1},{64,199},{65,196},... | collective-permute-start | bytes 983048 | tf_op jit(solution)/shard_map/ppermute | solution.py:75
  38.1 7.6 %collective-permute-start.10 = (bf16[1024,128]{1,0:T(8,128)(2,1)S(1)}, bf16[1024,128]{1,0:T(8,128)(2,1)S(1)}, u32[]{:S(2)}, u32[]{:S(2)}) collective-permute-start(bf16[1024,128]{1,0:T(8,128)(2,1)S(1)} %collective-permute-done.5.refs_6_), channel_id=1, source_target_pairs={{0,8},{8,16},{16,24},{24,32},{32,40},{40,48},{48,56},{56,0},{1,9},... | collective-permute-start | bytes 786440 | tf_op jit(solution)/shard_map/ppermute | solution.py:27
  45.8 10.0 %collective-permute-start.15 = (bf16[4,1280,128]{2,1,0:T(8,128)(2,1)S(1)}, bf16[4,1280,128]{2,1,0:T(8,128)(2,1)S(1)}, u32[]{:S(2)}, u32[]{:S(2)}) collective-permute-start(bf16[4,1280,128]{2,1,0:T(8,128)(2,1)S(1)} %stack.1), channel_id=1, source_target_pairs={{0,64},{64,0},{1,65},{65,1},{2,66},{66,2},{3,67},{67,3},{4,68},{68... | collective-permute-start | bytes 3932168 | tf_op jit(solution)/shard_map/ppermute | solution.py:43
  45.9 9.9 %collective-permute-start.14 = (bf16[1024,128]{1,0:T(8,128)(2,1)S(1)}, bf16[1024,128]{1,0:T(8,128)(2,1)S(1)}, u32[]{:S(2)}, u32[]{:S(2)}) collective-permute-start(bf16[1024,128]{1,0:T(8,128)(2,1)S(1)} %collective-permute-done.10.refs_5_), channel_id=1, source_target_pairs={{0,8},{8,16},{16,24},{24,32},{32,40},{40,48},{48,56},{56,0},{1,9},... | collective-permute-start | bytes 786440 | tf_op jit(solution)/shard_map/ppermute | solution.py:27
  46.6 7.6 %collective-permute-start.12 = (bf16[16,32,128]{2,1,0:T(8,128)(2,1)S(1)}, bf16[16,32,128]{2,1,0:T(8,128)(2,1)S(1)}, u32[]{:S(2)}, u32[]{:S(2)}) collective-permute-start(bf16[16,32,128]{2,1,0:T(8,128)(2,1)S(1)} %copy-done.3), channel_id=1, source_target_pairs={{0,128},{128,0},{1,129},{129,1},{2,130},{130,2},{3,131},{131,3},{4... | collective-permute-start | bytes 393224 | tf_op jit(solution)/shard_map/ppermute | solution.py:47
  57.3 7.9 %collective-permute-start.17 = (bf16[576,128]{1,0:T(8,128)(2,1)S(1)}, bf16[576,128]{1,0:T(8,128)(2,1)S(1)}, u32[]{:S(2)}, u32[]{:S(2)}) collective-permute-start(bf16[576,128]{1,0:T(8,128)(2,1)S(1)} %get-tuple-element.75), channel_id=1, source_target_pairs={{0,2},{1,3},{2,0},{3,1},{4,6},{5,7},{6,4},{7,5},{8,10},{9,11},{10,... | collective-permute-start | bytes 442376 | tf_op jit(solution)/shard_map/ppermute | solution.py:51
  59.2 8.3 %collective-permute-start.18 = (bf16[576,128]{1,0:T(8,128)(2,1)S(1)}, bf16[576,128]{1,0:T(8,128)(2,1)S(1)}, u32[]{:S(2)}, u32[]{:S(2)}) collective-permute-start(bf16[576,128]{1,0:T(8,128)(2,1)S(1)} %get-tuple-element.76), channel_id=1, source_target_pairs={{0,1},{1,2},{2,3},{3,0},{4,5},{5,6},{6,7},{7,4},{8,9},{9,10},{10,1... | collective-permute-start | bytes 442376 | tf_op jit(solution)/shard_map/ppermute | solution.py:51
  61.3 6.5 %collective-permute-start.19 = (bf16[576,128]{1,0:T(8,128)(2,1)S(1)}, bf16[576,128]{1,0:T(8,128)(2,1)S(1)}, u32[]{:S(2)}, u32[]{:S(2)}) collective-permute-start(bf16[576,128]{1,0:T(8,128)(2,1)S(1)} %get-tuple-element.77), channel_id=1, source_target_pairs={{0,3},{1,0},{2,1},{3,2},{4,7},{5,4},{6,5},{7,6},{8,11},{9,8},{10,9... | collective-permute-start | bytes 442376 | tf_op jit(solution)/shard_map/ppermute | solution.py:51
  67.9 17.1 %collective-permute-start.20 = (bf16[2048,128]{1,0:T(8,128)(2,1)S(1)}, bf16[2048,128]{1,0:T(8,128)(2,1)S(1)}, u32[]{:S(2)}, u32[]{:S(2)}) collective-permute-start(bf16[2048,128]{1,0:T(8,128)(2,1)S(1)} %get-tuple-element.79), channel_id=1, source_target_pairs={{0,4},{4,0},{1,5},{5,1},{2,6},{6,2},{3,7},{7,3},{8,12},{12,8},{9,1... | collective-permute-start | bytes 1572872 | tf_op jit(solution)/shard_map/ppermute | solution.py:39
  69.7 15.6 %collective-permute-start.26 = (bf16[1280,128]{1,0:T(8,128)(2,1)S(1)}, bf16[1280,128]{1,0:T(8,128)(2,1)S(1)}, u32[]{:S(2)}, u32[]{:S(2)}) collective-permute-start(bf16[1280,128]{1,0:T(8,128)(2,1)S(1)} %get-tuple-element.87), channel_id=1, source_target_pairs={{0,2},{1,3},{2,0},{3,1},{4,6},{5,7},{6,4},{7,5},{8,10},{9,11},{10,... | collective-permute-start | bytes 983048 | tf_op jit(solution)/shard_map/ppermute | solution.py:51
  72.7 14.9 %collective-permute-start.27 = (bf16[1280,128]{1,0:T(8,128)(2,1)S(1)}, bf16[1280,128]{1,0:T(8,128)(2,1)S(1)}, u32[]{:S(2)}, u32[]{:S(2)}) collective-permute-start(bf16[1280,128]{1,0:T(8,128)(2,1)S(1)} %get-tuple-element.88), channel_id=1, source_target_pairs={{0,1},{1,2},{2,3},{3,0},{4,5},{5,6},{6,7},{7,4},{8,9},{9,10},{10,1... | collective-permute-start | bytes 983048 | tf_op jit(solution)/shard_map/ppermute | solution.py:51
  73.3 15.6 %collective-permute-start.28 = (bf16[1280,128]{1,0:T(8,128)(2,1)S(1)}, bf16[1280,128]{1,0:T(8,128)(2,1)S(1)}, u32[]{:S(2)}, u32[]{:S(2)}) collective-permute-start(bf16[1280,128]{1,0:T(8,128)(2,1)S(1)} %get-tuple-element.89), channel_id=1, source_target_pairs={{0,3},{1,0},{2,1},{3,2},{4,7},{5,4},{6,5},{7,6},{8,11},{9,8},{10,9... | collective-permute-start | bytes 983048 | tf_op jit(solution)/shard_map/ppermute | solution.py:51
  85.2 14.9 %collective-permute-start.23 = (bf16[960,128]{1,0:T(8,128)(2,1)S(1)}, bf16[960,128]{1,0:T(8,128)(2,1)S(1)}, u32[]{:S(2)}, u32[]{:S(2)}) collective-permute-start(bf16[960,128]{1,0:T(8,128)(2,1)S(1)} %get-tuple-element.83), channel_id=1, source_target_pairs={{0,1},{1,2},{2,3},{3,0},{4,5},{5,6},{6,7},{7,4},{8,9},{9,10},{10,1... | collective-permute-start | bytes 737288 | tf_op jit(solution)/shard_map/ppermute | solution.py:51
  85.4 14.8 %collective-permute-start.24 = (bf16[960,128]{1,0:T(8,128)(2,1)S(1)}, bf16[960,128]{1,0:T(8,128)(2,1)S(1)}, u32[]{:S(2)}, u32[]{:S(2)}) collective-permute-start(bf16[960,128]{1,0:T(8,128)(2,1)S(1)} %get-tuple-element.84), channel_id=1, source_target_pairs={{0,2},{1,3},{2,0},{3,1},{4,6},{5,7},{6,4},{7,5},{8,10},{9,11},{10,... | collective-permute-start | bytes 737288 | tf_op jit(solution)/shard_map/ppermute | solution.py:51
  87.7 13.1 %collective-permute-start.25 = (bf16[960,128]{1,0:T(8,128)(2,1)S(1)}, bf16[960,128]{1,0:T(8,128)(2,1)S(1)}, u32[]{:S(2)}, u32[]{:S(2)}) collective-permute-start(bf16[960,128]{1,0:T(8,128)(2,1)S(1)} %get-tuple-element.85), channel_id=1, source_target_pairs={{0,3},{1,0},{2,1},{3,2},{4,7},{5,4},{6,5},{7,6},{8,11},{9,8},{10,9... | collective-permute-start | bytes 737288 | tf_op jit(solution)/shard_map/ppermute | solution.py:51
  (13 other events, 181.0 us)

commit v14 on v12

--- a/solution.py
+++ b/solution.py
@@ -17,7 +17,7 @@
 REQ_AXES = ("xh", "c")
 TP_AXES = ("z", "xl", "y")
 NP = NX * NY
-TA, TB = 384, 640
+TA, TB = 512, 512
 PACK_MIB = 56
 VMEM = pl.BlockSpec(memory_space=pltpu.VMEM)
 SMEM = pl.BlockSpec(memory_space=pltpu.SMEM)
@@ -364,7 +364,7 @@
 
     ring_step()
     mine = [weight_send(sends[0], 0), weight_send(after(sends[1], *ring[1]), 1), None, weight_send(sends[3], 3)]
-    near = jnp.stack([maps, after(twin, *ring[1])])
+    near = call(stack_kernel, "near", of((2, *maps.shape), bf16), maps, after(twin, *ring[1]))
     ring_step(mine[0], mine[3], near)
     far = core_swap(near)
     mine[2] = weight_send(after(sends[2], *ring[2]), 2)

time: 105 us -> 109 us (1.038)
  waiting for transfers between devices: 44.7 us -> 48.8 us
    ppermute x9, waiting for transfers between devices: 7.82 us -> 10.5 us  [y_shift(): return lax.ppermute(v, 'y', [(i, (i + s) % NY) for i in range(NY)])]
    ppermute x3, waiting for transfers between devices: 6.86 us -> 8.25 us  [x_swap(): return lax.ppermute(v, 'xl', [(0, 1), (1, 0)])]
    pallas_call x14 -> x15, Pallas kernels: 15.6 us -> 15.6 us  [call(): pl.pallas_call(kernel, out_shape=outs, in_specs=[SMEM] * scalars + [pl.Bl...]
  transfers between devices with their start and end apart: 29 -> 29, of which waited for: 12 -> 13; matrix products, arithmetic and copies ran while one was open for 1% -> 0% of each run, Pallas kernels for 8% -> 8%
where the time goes in v14:
time: 109 us; the launch traced here: 108 us
  waiting for transfers between devices  48.8 us (45%)
  starting transfers between devices  42.9 us (39%)
  Pallas kernels  15.6 us (14%)
    pallas_call x15, Pallas kernels, call(): pl.pallas_call(kernel, out_shape=outs, in_specs=[SMEM] * scalars + [pl.Bl...  15.6 us
    ppermute x3, waiting for transfers between devices, z_xor(): return lax.ppermute(v, 'z', [(i, i ^ s) for i in range(NZ)])  12.9 us
    ppermute x7, waiting for transfers between devices, z_shift(): return lax.ppermute(v, 'z', [(i, (i + s) % NZ) for i in range(NZ)])  12.1 us
    ppermute x9, starting transfers between devices, y_shift(): return lax.ppermute(v, 'y', [(i, (i + s) % NY) for i in range(NY)])  12 us
    ppermute x4, starting transfers between devices, weight_send(): return lax.ppermute(v, ('xh', 'c', 'xl', 'y'), route)  11.2 us
    ppermute x9, waiting for transfers between devices, y_shift(): return lax.ppermute(v, 'y', [(i, (i + s) % NY) for i in range(NY)])  10.5 us
    ppermute x7, starting transfers between devices, z_shift(): return lax.ppermute(v, 'z', [(i, (i + s) % NZ) for i in range(NZ)])  10.2 us
    ppermute x3, waiting for transfers between devices, x_swap(): return lax.ppermute(v, 'xl', [(0, 1), (1, 0)])  8.25 us
  transfers between devices with their start and end apart: 29, of which 13 were waited for; matrix products, arithmetic and copies ran while one was open for 0% of the time, Pallas kernels for 8%

profile of v14, /device:TPU:2, one launch (start us, length us, event | category | flops | bytes accessed | tf_op | source)
XLA Modules:
  0.0 108.4 jit_solution(11046952518396353177)
XLA Ops:
  0.0 1.9 %collective-permute-start.1 = (bf16[1024,128]{1,0:T(8,128)(2,1)}, bf16[1024,128]{1,0:T(8,128)(2,1)S(1)}, u32[]{:S(2)}, u32[]{:S(2)}) collective-permute-start(bf16[1024,128]{1,0:T(8,128)(2,1)} %refs_0_.1), channel_id=1, source_target_pairs={{0,8},{8,16},{16,24},{24,32},{32,40},{40,48},{48,56},{56,0},{1,9},... | collective-permute-start | bytes 786440 | tf_op jit(solution)/shard_map/ppermute | solution.py:27
  1.9 4.0 %collective-permute-start = (bf16[1024,128]{1,0:T(8,128)(2,1)}, bf16[1024,128]{1,0:T(8,128)(2,1)S(1)}, u32[]{:S(2)}, u32[]{:S(2)}) collective-permute-start(bf16[1024,128]{1,0:T(8,128)(2,1)} %refs_0_.1), channel_id=1, source_target_pairs={{0,56},{8,0},{16,8},{24,16},{32,24},{40,32},{48,40},{56,48},{1,57}... | collective-permute-start | bytes 786440 | tf_op jit(solution)/shard_map/ppermute | solution.py:27
  5.9 3.5 %pack.1 = (bf16[1280,128]{1,0:T(8,128)(2,1)}, bf16[1280,128]{1,0:T(8,128)(2,1)}, bf16[1280,128]{1,0:T(8,128)(2,1)}, bf16[1280,128]{1,0:T(8,128)(2,1)}, bf16[1280...) custom-call(bf16[8192,128]{1,0:T(8,128)(2,1)} %wq_ref.1, bf16[32,8192]{1,0:T(8,128)(2,1)} %bitcast.2, ...), custom_call_target="tpu_custom_call" | custom-call | tf_op jit(solution)/shard_map/pack/pallas_call | solution.py:313
  9.5 2.2 %collective-permute-start.4 = (bf16[16,64,128]{2,1,0:T(8,128)(2,1)}, bf16[16,64,128]{2,1,0:T(8,128)(2,1)S(1)}, u32[]{:S(2)}, u32[]{:S(2)}) collective-permute-start(bf16[16,64,128]{2,1,0:T(8,128)(2,1)} %get-tuple-element.52.refs_0_), channel_id=1, source_target_pairs={{0,128},{128,0},{1,129},{129,1},{2,130},{130,2},{3,131},{131,3},{4... | collective-permute-start | bytes 786440 | tf_op jit(solution)/shard_map/ppermute | solution.py:47
  13.9 5.1 %collective-permute-done.4.refs_1_ = bf16[16,64,128]{2,1,0:T(8,128)(2,1)S(1)} collective-permute-done((bf16[16,64,128]{2,1,0:T(8,128)(2,1)}, bf16[16,64,128]{2,1,0:T(8,128)(2,1)S(1)}, u32[]{:S(2)}, u32[]{:S(2)}) %collective-permute-start.4) | collective-permute-done | bytes 262176 | tf_op jit(solution)/shard_map/ppermute | solution.py:47
  20.7 1.9 %collective-permute-start.5 = (bf16[1024,128]{1,0:T(8,128)(2,1)S(1)}, bf16[1024,128]{1,0:T(8,128)(2,1)S(1)}, u32[]{:S(2)}, u32[]{:S(2)}) collective-permute-start(bf16[1024,128]{1,0:T(8,128)(2,1)S(1)} %collective-permute-done.refs_1_), channel_id=1, source_target_pairs={{0,56},{8,0},{16,8},{24,16},{32,24},{40,32},{48,40},{56,48},{1,57}... | collective-permute-start | bytes 786440 | tf_op jit(solution)/shard_map/ppermute | solution.py:27
  23.6 4.5 %collective-permute-start.9 = (bf16[32,1024]{1,0:T(8,128)(2,1)S(1)}, bf16[32,1024]{1,0:T(8,128)(2,1)S(1)}, u32[]{:S(2)}, u32[]{:S(2)}) collective-permute-start(bf16[32,1024]{1,0:T(8,128)(2,1)S(1)} %get-tuple-element.59), channel_id=1, source_target_pairs={{0,32},{8,40},{16,48},{24,56},{32,0},{40,8},{48,16},{56,24},{1,33}... | collective-permute-start | bytes 196616 | tf_op jit(solution)/shard_map/ppermute | solution.py:31
  28.1 3.2 %collective-permute-done.6.refs_6_ = bf16[1024,128]{1,0:T(8,128)(2,1)S(1)} collective-permute-done((bf16[1024,128]{1,0:T(8,128)(2,1)S(1)}, bf16[1024,128]{1,0:T(8,128)(2,1)S(1)}, u32[]{:S(2)}, u32[]{:S(2)}) %collective-permute-start.6) | collective-permute-done | bytes 262176 | tf_op jit(solution)/shard_map/ppermute | solution.py:27
  31.2 8.3 %collective-permute-start.12 = (bf16[1280,128]{1,0:T(8,128)(2,1)S(1)}, bf16[1280,128]{1,0:T(8,128)(2,1)S(1)}, u32[]{:S(2)}, u32[]{:S(2)}) collective-permute-start(bf16[1280,128]{1,0:T(8,128)(2,1)S(1)} %copy-done.5), channel_id=1, source_target_pairs={{0,6},{1,7},{2,4},{3,5},{4,2},{5,3},{6,0},{7,1},{64,199},{65,196},... | collective-permute-start | bytes 983048 | tf_op jit(solution)/shard_map/ppermute | solution.py:75
  41.7 4.3 %collective-permute-done.10.refs_3_ = bf16[1024,128]{1,0:T(8,128)(2,1)S(1)} collective-permute-done((bf16[1024,128]{1,0:T(8,128)(2,1)S(1)}, bf16[1024,128]{1,0:T(8,128)(2,1)S(1)}, u32[]{:S(2)}, u32[]{:S(2)}) %collective-permute-start.10) | collective-permute-done | bytes 262176 | tf_op jit(solution)/shard_map/ppermute | solution.py:27
  46.0 2.5 %collective-permute-done.11.refs_5_ = bf16[1024,128]{1,0:T(8,128)(2,1)S(1)} collective-permute-done((bf16[1024,128]{1,0:T(8,128)(2,1)S(1)}, bf16[1024,128]{1,0:T(8,128)(2,1)S(1)}, u32[]{:S(2)}, u32[]{:S(2)}) %collective-permute-start.11) | collective-permute-done | bytes 262176 | tf_op jit(solution)/shard_map/ppermute | solution.py:27
  49.0 7.7 %collective-permute-done.15.b_ref = bf16[32,1024]{1,0:T(8,128)(2,1)S(1)} collective-permute-done((bf16[32,1024]{1,0:T(8,128)(2,1)S(1)}, bf16[32,1024]{1,0:T(8,128)(2,1)S(1)}, u32[]{:S(2)}, u32[]{:S(2)}) %collective-permute-start.15) | collective-permute-done | bytes 65568 | tf_op jit(solution)/shard_map/ppermute | solution.py:31
  56.7 2.0 %collective-permute-done.13.refs_4_ = bf16[1024,128]{1,0:T(8,128)(2,1)S(1)} collective-permute-done((bf16[1024,128]{1,0:T(8,128)(2,1)S(1)}, bf16[1024,128]{1,0:T(8,128)(2,1)S(1)}, u32[]{:S(2)}, u32[]{:S(2)}) %collective-permute-start.13) | collective-permute-done | bytes 262176 | tf_op jit(solution)/shard_map/ppermute | solution.py:27
  61.9 1.9 %collective-permute-start.18 = (bf16[576,128]{1,0:T(8,128)(2,1)S(1)}, bf16[576,128]{1,0:T(8,128)(2,1)S(1)}, u32[]{:S(2)}, u32[]{:S(2)}) collective-permute-start(bf16[576,128]{1,0:T(8,128)(2,1)S(1)} %get-tuple-element.75), channel_id=1, source_target_pairs={{0,3},{1,0},{2,1},{3,2},{4,7},{5,4},{6,5},{7,6},{8,11},{9,8},{10,9... | collective-permute-start | bytes 442376 | tf_op jit(solution)/shard_map/ppermute | solution.py:51
  63.8 2.7 %q_product.1 = (bf16[2048,128]{1,0:T(8,128)(2,1)S(1)}, bf16[2048,128]{1,0:T(8,128)(2,1)S(1)}, bf16[1024,128]{1,0:T(8,128)(2,1)S(1)}, bf16[1024,128]{1,0:T(8,128)...) custom-call(bf16[1024,1024]{1,0:T(8,128)(2,1)S(1)} %get-tuple-element.70.hbuf, ...), custom_call_target="tpu_custom_call" | custom-call | tf_op jit(solution)/shard_map/q_product/pallas_call | solution.py:313
  66.5 2.2 %collective-permute-done.16.k1 = bf16[576,128]{1,0:T(8,128)(2,1)S(1)} collective-permute-done((bf16[576,128]{1,0:T(8,128)(2,1)S(1)}, bf16[576,128]{1,0:T(8,128)(2,1)S(1)}, u32[]{:S(2)}, u32[]{:S(2)}) %collective-permute-start.16) | collective-permute-done | bytes 147488 | tf_op jit(solution)/shard_map/ppermute | solution.py:51
  70.7 2.1 %collective-permute-start.25 = (bf16[1024,128]{1,0:T(8,128)(2,1)S(1)}, bf16[1024,128]{1,0:T(8,128)(2,1)S(1)}, u32[]{:S(2)}, u32[]{:S(2)}) collective-permute-start(bf16[1024,128]{1,0:T(8,128)(2,1)S(1)} %get-tuple-element.85), channel_id=1, source_target_pairs={{0,2},{1,3},{2,0},{3,1},{4,6},{5,7},{6,4},{7,5},{8,10},{9,11},{10,... | collective-permute-start | bytes 786440 | tf_op jit(solution)/shard_map/ppermute | solution.py:51
  76.0 5.2 %collective-permute-done.20.b_ref = f32[64,128]{1,0:T(8,128)S(1)} collective-permute-done((f32[64,128]{1,0:T(8,128)S(1)}, f32[64,128]{1,0:T(8,128)S(1)}, u32[]{:S(2)}, u32[]{:S(2)}) %collective-permute-start.20) | collective-permute-done | bytes 32800 | tf_op jit(solution)/shard_map/ppermute | solution.py:31
  81.4 6.2 %collective-permute-done.21.b_ref = f32[64,128]{1,0:T(8,128)S(1)} collective-permute-done((f32[64,128]{1,0:T(8,128)S(1)}, f32[64,128]{1,0:T(8,128)S(1)}, u32[]{:S(2)}, u32[]{:S(2)}) %collective-permute-start.21) | collective-permute-done | bytes 32800 | tf_op jit(solution)/shard_map/ppermute | solution.py:39
  88.0 2.0 %collective-permute-start.23 = (bf16[1088,128]{1,0:T(8,128)(2,1)S(1)}, bf16[1088,128]{1,0:T(8,128)(2,1)S(1)}, u32[]{:S(2)}, u32[]{:S(2)}) collective-permute-start(bf16[1088,128]{1,0:T(8,128)(2,1)S(1)} %get-tuple-element.82), channel_id=1, source_target_pairs={{0,2},{1,3},{2,0},{3,1},{4,6},{5,7},{6,4},{7,5},{8,10},{9,11},{10,... | collective-permute-start | bytes 835592 | tf_op jit(solution)/shard_map/ppermute | solution.py:51
  91.3 2.0 %collective-permute-start.28 = (bf16[512,128]{1,0:T(8,128)(2,1)S(1)}, bf16[512,128]{1,0:T(8,128)(2,1)S(1)}, u32[]{:S(2)}, u32[]{:S(2)}) collective-permute-start(bf16[512,128]{1,0:T(8,128)(2,1)S(1)} %get-tuple-element.89), channel_id=1, source_target_pairs={{0,4},{4,0},{1,5},{5,1},{2,6},{6,2},{3,7},{7,3},{8,12},{12,8},{9,1... | collective-permute-start | bytes 393224 | tf_op jit(solution)/shard_map/ppermute | solution.py:39
  94.6 2.0 %collective-permute-done.28.refs_5_ = bf16[512,128]{1,0:T(8,128)(2,1)S(1)} collective-permute-done((bf16[512,128]{1,0:T(8,128)(2,1)S(1)}, bf16[512,128]{1,0:T(8,128)(2,1)S(1)}, u32[]{:S(2)}, u32[]{:S(2)}) %collective-permute-start.28) | collective-permute-done | bytes 131104 | tf_op jit(solution)/shard_map/ppermute | solution.py:39
  96.6 6.0 %collective-permute-done.22.refs_1_ = bf16[1088,128]{1,0:T(8,128)(2,1)S(1)} collective-permute-done((bf16[1088,128]{1,0:T(8,128)(2,1)S(1)}, bf16[1088,128]{1,0:T(8,128)(2,1)S(1)}, u32[]{:S(2)}, u32[]{:S(2)}) %collective-permute-start.22) | collective-permute-done | bytes 278560 | tf_op jit(solution)/shard_map/ppermute | solution.py:51
  103.3 5.2 %attention.1 = bf16[1024,128]{1,0:T(8,128)(2,1)} custom-call(s32[8]{0:T(128)S(1)} %copy-done.4, s32[1024]{0:T(1024)S(1)} %copy-done.3, f32[512,128]{1,0:T(8,128)S(1)} %get-tuple-element.80.refs_0_, bf16[1088,128]{1,0:T(8,128)(2,1)S(1)} %collective-permute-done.22.refs_1_, bf16[1088,128]{1,0:T(8,128)(2,1)S(1)} %collective-permute-done.23.refs_2_, ...), custom_call_target="tpu_custom_call" | custom-call | tf_op jit(solution)/shard_map/attention/pallas_call | solution.py:313
  (61 shorter events, 19.6 us)
Async XLA Ops:
  0.0 13.9 %collective-permute-start.1 = (bf16[1024,128]{1,0:T(8,128)(2,1)}, bf16[1024,128]{1,0:T(8,128)(2,1)S(1)}, u32[]{:S(2)}, u32[]{:S(2)}) collective-permute-start(bf16[1024,128]{1,0:T(8,128)(2,1)} %refs_0_.1), channel_id=1, source_target_pairs={{0,8},{8,16},{16,24},{24,32},{32,40},{40,48},{48,56},{56,0},{1,9},... | collective-permute-start | bytes 786440 | tf_op jit(solution)/shard_map/ppermute | solution.py:27
  1.9 12.0 %collective-permute-start = (bf16[1024,128]{1,0:T(8,128)(2,1)}, bf16[1024,128]{1,0:T(8,128)(2,1)S(1)}, u32[]{:S(2)}, u32[]{:S(2)}) collective-permute-start(bf16[1024,128]{1,0:T(8,128)(2,1)} %refs_0_.1), channel_id=1, source_target_pairs={{0,56},{8,0},{16,8},{24,16},{32,24},{40,32},{48,40},{56,48},{1,57}... | collective-permute-start | bytes 786440 | tf_op jit(solution)/shard_map/ppermute | solution.py:27
  9.5 9.6 %collective-permute-start.4 = (bf16[16,64,128]{2,1,0:T(8,128)(2,1)}, bf16[16,64,128]{2,1,0:T(8,128)(2,1)S(1)}, u32[]{:S(2)}, u32[]{:S(2)}) collective-permute-start(bf16[16,64,128]{2,1,0:T(8,128)(2,1)} %get-tuple-element.52.refs_0_), channel_id=1, source_target_pairs={{0,128},{128,0},{1,129},{129,1},{2,130},{130,2},{3,131},{131,3},{4... | collective-permute-start | bytes 786440 | tf_op jit(solution)/shard_map/ppermute | solution.py:47
  11.7 9.1 %collective-permute-start.2 = (bf16[1280,128]{1,0:T(8,128)(2,1)}, bf16[1280,128]{1,0:T(8,128)(2,1)S(1)}, u32[]{:S(2)}, u32[]{:S(2)}) collective-permute-start(bf16[1280,128]{1,0:T(8,128)(2,1)} %get-tuple-element.50), channel_id=1, source_target_pairs={{0,1},{1,2},{2,3},{3,0},{4,5},{5,6},{6,7},{7,4},{64,67},{65,64},{6... | collective-permute-start | bytes 983048 | tf_op jit(solution)/shard_map/ppermute | solution.py:75
  13.2 7.5 %collective-permute-start.3 = (bf16[1280,128]{1,0:T(8,128)(2,1)}, bf16[1280,128]{1,0:T(8,128)(2,1)S(1)}, u32[]{:S(2)}, u32[]{:S(2)}) collective-permute-start(bf16[1280,128]{1,0:T(8,128)(2,1)} %get-tuple-element.51), channel_id=1, source_target_pairs={{64,66},{65,67},{66,64},{67,65},{68,70},{69,71},{70,68},{71,69},{1... | collective-permute-start | bytes 983048 | tf_op jit(solution)/shard_map/ppermute | solution.py:75
  20.1 19.5 %collective-permute-start.7 = (bf16[1280,128]{1,0:T(8,128)(2,1)}, bf16[1280,128]{1,0:T(8,128)(2,1)S(1)}, u32[]{:S(2)}, u32[]{:S(2)}) collective-permute-start(bf16[1280,128]{1,0:T(8,128)(2,1)} %get-tuple-element.57), channel_id=1, source_target_pairs={{0,4},{1,5},{2,6},{3,7},{4,0},{5,1},{6,2},{7,3},{64,197},{65,198},... | collective-permute-start | bytes 983048 | tf_op jit(solution)/shard_map/ppermute | solution.py:75
  20.7 7.3 %collective-permute-start.5 = (bf16[1024,128]{1,0:T(8,128)(2,1)S(1)}, bf16[1024,128]{1,0:T(8,128)(2,1)S(1)}, u32[]{:S(2)}, u32[]{:S(2)}) collective-permute-start(bf16[1024,128]{1,0:T(8,128)(2,1)S(1)} %collective-permute-done.refs_1_), channel_id=1, source_target_pairs={{0,56},{8,0},{16,8},{24,16},{32,24},{40,32},{48,40},{56,48},{1,57}... | collective-permute-start | bytes 786440 | tf_op jit(solution)/shard_map/ppermute | solution.py:27
  22.6 8.6 %collective-permute-start.6 = (bf16[1024,128]{1,0:T(8,128)(2,1)S(1)}, bf16[1024,128]{1,0:T(8,128)(2,1)S(1)}, u32[]{:S(2)}, u32[]{:S(2)}) collective-permute-start(bf16[1024,128]{1,0:T(8,128)(2,1)S(1)} %collective-permute-done.1.refs_7_), channel_id=1, source_target_pairs={{0,8},{8,16},{16,24},{24,32},{32,40},{40,48},{48,56},{56,0},{1,9},... | collective-permute-start | bytes 786440 | tf_op jit(solution)/shard_map/ppermute | solution.py:27
  23.6 16.0 %collective-permute-start.9 = (bf16[32,1024]{1,0:T(8,128)(2,1)S(1)}, bf16[32,1024]{1,0:T(8,128)(2,1)S(1)}, u32[]{:S(2)}, u32[]{:S(2)}) collective-permute-start(bf16[32,1024]{1,0:T(8,128)(2,1)S(1)} %get-tuple-element.59), channel_id=1, source_target_pairs={{0,32},{8,40},{16,48},{24,56},{32,0},{40,8},{48,16},{56,24},{1,33}... | collective-permute-start | bytes 196616 | tf_op jit(solution)/shard_map/ppermute | solution.py:31
  31.2 17.3 %collective-permute-start.12 = (bf16[1280,128]{1,0:T(8,128)(2,1)S(1)}, bf16[1280,128]{1,0:T(8,128)(2,1)S(1)}, u32[]{:S(2)}, u32[]{:S(2)}) collective-permute-start(bf16[1280,128]{1,0:T(8,128)(2,1)S(1)} %copy-done.5), channel_id=1, source_target_pairs={{0,6},{1,7},{2,4},{3,5},{4,2},{5,3},{6,0},{7,1},{64,199},{65,196},... | collective-permute-start | bytes 983048 | tf_op jit(solution)/shard_map/ppermute | solution.py:75
  41.0 7.6 %collective-permute-start.11 = (bf16[1024,128]{1,0:T(8,128)(2,1)S(1)}, bf16[1024,128]{1,0:T(8,128)(2,1)S(1)}, u32[]{:S(2)}, u32[]{:S(2)}) collective-permute-start(bf16[1024,128]{1,0:T(8,128)(2,1)S(1)} %collective-permute-done.6.refs_6_), channel_id=1, source_target_pairs={{0,8},{8,16},{16,24},{24,32},{32,40},{40,48},{48,56},{56,0},{1,9},... | collective-permute-start | bytes 786440 | tf_op jit(solution)/shard_map/ppermute | solution.py:27
  48.7 10.0 %collective-permute-start.14 = (bf16[4,1280,128]{2,1,0:T(8,128)(2,1)S(1)}, bf16[4,1280,128]{2,1,0:T(8,128)(2,1)S(1)}, u32[]{:S(2)}, u32[]{:S(2)}) collective-permute-start(bf16[4,1280,128]{2,1,0:T(8,128)(2,1)S(1)} %stack.1), channel_id=1, source_target_pairs={{0,64},{64,0},{1,65},{65,1},{2,66},{66,2},{3,67},{67,3},{4,68},{68... | collective-permute-start | bytes 3932168 | tf_op jit(solution)/shard_map/ppermute | solution.py:43
  48.8 9.9 %collective-permute-start.13 = (bf16[1024,128]{1,0:T(8,128)(2,1)S(1)}, bf16[1024,128]{1,0:T(8,128)(2,1)S(1)}, u32[]{:S(2)}, u32[]{:S(2)}) collective-permute-start(bf16[1024,128]{1,0:T(8,128)(2,1)S(1)} %collective-permute-done.11.refs_5_), channel_id=1, source_target_pairs={{0,8},{8,16},{16,24},{24,32},{32,40},{40,48},{48,56},{56,0},{1,9},... | collective-permute-start | bytes 786440 | tf_op jit(solution)/shard_map/ppermute | solution.py:27
  48.9 7.8 %collective-permute-start.15 = (bf16[32,1024]{1,0:T(8,128)(2,1)S(1)}, bf16[32,1024]{1,0:T(8,128)(2,1)S(1)}, u32[]{:S(2)}, u32[]{:S(2)}) collective-permute-start(bf16[32,1024]{1,0:T(8,128)(2,1)S(1)} %get-tuple-element.69), channel_id=1, source_target_pairs={{0,8},{8,0},{16,24},{24,16},{32,40},{40,32},{48,56},{56,48},{1,9},... | collective-permute-start | bytes 196616 | tf_op jit(solution)/shard_map/ppermute | solution.py:31
  60.3 8.4 %collective-permute-start.16 = (bf16[576,128]{1,0:T(8,128)(2,1)S(1)}, bf16[576,128]{1,0:T(8,128)(2,1)S(1)}, u32[]{:S(2)}, u32[]{:S(2)}) collective-permute-start(bf16[576,128]{1,0:T(8,128)(2,1)S(1)} %get-tuple-element.73), channel_id=1, source_target_pairs={{0,2},{1,3},{2,0},{3,1},{4,6},{5,7},{6,4},{7,5},{8,10},{9,11},{10,... | collective-permute-start | bytes 442376 | tf_op jit(solution)/shard_map/ppermute | solution.py:51
  60.4 9.8 %collective-permute-start.17 = (bf16[576,128]{1,0:T(8,128)(2,1)S(1)}, bf16[576,128]{1,0:T(8,128)(2,1)S(1)}, u32[]{:S(2)}, u32[]{:S(2)}) collective-permute-start(bf16[576,128]{1,0:T(8,128)(2,1)S(1)} %get-tuple-element.74), channel_id=1, source_target_pairs={{0,1},{1,2},{2,3},{3,0},{4,5},{5,6},{6,7},{7,4},{8,9},{9,10},{10,1... | collective-permute-start | bytes 442376 | tf_op jit(solution)/shard_map/ppermute | solution.py:51
  61.9 8.4 %collective-permute-start.18 = (bf16[576,128]{1,0:T(8,128)(2,1)S(1)}, bf16[576,128]{1,0:T(8,128)(2,1)S(1)}, u32[]{:S(2)}, u32[]{:S(2)}) collective-permute-start(bf16[576,128]{1,0:T(8,128)(2,1)S(1)} %get-tuple-element.75), channel_id=1, source_target_pairs={{0,3},{1,0},{2,1},{3,2},{4,7},{5,4},{6,5},{7,6},{8,11},{9,8},{10,9... | collective-permute-start | bytes 442376 | tf_op jit(solution)/shard_map/ppermute | solution.py:51
  70.4 17.2 %collective-permute-start.19 = (bf16[2560,128]{1,0:T(8,128)(2,1)S(1)}, bf16[2560,128]{1,0:T(8,128)(2,1)S(1)}, u32[]{:S(2)}, u32[]{:S(2)}) collective-permute-start(bf16[2560,128]{1,0:T(8,128)(2,1)S(1)} %get-tuple-element.77), channel_id=1, source_target_pairs={{0,4},{4,0},{1,5},{5,1},{2,6},{6,2},{3,7},{7,3},{8,12},{12,8},{9,1... | collective-permute-start | bytes 1966088 | tf_op jit(solution)/shard_map/ppermute | solution.py:39
  70.7 19.2 %collective-permute-start.25 = (bf16[1024,128]{1,0:T(8,128)(2,1)S(1)}, bf16[1024,128]{1,0:T(8,128)(2,1)S(1)}, u32[]{:S(2)}, u32[]{:S(2)}) collective-permute-start(bf16[1024,128]{1,0:T(8,128)(2,1)S(1)} %get-tuple-element.85), channel_id=1, source_target_pairs={{0,2},{1,3},{2,0},{3,1},{4,6},{5,7},{6,4},{7,5},{8,10},{9,11},{10,... | collective-permute-start | bytes 786440 | tf_op jit(solution)/shard_map/ppermute | solution.py:51
  72.8 18.4 %collective-permute-start.26 = (bf16[1024,128]{1,0:T(8,128)(2,1)S(1)}, bf16[1024,128]{1,0:T(8,128)(2,1)S(1)}, u32[]{:S(2)}, u32[]{:S(2)}) collective-permute-start(bf16[1024,128]{1,0:T(8,128)(2,1)S(1)} %get-tuple-element.86), channel_id=1, source_target_pairs={{0,1},{1,2},{2,3},{3,0},{4,5},{5,6},{6,7},{7,4},{8,9},{9,10},{10,1... | collective-permute-start | bytes 786440 | tf_op jit(solution)/shard_map/ppermute | solution.py:51
  74.3 16.9 %collective-permute-start.27 = (bf16[1024,128]{1,0:T(8,128)(2,1)S(1)}, bf16[1024,128]{1,0:T(8,128)(2,1)S(1)}, u32[]{:S(2)}, u32[]{:S(2)}) collective-permute-start(bf16[1024,128]{1,0:T(8,128)(2,1)S(1)} %get-tuple-element.87), channel_id=1, source_target_pairs={{0,3},{1,0},{2,1},{3,2},{4,7},{5,4},{6,5},{7,6},{8,11},{9,8},{10,9... | collective-permute-start | bytes 786440 | tf_op jit(solution)/shard_map/ppermute | solution.py:51
  87.9 14.8 %collective-permute-start.22 = (bf16[1088,128]{1,0:T(8,128)(2,1)S(1)}, bf16[1088,128]{1,0:T(8,128)(2,1)S(1)}, u32[]{:S(2)}, u32[]{:S(2)}) collective-permute-start(bf16[1088,128]{1,0:T(8,128)(2,1)S(1)} %get-tuple-element.81), channel_id=1, source_target_pairs={{0,1},{1,2},{2,3},{3,0},{4,5},{5,6},{6,7},{7,4},{8,9},{9,10},{10,1... | collective-permute-start | bytes 835592 | tf_op jit(solution)/shard_map/ppermute | solution.py:51
  88.0 14.7 %collective-permute-start.23 = (bf16[1088,128]{1,0:T(8,128)(2,1)S(1)}, bf16[1088,128]{1,0:T(8,128)(2,1)S(1)}, u32[]{:S(2)}, u32[]{:S(2)}) collective-permute-start(bf16[1088,128]{1,0:T(8,128)(2,1)S(1)} %get-tuple-element.82), channel_id=1, source_target_pairs={{0,2},{1,3},{2,0},{3,1},{4,6},{5,7},{6,4},{7,5},{8,10},{9,11},{10,... | collective-permute-start | bytes 835592 | tf_op jit(solution)/shard_map/ppermute | solution.py:51
  89.9 13.3 %collective-permute-start.24 = (bf16[1088,128]{1,0:T(8,128)(2,1)S(1)}, bf16[1088,128]{1,0:T(8,128)(2,1)S(1)}, u32[]{:S(2)}, u32[]{:S(2)}) collective-permute-start(bf16[1088,128]{1,0:T(8,128)(2,1)S(1)} %get-tuple-element.83), channel_id=1, source_target_pairs={{0,3},{1,0},{2,1},{3,2},{4,7},{5,4},{6,5},{7,6},{8,11},{9,8},{10,9... | collective-permute-start | bytes 835592 | tf_op jit(solution)/shard_map/ppermute | solution.py:51
  (11 other events, 149.4 us)

commit v15 on v12

--- a/solution.py
+++ b/solution.py
@@ -17,7 +17,7 @@
 REQ_AXES = ("xh", "c")
 TP_AXES = ("z", "xl", "y")
 NP = NX * NY
-TA, TB = 384, 640
+TA, TB = 256, 768
 PACK_MIB = 56
 VMEM = pl.BlockSpec(memory_space=pltpu.VMEM)
 SMEM = pl.BlockSpec(memory_space=pltpu.SMEM)

time: 105 us -> 107 us (1.019)
  waiting for transfers between devices: 44.7 us -> 47.5 us
  starting transfers between devices: 42.8 us -> 41.4 us
    ppermute x9, waiting for transfers between devices: 7.82 us -> 9.6 us  [y_shift(): return lax.ppermute(v, 'y', [(i, (i + s) % NY) for i in range(NY)])]
    ppermute x3, starting transfers between devices: 2.48 us -> 1.1 us  [x_swap(): return lax.ppermute(v, 'xl', [(0, 1), (1, 0)])]
  transfers between devices with their start and end apart: 29 -> 29, of which waited for: 12 -> 14; matrix products, arithmetic and copies ran while one was open for 1% -> 1% of each run, Pallas kernels for 8% -> 8%
where the time goes in v15:
time: 107 us; the launch traced here: 106 us
  waiting for transfers between devices  47.5 us (44%)
  starting transfers between devices  41.4 us (39%)
  Pallas kernels  15.5 us (14%)
    pallas_call x14, Pallas kernels, call(): pl.pallas_call(kernel, out_shape=outs, in_specs=[SMEM] * scalars + [pl.Bl...  15.5 us
    ppermute x3, waiting for transfers between devices, z_xor(): return lax.ppermute(v, 'z', [(i, i ^ s) for i in range(NZ)])  12.9 us
    ppermute x7, waiting for transfers between devices, z_shift(): return lax.ppermute(v, 'z', [(i, (i + s) % NZ) for i in range(NZ)])  12.1 us
    ppermute x9, starting transfers between devices, y_shift(): return lax.ppermute(v, 'y', [(i, (i + s) % NY) for i in range(NY)])  12 us
    ppermute x4, starting transfers between devices, weight_send(): return lax.ppermute(v, ('xh', 'c', 'xl', 'y'), route)  11.2 us
    ppermute x7, starting transfers between devices, z_shift(): return lax.ppermute(v, 'z', [(i, (i + s) % NZ) for i in range(NZ)])  10.2 us
    ppermute x9, waiting for transfers between devices, y_shift(): return lax.ppermute(v, 'y', [(i, (i + s) % NY) for i in range(NY)])  9.6 us
    ppermute x3, waiting for transfers between devices, x_swap(): return lax.ppermute(v, 'xl', [(0, 1), (1, 0)])  7.88 us
  transfers between devices with their start and end apart: 29, of which 14 were waited for; matrix products, arithmetic and copies ran while one was open for 1% of the time, Pallas kernels for 8%

profile of v15, /device:TPU:2, one launch (start us, length us, event | category | flops | bytes accessed | tf_op | source)
XLA Modules:
  0.0 105.7 jit_solution(11574068687432201513)
XLA Ops:
  0.0 1.9 %collective-permute-start.1 = (bf16[1024,128]{1,0:T(8,128)(2,1)}, bf16[1024,128]{1,0:T(8,128)(2,1)S(1)}, u32[]{:S(2)}, u32[]{:S(2)}) collective-permute-start(bf16[1024,128]{1,0:T(8,128)(2,1)} %refs_0_.1), channel_id=1, source_target_pairs={{0,8},{8,16},{16,24},{24,32},{32,40},{40,48},{48,56},{56,0},{1,9},... | collective-permute-start | bytes 786440 | tf_op jit(solution)/shard_map/ppermute | solution.py:27
  1.9 4.0 %collective-permute-start = (bf16[1024,128]{1,0:T(8,128)(2,1)}, bf16[1024,128]{1,0:T(8,128)(2,1)S(1)}, u32[]{:S(2)}, u32[]{:S(2)}) collective-permute-start(bf16[1024,128]{1,0:T(8,128)(2,1)} %refs_0_.1), channel_id=1, source_target_pairs={{0,56},{8,0},{16,8},{24,16},{32,24},{40,32},{48,40},{56,48},{1,57}... | collective-permute-start | bytes 786440 | tf_op jit(solution)/shard_map/ppermute | solution.py:27
  5.9 3.5 %pack.1 = (bf16[1280,128]{1,0:T(8,128)(2,1)}, bf16[1280,128]{1,0:T(8,128)(2,1)}, bf16[1280,128]{1,0:T(8,128)(2,1)}, bf16[1280,128]{1,0:T(8,128)(2,1)}, bf16[1280...) custom-call(bf16[8192,128]{1,0:T(8,128)(2,1)} %wq_ref.1, bf16[32,8192]{1,0:T(8,128)(2,1)} %bitcast.4, ...), custom_call_target="tpu_custom_call" | custom-call | tf_op jit(solution)/shard_map/pack/pallas_call | solution.py:313
  9.5 2.2 %collective-permute-start.4 = (bf16[16,64,128]{2,1,0:T(8,128)(2,1)}, bf16[16,64,128]{2,1,0:T(8,128)(2,1)S(1)}, u32[]{:S(2)}, u32[]{:S(2)}) collective-permute-start(bf16[16,64,128]{2,1,0:T(8,128)(2,1)} %get-tuple-element.52), channel_id=1, source_target_pairs={{0,128},{128,0},{1,129},{129,1},{2,130},{130,2},{3,131},{131,3},{4... | collective-permute-start | bytes 786440 | tf_op jit(solution)/shard_map/ppermute | solution.py:47
  13.9 5.1 %collective-permute-done.4 = bf16[16,64,128]{2,1,0:T(8,128)(2,1)S(1)} collective-permute-done((bf16[16,64,128]{2,1,0:T(8,128)(2,1)}, bf16[16,64,128]{2,1,0:T(8,128)(2,1)S(1)}, u32[]{:S(2)}, u32[]{:S(2)}) %collective-permute-start.4) | collective-permute-done | bytes 262176 | tf_op jit(solution)/shard_map/ppermute | solution.py:47
  20.8 1.9 %collective-permute-start.5 = (bf16[1024,128]{1,0:T(8,128)(2,1)S(1)}, bf16[1024,128]{1,0:T(8,128)(2,1)S(1)}, u32[]{:S(2)}, u32[]{:S(2)}) collective-permute-start(bf16[1024,128]{1,0:T(8,128)(2,1)S(1)} %collective-permute-done.refs_1_), channel_id=1, source_target_pairs={{0,56},{8,0},{16,8},{24,16},{32,24},{40,32},{48,40},{56,48},{1,57}... | collective-permute-start | bytes 786440 | tf_op jit(solution)/shard_map/ppermute | solution.py:27
  23.6 4.5 %collective-permute-start.9 = (bf16[32,1024]{1,0:T(8,128)(2,1)S(1)}, bf16[32,1024]{1,0:T(8,128)(2,1)S(1)}, u32[]{:S(2)}, u32[]{:S(2)}) collective-permute-start(bf16[32,1024]{1,0:T(8,128)(2,1)S(1)} %get-tuple-element.59), channel_id=1, source_target_pairs={{0,32},{8,40},{16,48},{24,56},{32,0},{40,8},{48,16},{56,24},{1,33}... | collective-permute-start | bytes 196616 | tf_op jit(solution)/shard_map/ppermute | solution.py:31
  28.1 3.2 %collective-permute-done.6.refs_6_ = bf16[1024,128]{1,0:T(8,128)(2,1)S(1)} collective-permute-done((bf16[1024,128]{1,0:T(8,128)(2,1)S(1)}, bf16[1024,128]{1,0:T(8,128)(2,1)S(1)}, u32[]{:S(2)}, u32[]{:S(2)}) %collective-permute-start.6) | collective-permute-done | bytes 262176 | tf_op jit(solution)/shard_map/ppermute | solution.py:27
  31.3 8.3 %collective-permute-start.12 = (bf16[1280,128]{1,0:T(8,128)(2,1)S(1)}, bf16[1280,128]{1,0:T(8,128)(2,1)S(1)}, u32[]{:S(2)}, u32[]{:S(2)}) collective-permute-start(bf16[1280,128]{1,0:T(8,128)(2,1)S(1)} %copy-done.4), channel_id=1, source_target_pairs={{0,6},{1,7},{2,4},{3,5},{4,2},{5,3},{6,0},{7,1},{64,199},{65,196},... | collective-permute-start | bytes 983048 | tf_op jit(solution)/shard_map/ppermute | solution.py:75
  41.7 4.3 %collective-permute-done.10.refs_3_ = bf16[1024,128]{1,0:T(8,128)(2,1)S(1)} collective-permute-done((bf16[1024,128]{1,0:T(8,128)(2,1)S(1)}, bf16[1024,128]{1,0:T(8,128)(2,1)S(1)}, u32[]{:S(2)}, u32[]{:S(2)}) %collective-permute-start.10) | collective-permute-done | bytes 262176 | tf_op jit(solution)/shard_map/ppermute | solution.py:27
  46.1 2.5 %collective-permute-done.11.refs_5_ = bf16[1024,128]{1,0:T(8,128)(2,1)S(1)} collective-permute-done((bf16[1024,128]{1,0:T(8,128)(2,1)S(1)}, bf16[1024,128]{1,0:T(8,128)(2,1)S(1)}, u32[]{:S(2)}, u32[]{:S(2)}) %collective-permute-start.11) | collective-permute-done | bytes 262176 | tf_op jit(solution)/shard_map/ppermute | solution.py:27
  49.0 7.7 %collective-permute-done.15.b_ref = bf16[32,1024]{1,0:T(8,128)(2,1)S(1)} collective-permute-done((bf16[32,1024]{1,0:T(8,128)(2,1)S(1)}, bf16[32,1024]{1,0:T(8,128)(2,1)S(1)}, u32[]{:S(2)}, u32[]{:S(2)}) %collective-permute-start.15) | collective-permute-done | bytes 65568 | tf_op jit(solution)/shard_map/ppermute | solution.py:31
  56.7 2.0 %collective-permute-done.13.refs_4_ = bf16[1024,128]{1,0:T(8,128)(2,1)S(1)} collective-permute-done((bf16[1024,128]{1,0:T(8,128)(2,1)S(1)}, bf16[1024,128]{1,0:T(8,128)(2,1)S(1)}, u32[]{:S(2)}, u32[]{:S(2)}) %collective-permute-start.13) | collective-permute-done | bytes 262176 | tf_op jit(solution)/shard_map/ppermute | solution.py:27
  58.7 1.6 %kv_product.1 = (bf16[576,128]{1,0:T(8,128)(2,1)S(1)}, bf16[576,128]{1,0:T(8,128)(2,1)S(1)}, bf16[576,128]{1,0:T(8,128)(2,1)S(1)}, bf16[576,128]{1,0:T(8,128)(2,1)S(1)}, bf16[1024,1024]{1,0:T(8,128)(2,1)S(1)}) custom-call(bf16[1024,128]{1,0:T(8,128)(2,1)S(1)} %copy-done.1, bf16[1024,128]{1,0:T(8,128)(2,1)S(1)} %collective-permute-done.refs_1_, ...), custom_call_target="tpu_custom_call" | custom-call | tf_op jit(solution)/shard_map/kv_product/pallas_call | solution.py:313
  61.9 1.9 %collective-permute-start.18 = (bf16[576,128]{1,0:T(8,128)(2,1)S(1)}, bf16[576,128]{1,0:T(8,128)(2,1)S(1)}, u32[]{:S(2)}, u32[]{:S(2)}) collective-permute-start(bf16[576,128]{1,0:T(8,128)(2,1)S(1)} %get-tuple-element.75), channel_id=1, source_target_pairs={{0,3},{1,0},{2,1},{3,2},{4,7},{5,4},{6,5},{7,6},{8,11},{9,8},{10,9... | collective-permute-start | bytes 442376 | tf_op jit(solution)/shard_map/ppermute | solution.py:51
  63.8 2.7 %q_product.1 = (bf16[1024,128]{1,0:T(8,128)(2,1)S(1)}, bf16[1024,128]{1,0:T(8,128)(2,1)S(1)}, bf16[1536,128]{1,0:T(8,128)(2,1)S(1)}, bf16[1536,128]{1,0:T(8,128)...) custom-call(bf16[1024,1024]{1,0:T(8,128)(2,1)S(1)} %get-tuple-element.70.hbuf, ...), custom_call_target="tpu_custom_call" | custom-call | tf_op jit(solution)/shard_map/q_product/pallas_call | solution.py:313
  66.5 2.2 %collective-permute-done.16.k1 = bf16[576,128]{1,0:T(8,128)(2,1)S(1)} collective-permute-done((bf16[576,128]{1,0:T(8,128)(2,1)S(1)}, bf16[576,128]{1,0:T(8,128)(2,1)S(1)}, u32[]{:S(2)}, u32[]{:S(2)}) %collective-permute-start.16) | collective-permute-done | bytes 147488 | tf_op jit(solution)/shard_map/ppermute | solution.py:51
  70.7 2.1 %collective-permute-start.25 = (bf16[1536,128]{1,0:T(8,128)(2,1)S(1)}, bf16[1536,128]{1,0:T(8,128)(2,1)S(1)}, u32[]{:S(2)}, u32[]{:S(2)}) collective-permute-start(bf16[1536,128]{1,0:T(8,128)(2,1)S(1)} %get-tuple-element.85), channel_id=1, source_target_pairs={{0,2},{1,3},{2,0},{3,1},{4,6},{5,7},{6,4},{7,5},{8,10},{9,11},{10,... | collective-permute-start | bytes 1179656 | tf_op jit(solution)/shard_map/ppermute | solution.py:51
  74.3 1.7 %collective-permute-start.27 = (bf16[1536,128]{1,0:T(8,128)(2,1)S(1)}, bf16[1536,128]{1,0:T(8,128)(2,1)S(1)}, u32[]{:S(2)}, u32[]{:S(2)}) collective-permute-start(bf16[1536,128]{1,0:T(8,128)(2,1)S(1)} %get-tuple-element.87), channel_id=1, source_target_pairs={{0,3},{1,0},{2,1},{3,2},{4,7},{5,4},{6,5},{7,6},{8,11},{9,8},{10,9... | collective-permute-start | bytes 1179656 | tf_op jit(solution)/shard_map/ppermute | solution.py:51
  76.1 5.2 %collective-permute-done.20.b_ref = f32[64,128]{1,0:T(8,128)S(1)} collective-permute-done((f32[64,128]{1,0:T(8,128)S(1)}, f32[64,128]{1,0:T(8,128)S(1)}, u32[]{:S(2)}, u32[]{:S(2)}) %collective-permute-start.20) | collective-permute-done | bytes 32800 | tf_op jit(solution)/shard_map/ppermute | solution.py:31
  81.4 3.7 %collective-permute-done.21.b_ref = f32[64,128]{1,0:T(8,128)S(1)} collective-permute-done((f32[64,128]{1,0:T(8,128)S(1)}, f32[64,128]{1,0:T(8,128)S(1)}, u32[]{:S(2)}, u32[]{:S(2)}) %collective-permute-start.21) | collective-permute-done | bytes 32800 | tf_op jit(solution)/shard_map/ppermute | solution.py:39
  88.6 2.9 %collective-permute-done.26.b2 = bf16[1536,128]{1,0:T(8,128)(2,1)S(1)} collective-permute-done((bf16[1536,128]{1,0:T(8,128)(2,1)S(1)}, bf16[1536,128]{1,0:T(8,128)(2,1)S(1)}, u32[]{:S(2)}, u32[]{:S(2)}) %collective-permute-start.26) | collective-permute-done | bytes 393248 | tf_op jit(solution)/shard_map/ppermute | solution.py:51
  94.8 4.2 %collective-permute-done.28.refs_5_ = bf16[768,128]{1,0:T(8,128)(2,1)S(1)} collective-permute-done((bf16[768,128]{1,0:T(8,128)(2,1)S(1)}, bf16[768,128]{1,0:T(8,128)(2,1)S(1)}, u32[]{:S(2)}, u32[]{:S(2)}) %collective-permute-start.28) | collective-permute-done | bytes 196640 | tf_op jit(solution)/shard_map/ppermute | solution.py:39
  100.5 5.2 %attention.1 = bf16[1024,128]{1,0:T(8,128)(2,1)} custom-call(s32[8]{0:T(128)S(1)} %copy-done.3, s32[1024]{0:T(1024)S(1)} %copy-done.2, f32[256,128]{1,0:T(8,128)S(1)} %get-tuple-element.80.refs_0_, bf16[832,128]{1,0:T(8,128)(2,1)S(1)} %collective-permute-done.22.refs_1_, bf16[832,128]{1,0:T(8,128)(2,1)S(1)} %collective-permute-done.23.refs_2_, ...), custom_call_target="tpu_custom_call" | custom-call | tf_op jit(solution)/shard_map/attention/pallas_call | solution.py:313
  (59 shorter events, 21.0 us)
Async XLA Ops:
  0.0 13.9 %collective-permute-start.1 = (bf16[1024,128]{1,0:T(8,128)(2,1)}, bf16[1024,128]{1,0:T(8,128)(2,1)S(1)}, u32[]{:S(2)}, u32[]{:S(2)}) collective-permute-start(bf16[1024,128]{1,0:T(8,128)(2,1)} %refs_0_.1), channel_id=1, source_target_pairs={{0,8},{8,16},{16,24},{24,32},{32,40},{40,48},{48,56},{56,0},{1,9},... | collective-permute-start | bytes 786440 | tf_op jit(solution)/shard_map/ppermute | solution.py:27
  1.9 12.0 %collective-permute-start = (bf16[1024,128]{1,0:T(8,128)(2,1)}, bf16[1024,128]{1,0:T(8,128)(2,1)S(1)}, u32[]{:S(2)}, u32[]{:S(2)}) collective-permute-start(bf16[1024,128]{1,0:T(8,128)(2,1)} %refs_0_.1), channel_id=1, source_target_pairs={{0,56},{8,0},{16,8},{24,16},{32,24},{40,32},{48,40},{56,48},{1,57}... | collective-permute-start | bytes 786440 | tf_op jit(solution)/shard_map/ppermute | solution.py:27
  9.5 9.6 %collective-permute-start.4 = (bf16[16,64,128]{2,1,0:T(8,128)(2,1)}, bf16[16,64,128]{2,1,0:T(8,128)(2,1)S(1)}, u32[]{:S(2)}, u32[]{:S(2)}) collective-permute-start(bf16[16,64,128]{2,1,0:T(8,128)(2,1)} %get-tuple-element.52), channel_id=1, source_target_pairs={{0,128},{128,0},{1,129},{129,1},{2,130},{130,2},{3,131},{131,3},{4... | collective-permute-start | bytes 786440 | tf_op jit(solution)/shard_map/ppermute | solution.py:47
  11.7 9.1 %collective-permute-start.2 = (bf16[1280,128]{1,0:T(8,128)(2,1)}, bf16[1280,128]{1,0:T(8,128)(2,1)S(1)}, u32[]{:S(2)}, u32[]{:S(2)}) collective-permute-start(bf16[1280,128]{1,0:T(8,128)(2,1)} %get-tuple-element.50), channel_id=1, source_target_pairs={{0,1},{1,2},{2,3},{3,0},{4,5},{5,6},{6,7},{7,4},{64,67},{65,64},{6... | collective-permute-start | bytes 983048 | tf_op jit(solution)/shard_map/ppermute | solution.py:75
  13.2 7.5 %collective-permute-start.3 = (bf16[1280,128]{1,0:T(8,128)(2,1)}, bf16[1280,128]{1,0:T(8,128)(2,1)S(1)}, u32[]{:S(2)}, u32[]{:S(2)}) collective-permute-start(bf16[1280,128]{1,0:T(8,128)(2,1)} %get-tuple-element.51), channel_id=1, source_target_pairs={{64,66},{65,67},{66,64},{67,65},{68,70},{69,71},{70,68},{71,69},{1... | collective-permute-start | bytes 983048 | tf_op jit(solution)/shard_map/ppermute | solution.py:75
  20.1 19.5 %collective-permute-start.7 = (bf16[1280,128]{1,0:T(8,128)(2,1)}, bf16[1280,128]{1,0:T(8,128)(2,1)S(1)}, u32[]{:S(2)}, u32[]{:S(2)}) collective-permute-start(bf16[1280,128]{1,0:T(8,128)(2,1)} %get-tuple-element.57), channel_id=1, source_target_pairs={{0,4},{1,5},{2,6},{3,7},{4,0},{5,1},{6,2},{7,3},{64,197},{65,198},... | collective-permute-start | bytes 983048 | tf_op jit(solution)/shard_map/ppermute | solution.py:75
  20.8 7.3 %collective-permute-start.5 = (bf16[1024,128]{1,0:T(8,128)(2,1)S(1)}, bf16[1024,128]{1,0:T(8,128)(2,1)S(1)}, u32[]{:S(2)}, u32[]{:S(2)}) collective-permute-start(bf16[1024,128]{1,0:T(8,128)(2,1)S(1)} %collective-permute-done.refs_1_), channel_id=1, source_target_pairs={{0,56},{8,0},{16,8},{24,16},{32,24},{40,32},{48,40},{56,48},{1,57}... | collective-permute-start | bytes 786440 | tf_op jit(solution)/shard_map/ppermute | solution.py:27
  22.6 8.6 %collective-permute-start.6 = (bf16[1024,128]{1,0:T(8,128)(2,1)S(1)}, bf16[1024,128]{1,0:T(8,128)(2,1)S(1)}, u32[]{:S(2)}, u32[]{:S(2)}) collective-permute-start(bf16[1024,128]{1,0:T(8,128)(2,1)S(1)} %collective-permute-done.1.refs_7_), channel_id=1, source_target_pairs={{0,8},{8,16},{16,24},{24,32},{32,40},{40,48},{48,56},{56,0},{1,9},... | collective-permute-start | bytes 786440 | tf_op jit(solution)/shard_map/ppermute | solution.py:27
  23.6 16.0 %collective-permute-start.9 = (bf16[32,1024]{1,0:T(8,128)(2,1)S(1)}, bf16[32,1024]{1,0:T(8,128)(2,1)S(1)}, u32[]{:S(2)}, u32[]{:S(2)}) collective-permute-start(bf16[32,1024]{1,0:T(8,128)(2,1)S(1)} %get-tuple-element.59), channel_id=1, source_target_pairs={{0,32},{8,40},{16,48},{24,56},{32,0},{40,8},{48,16},{56,24},{1,33}... | collective-permute-start | bytes 196616 | tf_op jit(solution)/shard_map/ppermute | solution.py:31
  31.3 17.4 %collective-permute-start.12 = (bf16[1280,128]{1,0:T(8,128)(2,1)S(1)}, bf16[1280,128]{1,0:T(8,128)(2,1)S(1)}, u32[]{:S(2)}, u32[]{:S(2)}) collective-permute-start(bf16[1280,128]{1,0:T(8,128)(2,1)S(1)} %copy-done.4), channel_id=1, source_target_pairs={{0,6},{1,7},{2,4},{3,5},{4,2},{5,3},{6,0},{7,1},{64,199},{65,196},... | collective-permute-start | bytes 983048 | tf_op jit(solution)/shard_map/ppermute | solution.py:75
  41.0 7.6 %collective-permute-start.11 = (bf16[1024,128]{1,0:T(8,128)(2,1)S(1)}, bf16[1024,128]{1,0:T(8,128)(2,1)S(1)}, u32[]{:S(2)}, u32[]{:S(2)}) collective-permute-start(bf16[1024,128]{1,0:T(8,128)(2,1)S(1)} %collective-permute-done.6.refs_6_), channel_id=1, source_target_pairs={{0,8},{8,16},{16,24},{24,32},{32,40},{40,48},{48,56},{56,0},{1,9},... | collective-permute-start | bytes 786440 | tf_op jit(solution)/shard_map/ppermute | solution.py:27
  48.7 10.0 %collective-permute-start.14 = (bf16[4,1280,128]{2,1,0:T(8,128)(2,1)S(1)}, bf16[4,1280,128]{2,1,0:T(8,128)(2,1)S(1)}, u32[]{:S(2)}, u32[]{:S(2)}) collective-permute-start(bf16[4,1280,128]{2,1,0:T(8,128)(2,1)S(1)} %stack.13), channel_id=1, source_target_pairs={{0,64},{64,0},{1,65},{65,1},{2,66},{66,2},{3,67},{67,3},{4,68},{68... | collective-permute-start | bytes 3932168 | tf_op jit(solution)/shard_map/ppermute | solution.py:43
  48.8 9.9 %collective-permute-start.13 = (bf16[1024,128]{1,0:T(8,128)(2,1)S(1)}, bf16[1024,128]{1,0:T(8,128)(2,1)S(1)}, u32[]{:S(2)}, u32[]{:S(2)}) collective-permute-start(bf16[1024,128]{1,0:T(8,128)(2,1)S(1)} %collective-permute-done.11.refs_5_), channel_id=1, source_target_pairs={{0,8},{8,16},{16,24},{24,32},{32,40},{40,48},{48,56},{56,0},{1,9},... | collective-permute-start | bytes 786440 | tf_op jit(solution)/shard_map/ppermute | solution.py:27
  48.9 7.8 %collective-permute-start.15 = (bf16[32,1024]{1,0:T(8,128)(2,1)S(1)}, bf16[32,1024]{1,0:T(8,128)(2,1)S(1)}, u32[]{:S(2)}, u32[]{:S(2)}) collective-permute-start(bf16[32,1024]{1,0:T(8,128)(2,1)S(1)} %get-tuple-element.69), channel_id=1, source_target_pairs={{0,8},{8,0},{16,24},{24,16},{32,40},{40,32},{48,56},{56,48},{1,9},... | collective-permute-start | bytes 196616 | tf_op jit(solution)/shard_map/ppermute | solution.py:31
  60.4 8.4 %collective-permute-start.16 = (bf16[576,128]{1,0:T(8,128)(2,1)S(1)}, bf16[576,128]{1,0:T(8,128)(2,1)S(1)}, u32[]{:S(2)}, u32[]{:S(2)}) collective-permute-start(bf16[576,128]{1,0:T(8,128)(2,1)S(1)} %get-tuple-element.73), channel_id=1, source_target_pairs={{0,2},{1,3},{2,0},{3,1},{4,6},{5,7},{6,4},{7,5},{8,10},{9,11},{10,... | collective-permute-start | bytes 442376 | tf_op jit(solution)/shard_map/ppermute | solution.py:51
  60.5 9.8 %collective-permute-start.17 = (bf16[576,128]{1,0:T(8,128)(2,1)S(1)}, bf16[576,128]{1,0:T(8,128)(2,1)S(1)}, u32[]{:S(2)}, u32[]{:S(2)}) collective-permute-start(bf16[576,128]{1,0:T(8,128)(2,1)S(1)} %get-tuple-element.74), channel_id=1, source_target_pairs={{0,1},{1,2},{2,3},{3,0},{4,5},{5,6},{6,7},{7,4},{8,9},{9,10},{10,1... | collective-permute-start | bytes 442376 | tf_op jit(solution)/shard_map/ppermute | solution.py:51
  61.9 8.4 %collective-permute-start.18 = (bf16[576,128]{1,0:T(8,128)(2,1)S(1)}, bf16[576,128]{1,0:T(8,128)(2,1)S(1)}, u32[]{:S(2)}, u32[]{:S(2)}) collective-permute-start(bf16[576,128]{1,0:T(8,128)(2,1)S(1)} %get-tuple-element.75), channel_id=1, source_target_pairs={{0,3},{1,0},{2,1},{3,2},{4,7},{5,4},{6,5},{7,6},{8,11},{9,8},{10,9... | collective-permute-start | bytes 442376 | tf_op jit(solution)/shard_map/ppermute | solution.py:51
  70.4 14.7 %collective-permute-start.19 = (bf16[1536,128]{1,0:T(8,128)(2,1)S(1)}, bf16[1536,128]{1,0:T(8,128)(2,1)S(1)}, u32[]{:S(2)}, u32[]{:S(2)}) collective-permute-start(bf16[1536,128]{1,0:T(8,128)(2,1)S(1)} %get-tuple-element.77), channel_id=1, source_target_pairs={{0,4},{4,0},{1,5},{5,1},{2,6},{6,2},{3,7},{7,3},{8,12},{12,8},{9,1... | collective-permute-start | bytes 1179656 | tf_op jit(solution)/shard_map/ppermute | solution.py:39
  70.7 16.5 %collective-permute-start.25 = (bf16[1536,128]{1,0:T(8,128)(2,1)S(1)}, bf16[1536,128]{1,0:T(8,128)(2,1)S(1)}, u32[]{:S(2)}, u32[]{:S(2)}) collective-permute-start(bf16[1536,128]{1,0:T(8,128)(2,1)S(1)} %get-tuple-element.85), channel_id=1, source_target_pairs={{0,2},{1,3},{2,0},{3,1},{4,6},{5,7},{6,4},{7,5},{8,10},{9,11},{10,... | collective-permute-start | bytes 1179656 | tf_op jit(solution)/shard_map/ppermute | solution.py:51
  72.8 18.7 %collective-permute-start.26 = (bf16[1536,128]{1,0:T(8,128)(2,1)S(1)}, bf16[1536,128]{1,0:T(8,128)(2,1)S(1)}, u32[]{:S(2)}, u32[]{:S(2)}) collective-permute-start(bf16[1536,128]{1,0:T(8,128)(2,1)S(1)} %get-tuple-element.86), channel_id=1, source_target_pairs={{0,1},{1,2},{2,3},{3,0},{4,5},{5,6},{6,7},{7,4},{8,9},{9,10},{10,1... | collective-permute-start | bytes 1179656 | tf_op jit(solution)/shard_map/ppermute | solution.py:51
  74.3 18.5 %collective-permute-start.27 = (bf16[1536,128]{1,0:T(8,128)(2,1)S(1)}, bf16[1536,128]{1,0:T(8,128)(2,1)S(1)}, u32[]{:S(2)}, u32[]{:S(2)}) collective-permute-start(bf16[1536,128]{1,0:T(8,128)(2,1)S(1)} %get-tuple-element.87), channel_id=1, source_target_pairs={{0,3},{1,0},{2,1},{3,2},{4,7},{5,4},{6,5},{7,6},{8,11},{9,8},{10,9... | collective-permute-start | bytes 1179656 | tf_op jit(solution)/shard_map/ppermute | solution.py:51
  85.3 13.7 %collective-permute-start.22 = (bf16[832,128]{1,0:T(8,128)(2,1)S(1)}, bf16[832,128]{1,0:T(8,128)(2,1)S(1)}, u32[]{:S(2)}, u32[]{:S(2)}) collective-permute-start(bf16[832,128]{1,0:T(8,128)(2,1)S(1)} %get-tuple-element.81), channel_id=1, source_target_pairs={{0,1},{1,2},{2,3},{3,0},{4,5},{5,6},{6,7},{7,4},{8,9},{9,10},{10,1... | collective-permute-start | bytes 638984 | tf_op jit(solution)/shard_map/ppermute | solution.py:51
  85.7 14.9 %collective-permute-start.23 = (bf16[832,128]{1,0:T(8,128)(2,1)S(1)}, bf16[832,128]{1,0:T(8,128)(2,1)S(1)}, u32[]{:S(2)}, u32[]{:S(2)}) collective-permute-start(bf16[832,128]{1,0:T(8,128)(2,1)S(1)} %get-tuple-element.82), channel_id=1, source_target_pairs={{0,2},{1,3},{2,0},{3,1},{4,6},{5,7},{6,4},{7,5},{8,10},{9,11},{10,... | collective-permute-start | bytes 638984 | tf_op jit(solution)/shard_map/ppermute | solution.py:51
  87.2 13.3 %collective-permute-start.24 = (bf16[832,128]{1,0:T(8,128)(2,1)S(1)}, bf16[832,128]{1,0:T(8,128)(2,1)S(1)}, u32[]{:S(2)}, u32[]{:S(2)}) collective-permute-start(bf16[832,128]{1,0:T(8,128)(2,1)S(1)} %get-tuple-element.83), channel_id=1, source_target_pairs={{0,3},{1,0},{2,1},{3,2},{4,7},{5,4},{6,5},{7,6},{8,11},{9,8},{10,9... | collective-permute-start | bytes 638984 | tf_op jit(solution)/shard_map/ppermute | solution.py:51
  (10 other events, 157.4 us)
